TPU v7x, 32 devices: a whole 2x2x4 slice. The times are simulated.
32 devices in a mesh: worker: 4 (over x, core), outer: 4 (over z), mp: 2 (over y).
Axes of the slice: x: 2, y: 2, z: 4, core: 2. Of those that a mesh axis runs over, the one named last changes fastest.
Arguments:
- grads: float32 [4, 4, 3584, 4096], P('worker', 'outer', None, 'mp'), as said below
- center: float32 [3584, 4096], P(('worker', 'outer'), 'mp'), may hold values from -6 to 6
- radius: float32 [1], replicated, may hold values from 1.5 to 3.5
Outputs:
- center_out: float32 [3584, 4096], P(('worker', 'outer'), 'mp')
Inputs may be any that keep to these rules, and one draw needn't show every extreme that they name: `grads`: finite values.
All inputs are finite; a program needn't handle non-finite values.
Results may differ from a plain program's by a relative error of at most 0.0001.
Values sent between devices are 32-bit elements; how exact they have to be, the bound alone decides.
No kernel may reach another device: no remote copies, remote signals or barrier semaphores. Data moves between devices by JAX's collectives and lax.ppermute only.
A program may use at most 192 MiB of HBM per device.

v0:
```python
import math

import jax
import jax.numpy as jnp
from jax import lax
from jax.sharding import PartitionSpec as P


D = 3584
ITERS = 2
KVW = 4096
AXES = ("worker", "outer", "mp")
LINE = 4
TILE = 8
SPREAD = 0.4

epsilon = 1e-06


def sum_over_devices(value):
    for axis in AXES:
        size = lax.axis_size(axis)
        step = 1
        while step < size:
            value = value + lax.ppermute(value, axis, [(i, i ^ step) for i in range(size)])
            step *= 2
    return value


def send(value, pairs, axis="outer"):
    return lax.ppermute(value, axis, pairs)


TO_MIDS = [(0, 1), (3, 2)]
ACROSS = [(1, 2), (2, 1)]
TO_ENDS = [(1, 0), (2, 3)]


def tie(value, earlier):
    return lax.optimization_barrier((value, earlier))[0]


def split(rows, outers):
    cut = int(rows * SPREAD) // TILE * TILE
    tiles = (rows - cut) // TILE
    if outers != LINE or (rows - cut) % TILE or tiles < 8:
        return None
    body = tiles - 4
    sizes = [1, 1] + [2] * (body // 2) + [1] * (body % 2) + [1, 1]
    return cut, [size * TILE for size in sizes]


def spread_only(mine, center, radius_total, worker_count):
    own_rows = center
    gathered = lax.all_to_all(mine, ("worker", "outer"), split_axis=0, concat_axis=0, tiled=True)
    for _ in range(ITERS):
        difference = gathered - own_rows[None]
        norm_sq = sum_over_devices(jnp.sum(difference * difference, axis=(1, 2)))
        factor = jnp.minimum(1.0, radius_total * lax.rsqrt(norm_sq + epsilon))
        own_rows = own_rows + jnp.sum(factor[:, None, None] * difference, axis=0) / worker_count
    return own_rows


def on_device(grads, center, radius):
    workers, outers = lax.axis_size("worker"), lax.axis_size("outer")
    worker_count = workers * outers
    radius_total = radius[0] * math.sqrt(D * KVW)
    rows, columns = center.shape
    mine = grads.reshape(worker_count, rows, columns)
    plan = split(rows, outers)
    if plan is None:
        return spread_only(mine, center, radius_total, worker_count)
    cut, sizes = plan
    rest = rows - cut

    w, o = lax.axis_index("worker"), lax.axis_index("outer")
    is_end = (o == 0) | (o == LINE - 1)
    is_low = o < LINE // 2

    def line_rows(source, worker):
        return lax.dynamic_slice(source, (worker * outers, cut, 0), (outers, rest, columns))

    tail = center[cut:]
    pair = send(tail, [(i, i ^ 1) for i in range(LINE)])
    steps = list(range(workers // 2, workers)) + list(range(1, workers // 2)) + [0]
    held, source = [], mine
    for step in steps:
        sent = line_rows(source, w ^ step)
        source = tie(source, sent)
        if step:
            swap = [(i, i ^ step) for i in range(workers)]
            sent = send(sent, swap, "worker")
        held.append(sent)
    spread = lax.all_to_all(
        mine[:, :cut], ("worker", "outer"), split_axis=0, concat_axis=0, tiled=True
    )
    first = (o % 2) == 0
    near = jnp.where(first, jnp.stack([tail, pair]), jnp.stack([pair, tail]))
    crossed = send(near, ACROSS)
    far = jnp.where(is_end, send(crossed, TO_ENDS), crossed)
    line_v = jnp.where(is_low, jnp.concatenate([near, far]), jnp.concatenate([far, near]))
    spread_v = center[:cut]

    places = [(w ^ step) * outers + o for step in steps]
    numbers = jnp.arange(worker_count)

    def factors(spread_sq, line_sq):
        both = spread_sq
        for place, value in zip(places, line_sq):
            both = both + jnp.where(numbers == place, value, 0.0)
        norm_sq = sum_over_devices(both)
        factor = jnp.minimum(1.0, radius_total * lax.rsqrt(norm_sq + epsilon))
        return factor, [jnp.sum(jnp.where(numbers == place, factor, 0.0)) for place in places]

    def spread_norms(v):
        difference = spread - v[None]
        return jnp.sum(difference * difference, axis=(1, 2))

    def spread_update(v, factor):
        return v + jnp.sum(factor[:, None, None] * (spread - v[None]), axis=0) / worker_count

    def line_step(values, v, factor):
        return sum(factor[i] * (value - v) for i, value in enumerate(values))

    line_sq, v = [None] * workers, line_v
    for place in reversed(range(workers)):
        line_sq[place] = jnp.sum(jnp.square(held[place] - v))
        v = tie(v, line_sq[place])
    factor, line_factor = factors(spread_norms(spread_v), line_sq)

    starts = [sum(sizes[:i]) for i in range(len(sizes))]
    pieces, sums = [], [[0.0] * workers]
    for chunk, (start, size) in enumerate(zip(starts, sizes)):
        part = slice(start, start + size)
        values, v = [value[:, part] for value in held], line_v[:, part]
        own = line_step(values, v, line_factor)
        own = own + send(own, TO_MIDS)
        own = own + send(own, ACROSS)
        if chunk >= 3:
            own = tie(own, sums[chunk - 2])
        own = jnp.where(is_end, send(own, TO_ENDS), own)
        v = v + own / worker_count
        sums.append(
            [
                total + jnp.sum(jnp.square(value - v), axis=(0, 1))
                for total, value in zip(sums[-1], values)
            ]
        )
        pieces.append(v)
    spread_v = spread_update(spread_v, factor)
    line_v = jnp.concatenate(pieces, axis=1)
    factor, line_factor = factors(spread_norms(spread_v), [jnp.sum(total) for total in sums[-1]])

    def at(value, place):
        index = jnp.where(is_low, LINE - 1 - place, place)
        return lax.dynamic_index_in_dim(value, index, 0, keepdims=False)

    block, v = [], line_v
    for place in range(LINE):
        block.append(line_step([at(value, place) for value in held], at(v, place), line_factor))
        v = tie(v, block[place])
    arrived = [send(block[place], TO_MIDS) for place in range(3)]
    passed = [send(block[place] + arrived[place], ACROSS) for place in range(2)]
    end_sum = block[3] + send(block[3] + passed[0], TO_ENDS)
    mid_sum = block[2] + arrived[2] + passed[1]
    own_v = lax.dynamic_index_in_dim(line_v, o, 0, keepdims=False)
    own_v = own_v + jnp.where(is_end, end_sum, mid_sum) / worker_count
    return jnp.concatenate([spread_update(spread_v, factor), own_v])


def solution(mesh):
    in_specs = (P("worker", "outer", None, "mp"), P(("worker", "outer"), "mp"), P())
    out_specs = P(("worker", "outer"), "mp")

    return jax.shard_map(on_device, mesh=mesh, in_specs=in_specs, out_specs=out_specs, check_vma=False)
```

profile of v0, /device:TPU:0, one launch (start us, length us, event | category | flops | bytes accessed | tf_op | source)
XLA Modules:
  0.0 821.3 jit_solution(8351006940402844710)
XLA Ops:
  0.0 10.5 %slice.232 = f32[16,88,2048]{2,1,0:T(8,128)} slice(f32[16,224,2048]{2,1,0:T(8,128)} %bitcast.24), slice={[0:16], [0:88], [0:2048]} | slice | bytes 23068672 | tf_op jit(solution)/shard_map/slice | solution.py:95
  10.5 7.6 all-to-all-start
  21.2 207.4 %collective-permute-done.1 = f32[136,2048]{1,0:T(8,128)S(1)} collective-permute-done((f32[136,2048]{1,0:T(8,128)}, f32[136,2048]{1,0:T(8,128)S(1)}, u32[]{:S(2)}, u32[]{:S(2)}) %collective-permute-start.1) | collective-permute-done | bytes 1114144 | tf_op jit(solution)/shard_map/ppermute | solution.py:31
  231.4 2.1 collective-permute-start.2
  233.5 4.8 constant_dynamic-slice_fusion.2
  238.4 4.8 constant_dynamic-slice_fusion.1
  243.2 4.9 constant_dynamic-slice_fusion
  253.4 114.0 %collective-permute-done.3 = f32[2,136,2048]{2,1,0:T(8,128)} collective-permute-done((f32[2,136,2048]{2,1,0:T(8,128)}, f32[2,136,2048]{2,1,0:T(8,128)}, u32[]{:S(2)}, u32[]{:S(2)}) %collective-permute-start.3) | collective-permute-done | bytes 2228256 | tf_op jit(solution)/shard_map/ppermute | solution.py:31
  369.3 4.0 multiply_reduce_fusion.7
  373.2 5.6 multiply_reduce_fusion.6
  378.9 4.1 multiply_reduce_fusion.5
  383.0 67.1 %collective-permute-done = f32[4,136,2048]{2,1,0:T(8,128)} collective-permute-done((f32[4,136,2048]{2,1,0:T(8,128)}, f32[4,136,2048]{2,1,0:T(8,128)}, u32[]{:S(2)}, u32[]{:S(2)}) %collective-permute-start) | collective-permute-done | bytes 4456480 | tf_op jit(solution)/shard_map/ppermute | solution.py:31
  450.1 4.0 multiply_reduce_fusion.4
  454.1 5.6 multiply_reduce_fusion.3
  459.7 2.5 select_add_fusion.1
  463.5 2.5 fusion.12
  469.7 3.6 collective-permute-done.8
  473.2 4.5 collective-permute-done.9
  479.2 2.0 collective-permute-done.10
  482.0 5.4 multiply_add_fusion.20
  489.3 5.5 multiply_add_fusion.14
  496.1 3.8 multiply_add_fusion.24
  501.2 4.9 multiply_add_fusion.18
  507.6 5.2 multiply_add_fusion.6
  514.9 5.2 multiply_add_fusion.8
  520.1 6.8 collective-permute-start.26
  527.0 2.1 collective-permute-start.17
  539.5 19.5 %collective-permute-done.38 = f32[4,8,2048]{2,1,0:T(8,128)} collective-permute-done((f32[4,8,2048]{2,1,0:T(8,128)}, f32[4,8,2048]{2,1,0:T(8,128)}, u32[]{:S(2)}, u32[]{:S(2)}) %collective-permute-start.38) | collective-permute-done | bytes 262176 | tf_op jit(solution)/shard_map/ppermute | solution.py:31
  559.0 4.4 collective-permute-start.29
  564.7 4.4 collective-permute-start.32
  571.8 6.0 multiply_reduce_fusion.2
  588.5 9.1 %collective-permute-done.16 = f32[4,8,2048]{2,1,0:T(8,128)S(1)} collective-permute-done((f32[4,8,2048]{2,1,0:T(8,128)S(1)}, f32[4,8,2048]{2,1,0:T(8,128)S(1)}, u32[]{:S(2)}, u32[]{:S(2)}) %collective-permute-start.16) | collective-permute-done | bytes 262176 | tf_op jit(solution)/shard_map/ppermute | solution.py:31
  599.7 2.0 multiply_reduce_fusion.50
  607.3 5.6 multiply_reduce_fusion.1
  613.3 27.0 %collective-permute-done.19 = f32[4,16,2048]{2,1,0:T(8,128)S(1)} collective-permute-done((f32[4,16,2048]{2,1,0:T(8,128)S(1)}, f32[4,16,2048]{2,1,0:T(8,128)S(1)}, u32[]{:S(2)}, u32[]{:S(2)}) %collective-permute-start.19) | collective-permute-done | bytes 524320 | tf_op jit(solution)/shard_map/ppermute | solution.py:31
  640.3 5.6 collective-permute-done.22
  645.9 6.8 collective-permute-done.25
  652.7 4.3 multiply_reduce_fusion.29
  661.2 12.5 %collective-permute-done.28 = f32[4,16,2048]{2,1,0:T(8,128)S(1)} collective-permute-done((f32[4,16,2048]{2,1,0:T(8,128)S(1)}, f32[4,16,2048]{2,1,0:T(8,128)S(1)}, u32[]{:S(2)}, u32[]{:S(2)}) %collective-permute-start.28) | collective-permute-done | bytes 524320 | tf_op jit(solution)/shard_map/ppermute | solution.py:31
  673.7 5.9 collective-permute-done.31
  679.6 7.6 collective-permute-done.34
  687.2 4.3 multiply_reduce_fusion.17
  695.5 4.3 collective-permute-done.37
  699.8 2.8 collective-permute-done.40
  702.6 2.8 collective-permute-done.43
  705.4 2.6 multiply_reduce_fusion.37
  710.6 2.6 select_add_fusion
  714.4 2.6 fusion.11
  720.6 3.5 collective-permute-done.46
  724.8 3.8 collective-permute-done.47
  730.2 2.0 collective-permute-done.48
  732.9 5.4 add_bitcast_fusion.2
  738.2 2.9 collective-permute-start.49
  741.1 5.7 add_bitcast_fusion.1
  746.8 2.3 collective-permute-start.53
  749.1 15.9 %collective-permute-done.49 = f32[136,2048]{1,0:T(8,128)} collective-permute-done((f32[136,2048]{1,0:T(8,128)S(1)}, f32[136,2048]{1,0:T(8,128)}, u32[]{:S(2)}, u32[]{:S(2)}) %collective-permute-start.49) | collective-permute-done | bytes 1114144 | tf_op jit(solution)/shard_map/ppermute | solution.py:31
  765.1 2.4 add.676
  768.2 5.7 add_bitcast_fusion
  773.9 6.9 collective-permute-start.52
  780.8 8.1 collective-permute-done.53
  791.1 5.8 bitcast_add_fusion.1
  798.2 6.0 multiply_reduce_fusion
  804.3 3.7 collective-permute-done.52
  808.0 10.0 %collective-permute-done.51 = f32[136,2048]{1,0:T(8,128)S(1)} collective-permute-done((f32[136,2048]{1,0:T(8,128)S(1)}, f32[136,2048]{1,0:T(8,128)S(1)}, u32[]{:S(2)}, u32[]{:S(2)}) %collective-permute-start.51) | collective-permute-done | bytes 1114144 | tf_op jit(solution)/shard_map/ppermute | solution.py:31
  (180 shorter events, 86.3 us)
Async XLA Ops:
  10.5 443.7 %all-to-all-start = ((f32[16,88,2048]{2,1,0:T(8,128)}), f32[16,88,2048]{2,1,0:T(8,128)}, u32[]{:S(2)}, u32[]{:S(2)}) async-start(f32[16,88,2048]{2,1,0:T(8,128)} %slice.232), calls=%async_computation | async-start | bytes 23068672 | tf_op jit(solution)/shard_map/all_to_all | solution.py:94
  19.3 209.3 %collective-permute-start.1 = (f32[136,2048]{1,0:T(8,128)}, f32[136,2048]{1,0:T(8,128)S(1)}, u32[]{:S(2)}, u32[]{:S(2)}) collective-permute-start(f32[136,2048]{1,0:T(8,128)} %get-tuple-element.176), channel_id=1, source_target_pairs={{0,2},{2,0},{4,6},{6,4},{1,3},{3,1},{5,7},{7,5},{8,10},{10,8},{12,... | collective-permute-start | bytes 3342344 | tf_op jit(solution)/shard_map/ppermute | solution.py:31
  231.4 18.8 %collective-permute-start.2 = (f32[2,136,2048]{2,1,0:T(8,128)S(1)}, f32[2,136,2048]{2,1,0:T(8,128)}, u32[]{:S(2)}, u32[]{:S(2)}) collective-permute-start(f32[2,136,2048]{2,1,0:T(8,128)S(1)} %maximum_select_fusion.1), channel_id=1, source_target_pairs={{2,4},{4,2},{3,5},{5,3},{10,12},{12,10},{11,13},{13,11},{18,20},{2... | collective-permute-start | bytes 6684680 | tf_op jit(solution)/shard_map/ppermute | solution.py:31
  248.1 125.2 %collective-permute-start.4 = (f32[4,136,2048]{2,1,0:T(8,128)}, f32[4,136,2048]{2,1,0:T(8,128)}, u32[]{:S(2)}, u32[]{:S(2)}) collective-permute-start(f32[4,136,2048]{2,1,0:T(8,128)} %constant_dynamic-slice_fusion), channel_id=1, source_target_pairs={{0,8},{8,0},{16,24},{24,16},{1,9},{9,1},{17,25},{25,17},{2,10},{10... | collective-permute-start | bytes 13369352 | tf_op jit(solution)/shard_map/ppermute | solution.py:31
  248.1 130.8 %collective-permute-start.5 = (f32[4,136,2048]{2,1,0:T(8,128)}, f32[4,136,2048]{2,1,0:T(8,128)}, u32[]{:S(2)}, u32[]{:S(2)}) collective-permute-start(f32[4,136,2048]{2,1,0:T(8,128)} %constant_dynamic-slice_fusion.1), channel_id=1, source_target_pairs={{0,24},{8,16},{16,8},{24,0},{1,25},{9,17},{17,9},{25,1},{2,26},{10... | collective-permute-start | bytes 13369352 | tf_op jit(solution)/shard_map/ppermute | solution.py:31
  249.8 200.3 %collective-permute-start = (f32[4,136,2048]{2,1,0:T(8,128)}, f32[4,136,2048]{2,1,0:T(8,128)}, u32[]{:S(2)}, u32[]{:S(2)}) collective-permute-start(f32[4,136,2048]{2,1,0:T(8,128)} %constant_dynamic-slice_fusion.2), channel_id=1, source_target_pairs={{0,16},{8,24},{16,0},{24,8},{1,17},{9,25},{17,1},{25,9},{2,18},{10... | collective-permute-start | bytes 13369352 | tf_op jit(solution)/shard_map/ppermute | solution.py:31
  250.2 117.1 %collective-permute-start.3 = (f32[2,136,2048]{2,1,0:T(8,128)}, f32[2,136,2048]{2,1,0:T(8,128)}, u32[]{:S(2)}, u32[]{:S(2)}) collective-permute-start(f32[2,136,2048]{2,1,0:T(8,128)} %collective-permute-done.2), channel_id=1, source_target_pairs={{2,0},{4,6},{3,1},{5,7},{10,8},{12,14},{11,9},{13,15},{18,16},{20,... | collective-permute-start | bytes 6684680 | tf_op jit(solution)/shard_map/ppermute | solution.py:31
  373.2 76.9 %copy-start = (f32[4,136,2048]{2,1,0:T(8,128)}, f32[4,136,2048]{2,1,0:T(8,128)S(1)}, u32[]{:S(2)}) copy-start(f32[4,136,2048]{2,1,0:T(8,128)S(1)} %get-tuple-element.27) | copy-start | bytes 13369348
  462.3 1.2 collective-permute-start.6
  466.0 3.6 collective-permute-start.7
  469.7 3.6 collective-permute-start.8
  473.2 4.5 collective-permute-start.9
  477.7 3.6 collective-permute-start.10
  482.0 14.2 %copy-start.1 = (f32[4,136,2048]{2,1,0:T(8,128)S(1)}, f32[4,136,2048]{2,1,0:T(8,128)}, u32[]{:S(2)}) copy-start(f32[4,136,2048]{2,1,0:T(8,128)} %copy-done) | copy-start | bytes 13369348
  487.4 18.8 %copy-start.9 = (f32[4,8,2048]{2,1,0:T(8,128)}, f32[4,8,2048]{2,1,0:T(8,128)S(1)}, u32[]{:S(2)}) copy-start(f32[4,8,2048]{2,1,0:T(8,128)S(1)} %get-tuple-element.165) | copy-start | bytes 786436
  487.4 32.7 %collective-permute-start.35 = (f32[4,8,2048]{2,1,0:T(8,128)S(1)}, f32[4,8,2048]{2,1,0:T(8,128)S(1)}, u32[]{:S(2)}, u32[]{:S(2)}) collective-permute-start(f32[4,8,2048]{2,1,0:T(8,128)S(1)} %get-tuple-element.165), channel_id=1, source_target_pairs={{0,2},{6,4},{1,3},{7,5},{8,10},{14,12},{9,11},{15,13},{16,18},{22,... | collective-permute-start | bytes 786440 | tf_op jit(solution)/shard_map/ppermute | solution.py:31
  494.8 18.0 %copy-start.6 = (f32[4,16,2048]{2,1,0:T(8,128)}, f32[4,16,2048]{2,1,0:T(8,128)S(1)}, u32[]{:S(2)}) copy-start(f32[4,16,2048]{2,1,0:T(8,128)S(1)} %get-tuple-element.174) | copy-start | bytes 1572868
  494.8 34.3 %collective-permute-start.20 = (f32[4,16,2048]{2,1,0:T(8,128)S(1)}, f32[4,16,2048]{2,1,0:T(8,128)S(1)}, u32[]{:S(2)}, u32[]{:S(2)}) collective-permute-start(f32[4,16,2048]{2,1,0:T(8,128)S(1)} %get-tuple-element.174), channel_id=1, source_target_pairs={{0,2},{6,4},{1,3},{7,5},{8,10},{14,12},{9,11},{15,13},{16,18},{22,... | collective-permute-start | bytes 1572872 | tf_op jit(solution)/shard_map/ppermute | solution.py:31
  499.9 14.3 %collective-permute-start.11 = (f32[4,8,2048]{2,1,0:T(8,128)S(1)}, f32[4,8,2048]{2,1,0:T(8,128)S(1)}, u32[]{:S(2)}, u32[]{:S(2)}) collective-permute-start(f32[4,8,2048]{2,1,0:T(8,128)S(1)} %multiply_add_fusion.24), channel_id=1, source_target_pairs={{0,2},{6,4},{1,3},{7,5},{8,10},{14,12},{9,11},{15,13},{16,18},{22,... | collective-permute-start | bytes 786440 | tf_op jit(solution)/shard_map/ppermute | solution.py:31
  506.2 20.8 %collective-permute-start.14 = (f32[4,8,2048]{2,1,0:T(8,128)S(1)}, f32[4,8,2048]{2,1,0:T(8,128)S(1)}, u32[]{:S(2)}, u32[]{:S(2)}) collective-permute-start(f32[4,8,2048]{2,1,0:T(8,128)S(1)} %get-tuple-element.168), channel_id=1, source_target_pairs={{0,2},{6,4},{1,3},{7,5},{8,10},{14,12},{9,11},{15,13},{16,18},{22,... | collective-permute-start | bytes 786440 | tf_op jit(solution)/shard_map/ppermute | solution.py:31
  512.8 16.3 %copy-start.7 = (f32[4,16,2048]{2,1,0:T(8,128)}, f32[4,16,2048]{2,1,0:T(8,128)S(1)}, u32[]{:S(2)}) copy-start(f32[4,16,2048]{2,1,0:T(8,128)S(1)} %get-tuple-element.172) | copy-start | bytes 1572868
  512.9 21.0 %collective-permute-start.23 = (f32[4,16,2048]{2,1,0:T(8,128)S(1)}, f32[4,16,2048]{2,1,0:T(8,128)S(1)}, u32[]{:S(2)}, u32[]{:S(2)}) collective-permute-start(f32[4,16,2048]{2,1,0:T(8,128)S(1)} %get-tuple-element.172), channel_id=1, source_target_pairs={{0,2},{6,4},{1,3},{7,5},{8,10},{14,12},{9,11},{15,13},{16,18},{22,... | collective-permute-start | bytes 1572872 | tf_op jit(solution)/shard_map/ppermute | solution.py:31
  514.2 16.9 %collective-permute-start.12 = (f32[4,8,2048]{2,1,0:T(8,128)S(1)}, f32[4,8,2048]{2,1,0:T(8,128)S(1)}, u32[]{:S(2)}, u32[]{:S(2)}) collective-permute-start(f32[4,8,2048]{2,1,0:T(8,128)S(1)} %add.545), channel_id=1, source_target_pairs={{2,4},{4,2},{3,5},{5,3},{10,12},{12,10},{11,13},{13,11},{18,20},{2... | collective-permute-start | bytes 786440 | tf_op jit(solution)/shard_map/ppermute | solution.py:31
  520.1 51.7 %copy-start.4 = (f32[4,16,2048]{2,1,0:T(8,128)}, f32[4,16,2048]{2,1,0:T(8,128)S(1)}, u32[]{:S(2)}) copy-start(f32[4,16,2048]{2,1,0:T(8,128)S(1)} %get-tuple-element.169) | copy-start | bytes 1572868
  520.1 49.0 %collective-permute-start.26 = (f32[4,16,2048]{2,1,0:T(8,128)S(1)}, f32[4,16,2048]{2,1,0:T(8,128)}, u32[]{:S(2)}, u32[]{:S(2)}) collective-permute-start(f32[4,16,2048]{2,1,0:T(8,128)S(1)} %get-tuple-element.169), channel_id=1, source_target_pairs={{0,2},{6,4},{1,3},{7,5},{8,10},{14,12},{9,11},{15,13},{16,18},{22,... | collective-permute-start | bytes 1572872 | tf_op jit(solution)/shard_map/ppermute | solution.py:31
  527.0 42.8 %collective-permute-start.17 = (f32[4,16,2048]{2,1,0:T(8,128)S(1)}, f32[4,16,2048]{2,1,0:T(8,128)}, u32[]{:S(2)}, u32[]{:S(2)}) collective-permute-start(f32[4,16,2048]{2,1,0:T(8,128)S(1)} %get-tuple-element.173), channel_id=1, source_target_pairs={{0,2},{6,4},{1,3},{7,5},{8,10},{14,12},{9,11},{15,13},{16,18},{22,... | collective-permute-start | bytes 1572872 | tf_op jit(solution)/shard_map/ppermute | solution.py:31
  529.1 30.0 %collective-permute-start.38 = (f32[4,8,2048]{2,1,0:T(8,128)}, f32[4,8,2048]{2,1,0:T(8,128)}, u32[]{:S(2)}, u32[]{:S(2)}) collective-permute-start(f32[4,8,2048]{2,1,0:T(8,128)} %get-tuple-element.167), channel_id=1, source_target_pairs={{0,2},{6,4},{1,3},{7,5},{8,10},{14,12},{9,11},{15,13},{16,18},{22,... | collective-permute-start | bytes 786440 | tf_op jit(solution)/shard_map/ppermute | solution.py:31
  531.8 32.9 %collective-permute-start.41 = (f32[4,8,2048]{2,1,0:T(8,128)}, f32[4,8,2048]{2,1,0:T(8,128)}, u32[]{:S(2)}, u32[]{:S(2)}) collective-permute-start(f32[4,8,2048]{2,1,0:T(8,128)} %get-tuple-element.166), channel_id=1, source_target_pairs={{0,2},{6,4},{1,3},{7,5},{8,10},{14,12},{9,11},{15,13},{16,18},{22,... | collective-permute-start | bytes 786440 | tf_op jit(solution)/shard_map/ppermute | solution.py:31
  534.7 36.5 %collective-permute-start.15 = (f32[4,8,2048]{2,1,0:T(8,128)S(1)}, f32[4,8,2048]{2,1,0:T(8,128)}, u32[]{:S(2)}, u32[]{:S(2)}) collective-permute-start(f32[4,8,2048]{2,1,0:T(8,128)S(1)} %add.551), channel_id=1, source_target_pairs={{2,4},{4,2},{3,5},{5,3},{10,12},{12,10},{11,13},{13,11},{18,20},{2... | collective-permute-start | bytes 786440 | tf_op jit(solution)/shard_map/ppermute | solution.py:31
  559.0 22.5 %collective-permute-start.29 = (f32[4,16,2048]{2,1,0:T(8,128)S(1)}, f32[4,16,2048]{2,1,0:T(8,128)S(1)}, u32[]{:S(2)}, u32[]{:S(2)}) collective-permute-start(f32[4,16,2048]{2,1,0:T(8,128)S(1)} %get-tuple-element.171), channel_id=1, source_target_pairs={{0,2},{6,4},{1,3},{7,5},{8,10},{14,12},{9,11},{15,13},{16,18},{22,... | collective-permute-start | bytes 1572872 | tf_op jit(solution)/shard_map/ppermute | solution.py:31
  564.7 18.4 %collective-permute-start.32 = (f32[4,16,2048]{2,1,0:T(8,128)S(1)}, f32[4,16,2048]{2,1,0:T(8,128)S(1)}, u32[]{:S(2)}, u32[]{:S(2)}) collective-permute-start(f32[4,16,2048]{2,1,0:T(8,128)S(1)} %get-tuple-element.170), channel_id=1, source_target_pairs={{0,2},{6,4},{1,3},{7,5},{8,10},{14,12},{9,11},{15,13},{16,18},{22,... | collective-permute-start | bytes 1572872 | tf_op jit(solution)/shard_map/ppermute | solution.py:31
  569.1 29.2 %collective-permute-start.21 = (f32[4,16,2048]{2,1,0:T(8,128)S(1)}, f32[4,16,2048]{2,1,0:T(8,128)S(1)}, u32[]{:S(2)}, u32[]{:S(2)}) collective-permute-start(f32[4,16,2048]{2,1,0:T(8,128)S(1)} %add.565), channel_id=1, source_target_pairs={{2,4},{4,2},{3,5},{5,3},{10,12},{12,10},{11,13},{13,11},{18,20},{2... | collective-permute-start | bytes 1572872 | tf_op jit(solution)/shard_map/ppermute | solution.py:31
  569.8 13.9 %collective-permute-start.13 = (f32[4,8,2048]{2,1,0:T(8,128)S(1)}, f32[4,8,2048]{2,1,0:T(8,128)S(1)}, u32[]{:S(2)}, u32[]{:S(2)}) collective-permute-start(f32[4,8,2048]{2,1,0:T(8,128)S(1)} %add.546), channel_id=1, source_target_pairs={{2,0},{4,6},{3,1},{5,7},{10,8},{12,14},{11,9},{13,15},{18,16},{20,... | collective-permute-start | bytes 786440 | tf_op jit(solution)/shard_map/ppermute | solution.py:31
  571.1 27.9 %collective-permute-start.24 = (f32[4,16,2048]{2,1,0:T(8,128)S(1)}, f32[4,16,2048]{2,1,0:T(8,128)S(1)}, u32[]{:S(2)}, u32[]{:S(2)}) collective-permute-start(f32[4,16,2048]{2,1,0:T(8,128)S(1)} %add.572), channel_id=1, source_target_pairs={{2,4},{4,2},{3,5},{5,3},{10,12},{12,10},{11,13},{13,11},{18,20},{2... | collective-permute-start | bytes 1572872 | tf_op jit(solution)/shard_map/ppermute | solution.py:31
  577.9 21.8 %slice-start = ((s8[4456448]{0:T(1024)(128)(4,1)}), s8[4194304]{0:T(1024)(128)(4,1)S(1)}, s32[]{:S(2)}) async-start(s8[4456448]{0:T(1024)(128)(4,1)} %bitcast.22), calls=%async_computation.1 | async-start | bytes 8388608
  581.5 18.2 %slice-start.1 = ((s8[4456448]{0:T(1024)(128)(4,1)}), s8[262144]{0:T(1024)(128)(4,1)S(1)}, s32[]{:S(2)}) async-start(s8[4456448]{0:T(1024)(128)(4,1)} %bitcast.22), calls=%async_computation.2 | async-start | bytes 524288
  581.6 24.5 %collective-permute-start.27 = (f32[4,16,2048]{2,1,0:T(8,128)S(1)}, f32[4,16,2048]{2,1,0:T(8,128)S(1)}, u32[]{:S(2)}, u32[]{:S(2)}) collective-permute-start(f32[4,16,2048]{2,1,0:T(8,128)S(1)} %add.582), channel_id=1, source_target_pairs={{2,4},{4,2},{3,5},{5,3},{10,12},{12,10},{11,13},{13,11},{18,20},{2... | collective-permute-start | bytes 1572872 | tf_op jit(solution)/shard_map/ppermute | solution.py:31
  583.0 18.9 %collective-permute-start.18 = (f32[4,16,2048]{2,1,0:T(8,128)S(1)}, f32[4,16,2048]{2,1,0:T(8,128)S(1)}, u32[]{:S(2)}, u32[]{:S(2)}) collective-permute-start(f32[4,16,2048]{2,1,0:T(8,128)S(1)} %add.558), channel_id=1, source_target_pairs={{2,4},{4,2},{3,5},{5,3},{10,12},{12,10},{11,13},{13,11},{18,20},{2... | collective-permute-start | bytes 1572872 | tf_op jit(solution)/shard_map/ppermute | solution.py:31
  583.7 13.9 %collective-permute-start.16 = (f32[4,8,2048]{2,1,0:T(8,128)S(1)}, f32[4,8,2048]{2,1,0:T(8,128)S(1)}, u32[]{:S(2)}, u32[]{:S(2)}) collective-permute-start(f32[4,8,2048]{2,1,0:T(8,128)S(1)} %add.552), channel_id=1, source_target_pairs={{2,0},{4,6},{3,1},{5,7},{10,8},{12,14},{11,9},{13,15},{18,16},{20,... | collective-permute-start | bytes 786440 | tf_op jit(solution)/shard_map/ppermute | solution.py:31
  597.6 5.1 collective-permute-start.36
  598.3 5.1 collective-permute-start.39
  599.0 5.7 collective-permute-start.42
  601.9 11.2 %collective-permute-start.30 = (f32[4,16,2048]{2,1,0:T(8,128)S(1)}, f32[4,16,2048]{2,1,0:T(8,128)S(1)}, u32[]{:S(2)}, u32[]{:S(2)}) collective-permute-start(f32[4,16,2048]{2,1,0:T(8,128)S(1)} %add.592), channel_id=1, source_target_pairs={{2,4},{4,2},{3,5},{5,3},{10,12},{12,10},{11,13},{13,11},{18,20},{2... | collective-permute-start | bytes 1572872 | tf_op jit(solution)/shard_map/ppermute | solution.py:31
  602.7 10.5 %collective-permute-start.33 = (f32[4,16,2048]{2,1,0:T(8,128)S(1)}, f32[4,16,2048]{2,1,0:T(8,128)S(1)}, u32[]{:S(2)}, u32[]{:S(2)}) collective-permute-start(f32[4,16,2048]{2,1,0:T(8,128)S(1)} %add.602), channel_id=1, source_target_pairs={{2,4},{4,2},{3,5},{5,3},{10,12},{12,10},{11,13},{13,11},{18,20},{2... | collective-permute-start | bytes 1572872 | tf_op jit(solution)/shard_map/ppermute | solution.py:31
  603.4 36.9 %collective-permute-start.19 = (f32[4,16,2048]{2,1,0:T(8,128)S(1)}, f32[4,16,2048]{2,1,0:T(8,128)S(1)}, u32[]{:S(2)}, u32[]{:S(2)}) collective-permute-start(f32[4,16,2048]{2,1,0:T(8,128)S(1)} %add.559), channel_id=1, source_target_pairs={{2,0},{4,6},{3,1},{5,7},{10,8},{12,14},{11,9},{13,15},{18,16},{20,... | collective-permute-start | bytes 1572872 | tf_op jit(solution)/shard_map/ppermute | solution.py:31
  604.7 41.2 %collective-permute-start.22 = (f32[4,16,2048]{2,1,0:T(8,128)S(1)}, f32[4,16,2048]{2,1,0:T(8,128)S(1)}, u32[]{:S(2)}, u32[]{:S(2)}) collective-permute-start(f32[4,16,2048]{2,1,0:T(8,128)S(1)} %add.566), channel_id=1, source_target_pairs={{2,0},{4,6},{3,1},{5,7},{10,8},{12,14},{11,9},{13,15},{18,16},{20,... | collective-permute-start | bytes 1572872 | tf_op jit(solution)/shard_map/ppermute | solution.py:31
  606.0 46.6 %collective-permute-start.25 = (f32[4,16,2048]{2,1,0:T(8,128)S(1)}, f32[4,16,2048]{2,1,0:T(8,128)S(1)}, u32[]{:S(2)}, u32[]{:S(2)}) collective-permute-start(f32[4,16,2048]{2,1,0:T(8,128)S(1)} %add.573), channel_id=1, source_target_pairs={{2,0},{4,6},{3,1},{5,7},{10,8},{12,14},{11,9},{13,15},{18,16},{20,... | collective-permute-start | bytes 1572872 | tf_op jit(solution)/shard_map/ppermute | solution.py:31
  657.0 16.7 %collective-permute-start.28 = (f32[4,16,2048]{2,1,0:T(8,128)S(1)}, f32[4,16,2048]{2,1,0:T(8,128)S(1)}, u32[]{:S(2)}, u32[]{:S(2)}) collective-permute-start(f32[4,16,2048]{2,1,0:T(8,128)S(1)} %add.583), channel_id=1, source_target_pairs={{2,0},{4,6},{3,1},{5,7},{10,8},{12,14},{11,9},{13,15},{18,16},{20,... | collective-permute-start | bytes 1572872 | tf_op jit(solution)/shard_map/ppermute | solution.py:31
  658.3 21.3 %collective-permute-start.31 = (f32[4,16,2048]{2,1,0:T(8,128)S(1)}, f32[4,16,2048]{2,1,0:T(8,128)S(1)}, u32[]{:S(2)}, u32[]{:S(2)}) collective-permute-start(f32[4,16,2048]{2,1,0:T(8,128)S(1)} %add.593), channel_id=1, source_target_pairs={{2,0},{4,6},{3,1},{5,7},{10,8},{12,14},{11,9},{13,15},{18,16},{20,... | collective-permute-start | bytes 1572872 | tf_op jit(solution)/shard_map/ppermute | solution.py:31
  659.6 27.6 %collective-permute-start.34 = (f32[4,16,2048]{2,1,0:T(8,128)S(1)}, f32[4,16,2048]{2,1,0:T(8,128)S(1)}, u32[]{:S(2)}, u32[]{:S(2)}) collective-permute-start(f32[4,16,2048]{2,1,0:T(8,128)S(1)} %add.603), channel_id=1, source_target_pairs={{2,0},{4,6},{3,1},{5,7},{10,8},{12,14},{11,9},{13,15},{18,16},{20,... | collective-permute-start | bytes 1572872 | tf_op jit(solution)/shard_map/ppermute | solution.py:31
  691.5 8.3 %collective-permute-start.37 = (f32[4,8,2048]{2,1,0:T(8,128)S(1)}, f32[4,8,2048]{2,1,0:T(8,128)S(1)}, u32[]{:S(2)}, u32[]{:S(2)}) collective-permute-start(f32[4,8,2048]{2,1,0:T(8,128)S(1)} %add.613), channel_id=1, source_target_pairs={{2,0},{4,6},{3,1},{5,7},{10,8},{12,14},{11,9},{13,15},{18,16},{20,... | collective-permute-start | bytes 786440 | tf_op jit(solution)/shard_map/ppermute | solution.py:31
  692.8 9.8 %collective-permute-start.40 = (f32[4,8,2048]{2,1,0:T(8,128)S(1)}, f32[4,8,2048]{2,1,0:T(8,128)S(1)}, u32[]{:S(2)}, u32[]{:S(2)}) collective-permute-start(f32[4,8,2048]{2,1,0:T(8,128)S(1)} %add.623), channel_id=1, source_target_pairs={{2,0},{4,6},{3,1},{5,7},{10,8},{12,14},{11,9},{13,15},{18,16},{20,... | collective-permute-start | bytes 786440 | tf_op jit(solution)/shard_map/ppermute | solution.py:31
  694.1 11.3 %collective-permute-start.43 = (f32[4,8,2048]{2,1,0:T(8,128)S(1)}, f32[4,8,2048]{2,1,0:T(8,128)S(1)}, u32[]{:S(2)}, u32[]{:S(2)}) collective-permute-start(f32[4,8,2048]{2,1,0:T(8,128)S(1)} %add.633), channel_id=1, source_target_pairs={{2,0},{4,6},{3,1},{5,7},{10,8},{12,14},{11,9},{13,15},{18,16},{20,... | collective-permute-start | bytes 786440 | tf_op jit(solution)/shard_map/ppermute | solution.py:31
  713.1 1.2 collective-permute-start.44
  716.9 3.6 collective-permute-start.45
  720.6 3.6 collective-permute-start.46
  724.2 4.5 collective-permute-start.47
  728.6 3.6 collective-permute-start.48
  738.2 26.9 %collective-permute-start.49 = (f32[136,2048]{1,0:T(8,128)S(1)}, f32[136,2048]{1,0:T(8,128)}, u32[]{:S(2)}, u32[]{:S(2)}) collective-permute-start(f32[136,2048]{1,0:T(8,128)S(1)} %add_bitcast_fusion.2), channel_id=1, source_target_pairs={{0,2},{6,4},{1,3},{7,5},{8,10},{14,12},{9,11},{15,13},{16,18},{22,... | collective-permute-start | bytes 3342344 | tf_op jit(solution)/shard_map/ppermute | solution.py:31
  746.8 42.1 %collective-permute-start.53 = (f32[136,2048]{1,0:T(8,128)S(1)}, f32[136,2048]{1,0:T(8,128)}, u32[]{:S(2)}, u32[]{:S(2)}) collective-permute-start(f32[136,2048]{1,0:T(8,128)S(1)} %add_bitcast_fusion.1), channel_id=1, source_target_pairs={{0,2},{6,4},{1,3},{7,5},{8,10},{14,12},{9,11},{15,13},{16,18},{22,... | collective-permute-start | bytes 3342344 | tf_op jit(solution)/shard_map/ppermute | solution.py:31
  767.4 23.6 %collective-permute-start.50 = (f32[136,2048]{1,0:T(8,128)}, f32[136,2048]{1,0:T(8,128)S(1)}, u32[]{:S(2)}, u32[]{:S(2)}) collective-permute-start(f32[136,2048]{1,0:T(8,128)} %add.676), channel_id=1, source_target_pairs={{2,4},{4,2},{3,5},{5,3},{10,12},{12,10},{11,13},{13,11},{18,20},{2... | collective-permute-start | bytes 3342344 | tf_op jit(solution)/shard_map/ppermute | solution.py:31
  773.9 34.1 %collective-permute-start.52 = (f32[136,2048]{1,0:T(8,128)S(1)}, f32[136,2048]{1,0:T(8,128)S(1)}, u32[]{:S(2)}, u32[]{:S(2)}) collective-permute-start(f32[136,2048]{1,0:T(8,128)S(1)} %add_bitcast_fusion), channel_id=1, source_target_pairs={{0,2},{6,4},{1,3},{7,5},{8,10},{14,12},{9,11},{15,13},{16,18},{22,... | collective-permute-start | bytes 3342344 | tf_op jit(solution)/shard_map/ppermute | solution.py:31
  790.3 17.7 %collective-permute-start.54 = (f32[136,2048]{1,0:T(8,128)S(1)}, f32[136,2048]{1,0:T(8,128)S(1)}, u32[]{:S(2)}, u32[]{:S(2)}) collective-permute-start(f32[136,2048]{1,0:T(8,128)S(1)} %add.680), channel_id=1, source_target_pairs={{2,4},{4,2},{3,5},{5,3},{10,12},{12,10},{11,13},{13,11},{18,20},{2... | collective-permute-start | bytes 3342344 | tf_op jit(solution)/shard_map/ppermute | solution.py:31
  796.9 21.1 %collective-permute-start.51 = (f32[136,2048]{1,0:T(8,128)S(1)}, f32[136,2048]{1,0:T(8,128)S(1)}, u32[]{:S(2)}, u32[]{:S(2)}) collective-permute-start(f32[136,2048]{1,0:T(8,128)S(1)} %get-tuple-element.124), channel_id=1, source_target_pairs={{2,0},{4,6},{3,1},{5,7},{10,8},{12,14},{11,9},{13,15},{18,16},{20,... | collective-permute-start | bytes 3342344 | tf_op jit(solution)/shard_map/ppermute | solution.py:31
  (10 other events, 54.0 us)
where the time goes:
time: 824 us; the launch traced here: 821 us
  waiting for transfers between devices  558 us (68%)
  other arithmetic  143 us (17%)
  starting transfers between devices  89 us (11%)
  local copies, waits for them, and re-layouts  30.3 us (4%)
    ppermute x45, waiting for transfers between devices, send(): return lax.ppermute(value, axis, pairs)  532 us
    ppermute x45, starting transfers between devices, send(): return lax.ppermute(value, axis, pairs)  74.2 us
    add x9, other arithmetic, line_step(): return sum((factor[i] * (value - v) for i, value in enumerate(values)))  46.7 us
    ppermute x10, waiting for transfers between devices, sum_over_devices(): lax.ppermute(value, axis, [(i, i ^ step) for i in range(size)])  25.5 us
    reduce_sum x4, other arithmetic, on_device(): line_sq[place] = jnp.sum(jnp.square(held[place] - v))  17.7 us
  transfers between devices with their start and end apart: 56, of which 30 were waited for; matrix products, arithmetic and copies ran while one was open for 14% of the time, Pallas kernels for 0%

commit v1 on v0

--- a/solution.py
+++ b/solution.py
@@ -3,6 +3,8 @@
 import jax
 import jax.numpy as jnp
 from jax import lax
+from jax.experimental import pallas as pl
+from jax.experimental.pallas import tpu as pltpu
 from jax.sharding import PartitionSpec as P
 
 
@@ -42,12 +44,102 @@
 
 def split(rows, outers):
     cut = int(rows * SPREAD) // TILE * TILE
-    tiles = (rows - cut) // TILE
-    if outers != LINE or (rows - cut) % TILE or tiles < 8:
+    rest = rows - cut
+    if outers != LINE or rest % TILE or rest // TILE < 12:
         return None
+    tiles = rest // TILE
     body = tiles - 4
-    sizes = [1, 1] + [2] * (body // 2) + [1] * (body % 2) + [1, 1]
-    return cut, [size * TILE for size in sizes]
+    sizes = [1, 2] + [3] * (body // 3) + [body % 3] * (body % 3 > 0) + [1]
+    return cut, sizes
+
+
+SMEM = pl.BlockSpec(memory_space=pltpu.SMEM)
+
+
+def tiles_at(start, shape):
+    return pl.BlockSpec(shape, lambda i: (start + i, 0))
+
+
+def run(kernel, grid, in_specs, out_specs, out_shape, operands, moved, aliases={}, prefetch=0):
+    return pl.pallas_call(
+        kernel,
+        grid_spec=pltpu.PrefetchScalarGridSpec(
+            num_scalar_prefetch=prefetch, grid=grid, in_specs=in_specs, out_specs=out_specs
+        ),
+        out_shape=out_shape,
+        input_output_aliases=aliases,
+        compiler_params=pltpu.CompilerParams(vmem_limit_bytes=24 << 20),
+        cost_estimate=pl.CostEstimate(flops=4 * moved, bytes_accessed=4 * moved, transcendentals=0),
+    )(*operands)
+
+
+def step_of(factor, values, v):
+    return sum(factor[i] * (value[...] - v) for i, value in enumerate(values))
+
+
+def step_chunk(factor, values, v, start, tiles):
+    columns, tile = v.shape[1], TILE * LINE
+
+    def kernel(factor, *refs):
+        *values, v, out = refs
+        out[...] = step_of(factor, values, v[...])
+
+    at, own = tiles_at(start, (tile, columns)), tiles_at(0, (tile, columns))
+    shape = jax.ShapeDtypeStruct((tiles * tile, columns), v.dtype)
+    moved = (len(values) + 2) * tiles * tile * columns
+    operands = (factor, *values, v)
+    return run(kernel, (tiles,), [SMEM] + [at] * (len(values) + 1), own, shape, operands, moved)
+
+
+def move_chunk(is_end, share, total, back, values, v, start, tiles, carried):
+    columns, tile, count = v.shape[1], TILE * LINE, len(values)
+
+    def kernel(is_end, total, back, v, *refs):
+        values, (v_out, sq_out) = refs[:count], refs[-2:]
+        moved = v[...] + jnp.where(is_end[0] > 0, back[...], total[...]) * share
+        v_out[...] = moved
+
+        @pl.when(pl.program_id(0) == 0)
+        def _():
+            sq_out[...] = refs[-3][...] if carried else jnp.zeros_like(sq_out)
+
+        for i, value in enumerate(values):
+            square = jnp.square(value[...] - moved)
+            folded = sum(square[j : j + 8] for j in range(0, tile, 8))
+            sq_out[i] += sum(folded[:, j : j + 128] for j in range(0, columns, 128))
+
+    at, own = tiles_at(start, (tile, columns)), tiles_at(0, (tile, columns))
+    squares = pl.BlockSpec((count, 8, 128), lambda i: (0, 0, 0))
+    in_specs = [SMEM, own, own] + [at] * (count + 1)
+    operands = (is_end, total, back, v, *values)
+    aliases = {}
+    if carried:
+        in_specs += [pl.BlockSpec(memory_space=pl.ANY), squares]
+        aliases = {len(operands): 0, len(operands) + 1: 1}
+        operands += carried
+    shapes = (
+        jax.ShapeDtypeStruct(v.shape, v.dtype),
+        jax.ShapeDtypeStruct((count, 8, 128), v.dtype),
+    )
+    moved = (count + 4) * tiles * tile * columns
+    return run(kernel, (tiles,), in_specs, (at, squares), shapes, operands, moved, aliases)
+
+
+def step_block(place, factor, values, v):
+    _, rows, columns = v.shape
+    parts = 4
+
+    def kernel(place, factor, *refs):
+        *values, v, out = refs
+        out[...] = step_of(factor, values, v[...])
+
+    at = pl.BlockSpec((None, rows, columns // parts), lambda i, place: (place[0], 0, i))
+    own = pl.BlockSpec((rows, columns // parts), lambda i, place: (0, i))
+    shape = jax.ShapeDtypeStruct((rows, columns), v.dtype)
+    moved = (len(values) + 2) * rows * columns
+    operands = (place, factor, *values, v)
+    in_specs = [SMEM] + [at] * (len(values) + 1)
+    return run(kernel, (parts,), in_specs, own, shape, operands, moved, prefetch=1)
 
 
 def spread_only(mine, center, radius_total, worker_count):
@@ -101,16 +193,16 @@
     line_v = jnp.where(is_low, jnp.concatenate([near, far]), jnp.concatenate([far, near]))
     spread_v = center[:cut]
 
-    places = [(w ^ step) * outers + o for step in steps]
-    numbers = jnp.arange(worker_count)
-
-    def factors(spread_sq, line_sq):
-        both = spread_sq
-        for place, value in zip(places, line_sq):
-            both = both + jnp.where(numbers == place, value, 0.0)
+    places = jnp.stack([(w ^ step) * outers + o for step in steps])
+    hit = places[:, None] == jnp.arange(worker_count)[None]
+
+    def placed(line_sq):
+        return jnp.sum(jnp.where(hit, line_sq[:, None], 0.0), axis=0)
+
+    def factors(both):
         norm_sq = sum_over_devices(both)
         factor = jnp.minimum(1.0, radius_total * lax.rsqrt(norm_sq + epsilon))
-        return factor, [jnp.sum(jnp.where(numbers == place, factor, 0.0)) for place in places]
+        return factor, jnp.sum(jnp.where(hit, factor[None], 0.0), axis=1)
 
     def spread_norms(v):
         difference = spread - v[None]
@@ -119,45 +211,37 @@
     def spread_update(v, factor):
         return v + jnp.sum(factor[:, None, None] * (spread - v[None]), axis=0) / worker_count
 
-    def line_step(values, v, factor):
-        return sum(factor[i] * (value - v) for i, value in enumerate(values))
-
-    line_sq, v = [None] * workers, line_v
+    line_sq, v = jnp.zeros((worker_count,), jnp.float32), line_v
     for place in reversed(range(workers)):
-        line_sq[place] = jnp.sum(jnp.square(held[place] - v))
-        v = tie(v, line_sq[place])
-    factor, line_factor = factors(spread_norms(spread_v), line_sq)
-
-    starts = [sum(sizes[:i]) for i in range(len(sizes))]
-    pieces, sums = [], [[0.0] * workers]
-    for chunk, (start, size) in enumerate(zip(starts, sizes)):
-        part = slice(start, start + size)
-        values, v = [value[:, part] for value in held], line_v[:, part]
-        own = line_step(values, v, line_factor)
+        square = jnp.sum(jnp.square(held[place] - v))
+        line_sq = lax.optimization_barrier(line_sq + jnp.where(hit[place], square, 0.0))
+        v = tie(v, line_sq)
+    factor, line_factor = factors(spread_norms(spread_v) + line_sq)
+
+    flat = [value.reshape(outers * rest, columns) for value in held]
+    flat_v = line_v.reshape(outers * rest, columns)
+    end_flag = is_end.astype(jnp.int32).reshape(1)
+    start, carried, squares = 0, (), []
+    for chunk, tiles in enumerate(sizes):
+        own = step_chunk(line_factor, flat, flat_v, start, tiles)
         own = own + send(own, TO_MIDS)
         own = own + send(own, ACROSS)
         if chunk >= 3:
-            own = tie(own, sums[chunk - 2])
-        own = jnp.where(is_end, send(own, TO_ENDS), own)
-        v = v + own / worker_count
-        sums.append(
-            [
-                total + jnp.sum(jnp.square(value - v), axis=(0, 1))
-                for total, value in zip(sums[-1], values)
-            ]
+            own = tie(own, squares[chunk - 2])
+        back = send(own, TO_ENDS)
+        carried = tuple(
+            move_chunk(end_flag, 1 / worker_count, own, back, flat, flat_v, start, tiles, carried)
         )
-        pieces.append(v)
+        squares.append(carried[1])
+        start += tiles
     spread_v = spread_update(spread_v, factor)
-    line_v = jnp.concatenate(pieces, axis=1)
-    factor, line_factor = factors(spread_norms(spread_v), [jnp.sum(total) for total in sums[-1]])
-
-    def at(value, place):
-        index = jnp.where(is_low, LINE - 1 - place, place)
-        return lax.dynamic_index_in_dim(value, index, 0, keepdims=False)
+    line_v = carried[0].reshape(line_v.shape)
+    factor, line_factor = factors(spread_norms(spread_v) + placed(jnp.sum(carried[1], axis=(1, 2))))
 
     block, v = [], line_v
     for place in range(LINE):
-        block.append(line_step([at(value, place) for value in held], at(v, place), line_factor))
+        index = jnp.where(is_low, LINE - 1 - place, place).astype(jnp.int32).reshape(1)
+        block.append(step_block(index, line_factor, held, v))
         v = tie(v, block[place])
     arrived = [send(block[place], TO_MIDS) for place in range(3)]
     passed = [send(block[place] + arrived[place], ACROSS) for place in range(2)]

time: 824 us -> 784 us (0.951)
  other arithmetic: 143 us -> 68.7 us
  Pallas kernels: 0 us -> 43.8 us
  waiting for transfers between devices: 558 us -> 530 us
  local copies, waits for them, and re-layouts: 30.3 us -> 54.3 us
    add x21 -> x5, other arithmetic: 51.8 us -> 1.96 us  [the longest x3 1.95 us: on_device(): line_sq + jnp.where(hit[place], square, 0.0)]
    pallas_call x0 -> x20, Pallas kernels: none -> 43.8 us  [run(): pl.pallas_call(kernel, grid_spec=pltpu.PrefetchScalarGridSpec(num_scalar_...]
    ppermute x45 -> x36, waiting for transfers between devices: 532 us -> 508 us  [send(): return lax.ppermute(value, axis, pairs)]
    unnamed x46, local copies, waits for them, and re-layouts: 2.85 us -> 26.9 us
    reduce_sum x14 -> x8, other arithmetic: 34.8 us -> 19.4 us  [the longest x4 18.9 us: on_device(): square = jnp.sum(jnp.square(held[place] - v))]
    ppermute x45 -> x36, starting transfers between devices: 74.2 us -> 65.1 us  [send(): return lax.ppermute(value, axis, pairs)]
  transfers between devices with their start and end apart: 56 -> 47, of which waited for: 30 -> 27; matrix products, arithmetic and copies ran while one was open for 14% -> 10% of each run, Pallas kernels for 0% -> 5%
where the time goes in v1:
time: 784 us; the launch traced here: 781 us
  waiting for transfers between devices  530 us (68%)
  starting transfers between devices  82.8 us (11%)
  other arithmetic  68.7 us (9%)
  local copies, waits for them, and re-layouts  54.3 us (7%)
  Pallas kernels  43.8 us (6%)
    ppermute x36, waiting for transfers between devices, send(): return lax.ppermute(value, axis, pairs)  508 us
    ppermute x36, starting transfers between devices, send(): return lax.ppermute(value, axis, pairs)  65.1 us
    pallas_call x20, Pallas kernels, run(): pl.pallas_call(kernel, grid_spec=pltpu.PrefetchScalarGridSpec(num_scalar_...  43.8 us
    unnamed x46, local copies, waits for them, and re-layouts  26.9 us
    ppermute x10, waiting for transfers between devices, sum_over_devices(): lax.ppermute(value, axis, [(i, i ^ step) for i in range(size)])  21.9 us
    reduce_sum x4, other arithmetic, on_device(): square = jnp.sum(jnp.square(held[place] - v))  18.9 us
  transfers between devices with their start and end apart: 47, of which 27 were waited for; matrix products, arithmetic and copies ran while one was open for 10% of the time, Pallas kernels for 5%

profile of v1, /device:TPU:0, one launch (start us, length us, event | category | flops | bytes accessed | tf_op | source)
XLA Modules:
  0.0 780.8 jit_solution(7040988722052420855)
XLA Ops:
  0.0 10.5 %slice.28 = f32[16,88,2048]{2,1,0:T(8,128)} slice(f32[16,224,2048]{2,1,0:T(8,128)} %bitcast.77), slice={[0:16], [0:88], [0:2048]} | slice | bytes 23068672 | tf_op jit(solution)/shard_map/slice | solution.py:187
  10.5 7.6 all-to-all-start
  21.2 207.4 %collective-permute-done = f32[136,2048]{1,0:T(8,128)S(1)} collective-permute-done((f32[136,2048]{1,0:T(8,128)}, f32[136,2048]{1,0:T(8,128)S(1)}, u32[]{:S(2)}, u32[]{:S(2)}) %collective-permute-start) | collective-permute-done | bytes 1114144 | tf_op jit(solution)/shard_map/ppermute | solution.py:33
  231.5 2.0 collective-permute-start.1
  233.5 4.8 constant_dynamic-slice_fusion.3
  238.3 4.9 constant_dynamic-slice_fusion.2
  243.2 4.9 constant_dynamic-slice_fusion.1
  252.9 114.5 %collective-permute-done.2 = f32[2,136,2048]{2,1,0:T(8,128)} collective-permute-done((f32[2,136,2048]{2,1,0:T(8,128)}, f32[2,136,2048]{2,1,0:T(8,128)}, u32[]{:S(2)}, u32[]{:S(2)}) %collective-permute-start.2) | collective-permute-done | bytes 2228256 | tf_op jit(solution)/shard_map/ppermute | solution.py:33
  369.4 5.9 multiply_reduce_fusion.7
  375.9 4.9 multiply_reduce_fusion.6
  381.5 4.0 multiply_reduce_fusion.5
  386.2 63.9 %collective-permute-done.5.refs_0_ = f32[4,136,2048]{2,1,0:T(8,128)} collective-permute-done((f32[4,136,2048]{2,1,0:T(8,128)}, f32[4,136,2048]{2,1,0:T(8,128)}, u32[]{:S(2)}, u32[]{:S(2)}) %collective-permute-start.5) | collective-permute-done | bytes 4456480 | tf_op jit(solution)/shard_map/ppermute | solution.py:33
  450.1 4.0 multiply_reduce_fusion.4
  454.8 5.8 multiply_reduce_fusion.3
  465.3 3.6 collective-permute-done.8
  469.5 3.8 collective-permute-done.9
  474.9 2.0 collective-permute-done.10
  477.1 2.3 copy-done
  482.8 2.5 shard_map.44
  486.7 2.5 shard_map.39
  490.6 4.5 collective-permute-done.17
  497.1 6.2 collective-permute-start.20
  503.3 2.5 shard_map.47
  507.1 2.5 shard_map.38
  509.7 24.8 %collective-permute-done.20 = f32[32,2048]{1,0:T(8,128)S(1)} collective-permute-done((f32[32,2048]{1,0:T(8,128)S(1)}, f32[32,2048]{1,0:T(8,128)S(1)}, u32[]{:S(2)}, u32[]{:S(2)}) %collective-permute-start.20) | collective-permute-done | bytes 262176 | tf_op jit(solution)/shard_map/ppermute | solution.py:33
  534.4 5.3 collective-permute-start.13
  547.8 3.5 collective-permute-done.28
  554.7 8.3 %collective-permute-done.13 = f32[96,2048]{1,0:T(8,128)} collective-permute-done((f32[96,2048]{1,0:T(8,128)S(1)}, f32[96,2048]{1,0:T(8,128)}, u32[]{:S(2)}, u32[]{:S(2)}) %collective-permute-start.13) | collective-permute-done | bytes 786464 | tf_op jit(solution)/shard_map/ppermute | solution.py:33
  565.0 20.6 %collective-permute-done.22.back = f32[32,2048]{1,0:T(8,128)S(1)} collective-permute-done((f32[32,2048]{1,0:T(8,128)S(1)}, f32[32,2048]{1,0:T(8,128)S(1)}, u32[]{:S(2)}, u32[]{:S(2)}) %collective-permute-start.22) | collective-permute-done | bytes 262176 | tf_op jit(solution)/shard_map/ppermute | solution.py:33
  587.0 2.3 copy-done.1
  589.2 2.3 copy-done.7
  603.8 4.7 collective-permute-start.32
  611.2 2.5 collective-permute-done.26.back
  613.7 2.7 shard_map.45
  616.4 11.7 %collective-permute-done.23.back = f32[96,2048]{1,0:T(8,128)S(1)} collective-permute-done((f32[96,2048]{1,0:T(8,128)S(1)}, f32[96,2048]{1,0:T(8,128)S(1)}, u32[]{:S(2)}, u32[]{:S(2)}) %collective-permute-start.23) | collective-permute-done | bytes 786464 | tf_op jit(solution)/shard_map/ppermute | solution.py:33
  628.1 2.7 shard_map.46
  633.6 6.8 multiply_reduce_fusion.2
  643.4 4.0 collective-permute-done.30.back
  647.4 2.7 shard_map.48
  650.1 11.4 %collective-permute-done.27.back = f32[96,2048]{1,0:T(8,128)} collective-permute-done((f32[96,2048]{1,0:T(8,128)S(1)}, f32[96,2048]{1,0:T(8,128)}, u32[]{:S(2)}, u32[]{:S(2)}) %collective-permute-start.27) | collective-permute-done | bytes 786464 | tf_op jit(solution)/shard_map/ppermute | solution.py:33
  661.6 2.9 shard_map.49
  667.0 6.3 multiply_reduce_fusion.1
  676.9 2.0 copy-done.8
  689.4 2.6 collective-permute-done.38
  693.4 2.0 collective-permute-done.39
  695.7 2.3 copy-done.2
  698.0 2.3 copy-done.9
  700.2 2.9 shard_map.53
  703.1 4.9 collective-permute-start.40
  708.0 2.3 copy-done.3
  710.3 2.3 copy-done.10
  712.5 2.9 shard_map.54
  715.5 2.3 collective-permute-start.44
  717.8 14.1 %collective-permute-done.40 = f32[136,2048]{1,0:T(8,128)} collective-permute-done((f32[136,2048]{1,0:T(8,128)S(1)}, f32[136,2048]{1,0:T(8,128)}, u32[]{:S(2)}, u32[]{:S(2)}) %collective-permute-start.40) | collective-permute-done | bytes 1114144 | tf_op jit(solution)/shard_map/ppermute | solution.py:33
  731.9 2.4 add.203
  735.0 2.3 copy-done.4
  737.3 2.3 copy-done.11
  739.6 2.9 shard_map.55
  742.5 6.3 collective-permute-start.43
  748.8 3.0 shard_map.56
  751.8 4.0 collective-permute-done.44
  759.6 6.0 multiply_reduce_fusion
  765.7 8.6 %collective-permute-done.43 = f32[136,2048]{1,0:T(8,128)S(1)} collective-permute-done((f32[136,2048]{1,0:T(8,128)S(1)}, f32[136,2048]{1,0:T(8,128)S(1)}, u32[]{:S(2)}, u32[]{:S(2)}) %collective-permute-start.43) | collective-permute-done | bytes 1114144 | tf_op jit(solution)/shard_map/ppermute | solution.py:33
  774.3 3.2 collective-permute-done.42
  (159 shorter events, 92.9 us)
Async XLA Ops:
  10.5 7.6 copy-start.16
  10.5 444.3 %all-to-all-start = ((f32[16,88,2048]{2,1,0:T(8,128)}), f32[16,88,2048]{2,1,0:T(8,128)}, u32[]{:S(2)}, u32[]{:S(2)}) async-start(f32[16,88,2048]{2,1,0:T(8,128)} %slice.28), calls=%async_computation | async-start | bytes 23068672 | tf_op jit(solution)/shard_map/all_to_all | solution.py:186
  19.3 209.3 %collective-permute-start = (f32[136,2048]{1,0:T(8,128)}, f32[136,2048]{1,0:T(8,128)S(1)}, u32[]{:S(2)}, u32[]{:S(2)}) collective-permute-start(f32[136,2048]{1,0:T(8,128)} %get-tuple-element.69), channel_id=1, source_target_pairs={{0,2},{2,0},{4,6},{6,4},{1,3},{3,1},{5,7},{7,5},{8,10},{10,8},{12,... | collective-permute-start | bytes 3342344 | tf_op jit(solution)/shard_map/ppermute | solution.py:33
  231.5 18.3 %collective-permute-start.1 = (f32[2,136,2048]{2,1,0:T(8,128)S(1)}, f32[2,136,2048]{2,1,0:T(8,128)}, u32[]{:S(2)}, u32[]{:S(2)}) collective-permute-start(f32[2,136,2048]{2,1,0:T(8,128)S(1)} %maximum_select_fusion.1), channel_id=1, source_target_pairs={{2,4},{4,2},{3,5},{5,3},{10,12},{12,10},{11,13},{13,11},{18,20},{2... | collective-permute-start | bytes 6684680 | tf_op jit(solution)/shard_map/ppermute | solution.py:33
  248.1 127.8 %collective-permute-start.3 = (f32[4,136,2048]{2,1,0:T(8,128)}, f32[4,136,2048]{2,1,0:T(8,128)}, u32[]{:S(2)}, u32[]{:S(2)}) collective-permute-start(f32[4,136,2048]{2,1,0:T(8,128)} %constant_dynamic-slice_fusion.1), channel_id=1, source_target_pairs={{0,8},{8,0},{16,24},{24,16},{1,9},{9,1},{17,25},{25,17},{2,10},{10... | collective-permute-start | bytes 13369352 | tf_op jit(solution)/shard_map/ppermute | solution.py:33
  248.1 133.4 %collective-permute-start.4 = (f32[4,136,2048]{2,1,0:T(8,128)}, f32[4,136,2048]{2,1,0:T(8,128)}, u32[]{:S(2)}, u32[]{:S(2)}) collective-permute-start(f32[4,136,2048]{2,1,0:T(8,128)} %constant_dynamic-slice_fusion.2), channel_id=1, source_target_pairs={{0,24},{8,16},{16,8},{24,0},{1,25},{9,17},{17,9},{25,1},{2,26},{10... | collective-permute-start | bytes 13369352 | tf_op jit(solution)/shard_map/ppermute | solution.py:33
  249.8 117.6 %collective-permute-start.2 = (f32[2,136,2048]{2,1,0:T(8,128)}, f32[2,136,2048]{2,1,0:T(8,128)}, u32[]{:S(2)}, u32[]{:S(2)}) collective-permute-start(f32[2,136,2048]{2,1,0:T(8,128)} %collective-permute-done.1), channel_id=1, source_target_pairs={{2,0},{4,6},{3,1},{5,7},{10,8},{12,14},{11,9},{13,15},{18,16},{20,... | collective-permute-start | bytes 6684680 | tf_op jit(solution)/shard_map/ppermute | solution.py:33
  251.1 199.0 %collective-permute-start.5 = (f32[4,136,2048]{2,1,0:T(8,128)}, f32[4,136,2048]{2,1,0:T(8,128)}, u32[]{:S(2)}, u32[]{:S(2)}) collective-permute-start(f32[4,136,2048]{2,1,0:T(8,128)} %constant_dynamic-slice_fusion.3), channel_id=1, source_target_pairs={{0,16},{8,24},{16,0},{24,8},{1,17},{9,25},{17,1},{25,9},{2,18},{10... | collective-permute-start | bytes 13369352 | tf_op jit(solution)/shard_map/ppermute | solution.py:33
  375.2 74.9 %copy-start.5 = (f32[4,136,2048]{2,1,0:T(8,128)}, f32[4,136,2048]{2,1,0:T(8,128)S(1)}, u32[]{:S(2)}) copy-start(f32[4,136,2048]{2,1,0:T(8,128)S(1)} %get-tuple-element.40) | copy-start | bytes 13369348
  454.8 22.3 %copy-start.6 = (f32[4,136,2048]{2,1,0:T(8,128)S(1)}, f32[4,136,2048]{2,1,0:T(8,128)}, u32[]{:S(2)}) copy-start(f32[4,136,2048]{2,1,0:T(8,128)} %copy-done.5) | copy-start | bytes 13369348
  460.6 1.2 collective-permute-start.6
  461.7 3.6 collective-permute-start.7
  465.3 3.6 collective-permute-start.8
  468.9 4.5 collective-permute-start.9
  473.4 3.6 collective-permute-start.10
  477.1 2.3 copy-start
  480.9 14.2 %collective-permute-start.17 = (f32[64,2048]{1,0:T(8,128)S(1)}, f32[64,2048]{1,0:T(8,128)S(1)}, u32[]{:S(2)}, u32[]{:S(2)}) collective-permute-start(f32[64,2048]{1,0:T(8,128)S(1)} %shard_map.40), channel_id=1, source_target_pairs={{0,2},{6,4},{1,3},{7,5},{8,10},{14,12},{9,11},{15,13},{16,18},{22,... | collective-permute-start | bytes 1572872 | tf_op jit(solution)/shard_map/ppermute | solution.py:33
  485.3 54.4 %collective-permute-start.24 = (f32[96,2048]{1,0:T(8,128)S(1)}, f32[96,2048]{1,0:T(8,128)S(1)}, u32[]{:S(2)}, u32[]{:S(2)}) collective-permute-start(f32[96,2048]{1,0:T(8,128)S(1)} %shard_map.44), channel_id=1, source_target_pairs={{0,2},{6,4},{1,3},{7,5},{8,10},{14,12},{9,11},{15,13},{16,18},{22,... | collective-permute-start | bytes 2359304 | tf_op jit(solution)/shard_map/ppermute | solution.py:33
  489.2 53.1 %collective-permute-start.15 = (f32[96,2048]{1,0:T(8,128)S(1)}, f32[96,2048]{1,0:T(8,128)S(1)}, u32[]{:S(2)}, u32[]{:S(2)}) collective-permute-start(f32[96,2048]{1,0:T(8,128)S(1)} %shard_map.39), channel_id=1, source_target_pairs={{0,2},{6,4},{1,3},{7,5},{8,10},{14,12},{9,11},{15,13},{16,18},{22,... | collective-permute-start | bytes 2359304 | tf_op jit(solution)/shard_map/ppermute | solution.py:33
  495.2 49.7 %collective-permute-start.18 = (f32[64,2048]{1,0:T(8,128)S(1)}, f32[64,2048]{1,0:T(8,128)S(1)}, u32[]{:S(2)}, u32[]{:S(2)}) collective-permute-start(f32[64,2048]{1,0:T(8,128)S(1)} %add.184), channel_id=1, source_target_pairs={{2,4},{4,2},{3,5},{5,3},{10,12},{12,10},{11,13},{13,11},{18,20},{2... | collective-permute-start | bytes 1572872 | tf_op jit(solution)/shard_map/ppermute | solution.py:33
  497.1 37.3 %collective-permute-start.20 = (f32[32,2048]{1,0:T(8,128)S(1)}, f32[32,2048]{1,0:T(8,128)S(1)}, u32[]{:S(2)}, u32[]{:S(2)}) collective-permute-start(f32[32,2048]{1,0:T(8,128)S(1)} %shard_map.41), channel_id=1, source_target_pairs={{0,2},{6,4},{1,3},{7,5},{8,10},{14,12},{9,11},{15,13},{16,18},{22,... | collective-permute-start | bytes 786440 | tf_op jit(solution)/shard_map/ppermute | solution.py:33
  505.8 45.5 %collective-permute-start.28 = (f32[96,2048]{1,0:T(8,128)S(1)}, f32[96,2048]{1,0:T(8,128)S(1)}, u32[]{:S(2)}, u32[]{:S(2)}) collective-permute-start(f32[96,2048]{1,0:T(8,128)S(1)} %shard_map.47), channel_id=1, source_target_pairs={{0,2},{6,4},{1,3},{7,5},{8,10},{14,12},{9,11},{15,13},{16,18},{22,... | collective-permute-start | bytes 2359304 | tf_op jit(solution)/shard_map/ppermute | solution.py:33
  534.4 28.6 %collective-permute-start.13 = (f32[96,2048]{1,0:T(8,128)S(1)}, f32[96,2048]{1,0:T(8,128)}, u32[]{:S(2)}, u32[]{:S(2)}) collective-permute-start(f32[96,2048]{1,0:T(8,128)S(1)} %shard_map.38), channel_id=1, source_target_pairs={{0,2},{6,4},{1,3},{7,5},{8,10},{14,12},{9,11},{15,13},{16,18},{22,... | collective-permute-start | bytes 2359304 | tf_op jit(solution)/shard_map/ppermute | solution.py:33
  540.7 54.0 %collective-permute-start.25 = (f32[96,2048]{1,0:T(8,128)}, f32[96,2048]{1,0:T(8,128)}, u32[]{:S(2)}, u32[]{:S(2)}) collective-permute-start(f32[96,2048]{1,0:T(8,128)} %add.188), channel_id=1, source_target_pairs={{2,4},{4,2},{3,5},{5,3},{10,12},{12,10},{11,13},{13,11},{18,20},{2... | collective-permute-start | bytes 2359304 | tf_op jit(solution)/shard_map/ppermute | solution.py:33
  543.3 54.5 %collective-permute-start.16 = (f32[96,2048]{1,0:T(8,128)}, f32[96,2048]{1,0:T(8,128)}, u32[]{:S(2)}, u32[]{:S(2)}) collective-permute-start(f32[96,2048]{1,0:T(8,128)} %add.182), channel_id=1, source_target_pairs={{2,4},{4,2},{3,5},{5,3},{10,12},{12,10},{11,13},{13,11},{18,20},{2... | collective-permute-start | bytes 2359304 | tf_op jit(solution)/shard_map/ppermute | solution.py:33
  544.9 1.6 collective-permute-start.21
  546.5 52.8 %collective-permute-start.19 = (f32[64,2048]{1,0:T(8,128)}, f32[64,2048]{1,0:T(8,128)}, u32[]{:S(2)}, u32[]{:S(2)}) collective-permute-start(f32[64,2048]{1,0:T(8,128)} %add.185.total), channel_id=1, source_target_pairs={{2,0},{4,6},{3,1},{5,7},{10,8},{12,14},{11,9},{13,15},{18,16},{20,... | collective-permute-start | bytes 1572872 | tf_op jit(solution)/shard_map/ppermute | solution.py:33
  547.8 39.2 %copy-start.12 = (f32[32,2048]{1,0:T(8,128)}, f32[32,2048]{1,0:T(8,128)S(1)}, u32[]{:S(2)}) copy-start(f32[32,2048]{1,0:T(8,128)S(1)} %add.187.total) | copy-start | bytes 786436
  552.1 33.4 %collective-permute-start.22 = (f32[32,2048]{1,0:T(8,128)S(1)}, f32[32,2048]{1,0:T(8,128)S(1)}, u32[]{:S(2)}, u32[]{:S(2)}) collective-permute-start(f32[32,2048]{1,0:T(8,128)S(1)} %add.187.total), channel_id=1, source_target_pairs={{2,0},{4,6},{3,1},{5,7},{10,8},{12,14},{11,9},{13,15},{18,16},{20,... | collective-permute-start | bytes 786440 | tf_op jit(solution)/shard_map/ppermute | solution.py:33
  563.0 46.7 %collective-permute-start.29 = (f32[96,2048]{1,0:T(8,128)S(1)}, f32[96,2048]{1,0:T(8,128)S(1)}, u32[]{:S(2)}, u32[]{:S(2)}) collective-permute-start(f32[96,2048]{1,0:T(8,128)S(1)} %add.190), channel_id=1, source_target_pairs={{2,4},{4,2},{3,5},{5,3},{10,12},{12,10},{11,13},{13,11},{18,20},{2... | collective-permute-start | bytes 2359304 | tf_op jit(solution)/shard_map/ppermute | solution.py:33
  586.2 24.9 %collective-permute-start.14 = (f32[96,2048]{1,0:T(8,128)S(1)}, f32[96,2048]{1,0:T(8,128)S(1)}, u32[]{:S(2)}, u32[]{:S(2)}) collective-permute-start(f32[96,2048]{1,0:T(8,128)S(1)} %add.180), channel_id=1, source_target_pairs={{2,4},{4,2},{3,5},{5,3},{10,12},{12,10},{11,13},{13,11},{18,20},{2... | collective-permute-start | bytes 2359304 | tf_op jit(solution)/shard_map/ppermute | solution.py:33
  587.0 2.3 copy-start.1
  589.2 2.3 copy-start.7
  594.7 7.8 slice-start
  596.3 17.4 %collective-permute-start.26 = (f32[96,2048]{1,0:T(8,128)S(1)}, f32[96,2048]{1,0:T(8,128)S(1)}, u32[]{:S(2)}, u32[]{:S(2)}) collective-permute-start(f32[96,2048]{1,0:T(8,128)S(1)} %add.189.total), channel_id=1, source_target_pairs={{2,0},{4,6},{3,1},{5,7},{10,8},{12,14},{11,9},{13,15},{18,16},{20,... | collective-permute-start | bytes 2359304 | tf_op jit(solution)/shard_map/ppermute | solution.py:33
  599.2 3.3 slice-start.1
  601.2 26.8 %collective-permute-start.23 = (f32[96,2048]{1,0:T(8,128)S(1)}, f32[96,2048]{1,0:T(8,128)S(1)}, u32[]{:S(2)}, u32[]{:S(2)}) collective-permute-start(f32[96,2048]{1,0:T(8,128)S(1)} %add.183.total), channel_id=1, source_target_pairs={{2,0},{4,6},{3,1},{5,7},{10,8},{12,14},{11,9},{13,15},{18,16},{20,... | collective-permute-start | bytes 2359304 | tf_op jit(solution)/shard_map/ppermute | solution.py:33
  603.8 36.7 %collective-permute-start.32 = (f32[32,2048]{1,0:T(8,128)S(1)}, f32[32,2048]{1,0:T(8,128)S(1)}, u32[]{:S(2)}, u32[]{:S(2)}) collective-permute-start(f32[32,2048]{1,0:T(8,128)S(1)} %shard_map.50), channel_id=1, source_target_pairs={{0,2},{6,4},{1,3},{7,5},{8,10},{14,12},{9,11},{15,13},{16,18},{22,... | collective-permute-start | bytes 786440 | tf_op jit(solution)/shard_map/ppermute | solution.py:33
  609.7 31.5 %collective-permute-start.11 = (f32[32,2048]{1,0:T(8,128)S(1)}, f32[32,2048]{1,0:T(8,128)S(1)}, u32[]{:S(2)}, u32[]{:S(2)}) collective-permute-start(f32[32,2048]{1,0:T(8,128)S(1)} %shard_map.37), channel_id=1, source_target_pairs={{0,2},{6,4},{1,3},{7,5},{8,10},{14,12},{9,11},{15,13},{16,18},{22,... | collective-permute-start | bytes 786440 | tf_op jit(solution)/shard_map/ppermute | solution.py:33
  630.7 16.7 %slice-start.2 = ((s8[4456448]{0:T(1024)(128)(4,1)}), s8[4194304]{0:T(1024)(128)(4,1)S(1)}, s32[]{:S(2)}) async-start(s8[4456448]{0:T(1024)(128)(4,1)} %bitcast.66), calls=%async_computation.3 | async-start | bytes 8388608
  630.8 16.6 %slice-start.3 = ((s8[4456448]{0:T(1024)(128)(4,1)}), s8[262144]{0:T(1024)(128)(4,1)S(1)}, s32[]{:S(2)}) async-start(s8[4456448]{0:T(1024)(128)(4,1)} %bitcast.66), calls=%async_computation.4 | async-start | bytes 524288
  630.8 16.6 %collective-permute-start.30 = (f32[96,2048]{1,0:T(8,128)S(1)}, f32[96,2048]{1,0:T(8,128)S(1)}, u32[]{:S(2)}, u32[]{:S(2)}) collective-permute-start(f32[96,2048]{1,0:T(8,128)S(1)} %add.191.total), channel_id=1, source_target_pairs={{2,0},{4,6},{3,1},{5,7},{10,8},{12,14},{11,9},{13,15},{18,16},{20,... | collective-permute-start | bytes 2359304 | tf_op jit(solution)/shard_map/ppermute | solution.py:33
  632.3 29.2 %collective-permute-start.27 = (f32[96,2048]{1,0:T(8,128)S(1)}, f32[96,2048]{1,0:T(8,128)}, u32[]{:S(2)}, u32[]{:S(2)}) collective-permute-start(f32[96,2048]{1,0:T(8,128)S(1)} %add.181.total), channel_id=1, source_target_pairs={{2,0},{4,6},{3,1},{5,7},{10,8},{12,14},{11,9},{13,15},{18,16},{20,... | collective-permute-start | bytes 2359304 | tf_op jit(solution)/shard_map/ppermute | solution.py:33
  640.5 2.8 collective-permute-start.33
  641.2 2.1 collective-permute-start.12
  664.4 9.0 %collective-permute-start.34 = (f32[32,2048]{1,0:T(8,128)S(1)}, f32[32,2048]{1,0:T(8,128)S(1)}, u32[]{:S(2)}, u32[]{:S(2)}) collective-permute-start(f32[32,2048]{1,0:T(8,128)S(1)} %add.193.total), channel_id=1, source_target_pairs={{2,0},{4,6},{3,1},{5,7},{10,8},{12,14},{11,9},{13,15},{18,16},{20,... | collective-permute-start | bytes 786440 | tf_op jit(solution)/shard_map/ppermute | solution.py:33
  665.7 9.8 %collective-permute-start.31 = (f32[32,2048]{1,0:T(8,128)S(1)}, f32[32,2048]{1,0:T(8,128)S(1)}, u32[]{:S(2)}, u32[]{:S(2)}) collective-permute-start(f32[32,2048]{1,0:T(8,128)S(1)} %add.179.total), channel_id=1, source_target_pairs={{2,0},{4,6},{3,1},{5,7},{10,8},{12,14},{11,9},{13,15},{18,16},{20,... | collective-permute-start | bytes 786440 | tf_op jit(solution)/shard_map/ppermute | solution.py:33
  679.1 1.2 collective-permute-start.35
  680.3 3.6 collective-permute-start.36
  683.9 3.6 collective-permute-start.37
  687.5 4.5 collective-permute-start.38
  691.9 3.6 collective-permute-start.39
  695.7 2.3 copy-start.2
  698.0 2.3 copy-start.9
  703.1 28.8 %collective-permute-start.40 = (f32[136,2048]{1,0:T(8,128)S(1)}, f32[136,2048]{1,0:T(8,128)}, u32[]{:S(2)}, u32[]{:S(2)}) collective-permute-start(f32[136,2048]{1,0:T(8,128)S(1)} %shard_map.53), channel_id=1, source_target_pairs={{0,2},{6,4},{1,3},{7,5},{8,10},{14,12},{9,11},{15,13},{16,18},{22,... | collective-permute-start | bytes 3342344 | tf_op jit(solution)/shard_map/ppermute | solution.py:33
  708.0 2.3 copy-start.3
  710.3 2.3 copy-start.10
  715.5 40.3 %collective-permute-start.44 = (f32[136,2048]{1,0:T(8,128)S(1)}, f32[136,2048]{1,0:T(8,128)}, u32[]{:S(2)}, u32[]{:S(2)}) collective-permute-start(f32[136,2048]{1,0:T(8,128)S(1)} %shard_map.54), channel_id=1, source_target_pairs={{0,2},{6,4},{1,3},{7,5},{8,10},{14,12},{9,11},{15,13},{16,18},{22,... | collective-permute-start | bytes 3342344 | tf_op jit(solution)/shard_map/ppermute | solution.py:33
  734.3 23.6 %collective-permute-start.41 = (f32[136,2048]{1,0:T(8,128)}, f32[136,2048]{1,0:T(8,128)S(1)}, u32[]{:S(2)}, u32[]{:S(2)}) collective-permute-start(f32[136,2048]{1,0:T(8,128)} %add.203), channel_id=1, source_target_pairs={{2,4},{4,2},{3,5},{5,3},{10,12},{12,10},{11,13},{13,11},{18,20},{2... | collective-permute-start | bytes 3342344 | tf_op jit(solution)/shard_map/ppermute | solution.py:33
  735.0 2.3 copy-start.4
  737.3 2.3 copy-start.11
  742.5 31.8 %collective-permute-start.43 = (f32[136,2048]{1,0:T(8,128)S(1)}, f32[136,2048]{1,0:T(8,128)S(1)}, u32[]{:S(2)}, u32[]{:S(2)}) collective-permute-start(f32[136,2048]{1,0:T(8,128)S(1)} %shard_map.55), channel_id=1, source_target_pairs={{0,2},{6,4},{1,3},{7,5},{8,10},{14,12},{9,11},{15,13},{16,18},{22,... | collective-permute-start | bytes 3342344 | tf_op jit(solution)/shard_map/ppermute | solution.py:33
  757.2 17.1 %collective-permute-start.45 = (f32[136,2048]{1,0:T(8,128)S(1)}, f32[136,2048]{1,0:T(8,128)S(1)}, u32[]{:S(2)}, u32[]{:S(2)}) collective-permute-start(f32[136,2048]{1,0:T(8,128)S(1)} %add.207), channel_id=1, source_target_pairs={{2,4},{4,2},{3,5},{5,3},{10,12},{12,10},{11,13},{13,11},{18,20},{2... | collective-permute-start | bytes 3342344 | tf_op jit(solution)/shard_map/ppermute | solution.py:33
  758.1 19.4 %collective-permute-start.42 = (f32[136,2048]{1,0:T(8,128)S(1)}, f32[136,2048]{1,0:T(8,128)S(1)}, u32[]{:S(2)}, u32[]{:S(2)}) collective-permute-start(f32[136,2048]{1,0:T(8,128)S(1)} %add.204), channel_id=1, source_target_pairs={{2,0},{4,6},{3,1},{5,7},{10,8},{12,14},{11,9},{13,15},{18,16},{20,... | collective-permute-start | bytes 3342344 | tf_op jit(solution)/shard_map/ppermute | solution.py:33
  (6 other events, 6.5 us)

commit v2 on v1

--- a/solution.py
+++ b/solution.py
@@ -48,8 +48,8 @@
     if outers != LINE or rest % TILE or rest // TILE < 12:
         return None
     tiles = rest // TILE
-    body = tiles - 4
-    sizes = [1, 2] + [3] * (body // 3) + [body % 3] * (body % 3 > 0) + [1]
+    body = tiles - 6
+    sizes = [1, 2] + [3] * (body // 3) + [body % 3] * (body % 3 > 0) + [1, 1, 1]
     return cut, sizes
 
 
@@ -68,7 +68,7 @@
         ),
         out_shape=out_shape,
         input_output_aliases=aliases,
-        compiler_params=pltpu.CompilerParams(vmem_limit_bytes=24 << 20),
+        compiler_params=pltpu.CompilerParams(vmem_limit_bytes=60 << 20),
         cost_estimate=pl.CostEstimate(flops=4 * moved, bytes_accessed=4 * moved, transcendentals=0),
     )(*operands)
 
@@ -221,22 +221,31 @@
     flat = [value.reshape(outers * rest, columns) for value in held]
     flat_v = line_v.reshape(outers * rest, columns)
     end_flag = is_end.astype(jnp.int32).reshape(1)
-    start, carried, squares = 0, (), []
+    start, carried, squares, totals = 0, (), [], []
+    next_spread_v = spread_update(spread_v, factor)
+    spread_sq = spread_norms(next_spread_v)
+    early = {1: next_spread_v, 2: spread_sq}
     for chunk, tiles in enumerate(sizes):
         own = step_chunk(line_factor, flat, flat_v, start, tiles)
-        own = own + send(own, TO_MIDS)
+        got = send(own, TO_MIDS)
+        if chunk >= 2:
+            got = tie(got, totals[chunk - 2])
+        own = own + got
         own = own + send(own, ACROSS)
+        if chunk in early:
+            own = tie(own, early[chunk])
         if chunk >= 3:
-            own = tie(own, squares[chunk - 2])
+            own = tie(own, squares[chunk - 3])
+        totals.append(own)
         back = send(own, TO_ENDS)
         carried = tuple(
             move_chunk(end_flag, 1 / worker_count, own, back, flat, flat_v, start, tiles, carried)
         )
         squares.append(carried[1])
         start += tiles
-    spread_v = spread_update(spread_v, factor)
+    spread_v = next_spread_v
     line_v = carried[0].reshape(line_v.shape)
-    factor, line_factor = factors(spread_norms(spread_v) + placed(jnp.sum(carried[1], axis=(1, 2))))
+    factor, line_factor = factors(spread_sq + placed(jnp.sum(carried[1], axis=(1, 2))))
 
     block, v = [], line_v
     for place in range(LINE):

time: 784 us -> 751 us (0.958)
  waiting for transfers between devices: 530 us -> 473 us
  Pallas kernels: 43.8 us -> 69.4 us
  local copies, waits for them, and re-layouts: 54.3 us -> 31.4 us
  starting transfers between devices: 82.8 us -> 96.4 us
    ppermute x36 -> x39, waiting for transfers between devices: 508 us -> 451 us  [send(): return lax.ppermute(value, axis, pairs)]
    pallas_call x20 -> x22, Pallas kernels: 43.8 us -> 69.4 us  [run(): pl.pallas_call(kernel, grid_spec=pltpu.PrefetchScalarGridSpec(num_scalar_...]
    unnamed x46 -> x62, local copies, waits for them, and re-layouts: 26.9 us -> 3.92 us
    ppermute x36 -> x39, starting transfers between devices: 65.1 us -> 78.4 us  [send(): return lax.ppermute(value, axis, pairs)]
  transfers between devices with their start and end apart: 47 -> 50, of which waited for: 27 -> 24; matrix products, arithmetic and copies ran while one was open for 10% -> 11% of each run, Pallas kernels for 5% -> 8%
where the time goes in v2:
time: 751 us; the launch traced here: 748 us
  waiting for transfers between devices  473 us (63%)
  starting transfers between devices  96.4 us (13%)
  other arithmetic  76.2 us (10%)
  Pallas kernels  69.4 us (9%)
  local copies, waits for them, and re-layouts  31.4 us (4%)
    ppermute x39, waiting for transfers between devices, send(): return lax.ppermute(value, axis, pairs)  451 us
    ppermute x39, starting transfers between devices, send(): return lax.ppermute(value, axis, pairs)  78.4 us
    pallas_call x22, Pallas kernels, run(): pl.pallas_call(kernel, grid_spec=pltpu.PrefetchScalarGridSpec(num_scalar_...  69.4 us
    ppermute x10, waiting for transfers between devices, sum_over_devices(): lax.ppermute(value, axis, [(i, i ^ step) for i in range(size)])  21.6 us
    reduce_sum x4, other arithmetic, on_device(): square = jnp.sum(jnp.square(held[place] - v))  18.9 us
  transfers between devices with their start and end apart: 50, of which 24 were waited for; matrix products, arithmetic and copies ran while one was open for 11% of the time, Pallas kernels for 8%

profile of v2, /device:TPU:0, one launch (start us, length us, event | category | flops | bytes accessed | tf_op | source)
XLA Modules:
  0.0 747.8 jit_solution(8766707890403228571)
XLA Ops:
  0.0 10.5 %slice.28 = f32[16,88,2048]{2,1,0:T(8,128)} slice(f32[16,224,2048]{2,1,0:T(8,128)} %bitcast.77), slice={[0:16], [0:88], [0:2048]} | slice | bytes 23068672 | tf_op jit(solution)/shard_map/slice | solution.py:187
  10.5 7.6 %all-to-all-start = ((f32[16,88,2048]{2,1,0:T(8,128)}), f32[16,88,2048]{2,1,0:T(8,128)}, u32[]{:S(2)}, u32[]{:S(2)}) async-start(f32[16,88,2048]{2,1,0:T(8,128)} %slice.28), calls=%async_computation | async-start | bytes 23068672 | tf_op jit(solution)/shard_map/all_to_all | solution.py:186
  21.2 207.3 %collective-permute-done = f32[136,2048]{1,0:T(8,128)S(1)} collective-permute-done((f32[136,2048]{1,0:T(8,128)S(1)}, f32[136,2048]{1,0:T(8,128)S(1)}, u32[]{:S(2)}, u32[]{:S(2)}) %collective-permute-start) | collective-permute-done | bytes 1114144 | tf_op jit(solution)/shard_map/ppermute | solution.py:33
  229.5 2.6 maximum_select_fusion.1
  234.1 4.8 constant_dynamic-slice_fusion.3
  238.9 4.9 constant_dynamic-slice_fusion.2
  243.8 4.9 constant_dynamic-slice_fusion.1
  253.5 113.8 %collective-permute-done.2 = f32[2,136,2048]{2,1,0:T(8,128)} collective-permute-done((f32[2,136,2048]{2,1,0:T(8,128)}, f32[2,136,2048]{2,1,0:T(8,128)}, u32[]{:S(2)}, u32[]{:S(2)}) %collective-permute-start.2) | collective-permute-done | bytes 2228256 | tf_op jit(solution)/shard_map/ppermute | solution.py:33
  369.4 5.9 multiply_reduce_fusion.7
  375.9 4.9 multiply_reduce_fusion.6
  381.5 4.0 multiply_reduce_fusion.5
  386.2 64.5 %collective-permute-done.5.refs_0_ = f32[4,136,2048]{2,1,0:T(8,128)} collective-permute-done((f32[4,136,2048]{2,1,0:T(8,128)}, f32[4,136,2048]{2,1,0:T(8,128)}, u32[]{:S(2)}, u32[]{:S(2)}) %collective-permute-start.5) | collective-permute-done | bytes 4456480 | tf_op jit(solution)/shard_map/ppermute | solution.py:33
  450.7 4.0 multiply_reduce_fusion.4
  455.4 5.6 multiply_reduce_fusion.3
  465.8 3.6 collective-permute-done.8
  470.0 3.8 collective-permute-done.9
  475.4 2.0 collective-permute-done.10
  478.1 2.5 shard_map.42
  482.5 2.1 shard_map.41
  485.9 3.7 shard_map.40
  491.0 3.7 shard_map.45
  494.7 2.3 collective-permute-start.24
  497.0 3.7 shard_map.39
  500.7 2.2 collective-permute-start.13
  505.4 6.0 multiply_reduce_fusion.2
  511.4 6.1 collective-permute-done.14
  520.4 2.6 shard_map.48
  523.0 6.0 collective-permute-start.29
  532.2 2.2 collective-permute-done.24
  537.3 5.6 multiply_reduce_fusion.1
  544.2 7.1 collective-permute-done.13
  557.4 2.3 shard_map.43
  565.8 2.1 shard_map.38
  567.9 3.9 collective-permute-done.21.back
  571.9 5.8 collective-permute-start.12
  577.7 2.8 shard_map.44
  583.4 2.1 shard_map.51
  585.5 6.1 collective-permute-start.34
  592.4 2.1 shard_map.37
  594.4 3.1 collective-permute-start.11
  598.8 4.4 shard_map.46
  606.9 4.3 shard_map.47
  615.3 5.3 collective-permute-done.32.back
  620.6 4.1 shard_map.49
  626.0 5.0 collective-permute-done.31.back
  631.0 2.8 shard_map.50
  635.8 2.2 shard_map.52
  638.7 2.2 shard_map.53
  642.7 2.2 shard_map.54
  654.3 2.5 collective-permute-start.41
  660.3 2.0 collective-permute-done.42
  663.1 4.4 shard_map.55
  667.4 4.5 collective-permute-start.43
  671.9 4.4 shard_map.56
  676.3 2.3 collective-permute-start.47
  678.6 17.5 %collective-permute-done.43 = f32[136,2048]{1,0:T(8,128)} collective-permute-done((f32[136,2048]{1,0:T(8,128)}, f32[136,2048]{1,0:T(8,128)}, u32[]{:S(2)}, u32[]{:S(2)}) %collective-permute-start.43) | collective-permute-done | bytes 1114144 | tf_op jit(solution)/shard_map/ppermute | solution.py:33
  699.2 4.4 shard_map.57
  703.6 7.1 collective-permute-start.46
  710.7 4.4 shard_map.58
  715.1 4.9 collective-permute-done.47
  725.5 6.0 multiply_reduce_fusion
  731.6 6.9 collective-permute-done.46
  738.5 5.7 collective-permute-done.45
  744.2 2.2 bitcast_add_fusion
  (183 shorter events, 93.7 us)
Async XLA Ops:
  10.5 444.9 %all-to-all-start = ((f32[16,88,2048]{2,1,0:T(8,128)}), f32[16,88,2048]{2,1,0:T(8,128)}, u32[]{:S(2)}, u32[]{:S(2)}) async-start(f32[16,88,2048]{2,1,0:T(8,128)} %slice.28), calls=%async_computation | async-start | bytes 23068672 | tf_op jit(solution)/shard_map/all_to_all | solution.py:186
  19.3 209.2 %collective-permute-start = (f32[136,2048]{1,0:T(8,128)S(1)}, f32[136,2048]{1,0:T(8,128)S(1)}, u32[]{:S(2)}, u32[]{:S(2)}) collective-permute-start(f32[136,2048]{1,0:T(8,128)S(1)} %get-tuple-element.93), channel_id=1, source_target_pairs={{0,2},{2,0},{4,6},{6,4},{1,3},{3,1},{5,7},{7,5},{8,10},{10,8},{12,... | collective-permute-start | bytes 3342344 | tf_op jit(solution)/shard_map/ppermute | solution.py:33
  232.1 18.3 %collective-permute-start.1 = (f32[2,136,2048]{2,1,0:T(8,128)S(1)}, f32[2,136,2048]{2,1,0:T(8,128)}, u32[]{:S(2)}, u32[]{:S(2)}) collective-permute-start(f32[2,136,2048]{2,1,0:T(8,128)S(1)} %maximum_select_fusion.1), channel_id=1, source_target_pairs={{2,4},{4,2},{3,5},{5,3},{10,12},{12,10},{11,13},{13,11},{18,20},{2... | collective-permute-start | bytes 6684680 | tf_op jit(solution)/shard_map/ppermute | solution.py:33
  248.7 127.2 %collective-permute-start.3 = (f32[4,136,2048]{2,1,0:T(8,128)}, f32[4,136,2048]{2,1,0:T(8,128)}, u32[]{:S(2)}, u32[]{:S(2)}) collective-permute-start(f32[4,136,2048]{2,1,0:T(8,128)} %constant_dynamic-slice_fusion.1), channel_id=1, source_target_pairs={{0,8},{8,0},{16,24},{24,16},{1,9},{9,1},{17,25},{25,17},{2,10},{10... | collective-permute-start | bytes 13369352 | tf_op jit(solution)/shard_map/ppermute | solution.py:33
  248.7 132.8 %collective-permute-start.4 = (f32[4,136,2048]{2,1,0:T(8,128)}, f32[4,136,2048]{2,1,0:T(8,128)}, u32[]{:S(2)}, u32[]{:S(2)}) collective-permute-start(f32[4,136,2048]{2,1,0:T(8,128)} %constant_dynamic-slice_fusion.2), channel_id=1, source_target_pairs={{0,24},{8,16},{16,8},{24,0},{1,25},{9,17},{17,9},{25,1},{2,26},{10... | collective-permute-start | bytes 13369352 | tf_op jit(solution)/shard_map/ppermute | solution.py:33
  250.4 116.9 %collective-permute-start.2 = (f32[2,136,2048]{2,1,0:T(8,128)}, f32[2,136,2048]{2,1,0:T(8,128)}, u32[]{:S(2)}, u32[]{:S(2)}) collective-permute-start(f32[2,136,2048]{2,1,0:T(8,128)} %collective-permute-done.1), channel_id=1, source_target_pairs={{2,0},{4,6},{3,1},{5,7},{10,8},{12,14},{11,9},{13,15},{18,16},{20,... | collective-permute-start | bytes 6684680 | tf_op jit(solution)/shard_map/ppermute | solution.py:33
  251.7 199.0 %collective-permute-start.5 = (f32[4,136,2048]{2,1,0:T(8,128)}, f32[4,136,2048]{2,1,0:T(8,128)}, u32[]{:S(2)}, u32[]{:S(2)}) collective-permute-start(f32[4,136,2048]{2,1,0:T(8,128)} %constant_dynamic-slice_fusion.3), channel_id=1, source_target_pairs={{0,16},{8,24},{16,0},{24,8},{1,17},{9,25},{17,1},{25,9},{2,18},{10... | collective-permute-start | bytes 13369352 | tf_op jit(solution)/shard_map/ppermute | solution.py:33
  375.2 75.5 %copy-start = (f32[4,136,2048]{2,1,0:T(8,128)}, f32[4,136,2048]{2,1,0:T(8,128)S(1)}, u32[]{:S(2)}) copy-start(f32[4,136,2048]{2,1,0:T(8,128)S(1)} %get-tuple-element.52) | copy-start | bytes 13369348
  461.1 1.2 collective-permute-start.6
  462.2 3.6 collective-permute-start.7
  465.8 3.6 collective-permute-start.8
  469.4 4.5 collective-permute-start.9
  473.8 3.6 collective-permute-start.10
  480.6 23.1 %collective-permute-start.19 = (f32[64,2048]{1,0:T(8,128)}, f32[64,2048]{1,0:T(8,128)S(1)}, u32[]{:S(2)}, u32[]{:S(2)}) collective-permute-start(f32[64,2048]{1,0:T(8,128)} %shard_map.42), channel_id=1, source_target_pairs={{0,2},{6,4},{1,3},{7,5},{8,10},{14,12},{9,11},{15,13},{16,18},{22,... | collective-permute-start | bytes 1572872 | tf_op jit(solution)/shard_map/ppermute | solution.py:33
  484.6 18.4 %collective-permute-start.15 = (f32[32,2048]{1,0:T(8,128)}, f32[32,2048]{1,0:T(8,128)S(1)}, u32[]{:S(2)}, u32[]{:S(2)}) collective-permute-start(f32[32,2048]{1,0:T(8,128)} %shard_map.41), channel_id=1, source_target_pairs={{0,2},{6,4},{1,3},{7,5},{8,10},{14,12},{9,11},{15,13},{16,18},{22,... | collective-permute-start | bytes 786440 | tf_op jit(solution)/shard_map/ppermute | solution.py:33
  489.6 27.9 %collective-permute-start.14 = (f32[96,2048]{1,0:T(8,128)}, f32[96,2048]{1,0:T(8,128)S(1)}, u32[]{:S(2)}, u32[]{:S(2)}) collective-permute-start(f32[96,2048]{1,0:T(8,128)} %shard_map.40), channel_id=1, source_target_pairs={{0,2},{6,4},{1,3},{7,5},{8,10},{14,12},{9,11},{15,13},{16,18},{22,... | collective-permute-start | bytes 2359304 | tf_op jit(solution)/shard_map/ppermute | solution.py:33
  494.7 9.0 %copy-start.16 = (f32[64,2048]{1,0:T(8,128)S(1)}, f32[64,2048]{1,0:T(8,128)}, u32[]{:S(2)}) copy-start(f32[64,2048]{1,0:T(8,128)} %shard_map.42) | copy-start | bytes 1572868
  494.7 39.7 %collective-permute-start.24 = (f32[96,2048]{1,0:T(8,128)}, f32[96,2048]{1,0:T(8,128)}, u32[]{:S(2)}, u32[]{:S(2)}) collective-permute-start(f32[96,2048]{1,0:T(8,128)} %shard_map.45), channel_id=1, source_target_pairs={{0,2},{6,4},{1,3},{7,5},{8,10},{14,12},{9,11},{15,13},{16,18},{22,... | collective-permute-start | bytes 2359304 | tf_op jit(solution)/shard_map/ppermute | solution.py:33
  500.7 50.5 %collective-permute-start.13 = (f32[96,2048]{1,0:T(8,128)}, f32[96,2048]{1,0:T(8,128)}, u32[]{:S(2)}, u32[]{:S(2)}) collective-permute-start(f32[96,2048]{1,0:T(8,128)} %shard_map.39), channel_id=1, source_target_pairs={{0,2},{6,4},{1,3},{7,5},{8,10},{14,12},{9,11},{15,13},{16,18},{22,... | collective-permute-start | bytes 2359304 | tf_op jit(solution)/shard_map/ppermute | solution.py:33
  503.0 8.4 %collective-permute-start.16 = (f32[32,2048]{1,0:T(8,128)S(1)}, f32[32,2048]{1,0:T(8,128)S(1)}, u32[]{:S(2)}, u32[]{:S(2)}) collective-permute-start(f32[32,2048]{1,0:T(8,128)S(1)} %add.184), channel_id=1, source_target_pairs={{2,4},{4,2},{3,5},{5,3},{10,12},{12,10},{11,13},{13,11},{18,20},{2... | collective-permute-start | bytes 786440 | tf_op jit(solution)/shard_map/ppermute | solution.py:33
  503.8 13.8 %copy-start.11 = (f32[96,2048]{1,0:T(8,128)S(1)}, f32[96,2048]{1,0:T(8,128)}, u32[]{:S(2)}) copy-start(f32[96,2048]{1,0:T(8,128)} %shard_map.40) | copy-start | bytes 2359300
  503.8 25.2 %collective-permute-start.20 = (f32[64,2048]{1,0:T(8,128)S(1)}, f32[64,2048]{1,0:T(8,128)}, u32[]{:S(2)}, u32[]{:S(2)}) collective-permute-start(f32[64,2048]{1,0:T(8,128)S(1)} %add.190), channel_id=1, source_target_pairs={{2,4},{4,2},{3,5},{5,3},{10,12},{12,10},{11,13},{13,11},{18,20},{2... | collective-permute-start | bytes 1572872 | tf_op jit(solution)/shard_map/ppermute | solution.py:33
  511.4 17.6 %copy-start.19 = (f32[32,2048]{1,0:T(8,128)}, f32[32,2048]{1,0:T(8,128)S(1)}, u32[]{:S(2)}) copy-start(f32[32,2048]{1,0:T(8,128)S(1)} %add.185.total) | copy-start | bytes 786436
  517.7 25.3 %collective-permute-start.17 = (f32[96,2048]{1,0:T(8,128)S(1)}, f32[96,2048]{1,0:T(8,128)}, u32[]{:S(2)}, u32[]{:S(2)}) collective-permute-start(f32[96,2048]{1,0:T(8,128)S(1)} %add.186), channel_id=1, source_target_pairs={{2,4},{4,2},{3,5},{5,3},{10,12},{12,10},{11,13},{13,11},{18,20},{2... | collective-permute-start | bytes 2359304 | tf_op jit(solution)/shard_map/ppermute | solution.py:33
  520.4 14.0 %copy-start.10 = (f32[96,2048]{1,0:T(8,128)S(1)}, f32[96,2048]{1,0:T(8,128)}, u32[]{:S(2)}) copy-start(f32[96,2048]{1,0:T(8,128)} %shard_map.45) | copy-start | bytes 2359300
  523.0 39.5 %collective-permute-start.29 = (f32[64,2048]{1,0:T(8,128)}, f32[64,2048]{1,0:T(8,128)}, u32[]{:S(2)}, u32[]{:S(2)}) collective-permute-start(f32[64,2048]{1,0:T(8,128)} %shard_map.48), channel_id=1, source_target_pairs={{0,2},{6,4},{1,3},{7,5},{8,10},{14,12},{9,11},{15,13},{16,18},{22,... | collective-permute-start | bytes 1572872 | tf_op jit(solution)/shard_map/ppermute | solution.py:33
  529.0 26.4 %collective-permute-start.22 = (f32[32,2048]{1,0:T(8,128)S(1)}, f32[32,2048]{1,0:T(8,128)S(1)}, u32[]{:S(2)}, u32[]{:S(2)}) collective-permute-start(f32[32,2048]{1,0:T(8,128)S(1)} %add.185.total), channel_id=1, source_target_pairs={{2,0},{4,6},{3,1},{5,7},{10,8},{12,14},{11,9},{13,15},{18,16},{20,... | collective-permute-start | bytes 786440 | tf_op jit(solution)/shard_map/ppermute | solution.py:33
  535.6 15.6 %copy-start.9 = (f32[96,2048]{1,0:T(8,128)S(1)}, f32[96,2048]{1,0:T(8,128)}, u32[]{:S(2)}) copy-start(f32[96,2048]{1,0:T(8,128)} %shard_map.39) | copy-start | bytes 2359300
  535.7 24.0 %collective-permute-start.25 = (f32[96,2048]{1,0:T(8,128)S(1)}, f32[96,2048]{1,0:T(8,128)}, u32[]{:S(2)}, u32[]{:S(2)}) collective-permute-start(f32[96,2048]{1,0:T(8,128)S(1)} %add.194), channel_id=1, source_target_pairs={{2,4},{4,2},{3,5},{5,3},{10,12},{12,10},{11,13},{13,11},{18,20},{2... | collective-permute-start | bytes 2359304 | tf_op jit(solution)/shard_map/ppermute | solution.py:33
  544.2 15.5 %copy-start.6 = (f32[96,2048]{1,0:T(8,128)}, f32[96,2048]{1,0:T(8,128)S(1)}, u32[]{:S(2)}) copy-start(f32[96,2048]{1,0:T(8,128)S(1)} %add.187.total) | copy-start | bytes 2359300
  552.5 28.0 %collective-permute-start.18 = (f32[96,2048]{1,0:T(8,128)S(1)}, f32[96,2048]{1,0:T(8,128)}, u32[]{:S(2)}, u32[]{:S(2)}) collective-permute-start(f32[96,2048]{1,0:T(8,128)S(1)} %add.188), channel_id=1, source_target_pairs={{2,4},{4,2},{3,5},{5,3},{10,12},{12,10},{11,13},{13,11},{18,20},{2... | collective-permute-start | bytes 2359304 | tf_op jit(solution)/shard_map/ppermute | solution.py:33
  554.1 17.8 %collective-permute-start.21 = (f32[64,2048]{1,0:T(8,128)}, f32[64,2048]{1,0:T(8,128)}, u32[]{:S(2)}, u32[]{:S(2)}) collective-permute-start(f32[64,2048]{1,0:T(8,128)} %add.191.total), channel_id=1, source_target_pairs={{2,0},{4,6},{3,1},{5,7},{10,8},{12,14},{11,9},{13,15},{18,16},{20,... | collective-permute-start | bytes 1572872 | tf_op jit(solution)/shard_map/ppermute | solution.py:33
  556.1 35.6 %collective-permute-start.27 = (f32[96,2048]{1,0:T(8,128)S(1)}, f32[96,2048]{1,0:T(8,128)}, u32[]{:S(2)}, u32[]{:S(2)}) collective-permute-start(f32[96,2048]{1,0:T(8,128)S(1)} %add.187.total), channel_id=1, source_target_pairs={{2,0},{4,6},{3,1},{5,7},{10,8},{12,14},{11,9},{13,15},{18,16},{20,... | collective-permute-start | bytes 2359304 | tf_op jit(solution)/shard_map/ppermute | solution.py:33
  561.2 45.7 %collective-permute-start.26 = (f32[96,2048]{1,0:T(8,128)S(1)}, f32[96,2048]{1,0:T(8,128)}, u32[]{:S(2)}, u32[]{:S(2)}) collective-permute-start(f32[96,2048]{1,0:T(8,128)S(1)} %add.195.total), channel_id=1, source_target_pairs={{2,0},{4,6},{3,1},{5,7},{10,8},{12,14},{11,9},{13,15},{18,16},{20,... | collective-permute-start | bytes 2359304 | tf_op jit(solution)/shard_map/ppermute | solution.py:33
  564.4 30.1 %collective-permute-start.30 = (f32[64,2048]{1,0:T(8,128)}, f32[64,2048]{1,0:T(8,128)}, u32[]{:S(2)}, u32[]{:S(2)}) collective-permute-start(f32[64,2048]{1,0:T(8,128)} %add.198), channel_id=1, source_target_pairs={{2,4},{4,2},{3,5},{5,3},{10,12},{12,10},{11,13},{13,11},{18,20},{2... | collective-permute-start | bytes 1572872 | tf_op jit(solution)/shard_map/ppermute | solution.py:33
  571.9 13.6 %collective-permute-start.12 = (f32[32,2048]{1,0:T(8,128)}, f32[32,2048]{1,0:T(8,128)S(1)}, u32[]{:S(2)}, u32[]{:S(2)}) collective-permute-start(f32[32,2048]{1,0:T(8,128)} %shard_map.38), channel_id=1, source_target_pairs={{0,2},{6,4},{1,3},{7,5},{8,10},{14,12},{9,11},{15,13},{16,18},{22,... | collective-permute-start | bytes 786440 | tf_op jit(solution)/shard_map/ppermute | solution.py:33
  582.0 9.7 %copy-start.24 = (f32[32,2048]{1,0:T(8,128)S(1)}, f32[32,2048]{1,0:T(8,128)}, u32[]{:S(2)}) copy-start(f32[32,2048]{1,0:T(8,128)} %shard_map.38) | copy-start | bytes 786436
  582.0 38.6 %collective-permute-start.32 = (f32[96,2048]{1,0:T(8,128)S(1)}, f32[96,2048]{1,0:T(8,128)}, u32[]{:S(2)}, u32[]{:S(2)}) collective-permute-start(f32[96,2048]{1,0:T(8,128)S(1)} %add.189.total), channel_id=1, source_target_pairs={{2,0},{4,6},{3,1},{5,7},{10,8},{12,14},{11,9},{13,15},{18,16},{20,... | collective-permute-start | bytes 2359304 | tf_op jit(solution)/shard_map/ppermute | solution.py:33
  585.5 17.7 %collective-permute-start.34 = (f32[32,2048]{1,0:T(8,128)}, f32[32,2048]{1,0:T(8,128)}, u32[]{:S(2)}, u32[]{:S(2)}) collective-permute-start(f32[32,2048]{1,0:T(8,128)} %shard_map.51), channel_id=1, source_target_pairs={{0,2},{6,4},{1,3},{7,5},{8,10},{14,12},{9,11},{15,13},{16,18},{22,... | collective-permute-start | bytes 786440 | tf_op jit(solution)/shard_map/ppermute | solution.py:33
  591.7 13.8 %collective-permute-start.23 = (f32[32,2048]{1,0:T(8,128)S(1)}, f32[32,2048]{1,0:T(8,128)S(1)}, u32[]{:S(2)}, u32[]{:S(2)}) collective-permute-start(f32[32,2048]{1,0:T(8,128)S(1)} %add.192), channel_id=1, source_target_pairs={{2,4},{4,2},{3,5},{5,3},{10,12},{12,10},{11,13},{13,11},{18,20},{2... | collective-permute-start | bytes 786440 | tf_op jit(solution)/shard_map/ppermute | solution.py:33
  594.4 16.8 %collective-permute-start.11 = (f32[32,2048]{1,0:T(8,128)}, f32[32,2048]{1,0:T(8,128)}, u32[]{:S(2)}, u32[]{:S(2)}) collective-permute-start(f32[32,2048]{1,0:T(8,128)} %shard_map.37), channel_id=1, source_target_pairs={{0,2},{6,4},{1,3},{7,5},{8,10},{14,12},{9,11},{15,13},{16,18},{22,... | collective-permute-start | bytes 786440 | tf_op jit(solution)/shard_map/ppermute | solution.py:33
  603.2 27.8 %collective-permute-start.31 = (f32[64,2048]{1,0:T(8,128)S(1)}, f32[64,2048]{1,0:T(8,128)}, u32[]{:S(2)}, u32[]{:S(2)}) collective-permute-start(f32[64,2048]{1,0:T(8,128)S(1)} %add.199.total), channel_id=1, source_target_pairs={{2,0},{4,6},{3,1},{5,7},{10,8},{12,14},{11,9},{13,15},{18,16},{20,... | collective-permute-start | bytes 1572872 | tf_op jit(solution)/shard_map/ppermute | solution.py:33
  605.5 8.7 %collective-permute-start.35 = (f32[32,2048]{1,0:T(8,128)S(1)}, f32[32,2048]{1,0:T(8,128)}, u32[]{:S(2)}, u32[]{:S(2)}) collective-permute-start(f32[32,2048]{1,0:T(8,128)S(1)} %add.200), channel_id=1, source_target_pairs={{2,4},{4,2},{3,5},{5,3},{10,12},{12,10},{11,13},{13,11},{18,20},{2... | collective-permute-start | bytes 786440 | tf_op jit(solution)/shard_map/ppermute | solution.py:33
  612.2 3.1 collective-permute-start.28
  612.9 22.2 %collective-permute-start.37 = (f32[32,2048]{1,0:T(8,128)S(1)}, f32[32,2048]{1,0:T(8,128)S(1)}, u32[]{:S(2)}, u32[]{:S(2)}) collective-permute-start(f32[32,2048]{1,0:T(8,128)S(1)} %add.193.total), channel_id=1, source_target_pairs={{2,0},{4,6},{3,1},{5,7},{10,8},{12,14},{11,9},{13,15},{18,16},{20,... | collective-permute-start | bytes 786440 | tf_op jit(solution)/shard_map/ppermute | solution.py:33
  615.3 9.5 %copy-start.21 = (f32[32,2048]{1,0:T(8,128)}, f32[32,2048]{1,0:T(8,128)S(1)}, u32[]{:S(2)}) copy-start(f32[32,2048]{1,0:T(8,128)S(1)} %add.201.total) | copy-start | bytes 786436
  615.3 18.4 %copy-start.20 = (f32[32,2048]{1,0:T(8,128)}, f32[32,2048]{1,0:T(8,128)S(1)}, u32[]{:S(2)}) copy-start(f32[32,2048]{1,0:T(8,128)S(1)} %add.197.total) | copy-start | bytes 786436
  624.7 13.3 %collective-permute-start.36 = (f32[32,2048]{1,0:T(8,128)S(1)}, f32[32,2048]{1,0:T(8,128)S(1)}, u32[]{:S(2)}, u32[]{:S(2)}) collective-permute-start(f32[32,2048]{1,0:T(8,128)S(1)} %add.201.total), channel_id=1, source_target_pairs={{2,0},{4,6},{3,1},{5,7},{10,8},{12,14},{11,9},{13,15},{18,16},{20,... | collective-permute-start | bytes 786440 | tf_op jit(solution)/shard_map/ppermute | solution.py:33
  633.8 8.3 %collective-permute-start.33 = (f32[32,2048]{1,0:T(8,128)S(1)}, f32[32,2048]{1,0:T(8,128)S(1)}, u32[]{:S(2)}, u32[]{:S(2)}) collective-permute-start(f32[32,2048]{1,0:T(8,128)S(1)} %add.197.total), channel_id=1, source_target_pairs={{2,0},{4,6},{3,1},{5,7},{10,8},{12,14},{11,9},{13,15},{18,16},{20,... | collective-permute-start | bytes 786440 | tf_op jit(solution)/shard_map/ppermute | solution.py:33
  645.9 1.2 collective-permute-start.38
  647.1 3.6 collective-permute-start.39
  650.7 3.6 collective-permute-start.40
  654.3 4.5 collective-permute-start.41
  658.7 3.6 collective-permute-start.42
  667.4 28.7 %collective-permute-start.43 = (f32[136,2048]{1,0:T(8,128)}, f32[136,2048]{1,0:T(8,128)}, u32[]{:S(2)}, u32[]{:S(2)}) collective-permute-start(f32[136,2048]{1,0:T(8,128)} %shard_map.55), channel_id=1, source_target_pairs={{0,2},{6,4},{1,3},{7,5},{8,10},{14,12},{9,11},{15,13},{16,18},{22,... | collective-permute-start | bytes 3342344 | tf_op jit(solution)/shard_map/ppermute | solution.py:33
  671.9 24.3 %copy-start.3 = (f32[136,2048]{1,0:T(8,128)S(1)}, f32[136,2048]{1,0:T(8,128)}, u32[]{:S(2)}) copy-start(f32[136,2048]{1,0:T(8,128)} %shard_map.55) | copy-start | bytes 3342340
  676.3 43.7 %collective-permute-start.47 = (f32[136,2048]{1,0:T(8,128)}, f32[136,2048]{1,0:T(8,128)}, u32[]{:S(2)}, u32[]{:S(2)}) collective-permute-start(f32[136,2048]{1,0:T(8,128)} %shard_map.56), channel_id=1, source_target_pairs={{0,2},{6,4},{1,3},{7,5},{8,10},{14,12},{9,11},{15,13},{16,18},{22,... | collective-permute-start | bytes 3342344 | tf_op jit(solution)/shard_map/ppermute | solution.py:33
  697.5 24.6 %collective-permute-start.44 = (f32[136,2048]{1,0:T(8,128)S(1)}, f32[136,2048]{1,0:T(8,128)}, u32[]{:S(2)}, u32[]{:S(2)}) collective-permute-start(f32[136,2048]{1,0:T(8,128)S(1)} %add.211), channel_id=1, source_target_pairs={{2,4},{4,2},{3,5},{5,3},{10,12},{12,10},{11,13},{13,11},{18,20},{2... | collective-permute-start | bytes 3342344 | tf_op jit(solution)/shard_map/ppermute | solution.py:33
  703.6 34.9 %collective-permute-start.46 = (f32[136,2048]{1,0:T(8,128)}, f32[136,2048]{1,0:T(8,128)}, u32[]{:S(2)}, u32[]{:S(2)}) collective-permute-start(f32[136,2048]{1,0:T(8,128)} %shard_map.57), channel_id=1, source_target_pairs={{0,2},{6,4},{1,3},{7,5},{8,10},{14,12},{9,11},{15,13},{16,18},{22,... | collective-permute-start | bytes 3342344 | tf_op jit(solution)/shard_map/ppermute | solution.py:33
  710.7 9.3 %copy-start.2 = (f32[136,2048]{1,0:T(8,128)S(1)}, f32[136,2048]{1,0:T(8,128)}, u32[]{:S(2)}) copy-start(f32[136,2048]{1,0:T(8,128)} %shard_map.56) | copy-start | bytes 3342340
  721.4 17.1 %collective-permute-start.48 = (f32[136,2048]{1,0:T(8,128)S(1)}, f32[136,2048]{1,0:T(8,128)S(1)}, u32[]{:S(2)}, u32[]{:S(2)}) collective-permute-start(f32[136,2048]{1,0:T(8,128)S(1)} %add.215), channel_id=1, source_target_pairs={{2,4},{4,2},{3,5},{5,3},{10,12},{12,10},{11,13},{13,11},{18,20},{2... | collective-permute-start | bytes 3342344 | tf_op jit(solution)/shard_map/ppermute | solution.py:33
  723.9 20.3 %copy-start.1 = (f32[136,2048]{1,0:T(8,128)S(1)}, f32[136,2048]{1,0:T(8,128)}, u32[]{:S(2)}) copy-start(f32[136,2048]{1,0:T(8,128)} %shard_map.58) | copy-start | bytes 3342340
  723.9 20.3 %copy-start.4 = (f32[136,2048]{1,0:T(8,128)S(1)}, f32[136,2048]{1,0:T(8,128)}, u32[]{:S(2)}) copy-start(f32[136,2048]{1,0:T(8,128)} %shard_map.57) | copy-start | bytes 3342340
  723.9 20.3 %collective-permute-start.45 = (f32[136,2048]{1,0:T(8,128)S(1)}, f32[136,2048]{1,0:T(8,128)S(1)}, u32[]{:S(2)}, u32[]{:S(2)}) collective-permute-start(f32[136,2048]{1,0:T(8,128)S(1)} %add.212), channel_id=1, source_target_pairs={{2,0},{4,6},{3,1},{5,7},{10,8},{12,14},{11,9},{13,15},{18,16},{20,... | collective-permute-start | bytes 3342344 | tf_op jit(solution)/shard_map/ppermute | solution.py:33
  (17 other events, 75.6 us)

commit v3 on v2

v3 whole, which is shorter than its diff:
```python
import math

import jax
import jax.numpy as jnp
from jax import lax
from jax.experimental import pallas as pl
from jax.experimental.pallas import tpu as pltpu
from jax.sharding import PartitionSpec as P


D = 3584
ITERS = 2
KVW = 4096
AXES = ("worker", "outer", "mp")
LINE = 4
TILE = 8
SPREAD = 3 / 7
AHEAD = 16

epsilon = 1e-06


def sum_over_devices(value):
    for axis in AXES:
        size = lax.axis_size(axis)
        step = 1
        while step < size:
            value = value + lax.ppermute(value, axis, [(i, i ^ step) for i in range(size)])
            step *= 2
    return value


def send(value, pairs, axis="outer"):
    return lax.ppermute(value, axis, pairs)


TO_MIDS = [(0, 1), (3, 2)]
ACROSS = [(1, 2), (2, 1)]
TO_ENDS = [(1, 0), (2, 3)]


def tie(value, earlier):
    return lax.optimization_barrier((value, earlier))[0]


def split(rows, outers):
    cut = int(rows * SPREAD) // TILE * TILE
    rest = rows - cut
    tiles = rest // TILE
    if outers != LINE or rest % TILE or tiles < 10 or cut <= AHEAD:
        return None
    body = tiles - 7
    sizes = [1, 2] + [3] * (body // 3) + [body % 3] * (body % 3 > 0) + [2, 1, 1]
    return cut, sizes


SMEM = pl.BlockSpec(memory_space=pltpu.SMEM)


def run(kernel, grid, in_specs, out_specs, out_shape, operands, moved, aliases={}, prefetch=0):
    return pl.pallas_call(
        kernel,
        grid_spec=pltpu.PrefetchScalarGridSpec(
            num_scalar_prefetch=prefetch, grid=grid, in_specs=in_specs, out_specs=out_specs
        ),
        out_shape=out_shape,
        input_output_aliases=aliases,
        compiler_params=pltpu.CompilerParams(vmem_limit_bytes=60 << 20),
        cost_estimate=pl.CostEstimate(flops=4 * moved, bytes_accessed=4 * moved, transcendentals=0),
    )(*operands)


def group_spec(begin, count, tile, columns):
    return pl.BlockSpec((tile, columns), lambda i: (jnp.clip(i - begin, 0, count - 1), 0))


def begins(sizes):
    return [sum(sizes[:i]) for i in range(len(sizes))]


def step_of(factor, values, v):
    return sum(factor[i] * (value[...] - v) for i, value in enumerate(values))


def step_chunks(factor, values, v, start, sizes):
    columns, tile, count = v.shape[1], TILE * LINE, len(values)
    places = begins(sizes)

    def kernel(factor, *refs):
        values, v, outs = refs[:count], refs[count], refs[count + 1 :]
        i = pl.program_id(0)
        total = step_of(factor, values, v[...])
        for out, begin, size in zip(outs, places, sizes):

            @pl.when((i >= begin) & (i < begin + size))
            def _(out=out):
                out[...] = total

    at = pl.BlockSpec((tile, columns), lambda i: (start + i, 0))
    outs = [group_spec(begin, size, tile, columns) for begin, size in zip(places, sizes)]
    shapes = [jax.ShapeDtypeStruct((size * tile, columns), v.dtype) for size in sizes]
    moved = (count + 2) * sum(sizes) * tile * columns
    in_specs = [SMEM] + [at] * (count + 1)
    return run(kernel, (sum(sizes),), in_specs, outs, shapes, (factor, *values, v), moved)


def move_chunks(is_end, share, totals, backs, values, v, start, sizes, carried):
    columns, tile, count, chunks = v.shape[1], TILE * LINE, len(values), len(sizes)
    places = begins(sizes)

    def kernel(is_end, v, *refs):
        values, rest = refs[:count], refs[count:]
        totals, backs, (v_out, sq_out) = rest[:chunks], rest[chunks : 2 * chunks], rest[-2:]
        i = pl.program_id(0)

        @pl.when(i == 0)
        def _():
            sq_out[...] = rest[-3][...] if carried else jnp.zeros_like(sq_out)

        for total, back, begin, size in zip(totals, backs, places, sizes):

            @pl.when((i >= begin) & (i < begin + size))
            def _(total=total, back=back):
                step = jnp.where(is_end[0] > 0, back[...], total[...])
                v_out[...] = v[...] + step * share

        moved = v_out[...]
        for k, value in enumerate(values):
            square = jnp.square(value[...] - moved)
            folded = sum(square[j : j + 8] for j in range(0, tile, 8))
            sq_out[k] += sum(folded[:, j : j + 128] for j in range(0, columns, 128))

    at = pl.BlockSpec((tile, columns), lambda i: (start + i, 0))
    squares = pl.BlockSpec((count, 8, 128), lambda i: (0, 0, 0))
    parts = [group_spec(begin, size, tile, columns) for begin, size in zip(places, sizes)]
    in_specs = [SMEM] + [at] * (count + 1) + parts + parts
    operands = (is_end, v, *values, *totals, *backs)
    aliases = {}
    if carried:
        in_specs += [pl.BlockSpec(memory_space=pl.ANY), squares]
        aliases = {len(operands): 0, len(operands) + 1: 1}
        operands += tuple(carried)
    shapes = (
        jax.ShapeDtypeStruct(v.shape, v.dtype),
        jax.ShapeDtypeStruct((count, 8, 128), v.dtype),
    )
    moved = (count + 4) * sum(sizes) * tile * columns
    return run(kernel, (sum(sizes),), in_specs, (at, squares), shapes, operands, moved, aliases)


def step_blocks(places, factor, values, v, rest):
    columns, count, blocks = v.shape[1], len(values), len(places)
    tile = TILE * LINE if rest % (TILE * LINE) == 0 else TILE
    size = rest // tile

    def kernel(places, factor, *refs):
        values, v, outs = refs[:count], refs[count], refs[count + 1 :]
        i = pl.program_id(0)
        total = step_of(factor, values, v[...])
        for k, out in enumerate(outs):

            @pl.when(i // size == k)
            def _(out=out):
                out[...] = total

    at = pl.BlockSpec((tile, columns), lambda i, places: (places[i // size] * size + i % size, 0))
    outs = [
        pl.BlockSpec((tile, columns), lambda i, _, k=k: (jnp.clip(i - k * size, 0, size - 1), 0))
        for k in range(blocks)
    ]
    shapes = [jax.ShapeDtypeStruct((rest, columns), v.dtype)] * blocks
    moved = (count + 2) * blocks * rest * columns
    operands = (jnp.stack(places).astype(jnp.int32), factor, *values, v)
    in_specs = [SMEM] + [at] * (count + 1)
    return run(kernel, (blocks * size,), in_specs, outs, shapes, operands, moved, prefetch=1)


def spread_only(mine, center, radius_total, worker_count):
    own_rows = center
    gathered = lax.all_to_all(mine, ("worker", "outer"), split_axis=0, concat_axis=0, tiled=True)
    for _ in range(ITERS):
        difference = gathered - own_rows[None]
        norm_sq = sum_over_devices(jnp.sum(difference * difference, axis=(1, 2)))
        factor = jnp.minimum(1.0, radius_total * lax.rsqrt(norm_sq + epsilon))
        own_rows = own_rows + jnp.sum(factor[:, None, None] * difference, axis=0) / worker_count
    return own_rows


def on_device(grads, center, radius):
    workers, outers = lax.axis_size("worker"), lax.axis_size("outer")
    worker_count = workers * outers
    radius_total = radius[0] * math.sqrt(D * KVW)
    rows, columns = center.shape
    mine = grads.reshape(worker_count, rows, columns)
    plan = split(rows, outers)
    if plan is None:
        return spread_only(mine, center, radius_total, worker_count)
    cut, sizes = plan
    rest = rows - cut

    w, o = lax.axis_index("worker"), lax.axis_index("outer")
    is_end = (o == 0) | (o == LINE - 1)
    is_low = o < LINE // 2

    def line_rows(source, worker):
        return lax.dynamic_slice(source, (worker * outers, cut, 0), (outers, rest, columns))

    tail = center[cut:]
    pair = send(tail, [(i, i ^ 1) for i in range(LINE)])
    steps = list(range(workers // 2, workers)) + list(range(1, workers // 2)) + [0]
    held, source = [], mine
    for step in steps:
        sent = line_rows(source, w ^ step)
        source = tie(source, sent)
        if step:
            swap = [(i, i ^ step) for i in range(workers)]
            sent = send(sent, swap, "worker")
        held.append(sent)
    edges = [(0, AHEAD), (AHEAD, cut)]
    spread = []
    for low, high in edges:
        spread.append(
            lax.all_to_all(
                mine[:, low:high], ("worker", "outer"), split_axis=0, concat_axis=0, tiled=True
            )
        )
    first = (o % 2) == 0
    near = jnp.where(first, jnp.stack([tail, pair]), jnp.stack([pair, tail]))
    crossed = send(near, ACROSS)
    far = jnp.where(is_end, send(crossed, TO_ENDS), crossed)
    line_v = jnp.where(is_low, jnp.concatenate([near, far]), jnp.concatenate([far, near]))
    spread_v = [center[low:high] for low, high in edges]

    places = jnp.stack([(w ^ step) * outers + o for step in steps])
    hit = places[:, None] == jnp.arange(worker_count)[None]

    def placed(line_sq):
        return jnp.sum(jnp.where(hit, line_sq[:, None], 0.0), axis=0)

    def factors(both):
        norm_sq = sum_over_devices(both)
        factor = jnp.minimum(1.0, radius_total * lax.rsqrt(norm_sq + epsilon))
        return factor, jnp.sum(jnp.where(hit, factor[None], 0.0), axis=1)

    def spread_norms(values):
        return [
            jnp.sum(jnp.square(part - v[None]), axis=(1, 2)) for part, v in zip(spread, values)
        ]

    def spread_update(values, factor):
        weight = factor[:, None, None]
        return [
            v + jnp.sum(weight * (part - v[None]), axis=0) / worker_count
            for part, v in zip(spread, values)
        ]

    line_sq, v = jnp.zeros((worker_count,), jnp.float32), line_v
    for place in reversed(range(workers)):
        square = jnp.sum(jnp.square(held[place] - v))
        line_sq = lax.optimization_barrier(line_sq + jnp.where(hit[place], square, 0.0))
        v = tie(v, line_sq)
    ahead, last = spread_norms(spread_v)
    factor, line_factor = factors(last + lax.optimization_barrier(line_sq + ahead))

    flat = [value.reshape(outers * rest, columns) for value in held]
    flat_v = line_v.reshape(outers * rest, columns)
    end_flag = is_end.astype(jnp.int32).reshape(1)
    next_spread_v = spread_update(spread_v, factor)
    spread_sq = sum(spread_norms(next_spread_v))
    early = {1: next_spread_v, 2: spread_sq}
    count, places = len(sizes), begins(sizes)
    own = step_chunks(line_factor, flat, flat_v, 0, sizes[:2])
    own += step_chunks(line_factor, flat, tie(flat_v, own[0]), places[2], sizes[2:])
    groups = [slice(0, count - 5), slice(count - 5, count - 2), slice(count - 2, count)]
    totals, backs, carried = [], [], ()

    def move(part, carried):
        return move_chunks(
            end_flag, 1 / worker_count, totals[part], backs[part], flat, flat_v,
            places[part.start], sizes[part], carried,
        )

    for chunk in range(count):
        got = send(own[chunk], TO_MIDS)
        if chunk >= 2:
            got = tie(got, totals[chunk - 2])
        total = own[chunk] + got
        total = total + send(total, ACROSS)
        if chunk in early:
            total = tie(total, early[chunk])
        if chunk == count - 2:
            carried = move(groups[0], carried)
            total = tie(total, carried[1])
        totals.append(total)
        backs.append(send(total, TO_ENDS))
    for part in groups[1:]:
        carried = move(part, carried)
    spread_v = next_spread_v
    flat_v = carried[0]
    line_v = flat_v.reshape(line_v.shape)
    factor, line_factor = factors(spread_sq + placed(jnp.sum(carried[1], axis=(1, 2))))

    order = [jnp.where(is_low, LINE - 1 - place, place) for place in range(LINE)]
    block = step_blocks(order[:1], line_factor, flat, flat_v, rest)
    block += step_blocks(order[1:], line_factor, flat, tie(flat_v, block[0]), rest)
    arrived = [send(block[place], TO_MIDS) for place in range(3)]
    passed = [send(block[place] + arrived[place], ACROSS) for place in range(2)]
    end_sum = block[3] + send(block[3] + passed[0], TO_ENDS)
    mid_sum = block[2] + arrived[2] + passed[1]
    own_v = lax.dynamic_index_in_dim(line_v, o, 0, keepdims=False)
    own_v = own_v + jnp.where(is_end, end_sum, mid_sum) / worker_count
    return jnp.concatenate([*spread_update(spread_v, factor), own_v])


def solution(mesh):
    in_specs = (P("worker", "outer", None, "mp"), P(("worker", "outer"), "mp"), P())
    out_specs = P(("worker", "outer"), "mp")

    return jax.shard_map(on_device, mesh=mesh, in_specs=in_specs, out_specs=out_specs, check_vma=False)
```

time: 751 us -> 781 us (1.040)
  waiting for transfers between devices: 473 us -> 522 us
  Pallas kernels: 69.4 us -> 52 us
    all_to_all x1 -> x2, waiting for transfers between devices: 0.01 us -> 39.8 us  [on_device(): lax.all_to_all(mine[:, low:high], ('worker', 'outer'), split_axis=0, conc...]
    pallas_call x22 -> x7, Pallas kernels: 69.4 us -> 52 us  [run(): pl.pallas_call(kernel, grid_spec=pltpu.PrefetchScalarGridSpec(num_scalar_...]
    add x21 -> x23, other arithmetic: 16.3 us -> 8.63 us  [the longest x8 4.36 us: on_device(): total = total + send(total, ACROSS)]
    ppermute x39 -> x36, waiting for transfers between devices: 451 us -> 457 us  [send(): return lax.ppermute(value, axis, pairs)]
    ppermute x39 -> x36, starting transfers between devices: 78.4 us -> 82.1 us  [send(): return lax.ppermute(value, axis, pairs)]
    reduce_sum x4 -> x8, other arithmetic: 23.2 us -> 22.7 us  [the longest x4 11.7 us: spread_update(): jnp.sum(weight * (part - v[None]), axis=0) / worker_count]
  transfers between devices with their start and end apart: 50 -> 48, of which waited for: 24 -> 24; matrix products, arithmetic and copies ran while one was open for 11% -> 11% of each run, Pallas kernels for 8% -> 5%
where the time goes in v3:
time: 781 us; the launch traced here: 779 us
  waiting for transfers between devices  522 us (67%)
  starting transfers between devices  101 us (13%)
  other arithmetic  69.8 us (9%)
  Pallas kernels  52 us (7%)
  local copies, waits for them, and re-layouts  32.2 us (4%)
    ppermute x36, waiting for transfers between devices, send(): return lax.ppermute(value, axis, pairs)  457 us
    ppermute x36, starting transfers between devices, send(): return lax.ppermute(value, axis, pairs)  82.1 us
    pallas_call x7, Pallas kernels, run(): pl.pallas_call(kernel, grid_spec=pltpu.PrefetchScalarGridSpec(num_scalar_...  52 us
    all_to_all x2, waiting for transfers between devices, on_device(): lax.all_to_all(mine[:, low:high], ('worker', 'outer'), split_axis=0, conc...  39.8 us
    ppermute x10, waiting for transfers between devices, sum_over_devices(): lax.ppermute(value, axis, [(i, i ^ step) for i in range(size)])  25.5 us
    reduce_sum x4, other arithmetic, on_device(): square = jnp.sum(jnp.square(held[place] - v))  18.6 us
  transfers between devices with their start and end apart: 48, of which 24 were waited for; matrix products, arithmetic and copies ran while one was open for 11% of the time, Pallas kernels for 5%

profile of v3, /device:TPU:0, one launch (start us, length us, event | category | flops | bytes accessed | tf_op | source)
XLA Modules:
  0.0 778.6 jit_solution(1710826761851063226)
XLA Ops:
  0.0 3.2 slice.37
  3.2 7.4 all-to-all-start.1
  10.6 9.5 %slice.36 = f32[16,80,2048]{2,1,0:T(8,128)} slice(f32[16,224,2048]{2,1,0:T(8,128)} %bitcast.50), slice={[0:16], [16:96], [0:2048]} | slice | bytes 20971520 | tf_op jit(solution)/shard_map/slice | solution.py:224
  20.1 39.8 %all-to-all-done.1 = f32[16,16,2048]{2,1,0:T(8,128)S(1)} async-done(((f32[16,16,2048]{2,1,0:T(8,128)}), f32[16,16,2048]{2,1,0:T(8,128)S(1)}, u32[]{:S(2)}, u32[]{:S(2)}) %all-to-all-start.1) | async-done | bytes 2097184 | tf_op jit(solution)/shard_map/all_to_all | solution.py:223
  59.9 4.8 all-to-all-start
  64.7 2.4 slice_bitcast_fusion
  67.2 1.7 collective-permute-start
  68.9 188.0 %collective-permute-done = f32[128,2048]{1,0:T(8,128)} collective-permute-done((f32[128,2048]{1,0:T(8,128)}, f32[128,2048]{1,0:T(8,128)}, u32[]{:S(2)}, u32[]{:S(2)}) %collective-permute-start) | collective-permute-done | bytes 1048608 | tf_op jit(solution)/shard_map/ppermute | solution.py:34
  256.9 3.1 maximum_select_fusion.1
  260.0 2.0 collective-permute-start.1
  262.1 4.6 constant_dynamic-slice_fusion.3
  266.7 4.6 constant_dynamic-slice_fusion.2
  271.3 4.7 constant_dynamic-slice_fusion.1
  276.1 1.8 collective-permute-start.4
  282.1 103.7 %collective-permute-done.2 = f32[2,128,2048]{2,1,0:T(8,128)} collective-permute-done((f32[2,128,2048]{2,1,0:T(8,128)}, f32[2,128,2048]{2,1,0:T(8,128)}, u32[]{:S(2)}, u32[]{:S(2)}) %collective-permute-start.2) | collective-permute-done | bytes 2097184 | tf_op jit(solution)/shard_map/ppermute | solution.py:34
  385.9 1.8 broadcast_select_fusion
  387.7 6.2 multiply_reduce_fusion.7
  394.6 4.7 multiply_reduce_fusion.6
  400.0 3.9 multiply_reduce_fusion.5
  404.5 61.7 %collective-permute-done.5 = f32[4,128,2048]{2,1,0:T(8,128)} collective-permute-done((f32[4,128,2048]{2,1,0:T(8,128)}, f32[4,128,2048]{2,1,0:T(8,128)}, u32[]{:S(2)}, u32[]{:S(2)}) %collective-permute-start.5) | collective-permute-done | bytes 4194336 | tf_op jit(solution)/shard_map/ppermute | solution.py:34
  466.2 3.9 multiply_reduce_fusion.4
  470.8 5.2 multiply_reduce_fusion.3
  478.4 2.3 collective-permute-done.7
  480.7 3.6 collective-permute-done.8
  485.0 3.8 collective-permute-done.9
  488.8 1.5 collective-permute-start.10
  490.3 2.0 collective-permute-done.10
  493.1 3.9 shard_map.37
  497.0 1.9 collective-permute-start.14
  500.3 12.9 %shard_map.38 = (f32[96,2048]{1,0:T(8,128)}, f32[96,2048]{1,0:T(8,128)}, f32[96,2048]{1,0:T(8,128)}, f32[64,2048]{1,0:T(8,128)}, f32[32,2048]{1,0:T(8,128)}, /*index=5*/f32[32,2048]{1,0:T(8,128)}) custom-call(f32[4]{0:T(128)} %select_reduce_fusion.2.factor, f32[512,2048]{1,0:T(8,128)} %bitcast.14.refs_0_, f32[512,2048]{1,0:T(8,128)} %bitcast.15.refs_1_, ...), custom_call_target="tpu_custom_call" | custom-call | flops 20447232 | bytes 20447232 | tf_op jit(solution)/shard_map/pallas_call | solution.py:61
  514.5 1.7 collective-permute-start.13
  516.2 5.5 multiply_reduce_fusion.2
  527.4 15.6 %collective-permute-start.12 = (f32[96,2048]{1,0:T(8,128)S(1)}, f32[96,2048]{1,0:T(8,128)S(1)}, u32[]{:S(2)}, u32[]{:S(2)}) collective-permute-start(f32[96,2048]{1,0:T(8,128)S(1)} %copy-done.11), channel_id=1, source_target_pairs={{0,2},{6,4},{1,3},{7,5},{8,10},{14,12},{9,11},{15,13},{16,18},{22,... | collective-permute-start | bytes 2359304 | tf_op jit(solution)/shard_map/ppermute | solution.py:34
  543.1 6.5 collective-permute-done.13
  551.3 5.2 multiply_reduce_fusion.1
  556.9 16.8 %collective-permute-done.12 = f32[96,2048]{1,0:T(8,128)S(1)} collective-permute-done((f32[96,2048]{1,0:T(8,128)S(1)}, f32[96,2048]{1,0:T(8,128)S(1)}, u32[]{:S(2)}, u32[]{:S(2)}) %collective-permute-start.12) | collective-permute-done | bytes 786464 | tf_op jit(solution)/shard_map/ppermute | solution.py:34
  576.7 17.5 %collective-permute-start.11 = (f32[32,2048]{1,0:T(8,128)S(1)}, f32[32,2048]{1,0:T(8,128)S(1)}, u32[]{:S(2)}, u32[]{:S(2)}) collective-permute-start(f32[32,2048]{1,0:T(8,128)S(1)} %copy-done.19), channel_id=1, source_target_pairs={{0,2},{6,4},{1,3},{7,5},{8,10},{14,12},{9,11},{15,13},{16,18},{22,... | collective-permute-start | bytes 786440 | tf_op jit(solution)/shard_map/ppermute | solution.py:34
  599.4 1.5 collective-permute-done.24
  604.4 20.7 %collective-permute-done.21.refs_7_ = f32[32,2048]{1,0:T(8,128)S(1)} collective-permute-done((f32[32,2048]{1,0:T(8,128)S(1)}, f32[32,2048]{1,0:T(8,128)S(1)}, u32[]{:S(2)}, u32[]{:S(2)}) %collective-permute-start.21) | collective-permute-done | bytes 262176 | tf_op jit(solution)/shard_map/ppermute | solution.py:34
  631.5 6.7 shard_map.39
  643.2 26.6 %collective-permute-done.34.refs_9_ = f32[64,2048]{1,0:T(8,128)} collective-permute-done((f32[64,2048]{1,0:T(8,128)}, f32[64,2048]{1,0:T(8,128)}, u32[]{:S(2)}, u32[]{:S(2)}) %collective-permute-start.34) | collective-permute-done | bytes 524320 | tf_op jit(solution)/shard_map/ppermute | solution.py:34
  669.7 8.6 %shard_map.40 = (f32[512,2048]{1,0:T(8,128)}, f32[4,8,128]{2,1,0:T(8,128)}) custom-call(s32[1]{0:T(128)} %bitcast.12.is_end, f32[512,2048]{1,0:T(8,128)} %bitcast.39, f32[512,2048]{1,0:T(8,128)} %bitcast.14.refs_0_, f32[512,2048]{1,0:T(8,128)} %bitcast.15.refs_1_, f32[512,2048]{1,0:T(8,128)} %bitcast.16.refs_2_, ...), custom_call_target="tpu_custom_call", output_to_operand_aliasing={{0}: (12, {}), {1}: (13, {})} | custom-call | flops 16777216 | bytes 16777216 | tf_op jit(solution)/shard_map/pallas_call | solution.py:61
  678.4 2.8 shard_map.41
  684.7 2.3 collective-permute-done.36
  687.0 3.6 collective-permute-done.37
  691.4 3.6 collective-permute-done.38
  695.0 1.5 collective-permute-start.39
  696.5 2.0 collective-permute-done.39
  699.3 4.5 shard_map.42
  703.8 2.9 collective-permute-start.40
  707.4 12.5 %shard_map.43 = (f32[128,2048]{1,0:T(8,128)}, f32[128,2048]{1,0:T(8,128)}, f32[128,2048]{1,0:T(8,128)}) custom-call(s32[3]{0:T(128)} %pad_add_fusion.1.places, f32[4]{0:T(128)} %select_reduce_fusion.factor, f32[512,2048]{1,0:T(8,128)} %bitcast.14.refs_0_, f32[512,2048]{1,0:T(8,128)} %bitcast.15.refs_1_, f32[512,2048]{1,0:T(8,128)} %bitcast.16.refs_2_, ...), custom_call_target="tpu_custom_call" | custom-call | flops 18874368 | bytes 18874368 | tf_op jit(solution)/shard_map/pallas_call | solution.py:61
  719.9 2.3 collective-permute-start.44
  722.1 7.5 collective-permute-done.40
  729.6 2.6 add.219
  732.2 1.6 collective-permute-start.41
  733.9 6.3 collective-permute-start.43
  740.6 11.5 %collective-permute-done.44 = f32[128,2048]{1,0:T(8,128)} collective-permute-done((f32[128,2048]{1,0:T(8,128)}, f32[128,2048]{1,0:T(8,128)}, u32[]{:S(2)}, u32[]{:S(2)}) %collective-permute-start.44) | collective-permute-done | bytes 1048608 | tf_op jit(solution)/shard_map/ppermute | solution.py:34
  752.1 1.7 add.223
  755.9 1.6 collective-permute-start.42
  757.5 5.5 multiply_reduce_fusion
  763.2 6.3 collective-permute-done.43
  769.4 5.9 collective-permute-done.42
  775.3 1.8 bitcast_add_fusion
  777.2 1.4 pad_maximum_fusion
  (155 shorter events, 51.2 us)
Async XLA Ops:
  3.2 56.7 %all-to-all-start.1 = ((f32[16,16,2048]{2,1,0:T(8,128)}), f32[16,16,2048]{2,1,0:T(8,128)S(1)}, u32[]{:S(2)}, u32[]{:S(2)}) async-start(f32[16,16,2048]{2,1,0:T(8,128)} %slice.37), calls=%async_computation.1 | async-start | bytes 4194304 | tf_op jit(solution)/shard_map/all_to_all | solution.py:223
  59.9 410.9 %all-to-all-start = ((f32[16,80,2048]{2,1,0:T(8,128)}), f32[16,80,2048]{2,1,0:T(8,128)}, u32[]{:S(2)}, u32[]{:S(2)}) async-start(f32[16,80,2048]{2,1,0:T(8,128)} %slice.36), calls=%async_computation | async-start | bytes 20971520 | tf_op jit(solution)/shard_map/all_to_all | solution.py:223
  67.2 189.7 %collective-permute-start = (f32[128,2048]{1,0:T(8,128)}, f32[128,2048]{1,0:T(8,128)}, u32[]{:S(2)}, u32[]{:S(2)}) collective-permute-start(f32[128,2048]{1,0:T(8,128)} %get-tuple-element.77), channel_id=1, source_target_pairs={{0,2},{2,0},{4,6},{6,4},{1,3},{3,1},{5,7},{7,5},{8,10},{10,8},{12,... | collective-permute-start | bytes 3145736 | tf_op jit(solution)/shard_map/ppermute | solution.py:34
  260.0 17.9 %collective-permute-start.1 = (f32[2,128,2048]{2,1,0:T(8,128)}, f32[2,128,2048]{2,1,0:T(8,128)}, u32[]{:S(2)}, u32[]{:S(2)}) collective-permute-start(f32[2,128,2048]{2,1,0:T(8,128)} %maximum_select_fusion.1), channel_id=1, source_target_pairs={{2,4},{4,2},{3,5},{5,3},{10,12},{12,10},{11,13},{13,11},{18,20},{2... | collective-permute-start | bytes 6291464 | tf_op jit(solution)/shard_map/ppermute | solution.py:34
  276.1 118.5 %collective-permute-start.3 = (f32[4,128,2048]{2,1,0:T(8,128)}, f32[4,128,2048]{2,1,0:T(8,128)}, u32[]{:S(2)}, u32[]{:S(2)}) collective-permute-start(f32[4,128,2048]{2,1,0:T(8,128)} %constant_dynamic-slice_fusion.1), channel_id=1, source_target_pairs={{0,8},{8,0},{16,24},{24,16},{1,9},{9,1},{17,25},{25,17},{2,10},{10... | collective-permute-start | bytes 12582920 | tf_op jit(solution)/shard_map/ppermute | solution.py:34
  276.1 123.9 %collective-permute-start.4 = (f32[4,128,2048]{2,1,0:T(8,128)}, f32[4,128,2048]{2,1,0:T(8,128)}, u32[]{:S(2)}, u32[]{:S(2)}) collective-permute-start(f32[4,128,2048]{2,1,0:T(8,128)} %constant_dynamic-slice_fusion.2), channel_id=1, source_target_pairs={{0,24},{8,16},{16,8},{24,0},{1,25},{9,17},{17,9},{25,1},{2,26},{10... | collective-permute-start | bytes 12582920 | tf_op jit(solution)/shard_map/ppermute | solution.py:34
  277.9 108.0 %collective-permute-start.2 = (f32[2,128,2048]{2,1,0:T(8,128)}, f32[2,128,2048]{2,1,0:T(8,128)}, u32[]{:S(2)}, u32[]{:S(2)}) collective-permute-start(f32[2,128,2048]{2,1,0:T(8,128)} %collective-permute-done.1), channel_id=1, source_target_pairs={{2,0},{4,6},{3,1},{5,7},{10,8},{12,14},{11,9},{13,15},{18,16},{20,... | collective-permute-start | bytes 6291464 | tf_op jit(solution)/shard_map/ppermute | solution.py:34
  279.2 187.1 %collective-permute-start.5 = (f32[4,128,2048]{2,1,0:T(8,128)}, f32[4,128,2048]{2,1,0:T(8,128)}, u32[]{:S(2)}, u32[]{:S(2)}) collective-permute-start(f32[4,128,2048]{2,1,0:T(8,128)} %constant_dynamic-slice_fusion.3), channel_id=1, source_target_pairs={{0,16},{8,24},{16,0},{24,8},{1,17},{9,25},{17,1},{25,9},{2,18},{10... | collective-permute-start | bytes 12582920 | tf_op jit(solution)/shard_map/ppermute | solution.py:34
  394.0 72.3 %copy-start = (f32[4,128,2048]{2,1,0:T(8,128)}, f32[4,128,2048]{2,1,0:T(8,128)S(1)}, u32[]{:S(2)}) copy-start(f32[4,128,2048]{2,1,0:T(8,128)S(1)} %get-tuple-element.44) | copy-start | bytes 12582916
  476.0 1.2 collective-permute-start.6
  477.2 3.6 collective-permute-start.7
  480.7 3.6 collective-permute-start.8
  484.3 4.5 collective-permute-start.9
  488.8 3.6 collective-permute-start.10
  497.0 28.7 %collective-permute-start.14 = (f32[32,2048]{1,0:T(8,128)}, f32[32,2048]{1,0:T(8,128)S(1)}, u32[]{:S(2)}, u32[]{:S(2)}) collective-permute-start(f32[32,2048]{1,0:T(8,128)} %get-tuple-element.45), channel_id=1, source_target_pairs={{0,2},{6,4},{1,3},{7,5},{8,10},{14,12},{9,11},{15,13},{16,18},{22,... | collective-permute-start | bytes 786440 | tf_op jit(solution)/shard_map/ppermute | solution.py:34
  498.9 25.5 %collective-permute-start.19 = (f32[64,2048]{1,0:T(8,128)}, f32[64,2048]{1,0:T(8,128)S(1)}, u32[]{:S(2)}, u32[]{:S(2)}) collective-permute-start(f32[64,2048]{1,0:T(8,128)} %get-tuple-element.54), channel_id=1, source_target_pairs={{0,2},{6,4},{1,3},{7,5},{8,10},{14,12},{9,11},{15,13},{16,18},{22,... | collective-permute-start | bytes 1572872 | tf_op jit(solution)/shard_map/ppermute | solution.py:34
  513.2 37.3 %collective-permute-start.26 = (f32[96,2048]{1,0:T(8,128)}, f32[96,2048]{1,0:T(8,128)S(1)}, u32[]{:S(2)}, u32[]{:S(2)}) collective-permute-start(f32[96,2048]{1,0:T(8,128)} %get-tuple-element.60), channel_id=1, source_target_pairs={{0,2},{6,4},{1,3},{7,5},{8,10},{14,12},{9,11},{15,13},{16,18},{22,... | collective-permute-start | bytes 2359304 | tf_op jit(solution)/shard_map/ppermute | solution.py:34
  514.5 9.9 %copy-start.16 = (f32[64,2048]{1,0:T(8,128)S(1)}, f32[64,2048]{1,0:T(8,128)}, u32[]{:S(2)}) copy-start(f32[64,2048]{1,0:T(8,128)} %get-tuple-element.54) | copy-start | bytes 1572868
  514.5 35.0 %collective-permute-start.13 = (f32[96,2048]{1,0:T(8,128)}, f32[96,2048]{1,0:T(8,128)S(1)}, u32[]{:S(2)}, u32[]{:S(2)}) collective-permute-start(f32[96,2048]{1,0:T(8,128)} %get-tuple-element.49), channel_id=1, source_target_pairs={{0,2},{6,4},{1,3},{7,5},{8,10},{14,12},{9,11},{15,13},{16,18},{22,... | collective-permute-start | bytes 2359304 | tf_op jit(solution)/shard_map/ppermute | solution.py:34
  521.8 27.8 %copy-start.13 = (f32[96,2048]{1,0:T(8,128)S(1)}, f32[96,2048]{1,0:T(8,128)}, u32[]{:S(2)}) copy-start(f32[96,2048]{1,0:T(8,128)} %get-tuple-element.49) | copy-start | bytes 2359300
  523.1 51.5 %collective-permute-start.25 = (f32[64,2048]{1,0:T(8,128)S(1)}, f32[64,2048]{1,0:T(8,128)S(1)}, u32[]{:S(2)}, u32[]{:S(2)}) collective-permute-start(f32[64,2048]{1,0:T(8,128)S(1)} %copy-done.15), channel_id=1, source_target_pairs={{0,2},{6,4},{1,3},{7,5},{8,10},{14,12},{9,11},{15,13},{16,18},{22,... | collective-permute-start | bytes 1572872 | tf_op jit(solution)/shard_map/ppermute | solution.py:34
  524.5 25.9 %copy-start.12 = (f32[96,2048]{1,0:T(8,128)S(1)}, f32[96,2048]{1,0:T(8,128)}, u32[]{:S(2)}) copy-start(f32[96,2048]{1,0:T(8,128)} %get-tuple-element.60) | copy-start | bytes 2359300
  524.5 25.8 %collective-permute-start.20 = (f32[64,2048]{1,0:T(8,128)S(1)}, f32[64,2048]{1,0:T(8,128)S(1)}, u32[]{:S(2)}, u32[]{:S(2)}) collective-permute-start(f32[64,2048]{1,0:T(8,128)S(1)} %add.201), channel_id=1, source_target_pairs={{2,4},{4,2},{3,5},{5,3},{10,12},{12,10},{11,13},{13,11},{18,20},{2... | collective-permute-start | bytes 1572872 | tf_op jit(solution)/shard_map/ppermute | solution.py:34
  525.7 1.6 collective-permute-start.15
  527.4 29.1 %copy-start.4 = (f32[16,2048]{1,0:T(8,128)}, f32[16,2048]{1,0:T(8,128)S(1)}, u32[]{:S(2)}) copy-start(f32[16,2048]{1,0:T(8,128)S(1)} %multiply_add_fusion.3) | copy-start | bytes 393220
  527.4 46.3 %collective-permute-start.12 = (f32[96,2048]{1,0:T(8,128)S(1)}, f32[96,2048]{1,0:T(8,128)S(1)}, u32[]{:S(2)}, u32[]{:S(2)}) collective-permute-start(f32[96,2048]{1,0:T(8,128)S(1)} %copy-done.11), channel_id=1, source_target_pairs={{0,2},{6,4},{1,3},{7,5},{8,10},{14,12},{9,11},{15,13},{16,18},{22,... | collective-permute-start | bytes 2359304 | tf_op jit(solution)/shard_map/ppermute | solution.py:34
  543.1 55.1 %copy-start.10 = (f32[32,2048]{1,0:T(8,128)}, f32[32,2048]{1,0:T(8,128)S(1)}, u32[]{:S(2)}) copy-start(f32[32,2048]{1,0:T(8,128)S(1)} %add.194.refs_4_) | copy-start | bytes 786436
  549.6 7.2 collective-permute-start.16
  550.4 45.2 %copy-start.6 = (f32[64,2048]{1,0:T(8,128)}, f32[64,2048]{1,0:T(8,128)S(1)}, u32[]{:S(2)}) copy-start(f32[64,2048]{1,0:T(8,128)S(1)} %add.202.refs_5_) | copy-start | bytes 1572868
  550.5 24.0 %collective-permute-start.27 = (f32[96,2048]{1,0:T(8,128)S(1)}, f32[96,2048]{1,0:T(8,128)S(1)}, u32[]{:S(2)}, u32[]{:S(2)}) collective-permute-start(f32[96,2048]{1,0:T(8,128)S(1)} %add.203), channel_id=1, source_target_pairs={{2,4},{4,2},{3,5},{5,3},{10,12},{12,10},{11,13},{13,11},{18,20},{2... | collective-permute-start | bytes 2359304 | tf_op jit(solution)/shard_map/ppermute | solution.py:34
  556.8 19.9 %copy-start.19 = (f32[32,2048]{1,0:T(8,128)S(1)}, f32[32,2048]{1,0:T(8,128)}, u32[]{:S(2)}) copy-start(f32[32,2048]{1,0:T(8,128)} %get-tuple-element.47) | copy-start | bytes 786436
  556.8 37.5 %copy-start.18 = (f32[32,2048]{1,0:T(8,128)S(1)}, f32[32,2048]{1,0:T(8,128)}, u32[]{:S(2)}) copy-start(f32[32,2048]{1,0:T(8,128)} %get-tuple-element.58) | copy-start | bytes 786436
  556.9 41.0 %copy-start.3 = (f32[96,2048]{1,0:T(8,128)}, f32[96,2048]{1,0:T(8,128)S(1)}, u32[]{:S(2)}) copy-start(f32[96,2048]{1,0:T(8,128)S(1)} %add.196.refs_6_) | copy-start | bytes 2359300
  573.8 21.8 %collective-permute-start.17 = (f32[96,2048]{1,0:T(8,128)S(1)}, f32[96,2048]{1,0:T(8,128)S(1)}, u32[]{:S(2)}, u32[]{:S(2)}) collective-permute-start(f32[96,2048]{1,0:T(8,128)S(1)} %add.197), channel_id=1, source_target_pairs={{2,4},{4,2},{3,5},{5,3},{10,12},{12,10},{11,13},{13,11},{18,20},{2... | collective-permute-start | bytes 2359304 | tf_op jit(solution)/shard_map/ppermute | solution.py:34
  574.6 63.7 %copy-start.2 = (f32[96,2048]{1,0:T(8,128)}, f32[96,2048]{1,0:T(8,128)S(1)}, u32[]{:S(2)}) copy-start(f32[96,2048]{1,0:T(8,128)S(1)} %add.204.refs_4_) | copy-start | bytes 2359300
  574.7 27.5 %collective-permute-start.28 = (f32[64,2048]{1,0:T(8,128)S(1)}, f32[64,2048]{1,0:T(8,128)S(1)}, u32[]{:S(2)}, u32[]{:S(2)}) collective-permute-start(f32[64,2048]{1,0:T(8,128)S(1)} %add.205), channel_id=1, source_target_pairs={{2,4},{4,2},{3,5},{5,3},{10,12},{12,10},{11,13},{13,11},{18,20},{2... | collective-permute-start | bytes 1572872 | tf_op jit(solution)/shard_map/ppermute | solution.py:34
  575.4 53.9 %collective-permute-start.23 = (f32[96,2048]{1,0:T(8,128)S(1)}, f32[96,2048]{1,0:T(8,128)S(1)}, u32[]{:S(2)}, u32[]{:S(2)}) collective-permute-start(f32[96,2048]{1,0:T(8,128)S(1)} %add.196.refs_6_), channel_id=1, source_target_pairs={{2,0},{4,6},{3,1},{5,7},{10,8},{12,14},{11,9},{13,15},{18,16},{20,... | collective-permute-start | bytes 2359304 | tf_op jit(solution)/shard_map/ppermute | solution.py:34
  576.7 21.4 %collective-permute-start.11 = (f32[32,2048]{1,0:T(8,128)S(1)}, f32[32,2048]{1,0:T(8,128)S(1)}, u32[]{:S(2)}, u32[]{:S(2)}) collective-permute-start(f32[32,2048]{1,0:T(8,128)S(1)} %copy-done.19), channel_id=1, source_target_pairs={{0,2},{6,4},{1,3},{7,5},{8,10},{14,12},{9,11},{15,13},{16,18},{22,... | collective-permute-start | bytes 786440 | tf_op jit(solution)/shard_map/ppermute | solution.py:34
  594.3 6.7 collective-permute-start.24
  595.6 31.6 %collective-permute-start.22 = (f32[64,2048]{1,0:T(8,128)S(1)}, f32[64,2048]{1,0:T(8,128)S(1)}, u32[]{:S(2)}, u32[]{:S(2)}) collective-permute-start(f32[64,2048]{1,0:T(8,128)S(1)} %add.202.refs_5_), channel_id=1, source_target_pairs={{2,0},{4,6},{3,1},{5,7},{10,8},{12,14},{11,9},{13,15},{18,16},{20,... | collective-permute-start | bytes 1572872 | tf_op jit(solution)/shard_map/ppermute | solution.py:34
  598.1 27.0 %collective-permute-start.21 = (f32[32,2048]{1,0:T(8,128)S(1)}, f32[32,2048]{1,0:T(8,128)S(1)}, u32[]{:S(2)}, u32[]{:S(2)}) collective-permute-start(f32[32,2048]{1,0:T(8,128)S(1)} %add.194.refs_4_), channel_id=1, source_target_pairs={{2,0},{4,6},{3,1},{5,7},{10,8},{12,14},{11,9},{13,15},{18,16},{20,... | collective-permute-start | bytes 786440 | tf_op jit(solution)/shard_map/ppermute | solution.py:34
  600.9 42.2 %collective-permute-start.32 = (f32[96,2048]{1,0:T(8,128)S(1)}, f32[96,2048]{1,0:T(8,128)}, u32[]{:S(2)}, u32[]{:S(2)}) collective-permute-start(f32[96,2048]{1,0:T(8,128)S(1)} %add.204.refs_4_), channel_id=1, source_target_pairs={{2,0},{4,6},{3,1},{5,7},{10,8},{12,14},{11,9},{13,15},{18,16},{20,... | collective-permute-start | bytes 2359304 | tf_op jit(solution)/shard_map/ppermute | solution.py:34
  602.2 67.5 %collective-permute-start.33 = (f32[96,2048]{1,0:T(8,128)}, f32[96,2048]{1,0:T(8,128)}, u32[]{:S(2)}, u32[]{:S(2)}) collective-permute-start(f32[96,2048]{1,0:T(8,128)} %add.198.refs_5_), channel_id=1, source_target_pairs={{2,0},{4,6},{3,1},{5,7},{10,8},{12,14},{11,9},{13,15},{18,16},{20,... | collective-permute-start | bytes 2359304 | tf_op jit(solution)/shard_map/ppermute | solution.py:34
  625.1 44.6 %collective-permute-start.34 = (f32[64,2048]{1,0:T(8,128)}, f32[64,2048]{1,0:T(8,128)}, u32[]{:S(2)}, u32[]{:S(2)}) collective-permute-start(f32[64,2048]{1,0:T(8,128)} %add.206.refs_6_), channel_id=1, source_target_pairs={{2,0},{4,6},{3,1},{5,7},{10,8},{12,14},{11,9},{13,15},{18,16},{20,... | collective-permute-start | bytes 1572872 | tf_op jit(solution)/shard_map/ppermute | solution.py:34
  627.2 11.1 %collective-permute-start.18 = (f32[32,2048]{1,0:T(8,128)}, f32[32,2048]{1,0:T(8,128)}, u32[]{:S(2)}, u32[]{:S(2)}) collective-permute-start(f32[32,2048]{1,0:T(8,128)} %add.199), channel_id=1, source_target_pairs={{2,4},{4,2},{3,5},{5,3},{10,12},{12,10},{11,13},{13,11},{18,20},{2... | collective-permute-start | bytes 786440 | tf_op jit(solution)/shard_map/ppermute | solution.py:34
  630.2 9.2 %collective-permute-start.29 = (f32[32,2048]{1,0:T(8,128)}, f32[32,2048]{1,0:T(8,128)}, u32[]{:S(2)}, u32[]{:S(2)}) collective-permute-start(f32[32,2048]{1,0:T(8,128)} %add.207), channel_id=1, source_target_pairs={{2,4},{4,2},{3,5},{5,3},{10,12},{12,10},{11,13},{13,11},{18,20},{2... | collective-permute-start | bytes 786440 | tf_op jit(solution)/shard_map/ppermute | solution.py:34
  639.4 39.0 %copy-start.7 = (f32[32,2048]{1,0:T(8,128)}, f32[32,2048]{1,0:T(8,128)S(1)}, u32[]{:S(2)}) copy-start(f32[32,2048]{1,0:T(8,128)S(1)} %add.200.refs_4_) | copy-start | bytes 786436
  640.6 37.8 %copy-start.8 = (f32[32,2048]{1,0:T(8,128)}, f32[32,2048]{1,0:T(8,128)S(1)}, u32[]{:S(2)}) copy-start(f32[32,2048]{1,0:T(8,128)S(1)} %add.208.refs_5_) | copy-start | bytes 786436
  640.6 37.8 %collective-permute-start.31 = (f32[32,2048]{1,0:T(8,128)S(1)}, f32[32,2048]{1,0:T(8,128)}, u32[]{:S(2)}, u32[]{:S(2)}) collective-permute-start(f32[32,2048]{1,0:T(8,128)S(1)} %add.208.refs_5_), channel_id=1, source_target_pairs={{2,0},{4,6},{3,1},{5,7},{10,8},{12,14},{11,9},{13,15},{18,16},{20,... | collective-permute-start | bytes 786440 | tf_op jit(solution)/shard_map/ppermute | solution.py:34
  641.9 36.6 %collective-permute-start.30 = (f32[32,2048]{1,0:T(8,128)S(1)}, f32[32,2048]{1,0:T(8,128)}, u32[]{:S(2)}, u32[]{:S(2)}) collective-permute-start(f32[32,2048]{1,0:T(8,128)S(1)} %add.200.refs_4_), channel_id=1, source_target_pairs={{2,0},{4,6},{3,1},{5,7},{10,8},{12,14},{11,9},{13,15},{18,16},{20,... | collective-permute-start | bytes 786440 | tf_op jit(solution)/shard_map/ppermute | solution.py:34
  682.2 1.2 collective-permute-start.35
  683.4 3.6 collective-permute-start.36
  687.0 3.6 collective-permute-start.37
  690.5 4.5 collective-permute-start.38
  695.0 3.6 collective-permute-start.39
  703.8 25.8 %collective-permute-start.40 = (f32[128,2048]{1,0:T(8,128)}, f32[128,2048]{1,0:T(8,128)}, u32[]{:S(2)}, u32[]{:S(2)}) collective-permute-start(f32[128,2048]{1,0:T(8,128)} %shard_map.42), channel_id=1, source_target_pairs={{0,2},{6,4},{1,3},{7,5},{8,10},{14,12},{9,11},{15,13},{16,18},{22,... | collective-permute-start | bytes 3145736 | tf_op jit(solution)/shard_map/ppermute | solution.py:34
  707.4 32.8 %copy-start.5 = (f32[16,2048]{1,0:T(8,128)S(1)}, f32[16,2048]{1,0:T(8,128)}, u32[]{:S(2)}) copy-start(f32[16,2048]{1,0:T(8,128)} %copy-done.4) | copy-start | bytes 393220
  719.9 32.2 %collective-permute-start.44 = (f32[128,2048]{1,0:T(8,128)}, f32[128,2048]{1,0:T(8,128)}, u32[]{:S(2)}, u32[]{:S(2)}) collective-permute-start(f32[128,2048]{1,0:T(8,128)} %get-tuple-element.72), channel_id=1, source_target_pairs={{0,2},{6,4},{1,3},{7,5},{8,10},{14,12},{9,11},{15,13},{16,18},{22,... | collective-permute-start | bytes 3145736 | tf_op jit(solution)/shard_map/ppermute | solution.py:34
  732.2 22.2 %collective-permute-start.41 = (f32[128,2048]{1,0:T(8,128)}, f32[128,2048]{1,0:T(8,128)}, u32[]{:S(2)}, u32[]{:S(2)}) collective-permute-start(f32[128,2048]{1,0:T(8,128)} %add.219), channel_id=1, source_target_pairs={{2,4},{4,2},{3,5},{5,3},{10,12},{12,10},{11,13},{13,11},{18,20},{2... | collective-permute-start | bytes 3145736 | tf_op jit(solution)/shard_map/ppermute | solution.py:34
  733.9 20.6 %copy-start.1 = (f32[128,2048]{1,0:T(8,128)S(1)}, f32[128,2048]{1,0:T(8,128)}, u32[]{:S(2)}) copy-start(f32[128,2048]{1,0:T(8,128)} %get-tuple-element.70) | copy-start | bytes 3145732
  733.9 35.5 %collective-permute-start.43 = (f32[128,2048]{1,0:T(8,128)}, f32[128,2048]{1,0:T(8,128)S(1)}, u32[]{:S(2)}, u32[]{:S(2)}) collective-permute-start(f32[128,2048]{1,0:T(8,128)} %get-tuple-element.71), channel_id=1, source_target_pairs={{0,2},{6,4},{1,3},{7,5},{8,10},{14,12},{9,11},{15,13},{16,18},{22,... | collective-permute-start | bytes 3145736 | tf_op jit(solution)/shard_map/ppermute | solution.py:34
  753.7 15.7 %collective-permute-start.45 = (f32[128,2048]{1,0:T(8,128)S(1)}, f32[128,2048]{1,0:T(8,128)S(1)}, u32[]{:S(2)}, u32[]{:S(2)}) collective-permute-start(f32[128,2048]{1,0:T(8,128)S(1)} %add.223), channel_id=1, source_target_pairs={{2,4},{4,2},{3,5},{5,3},{10,12},{12,10},{11,13},{13,11},{18,20},{2... | collective-permute-start | bytes 3145736 | tf_op jit(solution)/shard_map/ppermute | solution.py:34
  755.9 19.5 %copy-start.9 = (f32[128,2048]{1,0:T(8,128)S(1)}, f32[128,2048]{1,0:T(8,128)}, u32[]{:S(2)}) copy-start(f32[128,2048]{1,0:T(8,128)} %get-tuple-element.71) | copy-start | bytes 3145732
  755.9 19.4 %collective-permute-start.42 = (f32[128,2048]{1,0:T(8,128)S(1)}, f32[128,2048]{1,0:T(8,128)S(1)}, u32[]{:S(2)}, u32[]{:S(2)}) collective-permute-start(f32[128,2048]{1,0:T(8,128)S(1)} %add.220), channel_id=1, source_target_pairs={{2,0},{4,6},{3,1},{5,7},{10,8},{12,14},{11,9},{13,15},{18,16},{20,... | collective-permute-start | bytes 3145736 | tf_op jit(solution)/shard_map/ppermute | solution.py:34
  (6 other events, 25.3 us)

commit v4 on v3

--- a/solution.py
+++ b/solution.py
@@ -15,7 +15,6 @@
 LINE = 4
 TILE = 8
 SPREAD = 3 / 7
-AHEAD = 16
 
 epsilon = 1e-06
 
@@ -47,11 +46,22 @@
     cut = int(rows * SPREAD) // TILE * TILE
     rest = rows - cut
     tiles = rest // TILE
-    if outers != LINE or rest % TILE or tiles < 10 or cut <= AHEAD:
+    if outers != LINE or rest % TILE or cut % TILE or tiles < 13 or not cut:
         return None
-    body = tiles - 7
-    sizes = [1, 2] + [3] * (body // 3) + [body % 3] * (body % 3 > 0) + [2, 1, 1]
+    body = tiles - 10
+    sizes = [1, 2] + [3] * (body // 3) + [body % 3] * (body % 3 > 0) + [2, 2, 1, 1, 1]
     return cut, sizes
+
+
+def hops(workers, outers):
+    near, far = range(workers // 2), range(workers // 2, workers)
+    wide = range(outers // 2, outers)
+    first = [(far[0], 0)]
+    second = [(0, j) for j in wide]
+    third = [(k, j) for k in near[1:] for j in wide] + [(k, j) for k in far for j in wide]
+    third += [(k, 0) for k in far[1:]] + [(k, 0) for k in near[1:]]
+    fourth = [(k, j) for k in range(workers) for j in range(1, outers // 2)]
+    return first, second, third, fourth
 
 
 SMEM = pl.BlockSpec(memory_space=pltpu.SMEM)
@@ -175,6 +185,74 @@
     return run(kernel, (blocks * size,), in_specs, outs, shapes, operands, moved, prefetch=1)
 
 
+def row_tile(rows):
+    return next(tile for tile in (32, 16, 8) if rows % tile == 0)
+
+
+def move_spread(share, factor, values, v):
+    (rows, columns), count = v.shape, len(values)
+    tile = row_tile(rows)
+
+    def kernel(factor, v, *refs):
+        values, (v_out, sq_out) = refs[:count], refs[-2:]
+        moved = v[...] + step_of(factor, values, v[...]) * share
+        v_out[...] = moved
+
+        @pl.when(pl.program_id(0) == 0)
+        def _():
+            sq_out[...] = jnp.zeros_like(sq_out)
+
+        for k, value in enumerate(values):
+            square = jnp.square(value[...] - moved)
+            folded = sum(square[j : j + 8] for j in range(0, tile, 8))
+            sq_out[k] += sum(folded[:, j : j + 128] for j in range(0, columns, 128))
+
+    at = pl.BlockSpec((tile, columns), lambda i: (i, 0))
+    squares = pl.BlockSpec((count, 8, 128), lambda i: (0, 0, 0))
+    shapes = (
+        jax.ShapeDtypeStruct(v.shape, v.dtype),
+        jax.ShapeDtypeStruct((count, 8, 128), v.dtype),
+    )
+    in_specs, moved = [SMEM] + [at] * (count + 1), (count + 2) * rows * columns
+    return run(kernel, (rows // tile,), in_specs, (at, squares), shapes, (factor, v, *values), moved)
+
+
+def end_spread(share, factor, values, v, rows):
+    (cut, columns), count = v.shape, len(values)
+    tile = row_tile(cut)
+
+    def kernel(factor, v, *refs):
+        refs[-1][...] = v[...] + step_of(factor, refs[:count], v[...]) * share
+
+    at = pl.BlockSpec((tile, columns), lambda i: (i, 0))
+    shape = jax.ShapeDtypeStruct((rows, columns), v.dtype)
+    in_specs, moved = [SMEM] + [at] * (count + 1), (count + 2) * cut * columns
+    return run(kernel, (cut // tile,), in_specs, at, shape, (factor, v, *values), moved)
+
+
+def end_line(share, place, is_end, v, end_parts, mid_parts, buffer, cut):
+    rows, columns = end_parts[0].shape
+    tile = row_tile(math.gcd(rows, cut))
+    ends = len(end_parts)
+    offset, size = cut // tile, rows // tile
+
+    def kernel(place, is_end, v, *refs):
+        parts, out = refs[:-2], refs[-1]
+        end = sum(part[...] for part in parts[:ends])
+        mid = sum(part[...] for part in parts[ends:])
+        out[...] = v[...] + jnp.where(is_end[0] > 0, end, mid) * share
+
+    at = pl.BlockSpec((tile, columns), lambda i, place: (i, 0))
+    own = pl.BlockSpec((tile, columns), lambda i, place: (place[0] * size + i, 0))
+    out = pl.BlockSpec((tile, columns), lambda i, place: (offset + i, 0))
+    operands = (place, is_end, v, *end_parts, *mid_parts, buffer)
+    in_specs = [SMEM, own] + [at] * (len(operands) - 4) + [pl.BlockSpec(memory_space=pl.ANY)]
+    shape = jax.ShapeDtypeStruct(buffer.shape, buffer.dtype)
+    aliases = {len(operands) - 1: 0}
+    moved = (len(operands) - 2) * rows * columns
+    return run(kernel, (size,), in_specs, out, shape, operands, moved, aliases, prefetch=1)
+
+
 def spread_only(mine, center, radius_total, worker_count):
     own_rows = center
     gathered = lax.all_to_all(mine, ("worker", "outer"), split_axis=0, concat_axis=0, tiled=True)
@@ -202,81 +280,91 @@
     is_end = (o == 0) | (o == LINE - 1)
     is_low = o < LINE // 2
 
-    def line_rows(source, worker):
-        return lax.dynamic_slice(source, (worker * outers, cut, 0), (outers, rest, columns))
+    source = [mine]
+
+    def take(step, turn, low, count, size):
+        begin = (w ^ step) * outers + (o ^ turn if count == 1 else 0)
+        rows_out = lax.dynamic_slice(source[0], (begin, low, 0), (count, size, columns))
+        if not (step or turn):
+            return rows_out
+        source[0] = tie(source[0], rows_out)
+        jump = step * outers + turn
+        pairs = [(i, i ^ jump) for i in range(worker_count)]
+        return send(rows_out, pairs, ("worker", "outer"))
 
     tail = center[cut:]
+    flows = hops(workers, outers)
+    spread = {(0, 0): take(0, 0, 0, 1, cut)}
+    held = {0: take(0, 0, cut, outers, rest)}
+    far, near = list(range(workers // 2, workers)), list(range(1, workers // 2))
+    for flow in flows[0]:
+        spread[flow] = take(*flow, 0, 1, cut)
     pair = send(tail, [(i, i ^ 1) for i in range(LINE)])
-    steps = list(range(workers // 2, workers)) + list(range(1, workers // 2)) + [0]
-    held, source = [], mine
-    for step in steps:
-        sent = line_rows(source, w ^ step)
-        source = tie(source, sent)
-        if step:
-            swap = [(i, i ^ step) for i in range(workers)]
-            sent = send(sent, swap, "worker")
-        held.append(sent)
-    edges = [(0, AHEAD), (AHEAD, cut)]
-    spread = []
-    for low, high in edges:
-        spread.append(
-            lax.all_to_all(
-                mine[:, low:high], ("worker", "outer"), split_axis=0, concat_axis=0, tiled=True
-            )
-        )
+    held[far[0]] = take(far[0], 0, cut, outers, rest)
+    for flow in flows[1]:
+        spread[flow] = take(*flow, 0, 1, cut)
+    for step in far[1:]:
+        held[step] = take(step, 0, cut, outers, rest)
+    for flow in flows[2]:
+        spread[flow] = take(*flow, 0, 1, cut)
+    for step in near:
+        held[step] = take(step, 0, cut, outers, rest)
+    for flow in flows[3]:
+        spread[flow] = take(*flow, 0, 1, cut)
     first = (o % 2) == 0
-    near = jnp.where(first, jnp.stack([tail, pair]), jnp.stack([pair, tail]))
-    crossed = send(near, ACROSS)
-    far = jnp.where(is_end, send(crossed, TO_ENDS), crossed)
-    line_v = jnp.where(is_low, jnp.concatenate([near, far]), jnp.concatenate([far, near]))
-    spread_v = [center[low:high] for low, high in edges]
-
-    places = jnp.stack([(w ^ step) * outers + o for step in steps])
-    hit = places[:, None] == jnp.arange(worker_count)[None]
-
-    def placed(line_sq):
+    side = jnp.where(first, jnp.stack([tail, pair]), jnp.stack([pair, tail]))
+    crossed = send(side, ACROSS)
+    other = jnp.where(is_end, send(crossed, TO_ENDS), crossed)
+    line_v = jnp.where(is_low, jnp.concatenate([side, other]), jnp.concatenate([other, side]))
+    spread_v, share = center[:cut], 1 / worker_count
+    numbers = jnp.arange(worker_count)
+    steps = [0] + near + far
+    hit = jnp.stack([(w ^ step) * outers + o for step in steps])[:, None] == numbers[None]
+    turns = [(step, turn) for step in range(workers) for turn in range(outers)]
+    spots = jnp.stack([(w ^ step) * outers + (o ^ turn) for step, turn in turns])
+    spread_hit = spots[:, None] == numbers[None]
+
+    def placed(line_sq, hit):
         return jnp.sum(jnp.where(hit, line_sq[:, None], 0.0), axis=0)
 
     def factors(both):
         norm_sq = sum_over_devices(both)
         factor = jnp.minimum(1.0, radius_total * lax.rsqrt(norm_sq + epsilon))
-        return factor, jnp.sum(jnp.where(hit, factor[None], 0.0), axis=1)
-
-    def spread_norms(values):
-        return [
-            jnp.sum(jnp.square(part - v[None]), axis=(1, 2)) for part, v in zip(spread, values)
-        ]
-
-    def spread_update(values, factor):
-        weight = factor[:, None, None]
-        return [
-            v + jnp.sum(weight * (part - v[None]), axis=0) / worker_count
-            for part, v in zip(spread, values)
-        ]
-
-    line_sq, v = jnp.zeros((worker_count,), jnp.float32), line_v
-    for place in reversed(range(workers)):
-        square = jnp.sum(jnp.square(held[place] - v))
-        line_sq = lax.optimization_barrier(line_sq + jnp.where(hit[place], square, 0.0))
-        v = tie(v, line_sq)
-    ahead, last = spread_norms(spread_v)
-    factor, line_factor = factors(last + lax.optimization_barrier(line_sq + ahead))
-
-    flat = [value.reshape(outers * rest, columns) for value in held]
+        return [jnp.sum(jnp.where(at, factor[None], 0.0), axis=1) for at in (spread_hit, hit)]
+
+    early = [(0, 0)] + flows[0] + flows[1] + [f for f in flows[2] if f[0] < workers // 2]
+    early += [f for f in flows[3] if f[0] < workers // 2]
+    late = [f for f in flows[2] if f[0] >= workers // 2] + [f for f in flows[3] if f[0] >= workers // 2]
+    norms = jnp.zeros((worker_count,), jnp.float32)
+
+    def add_norm(norms, value, base, spot):
+        square = jnp.sum(jnp.square(value - base))
+        return lax.optimization_barrier(norms + jnp.where(numbers == spot, square, 0.0))
+
+    for step, turn in early:
+        norms = add_norm(norms, spread[step, turn][0], tie(spread_v, norms), (w ^ step) * outers + (o ^ turn))
+    for step in steps:
+        norms = add_norm(norms, held[step], tie(line_v, norms), (w ^ step) * outers + o)
+    for step, turn in late:
+        norms = add_norm(norms, spread[step, turn][0], tie(spread_v, norms), (w ^ step) * outers + (o ^ turn))
+    factor, line_factor = factors(norms)
+
+    spread = [spread[turn].reshape(cut, columns) for turn in turns]
+    flat = [held[step].reshape(outers * rest, columns) for step in steps]
     flat_v = line_v.reshape(outers * rest, columns)
     end_flag = is_end.astype(jnp.int32).reshape(1)
-    next_spread_v = spread_update(spread_v, factor)
-    spread_sq = sum(spread_norms(next_spread_v))
-    early = {1: next_spread_v, 2: spread_sq}
+    next_spread_v, spread_sq = move_spread(share, factor, spread, spread_v)
+    early = {1: next_spread_v}
     count, places = len(sizes), begins(sizes)
-    own = step_chunks(line_factor, flat, flat_v, 0, sizes[:2])
-    own += step_chunks(line_factor, flat, tie(flat_v, own[0]), places[2], sizes[2:])
+    own = step_chunks(line_factor, flat, flat_v, 0, sizes[:1])
+    own += step_chunks(line_factor, flat, tie(flat_v, own[0]), places[1], sizes[1:2])
+    own += step_chunks(line_factor, flat, tie(flat_v, own[1]), places[2], sizes[2:])
     groups = [slice(0, count - 5), slice(count - 5, count - 2), slice(count - 2, count)]
     totals, backs, carried = [], [], ()
 
     def move(part, carried):
         return move_chunks(
-            end_flag, 1 / worker_count, totals[part], backs[part], flat, flat_v,
+            end_flag, share, totals[part], backs[part], flat, flat_v,
             places[part.start], sizes[part], carried,
         )
 
@@ -297,19 +385,20 @@
         carried = move(part, carried)
     spread_v = next_spread_v
     flat_v = carried[0]
-    line_v = flat_v.reshape(line_v.shape)
-    factor, line_factor = factors(spread_sq + placed(jnp.sum(carried[1], axis=(1, 2))))
+    line_sq = placed(jnp.sum(carried[1], axis=(1, 2)), hit)
+    spread_sq = lax.optimization_barrier(placed(jnp.sum(spread_sq, axis=(1, 2)), spread_hit))
+    factor, line_factor = factors(spread_sq + line_sq)
 
     order = [jnp.where(is_low, LINE - 1 - place, place) for place in range(LINE)]
     block = step_blocks(order[:1], line_factor, flat, flat_v, rest)
     block += step_blocks(order[1:], line_factor, flat, tie(flat_v, block[0]), rest)
     arrived = [send(block[place], TO_MIDS) for place in range(3)]
     passed = [send(block[place] + arrived[place], ACROSS) for place in range(2)]
-    end_sum = block[3] + send(block[3] + passed[0], TO_ENDS)
-    mid_sum = block[2] + arrived[2] + passed[1]
-    own_v = lax.dynamic_index_in_dim(line_v, o, 0, keepdims=False)
-    own_v = own_v + jnp.where(is_end, end_sum, mid_sum) / worker_count
-    return jnp.concatenate([*spread_update(spread_v, factor), own_v])
+    last = send(block[3] + passed[0], TO_ENDS)
+    buffer = end_spread(share, factor, spread, spread_v, rows)
+    place = o.astype(jnp.int32).reshape(1)
+    end_parts, mid_parts = [block[3], last], [block[2], arrived[2], passed[1]]
+    return end_line(share, place, end_flag, flat_v, end_parts, mid_parts, buffer, cut)
 
 
 def solution(mesh):

time: 781 us -> 838 us (1.073)
  starting transfers between devices: 101 us -> 170 us
  waiting for transfers between devices: 522 us -> 472 us
  local copies, waits for them, and re-layouts: 32.2 us -> 52.8 us
  Pallas kernels: 52 us -> 71.1 us
    ppermute x36 -> x54, starting transfers between devices: 82.1 us -> 154 us  [send(): return lax.ppermute(value, axis, pairs)]
    all_to_all x2 -> x0, waiting for transfers between devices: 39.8 us -> none  [on_device(): lax.all_to_all(mine[:, low:high], ('worker', 'outer'), split_axis=0, conc...]
    dynamic_slice x3 -> x18, local copies, waits for them, and re-layouts: 14 us -> 45.8 us  [take(): lax.dynamic_slice(source[0], (begin, low, 0), (count, size, columns))]
    pallas_call x7 -> x11, Pallas kernels: 52 us -> 71.1 us  [run(): pl.pallas_call(kernel, grid_spec=pltpu.PrefetchScalarGridSpec(num_scalar_...]
    slice x4 -> x1, local copies, waits for them, and re-layouts: 14.8 us -> 1.18 us  [on_device(): spread_v, share = (center[:cut], 1 / worker_count)]
    all_to_all x2 -> x0, starting transfers between devices: 12.2 us -> none  [on_device(): lax.all_to_all(mine[:, low:high], ('worker', 'outer'), split_axis=0, conc...]
    ppermute x10, starting transfers between devices: 6.52 us -> 15.8 us  [sum_over_devices(): lax.ppermute(value, axis, [(i, i ^ step) for i in range(size)])]
    reduce_sum x15 -> x26, other arithmetic: 43.7 us -> 38.6 us  [the longest x20 34.7 us: add_norm(): square = jnp.sum(jnp.square(value - base))]
  transfers between devices with their start and end apart: 48 -> 64, of which waited for: 24 -> 32; matrix products, arithmetic and copies ran while one was open for 11% -> 13% of each run, Pallas kernels for 5% -> 7%
where the time goes in v4:
time: 838 us; the launch traced here: 835 us
  waiting for transfers between devices  472 us (56%)
  starting transfers between devices  170 us (20%)
  Pallas kernels  71.1 us (8%)
  other arithmetic  66.9 us (8%)
  local copies, waits for them, and re-layouts  52.8 us (6%)
    ppermute x54, waiting for transfers between devices, send(): return lax.ppermute(value, axis, pairs)  453 us
    ppermute x54, starting transfers between devices, send(): return lax.ppermute(value, axis, pairs)  154 us
    pallas_call x11, Pallas kernels, run(): pl.pallas_call(kernel, grid_spec=pltpu.PrefetchScalarGridSpec(num_scalar_...  71.1 us
    dynamic_slice x18, local copies, waits for them, and re-layouts, take(): lax.dynamic_slice(source[0], (begin, low, 0), (count, size, columns))  45.8 us
    reduce_sum x20, other arithmetic, add_norm(): square = jnp.sum(jnp.square(value - base))  34.7 us
    ppermute x10, waiting for transfers between devices, sum_over_devices(): lax.ppermute(value, axis, [(i, i ^ step) for i in range(size)])  18.9 us
  transfers between devices with their start and end apart: 64, of which 32 were waited for; matrix products, arithmetic and copies ran while one was open for 13% of the time, Pallas kernels for 7%

profile of v4, /device:TPU:0, one launch (start us, length us, event | category | flops | bytes accessed | tf_op | source)
XLA Modules:
  0.0 834.8 jit_solution(6738887961747149617)
XLA Ops:
  0.0 2.2 constant_dynamic-slice_fusion.17
  2.2 3.0 collective-permute-start.6
  5.1 4.7 constant_dynamic-slice_fusion.16
  11.9 2.6 collective-permute-start.7
  16.6 4.8 constant_dynamic-slice_fusion.13
  21.3 2.1 constant_dynamic-slice_fusion.12
  25.5 3.7 collective-permute-start.10
  30.3 2.1 constant_dynamic-slice_fusion.10
  32.4 2.1 constant_dynamic-slice_fusion.9
  34.5 2.1 constant_dynamic-slice_fusion.8
  38.6 2.1 constant_dynamic-slice_fusion.6
  40.7 2.1 constant_dynamic-slice_fusion.5
  42.8 4.7 constant_dynamic-slice_fusion.4
  47.5 56.6 %collective-permute-done = f32[128,2048]{1,0:T(8,128)S(1)} collective-permute-done((f32[128,2048]{1,0:T(8,128)S(1)}, f32[128,2048]{1,0:T(8,128)S(1)}, u32[]{:S(2)}, u32[]{:S(2)}) %collective-permute-start) | collective-permute-done | bytes 1048608 | tf_op jit(solution)/shard_map/ppermute | solution.py:33
  105.1 2.5 maximum_select_fusion.1
  112.9 2.4 constant_dynamic-slice_fusion.2
  115.3 2.8 multiply_reduce_fusion.19
  118.1 2.1 constant_dynamic-slice_fusion.1
  120.8 2.2 constant_dynamic-slice_fusion
  123.0 2.1 collective-permute-start.8
  130.3 12.7 %collective-permute-done.8 = f32[1,96,2048]{2,1,0:T(8,128)S(1)} collective-permute-done((f32[1,96,2048]{2,1,0:T(8,128)}, f32[1,96,2048]{2,1,0:T(8,128)S(1)}, u32[]{:S(2)}, u32[]{:S(2)}) %collective-permute-start.8) | collective-permute-done | bytes 786464 | tf_op jit(solution)/shard_map/ppermute | solution.py:33
  143.0 52.7 %collective-permute-start.12 = (f32[1,96,2048]{2,1,0:T(8,128)S(1)}, f32[1,96,2048]{2,1,0:T(8,128)S(1)}, u32[]{:S(2)}, u32[]{:S(2)}) collective-permute-start(f32[1,96,2048]{2,1,0:T(8,128)S(1)} %copy-done.38), channel_id=1, source_target_pairs={{0,2},{2,0},{4,6},{6,4},{8,10},{10,8},{12,14},{14,12},{16,18},{18,... | collective-permute-start | bytes 2359304 | tf_op jit(solution)/shard_map/ppermute | solution.py:33
  204.0 10.2 %collective-permute-done.12 = f32[1,96,2048]{2,1,0:T(8,128)S(1)} collective-permute-done((f32[1,96,2048]{2,1,0:T(8,128)S(1)}, f32[1,96,2048]{2,1,0:T(8,128)S(1)}, u32[]{:S(2)}, u32[]{:S(2)}) %collective-permute-start.12) | collective-permute-done | bytes 786464 | tf_op jit(solution)/shard_map/ppermute | solution.py:33
  219.2 55.4 %collective-permute-done.13 = f32[1,96,2048]{2,1,0:T(8,128)S(1)} collective-permute-done((f32[1,96,2048]{2,1,0:T(8,128)S(1)}, f32[1,96,2048]{2,1,0:T(8,128)S(1)}, u32[]{:S(2)}, u32[]{:S(2)}) %collective-permute-start.13) | collective-permute-done | bytes 786464 | tf_op jit(solution)/shard_map/ppermute | solution.py:33
  276.3 4.6 collective-permute-start.14
  281.7 7.4 multiply_reduce_fusion.3
  292.8 50.3 %collective-permute-done.4 = f32[4,128,2048]{2,1,0:T(8,128)S(1)} collective-permute-done((f32[4,128,2048]{2,1,0:T(8,128)}, f32[4,128,2048]{2,1,0:T(8,128)S(1)}, u32[]{:S(2)}, u32[]{:S(2)}) %collective-permute-start.4) | collective-permute-done | bytes 4194336 | tf_op jit(solution)/shard_map/ppermute | solution.py:33
  345.8 102.9 %collective-permute-done.5 = f32[4,128,2048]{2,1,0:T(8,128)S(1)} collective-permute-done((f32[4,128,2048]{2,1,0:T(8,128)}, f32[4,128,2048]{2,1,0:T(8,128)S(1)}, u32[]{:S(2)}, u32[]{:S(2)}) %collective-permute-start.5) | collective-permute-done | bytes 4194336 | tf_op jit(solution)/shard_map/ppermute | solution.py:33
  448.7 3.2 collective-permute-start.17
  463.2 7.8 collective-permute-done.17
  472.5 32.6 %collective-permute-done.18 = f32[1,96,2048]{2,1,0:T(8,128)S(1)} collective-permute-done((f32[1,96,2048]{2,1,0:T(8,128)S(1)}, f32[1,96,2048]{2,1,0:T(8,128)S(1)}, u32[]{:S(2)}, u32[]{:S(2)}) %collective-permute-start.18) | collective-permute-done | bytes 786464 | tf_op jit(solution)/shard_map/ppermute | solution.py:33
  512.4 3.0 collective-permute-done.22
  515.5 4.4 collective-permute-start.23
  523.6 2.4 collective-permute-done.24
  532.2 2.6 shard_map.38
  534.9 4.1 collective-permute-start.29
  539.0 13.1 %shard_map.39 = (f32[96,2048]{1,0:T(8,128)}, f32[96,2048]{1,0:T(8,128)}, f32[64,2048]{1,0:T(8,128)}, f32[64,2048]{1,0:T(8,128)}, f32[32,2048]{1,0:T(8,128)}, /*index=5*/f32[32,2048]{1,0:T(8,128)}, f32[32,2048]{1,0:T(8,128)}) custom-call(f32[4]{0:T(128)} %select_reduce_fusion.5.factor, f32[512,2048]{1,0:T(8,128)} %bitcast.97, f32[512,2048]{1,0:T(8,128)} %bitcast.73, ...), custom_call_target="tpu_custom_call" | custom-call | flops 20447232 | bytes 20447232 | tf_op jit(solution)/shard_map/pallas_call | solution.py:71
  553.4 2.2 collective-permute-start.28
  558.4 30.1 %collective-permute-done.34 = f32[32,2048]{1,0:T(8,128)S(1)} collective-permute-done((f32[32,2048]{1,0:T(8,128)S(1)}, f32[32,2048]{1,0:T(8,128)S(1)}, u32[]{:S(2)}, u32[]{:S(2)}) %collective-permute-start.34) | collective-permute-done | bytes 262176 | tf_op jit(solution)/shard_map/ppermute | solution.py:33
  593.0 7.4 shard_map.40
  603.7 15.5 %collective-permute-start.44 = (f32[64,2048]{1,0:T(8,128)}, f32[64,2048]{1,0:T(8,128)S(1)}, u32[]{:S(2)}, u32[]{:S(2)}) collective-permute-start(f32[64,2048]{1,0:T(8,128)} %get-tuple-element.125), channel_id=1, source_target_pairs={{0,2},{6,4},{1,3},{7,5},{8,10},{14,12},{9,11},{15,13},{16,18},{22,... | collective-permute-start | bytes 1572872 | tf_op jit(solution)/shard_map/ppermute | solution.py:33
  624.5 7.4 collective-permute-done.44
  632.7 7.2 collective-permute-start.42
  640.1 2.9 collective-permute-done.27
  643.7 2.2 collective-permute-done.43
  656.1 41.1 %collective-permute-done.38.refs_8_ = f32[32,2048]{1,0:T(8,128)S(1)} collective-permute-done((f32[32,2048]{1,0:T(8,128)S(1)}, f32[32,2048]{1,0:T(8,128)S(1)}, u32[]{:S(2)}, u32[]{:S(2)}) %collective-permute-start.38) | collective-permute-done | bytes 262176 | tf_op jit(solution)/shard_map/ppermute | solution.py:33
  705.7 9.6 %shard_map.41 = (f32[512,2048]{1,0:T(8,128)}, f32[4,8,128]{2,1,0:T(8,128)}) custom-call(s32[1]{0:T(128)} %bitcast.1.is_end, f32[512,2048]{1,0:T(8,128)} %bitcast.68, f32[512,2048]{1,0:T(8,128)} %bitcast.98, f32[512,2048]{1,0:T(8,128)} %bitcast.74, f32[512,2048]{1,0:T(8,128)} %bitcast.82, f32[512,2048]{1,0:T(8,128)} %bitcast.90, f32[32,2048]{1,0:T(8,128)} %copy-done.23, ...), custom_call_target="tpu_custom_call" | custom-call | flops 18874368 | bytes 18874368 | tf_op jit(solution)/shard_map/pallas_call | solution.py:71
  721.6 5.8 shard_map.42
  729.4 2.8 collective-permute-done.49.refs_7_
  732.9 2.8 shard_map.43
  739.3 2.1 collective-permute-done.54
  741.4 2.3 collective-permute-start.55
  745.2 2.3 collective-permute-start.56
  747.6 2.1 collective-permute-done.56
  754.1 4.5 shard_map.44
  758.6 4.0 collective-permute-start.58
  763.2 12.4 %shard_map.45 = (f32[128,2048]{1,0:T(8,128)}, f32[128,2048]{1,0:T(8,128)}, f32[128,2048]{1,0:T(8,128)}) custom-call(s32[3]{0:T(128)} %pad_add_fusion.1.places, f32[4]{0:T(128)} %select_reduce_fusion.3.factor, f32[512,2048]{1,0:T(8,128)} %bitcast.102, f32[512,2048]{1,0:T(8,128)} %bitcast.78, f32[512,2048]{1,0:T(8,128)} %bitcast.86, f32[512,2048]{1,0:T(8,128)} %bitcast.94, ...), custom_call_target="tpu_custom_call" | custom-call | flops 18874368 | bytes 18874368 | tf_op jit(solution)/shard_map/pallas_call | solution.py:71
  777.2 9.2 %collective-permute-done.58 = f32[128,2048]{1,0:T(8,128)S(1)} collective-permute-done((f32[128,2048]{1,0:T(8,128)}, f32[128,2048]{1,0:T(8,128)S(1)}, u32[]{:S(2)}, u32[]{:S(2)}) %collective-permute-start.58) | collective-permute-done | bytes 1048608 | tf_op jit(solution)/shard_map/ppermute | solution.py:33
  787.2 7.3 collective-permute-start.61
  794.5 14.3 %collective-permute-done.62 = f32[128,2048]{1,0:T(8,128)S(1)} collective-permute-done((f32[128,2048]{1,0:T(8,128)}, f32[128,2048]{1,0:T(8,128)S(1)}, u32[]{:S(2)}, u32[]{:S(2)}) %collective-permute-start.62) | collective-permute-done | bytes 1048608 | tf_op jit(solution)/shard_map/ppermute | solution.py:33
  814.0 6.4 shard_map.46.refs_5_
  820.4 5.5 collective-permute-done.61.refs_3_
  825.9 3.6 collective-permute-done.60.refs_1_
  830.5 4.3 shard_map.47
  (283 shorter events, 137.4 us)
Async XLA Ops:
  2.2 120.9 %collective-permute-start.6 = (f32[1,96,2048]{2,1,0:T(8,128)}, f32[1,96,2048]{2,1,0:T(8,128)}, u32[]{:S(2)}, u32[]{:S(2)}) collective-permute-start(f32[1,96,2048]{2,1,0:T(8,128)} %constant_dynamic-slice_fusion.17), channel_id=1, source_target_pairs={{0,16},{2,18},{4,20},{6,22},{8,24},{10,26},{12,28},{14,30},{16,0},... | collective-permute-start | bytes 2359304 | tf_op jit(solution)/shard_map/ppermute | solution.py:33
  11.9 115.9 %collective-permute-start.7 = (f32[1,96,2048]{2,1,0:T(8,128)}, f32[1,96,2048]{2,1,0:T(8,128)}, u32[]{:S(2)}, u32[]{:S(2)}) collective-permute-start(f32[1,96,2048]{2,1,0:T(8,128)} %constant_dynamic-slice_fusion.15), channel_id=1, source_target_pairs={{0,4},{2,6},{4,0},{6,2},{8,12},{10,14},{12,8},{14,10},{16,20},{18,... | collective-permute-start | bytes 2359304 | tf_op jit(solution)/shard_map/ppermute | solution.py:33
  23.4 175.4 %collective-permute-start.9 = (f32[1,96,2048]{2,1,0:T(8,128)}, f32[1,96,2048]{2,1,0:T(8,128)}, u32[]{:S(2)}, u32[]{:S(2)}) collective-permute-start(f32[1,96,2048]{2,1,0:T(8,128)} %constant_dynamic-slice_fusion.12), channel_id=1, source_target_pairs={{0,12},{2,14},{4,8},{6,10},{8,4},{10,6},{12,0},{14,2},{16,28},{18,... | collective-permute-start | bytes 2359304 | tf_op jit(solution)/shard_map/ppermute | solution.py:33
  25.5 173.3 %collective-permute-start.10 = (f32[1,96,2048]{2,1,0:T(8,128)}, f32[1,96,2048]{2,1,0:T(8,128)}, u32[]{:S(2)}, u32[]{:S(2)}) collective-permute-start(f32[1,96,2048]{2,1,0:T(8,128)} %constant_dynamic-slice_fusion.11), channel_id=1, source_target_pairs={{0,14},{2,12},{4,10},{6,8},{8,6},{10,4},{12,2},{14,0},{16,30},{18,... | collective-permute-start | bytes 2359304 | tf_op jit(solution)/shard_map/ppermute | solution.py:33
  30.3 73.8 %collective-permute-start = (f32[128,2048]{1,0:T(8,128)S(1)}, f32[128,2048]{1,0:T(8,128)S(1)}, u32[]{:S(2)}, u32[]{:S(2)}) collective-permute-start(f32[128,2048]{1,0:T(8,128)S(1)} %get-tuple-element.144), channel_id=1, source_target_pairs={{0,2},{2,0},{4,6},{6,4},{1,3},{3,1},{5,7},{7,5},{8,10},{10,8},{12,... | collective-permute-start | bytes 3145736 | tf_op jit(solution)/shard_map/ppermute | solution.py:33
  107.6 89.0 %collective-permute-start.1 = (f32[2,128,2048]{2,1,0:T(8,128)S(1)}, f32[2,128,2048]{2,1,0:T(8,128)}, u32[]{:S(2)}, u32[]{:S(2)}) collective-permute-start(f32[2,128,2048]{2,1,0:T(8,128)S(1)} %maximum_select_fusion.1), channel_id=1, source_target_pairs={{2,4},{4,2},{3,5},{5,3},{10,12},{12,10},{11,13},{13,11},{18,20},{2... | collective-permute-start | bytes 6291464 | tf_op jit(solution)/shard_map/ppermute | solution.py:33
  123.0 20.0 %collective-permute-start.8 = (f32[1,96,2048]{2,1,0:T(8,128)}, f32[1,96,2048]{2,1,0:T(8,128)S(1)}, u32[]{:S(2)}, u32[]{:S(2)}) collective-permute-start(f32[1,96,2048]{2,1,0:T(8,128)} %constant_dynamic-slice_fusion.14), channel_id=1, source_target_pairs={{0,6},{2,4},{4,2},{6,0},{8,14},{10,12},{12,10},{14,8},{16,22},{18,... | collective-permute-start | bytes 2359304 | tf_op jit(solution)/shard_map/ppermute | solution.py:33
  127.8 162.0 %collective-permute-start.3 = (f32[4,128,2048]{2,1,0:T(8,128)}, f32[4,128,2048]{2,1,0:T(8,128)S(1)}, u32[]{:S(2)}, u32[]{:S(2)}) collective-permute-start(f32[4,128,2048]{2,1,0:T(8,128)} %constant_dynamic-slice_fusion.4), channel_id=1, source_target_pairs={{0,8},{2,10},{4,12},{6,14},{8,0},{10,2},{12,4},{14,6},{16,24},{18,... | collective-permute-start | bytes 12582920 | tf_op jit(solution)/shard_map/ppermute | solution.py:33
  143.0 71.1 %collective-permute-start.12 = (f32[1,96,2048]{2,1,0:T(8,128)S(1)}, f32[1,96,2048]{2,1,0:T(8,128)S(1)}, u32[]{:S(2)}, u32[]{:S(2)}) collective-permute-start(f32[1,96,2048]{2,1,0:T(8,128)S(1)} %copy-done.38), channel_id=1, source_target_pairs={{0,2},{2,0},{4,6},{6,4},{8,10},{10,8},{12,14},{14,12},{16,18},{18,... | collective-permute-start | bytes 2359304 | tf_op jit(solution)/shard_map/ppermute | solution.py:33
  196.6 79.7 %collective-permute-start.2 = (f32[2,128,2048]{2,1,0:T(8,128)}, f32[2,128,2048]{2,1,0:T(8,128)S(1)}, u32[]{:S(2)}, u32[]{:S(2)}) collective-permute-start(f32[2,128,2048]{2,1,0:T(8,128)} %collective-permute-done.1), channel_id=1, source_target_pairs={{2,0},{4,6},{3,1},{5,7},{10,8},{12,14},{11,9},{13,15},{18,16},{20,... | collective-permute-start | bytes 6291464 | tf_op jit(solution)/shard_map/ppermute | solution.py:33
  198.7 16.1 %collective-permute-start.11 = (f32[1,96,2048]{2,1,0:T(8,128)S(1)}, f32[1,96,2048]{2,1,0:T(8,128)S(1)}, u32[]{:S(2)}, u32[]{:S(2)}) collective-permute-start(f32[1,96,2048]{2,1,0:T(8,128)S(1)} %copy-done.36), channel_id=1, source_target_pairs={{0,8},{2,10},{4,12},{6,14},{8,0},{10,2},{12,4},{14,6},{16,24},{18,... | collective-permute-start | bytes 2359304 | tf_op jit(solution)/shard_map/ppermute | solution.py:33
  198.8 144.3 %collective-permute-start.4 = (f32[4,128,2048]{2,1,0:T(8,128)}, f32[4,128,2048]{2,1,0:T(8,128)S(1)}, u32[]{:S(2)}, u32[]{:S(2)}) collective-permute-start(f32[4,128,2048]{2,1,0:T(8,128)} %constant_dynamic-slice_fusion.16), channel_id=1, source_target_pairs={{0,16},{2,18},{4,20},{6,22},{8,24},{10,26},{12,28},{14,30},{16,0},... | collective-permute-start | bytes 12582920 | tf_op jit(solution)/shard_map/ppermute | solution.py:33
  214.1 234.6 %collective-permute-start.5 = (f32[4,128,2048]{2,1,0:T(8,128)}, f32[4,128,2048]{2,1,0:T(8,128)S(1)}, u32[]{:S(2)}, u32[]{:S(2)}) collective-permute-start(f32[4,128,2048]{2,1,0:T(8,128)} %constant_dynamic-slice_fusion.13), channel_id=1, source_target_pairs={{0,24},{2,26},{4,28},{6,30},{8,16},{10,18},{12,20},{14,22},{16,8},... | collective-permute-start | bytes 12582920 | tf_op jit(solution)/shard_map/ppermute | solution.py:33
  214.8 59.8 %collective-permute-start.13 = (f32[1,96,2048]{2,1,0:T(8,128)S(1)}, f32[1,96,2048]{2,1,0:T(8,128)S(1)}, u32[]{:S(2)}, u32[]{:S(2)}) collective-permute-start(f32[1,96,2048]{2,1,0:T(8,128)S(1)} %copy-done.37), channel_id=1, source_target_pairs={{0,10},{2,8},{4,14},{6,12},{8,2},{10,0},{12,6},{14,4},{16,26},{18,... | collective-permute-start | bytes 2359304 | tf_op jit(solution)/shard_map/ppermute | solution.py:33
  274.6 232.0 %collective-permute-start.19 = (f32[1,96,2048]{2,1,0:T(8,128)}, f32[1,96,2048]{2,1,0:T(8,128)}, u32[]{:S(2)}, u32[]{:S(2)}) collective-permute-start(f32[1,96,2048]{2,1,0:T(8,128)} %constant_dynamic-slice_fusion.1), channel_id=1, source_target_pairs={{0,18},{2,16},{4,22},{6,20},{8,26},{10,24},{12,30},{14,28},{16,2},... | collective-permute-start | bytes 2359304 | tf_op jit(solution)/shard_map/ppermute | solution.py:33
  276.3 178.1 %collective-permute-start.14 = (f32[1,96,2048]{2,1,0:T(8,128)}, f32[1,96,2048]{2,1,0:T(8,128)}, u32[]{:S(2)}, u32[]{:S(2)}) collective-permute-start(f32[1,96,2048]{2,1,0:T(8,128)} %constant_dynamic-slice_fusion.10), channel_id=1, source_target_pairs={{0,20},{2,22},{4,16},{6,18},{8,28},{10,30},{12,24},{14,26},{16,4},... | collective-permute-start | bytes 2359304 | tf_op jit(solution)/shard_map/ppermute | solution.py:33
  289.8 168.6 %collective-permute-start.15 = (f32[1,96,2048]{2,1,0:T(8,128)S(1)}, f32[1,96,2048]{2,1,0:T(8,128)S(1)}, u32[]{:S(2)}, u32[]{:S(2)}) collective-permute-start(f32[1,96,2048]{2,1,0:T(8,128)S(1)} %copy-done.34), channel_id=1, source_target_pairs={{0,22},{2,20},{4,18},{6,16},{8,30},{10,28},{12,26},{14,24},{16,6},... | collective-permute-start | bytes 2359304 | tf_op jit(solution)/shard_map/ppermute | solution.py:33
  343.1 118.6 %collective-permute-start.16 = (f32[1,96,2048]{2,1,0:T(8,128)S(1)}, f32[1,96,2048]{2,1,0:T(8,128)S(1)}, u32[]{:S(2)}, u32[]{:S(2)}) collective-permute-start(f32[1,96,2048]{2,1,0:T(8,128)S(1)} %copy-done.33), channel_id=1, source_target_pairs={{0,28},{2,30},{4,24},{6,26},{8,20},{10,22},{12,16},{14,18},{16,12}... | collective-permute-start | bytes 2359304 | tf_op jit(solution)/shard_map/ppermute | solution.py:33
  448.7 22.3 %collective-permute-start.17 = (f32[1,96,2048]{2,1,0:T(8,128)S(1)}, f32[1,96,2048]{2,1,0:T(8,128)S(1)}, u32[]{:S(2)}, u32[]{:S(2)}) collective-permute-start(f32[1,96,2048]{2,1,0:T(8,128)S(1)} %copy-done.32), channel_id=1, source_target_pairs={{0,30},{2,28},{4,26},{6,24},{8,22},{10,20},{12,18},{14,16},{16,14}... | collective-permute-start | bytes 2359304 | tf_op jit(solution)/shard_map/ppermute | solution.py:33
  454.4 50.6 %collective-permute-start.18 = (f32[1,96,2048]{2,1,0:T(8,128)S(1)}, f32[1,96,2048]{2,1,0:T(8,128)S(1)}, u32[]{:S(2)}, u32[]{:S(2)}) collective-permute-start(f32[1,96,2048]{2,1,0:T(8,128)S(1)} %copy-done.31), channel_id=1, source_target_pairs={{0,24},{2,26},{4,28},{6,30},{8,16},{10,18},{12,20},{14,22},{16,8},... | collective-permute-start | bytes 2359304 | tf_op jit(solution)/shard_map/ppermute | solution.py:33
  458.4 50.8 %collective-permute-start.20 = (f32[1,96,2048]{2,1,0:T(8,128)S(1)}, f32[1,96,2048]{2,1,0:T(8,128)S(1)}, u32[]{:S(2)}, u32[]{:S(2)}) collective-permute-start(f32[1,96,2048]{2,1,0:T(8,128)S(1)} %copy-done.35), channel_id=1, source_target_pairs={{0,26},{2,24},{4,30},{6,28},{8,18},{10,16},{12,22},{14,20},{16,10}... | collective-permute-start | bytes 2359304 | tf_op jit(solution)/shard_map/ppermute | solution.py:33
  510.7 1.2 collective-permute-start.21
  511.9 3.6 collective-permute-start.22
  515.5 6.0 collective-permute-start.23
  521.5 4.5 collective-permute-start.24
  525.9 3.6 collective-permute-start.25
  534.9 22.0 %collective-permute-start.29 = (f32[64,2048]{1,0:T(8,128)}, f32[64,2048]{1,0:T(8,128)S(1)}, u32[]{:S(2)}, u32[]{:S(2)}) collective-permute-start(f32[64,2048]{1,0:T(8,128)} %shard_map.38), channel_id=1, source_target_pairs={{0,2},{6,4},{1,3},{7,5},{8,10},{14,12},{9,11},{15,13},{16,18},{22,... | collective-permute-start | bytes 1572872 | tf_op jit(solution)/shard_map/ppermute | solution.py:33
  552.0 38.1 %collective-permute-start.36 = (f32[96,2048]{1,0:T(8,128)}, f32[96,2048]{1,0:T(8,128)S(1)}, u32[]{:S(2)}, u32[]{:S(2)}) collective-permute-start(f32[96,2048]{1,0:T(8,128)} %get-tuple-element.119), channel_id=1, source_target_pairs={{0,2},{6,4},{1,3},{7,5},{8,10},{14,12},{9,11},{15,13},{16,18},{22,... | collective-permute-start | bytes 2359304 | tf_op jit(solution)/shard_map/ppermute | solution.py:33
  553.4 48.2 %collective-permute-start.28 = (f32[96,2048]{1,0:T(8,128)}, f32[96,2048]{1,0:T(8,128)}, u32[]{:S(2)}, u32[]{:S(2)}) collective-permute-start(f32[96,2048]{1,0:T(8,128)} %get-tuple-element.113), channel_id=1, source_target_pairs={{0,2},{6,4},{1,3},{7,5},{8,10},{14,12},{9,11},{15,13},{16,18},{22,... | collective-permute-start | bytes 2359304 | tf_op jit(solution)/shard_map/ppermute | solution.py:33
  555.6 32.9 %collective-permute-start.34 = (f32[32,2048]{1,0:T(8,128)S(1)}, f32[32,2048]{1,0:T(8,128)S(1)}, u32[]{:S(2)}, u32[]{:S(2)}) collective-permute-start(f32[32,2048]{1,0:T(8,128)S(1)} %copy-done.27), channel_id=1, source_target_pairs={{0,2},{6,4},{1,3},{7,5},{8,10},{14,12},{9,11},{15,13},{16,18},{22,... | collective-permute-start | bytes 786440 | tf_op jit(solution)/shard_map/ppermute | solution.py:33
  557.0 43.5 %collective-permute-start.30 = (f32[64,2048]{1,0:T(8,128)S(1)}, f32[64,2048]{1,0:T(8,128)}, u32[]{:S(2)}, u32[]{:S(2)}) collective-permute-start(f32[64,2048]{1,0:T(8,128)S(1)} %add.373), channel_id=1, source_target_pairs={{2,4},{4,2},{3,5},{5,3},{10,12},{12,10},{11,13},{13,11},{18,20},{2... | collective-permute-start | bytes 1572872 | tf_op jit(solution)/shard_map/ppermute | solution.py:33
  588.5 1.5 collective-permute-start.35
  591.4 30.5 %collective-permute-start.37 = (f32[96,2048]{1,0:T(8,128)S(1)}, f32[96,2048]{1,0:T(8,128)}, u32[]{:S(2)}, u32[]{:S(2)}) collective-permute-start(f32[96,2048]{1,0:T(8,128)S(1)} %add.383), channel_id=1, source_target_pairs={{2,4},{4,2},{3,5},{5,3},{10,12},{12,10},{11,13},{13,11},{18,20},{2... | collective-permute-start | bytes 2359304 | tf_op jit(solution)/shard_map/ppermute | solution.py:33
  603.0 29.7 %collective-permute-start.31 = (f32[96,2048]{1,0:T(8,128)S(1)}, f32[96,2048]{1,0:T(8,128)S(1)}, u32[]{:S(2)}, u32[]{:S(2)}) collective-permute-start(f32[96,2048]{1,0:T(8,128)S(1)} %add.375), channel_id=1, source_target_pairs={{2,4},{4,2},{3,5},{5,3},{10,12},{12,10},{11,13},{13,11},{18,20},{2... | collective-permute-start | bytes 2359304 | tf_op jit(solution)/shard_map/ppermute | solution.py:33
  603.7 28.1 %collective-permute-start.44 = (f32[64,2048]{1,0:T(8,128)}, f32[64,2048]{1,0:T(8,128)S(1)}, u32[]{:S(2)}, u32[]{:S(2)}) collective-permute-start(f32[64,2048]{1,0:T(8,128)} %get-tuple-element.125), channel_id=1, source_target_pairs={{0,2},{6,4},{1,3},{7,5},{8,10},{14,12},{9,11},{15,13},{16,18},{22,... | collective-permute-start | bytes 1572872 | tf_op jit(solution)/shard_map/ppermute | solution.py:33
  619.2 23.7 %collective-permute-start.27 = (f32[64,2048]{1,0:T(8,128)S(1)}, f32[64,2048]{1,0:T(8,128)S(1)}, u32[]{:S(2)}, u32[]{:S(2)}) collective-permute-start(f32[64,2048]{1,0:T(8,128)S(1)} %copy-done.40), channel_id=1, source_target_pairs={{0,2},{6,4},{1,3},{7,5},{8,10},{14,12},{9,11},{15,13},{16,18},{22,... | collective-permute-start | bytes 1572872 | tf_op jit(solution)/shard_map/ppermute | solution.py:33
  620.6 25.4 %collective-permute-start.43 = (f32[32,2048]{1,0:T(8,128)}, f32[32,2048]{1,0:T(8,128)S(1)}, u32[]{:S(2)}, u32[]{:S(2)}) collective-permute-start(f32[32,2048]{1,0:T(8,128)} %get-tuple-element.124), channel_id=1, source_target_pairs={{0,2},{6,4},{1,3},{7,5},{8,10},{14,12},{9,11},{15,13},{16,18},{22,... | collective-permute-start | bytes 786440 | tf_op jit(solution)/shard_map/ppermute | solution.py:33
  621.9 26.7 %collective-permute-start.26 = (f32[32,2048]{1,0:T(8,128)S(1)}, f32[32,2048]{1,0:T(8,128)S(1)}, u32[]{:S(2)}, u32[]{:S(2)}) collective-permute-start(f32[32,2048]{1,0:T(8,128)S(1)} %copy-done.48), channel_id=1, source_target_pairs={{0,2},{6,4},{1,3},{7,5},{8,10},{14,12},{9,11},{15,13},{16,18},{22,... | collective-permute-start | bytes 786440 | tf_op jit(solution)/shard_map/ppermute | solution.py:33
  631.9 20.9 %collective-permute-start.45 = (f32[64,2048]{1,0:T(8,128)S(1)}, f32[64,2048]{1,0:T(8,128)S(1)}, u32[]{:S(2)}, u32[]{:S(2)}) collective-permute-start(f32[64,2048]{1,0:T(8,128)S(1)} %add.385), channel_id=1, source_target_pairs={{2,4},{4,2},{3,5},{5,3},{10,12},{12,10},{11,13},{13,11},{18,20},{2... | collective-permute-start | bytes 1572872 | tf_op jit(solution)/shard_map/ppermute | solution.py:33
  632.7 18.7 %collective-permute-start.42 = (f32[32,2048]{1,0:T(8,128)S(1)}, f32[32,2048]{1,0:T(8,128)S(1)}, u32[]{:S(2)}, u32[]{:S(2)}) collective-permute-start(f32[32,2048]{1,0:T(8,128)S(1)} %copy-done.47), channel_id=1, source_target_pairs={{0,2},{6,4},{1,3},{7,5},{8,10},{14,12},{9,11},{15,13},{16,18},{22,... | collective-permute-start | bytes 786440 | tf_op jit(solution)/shard_map/ppermute | solution.py:33
  643.0 12.3 %collective-permute-start.32 = (f32[64,2048]{1,0:T(8,128)S(1)}, f32[64,2048]{1,0:T(8,128)S(1)}, u32[]{:S(2)}, u32[]{:S(2)}) collective-permute-start(f32[64,2048]{1,0:T(8,128)S(1)} %add.377), channel_id=1, source_target_pairs={{2,4},{4,2},{3,5},{5,3},{10,12},{12,10},{11,13},{13,11},{18,20},{2... | collective-permute-start | bytes 1572872 | tf_op jit(solution)/shard_map/ppermute | solution.py:33
  646.0 56.2 %collective-permute-start.40 = (f32[96,2048]{1,0:T(8,128)S(1)}, f32[96,2048]{1,0:T(8,128)S(1)}, u32[]{:S(2)}, u32[]{:S(2)}) collective-permute-start(f32[96,2048]{1,0:T(8,128)S(1)} %add.384.refs_6_), channel_id=1, source_target_pairs={{2,0},{4,6},{3,1},{5,7},{10,8},{12,14},{11,9},{13,15},{18,16},{20,... | collective-permute-start | bytes 2359304 | tf_op jit(solution)/shard_map/ppermute | solution.py:33
  648.7 55.7 %collective-permute-start.41 = (f32[96,2048]{1,0:T(8,128)S(1)}, f32[96,2048]{1,0:T(8,128)}, u32[]{:S(2)}, u32[]{:S(2)}) collective-permute-start(f32[96,2048]{1,0:T(8,128)S(1)} %add.376.refs_7_), channel_id=1, source_target_pairs={{2,0},{4,6},{3,1},{5,7},{10,8},{12,14},{11,9},{13,15},{18,16},{20,... | collective-permute-start | bytes 2359304 | tf_op jit(solution)/shard_map/ppermute | solution.py:33
  651.5 47.1 %collective-permute-start.39 = (f32[64,2048]{1,0:T(8,128)S(1)}, f32[64,2048]{1,0:T(8,128)S(1)}, u32[]{:S(2)}, u32[]{:S(2)}) collective-permute-start(f32[64,2048]{1,0:T(8,128)S(1)} %add.374.refs_5_), channel_id=1, source_target_pairs={{2,0},{4,6},{3,1},{5,7},{10,8},{12,14},{11,9},{13,15},{18,16},{20,... | collective-permute-start | bytes 1572872 | tf_op jit(solution)/shard_map/ppermute | solution.py:33
  652.8 44.5 %collective-permute-start.38 = (f32[32,2048]{1,0:T(8,128)S(1)}, f32[32,2048]{1,0:T(8,128)S(1)}, u32[]{:S(2)}, u32[]{:S(2)}) collective-permute-start(f32[32,2048]{1,0:T(8,128)S(1)} %add.382.refs_4_), channel_id=1, source_target_pairs={{2,0},{4,6},{3,1},{5,7},{10,8},{12,14},{11,9},{13,15},{18,16},{20,... | collective-permute-start | bytes 786440 | tf_op jit(solution)/shard_map/ppermute | solution.py:33
  655.3 44.6 %collective-permute-start.46 = (f32[32,2048]{1,0:T(8,128)S(1)}, f32[32,2048]{1,0:T(8,128)S(1)}, u32[]{:S(2)}, u32[]{:S(2)}) collective-permute-start(f32[32,2048]{1,0:T(8,128)S(1)} %add.387), channel_id=1, source_target_pairs={{2,4},{4,2},{3,5},{5,3},{10,12},{12,10},{11,13},{13,11},{18,20},{2... | collective-permute-start | bytes 786440 | tf_op jit(solution)/shard_map/ppermute | solution.py:33
  697.3 23.6 %collective-permute-start.50 = (f32[64,2048]{1,0:T(8,128)S(1)}, f32[64,2048]{1,0:T(8,128)}, u32[]{:S(2)}, u32[]{:S(2)}) collective-permute-start(f32[64,2048]{1,0:T(8,128)S(1)} %add.386.refs_4_), channel_id=1, source_target_pairs={{2,0},{4,6},{3,1},{5,7},{10,8},{12,14},{11,9},{13,15},{18,16},{20,... | collective-permute-start | bytes 1572872 | tf_op jit(solution)/shard_map/ppermute | solution.py:33
  698.6 22.3 %collective-permute-start.51 = (f32[64,2048]{1,0:T(8,128)S(1)}, f32[64,2048]{1,0:T(8,128)}, u32[]{:S(2)}, u32[]{:S(2)}) collective-permute-start(f32[64,2048]{1,0:T(8,128)S(1)} %add.378.refs_5_), channel_id=1, source_target_pairs={{2,0},{4,6},{3,1},{5,7},{10,8},{12,14},{11,9},{13,15},{18,16},{20,... | collective-permute-start | bytes 1572872 | tf_op jit(solution)/shard_map/ppermute | solution.py:33
  699.9 15.4 %collective-permute-start.33 = (f32[32,2048]{1,0:T(8,128)S(1)}, f32[32,2048]{1,0:T(8,128)}, u32[]{:S(2)}, u32[]{:S(2)}) collective-permute-start(f32[32,2048]{1,0:T(8,128)S(1)} %add.379), channel_id=1, source_target_pairs={{2,4},{4,2},{3,5},{5,3},{10,12},{12,10},{11,13},{13,11},{18,20},{2... | collective-permute-start | bytes 786440 | tf_op jit(solution)/shard_map/ppermute | solution.py:33
  703.0 14.6 %collective-permute-start.47 = (f32[32,2048]{1,0:T(8,128)}, f32[32,2048]{1,0:T(8,128)}, u32[]{:S(2)}, u32[]{:S(2)}) collective-permute-start(f32[32,2048]{1,0:T(8,128)} %add.389), channel_id=1, source_target_pairs={{2,4},{4,2},{3,5},{5,3},{10,12},{12,10},{11,13},{13,11},{18,20},{2... | collective-permute-start | bytes 786440 | tf_op jit(solution)/shard_map/ppermute | solution.py:33
  704.4 16.5 %collective-permute-start.52 = (f32[32,2048]{1,0:T(8,128)S(1)}, f32[32,2048]{1,0:T(8,128)S(1)}, u32[]{:S(2)}, u32[]{:S(2)}) collective-permute-start(f32[32,2048]{1,0:T(8,128)S(1)} %add.388.refs_6_), channel_id=1, source_target_pairs={{2,0},{4,6},{3,1},{5,7},{10,8},{12,14},{11,9},{13,15},{18,16},{20,... | collective-permute-start | bytes 786440 | tf_op jit(solution)/shard_map/ppermute | solution.py:33
  716.4 13.0 %collective-permute-start.48 = (f32[32,2048]{1,0:T(8,128)S(1)}, f32[32,2048]{1,0:T(8,128)S(1)}, u32[]{:S(2)}, u32[]{:S(2)}) collective-permute-start(f32[32,2048]{1,0:T(8,128)S(1)} %add.380.refs_4_), channel_id=1, source_target_pairs={{2,0},{4,6},{3,1},{5,7},{10,8},{12,14},{11,9},{13,15},{18,16},{20,... | collective-permute-start | bytes 786440 | tf_op jit(solution)/shard_map/ppermute | solution.py:33
  718.7 13.4 %collective-permute-start.49 = (f32[32,2048]{1,0:T(8,128)S(1)}, f32[32,2048]{1,0:T(8,128)S(1)}, u32[]{:S(2)}, u32[]{:S(2)}) collective-permute-start(f32[32,2048]{1,0:T(8,128)S(1)} %add.390.refs_5_), channel_id=1, source_target_pairs={{2,0},{4,6},{3,1},{5,7},{10,8},{12,14},{11,9},{13,15},{18,16},{20,... | collective-permute-start | bytes 786440 | tf_op jit(solution)/shard_map/ppermute | solution.py:33
  736.6 1.2 collective-permute-start.53
  737.8 3.6 collective-permute-start.54
  741.4 3.8 collective-permute-start.55
  745.2 4.5 collective-permute-start.56
  749.7 3.6 collective-permute-start.57
  758.6 27.8 %collective-permute-start.58 = (f32[128,2048]{1,0:T(8,128)}, f32[128,2048]{1,0:T(8,128)S(1)}, u32[]{:S(2)}, u32[]{:S(2)}) collective-permute-start(f32[128,2048]{1,0:T(8,128)} %shard_map.44), channel_id=1, source_target_pairs={{0,2},{6,4},{1,3},{7,5},{8,10},{14,12},{9,11},{15,13},{16,18},{22,... | collective-permute-start | bytes 3145736 | tf_op jit(solution)/shard_map/ppermute | solution.py:33
  775.7 33.2 %collective-permute-start.62 = (f32[128,2048]{1,0:T(8,128)}, f32[128,2048]{1,0:T(8,128)S(1)}, u32[]{:S(2)}, u32[]{:S(2)}) collective-permute-start(f32[128,2048]{1,0:T(8,128)} %get-tuple-element.138), channel_id=1, source_target_pairs={{0,2},{6,4},{1,3},{7,5},{8,10},{14,12},{9,11},{15,13},{16,18},{22,... | collective-permute-start | bytes 3145736 | tf_op jit(solution)/shard_map/ppermute | solution.py:33
  786.5 25.4 %collective-permute-start.59 = (f32[128,2048]{1,0:T(8,128)S(1)}, f32[128,2048]{1,0:T(8,128)S(1)}, u32[]{:S(2)}, u32[]{:S(2)}) collective-permute-start(f32[128,2048]{1,0:T(8,128)S(1)} %add.398), channel_id=1, source_target_pairs={{2,4},{4,2},{3,5},{5,3},{10,12},{12,10},{11,13},{13,11},{18,20},{2... | collective-permute-start | bytes 3145736 | tf_op jit(solution)/shard_map/ppermute | solution.py:33
  787.2 38.7 %collective-permute-start.61 = (f32[128,2048]{1,0:T(8,128)}, f32[128,2048]{1,0:T(8,128)}, u32[]{:S(2)}, u32[]{:S(2)}) collective-permute-start(f32[128,2048]{1,0:T(8,128)} %get-tuple-element.137.refs_2_), channel_id=1, source_target_pairs={{0,2},{6,4},{1,3},{7,5},{8,10},{14,12},{9,11},{15,13},{16,18},{22,... | collective-permute-start | bytes 3145736 | tf_op jit(solution)/shard_map/ppermute | solution.py:33
  810.2 15.7 %collective-permute-start.63 = (f32[128,2048]{1,0:T(8,128)S(1)}, f32[128,2048]{1,0:T(8,128)}, u32[]{:S(2)}, u32[]{:S(2)}) collective-permute-start(f32[128,2048]{1,0:T(8,128)S(1)} %add.400), channel_id=1, source_target_pairs={{2,4},{4,2},{3,5},{5,3},{10,12},{12,10},{11,13},{13,11},{18,20},{2... | collective-permute-start | bytes 3145736 | tf_op jit(solution)/shard_map/ppermute | solution.py:33
  812.0 17.6 %collective-permute-start.60 = (f32[128,2048]{1,0:T(8,128)S(1)}, f32[128,2048]{1,0:T(8,128)S(1)}, u32[]{:S(2)}, u32[]{:S(2)}) collective-permute-start(f32[128,2048]{1,0:T(8,128)S(1)} %add.399), channel_id=1, source_target_pairs={{2,0},{4,6},{3,1},{5,7},{10,8},{12,14},{11,9},{13,15},{18,16},{20,... | collective-permute-start | bytes 3145736 | tf_op jit(solution)/shard_map/ppermute | solution.py:33
  (51 other events, 2296.1 us)

commit v5 on v3

--- a/solution.py
+++ b/solution.py
@@ -14,8 +14,9 @@
 AXES = ("worker", "outer", "mp")
 LINE = 4
 TILE = 8
-SPREAD = 3 / 7
-AHEAD = 16
+SPREAD = 0.4
+
+GRANT = 60 << 20
 
 epsilon = 1e-06
 
@@ -47,10 +48,10 @@
     cut = int(rows * SPREAD) // TILE * TILE
     rest = rows - cut
     tiles = rest // TILE
-    if outers != LINE or rest % TILE or tiles < 10 or cut <= AHEAD:
+    if outers != LINE or rest % TILE or tiles < 13 or not cut:
         return None
-    body = tiles - 7
-    sizes = [1, 2] + [3] * (body // 3) + [body % 3] * (body % 3 > 0) + [2, 1, 1]
+    body = tiles - 10
+    sizes = [1, 2] + [3] * (body // 3) + [body % 3] * (body % 3 > 0) + [2, 2, 1, 1, 1]
     return cut, sizes
 
 
@@ -65,7 +66,7 @@
         ),
         out_shape=out_shape,
         input_output_aliases=aliases,
-        compiler_params=pltpu.CompilerParams(vmem_limit_bytes=60 << 20),
+        compiler_params=pltpu.CompilerParams(vmem_limit_bytes=GRANT),
         cost_estimate=pl.CostEstimate(flops=4 * moved, bytes_accessed=4 * moved, transcendentals=0),
     )(*operands)
 
@@ -148,31 +149,60 @@
     return run(kernel, (sum(sizes),), in_specs, (at, squares), shapes, operands, moved, aliases)
 
 
-def step_blocks(places, factor, values, v, rest):
-    columns, count, blocks = v.shape[1], len(values), len(places)
-    tile = TILE * LINE if rest % (TILE * LINE) == 0 else TILE
-    size = rest // tile
+def step_blocks(places, factor, values, v):
+    _, rest, columns = v.shape
+    count, blocks, parts = len(values), len(places), 4
+    width = columns // parts
 
     def kernel(places, factor, *refs):
         values, v, outs = refs[:count], refs[count], refs[count + 1 :]
-        i = pl.program_id(0)
         total = step_of(factor, values, v[...])
         for k, out in enumerate(outs):
 
-            @pl.when(i // size == k)
+            @pl.when(pl.program_id(0) == k)
             def _(out=out):
                 out[...] = total
 
-    at = pl.BlockSpec((tile, columns), lambda i, places: (places[i // size] * size + i % size, 0))
+    at = pl.BlockSpec((None, rest, width), lambda b, i, places: (places[b], 0, i))
     outs = [
-        pl.BlockSpec((tile, columns), lambda i, _, k=k: (jnp.clip(i - k * size, 0, size - 1), 0))
+        pl.BlockSpec(
+            (rest, width), lambda b, i, _, k=k: (0, jnp.clip((b - k) * parts + i, 0, parts - 1))
+        )
         for k in range(blocks)
     ]
     shapes = [jax.ShapeDtypeStruct((rest, columns), v.dtype)] * blocks
     moved = (count + 2) * blocks * rest * columns
     operands = (jnp.stack(places).astype(jnp.int32), factor, *values, v)
     in_specs = [SMEM] + [at] * (count + 1)
-    return run(kernel, (blocks * size,), in_specs, outs, shapes, operands, moved, prefetch=1)
+    return run(kernel, (blocks, parts), in_specs, outs, shapes, operands, moved, prefetch=1)
+
+
+def move_spread(share, factor, values, v):
+    (rows, columns), count = v.shape, values.shape[0]
+
+    def kernel(factor, v, values, v_out, sq_out):
+        base = v[...]
+        moved = base + sum(factor[k] * (values[k] - base) for k in range(count)) * share
+        v_out[...] = moved
+
+        @pl.when(pl.program_id(0) == 0)
+        def _():
+            sq_out[...] = jnp.zeros_like(sq_out)
+
+        for k in range(count):
+            square = jnp.square(values[k] - moved)
+            sq_out[k] += sum(square[:, j : j + 128] for j in range(0, columns, 128))
+
+    at = pl.BlockSpec((TILE, columns), lambda i: (i, 0))
+    stack = pl.BlockSpec((count, TILE, columns), lambda i: (0, i, 0))
+    squares = pl.BlockSpec((count, TILE, 128), lambda i: (0, 0, 0))
+    shapes = (
+        jax.ShapeDtypeStruct(v.shape, v.dtype),
+        jax.ShapeDtypeStruct((count, TILE, 128), v.dtype),
+    )
+    moved = (count + 2) * rows * columns
+    operands = (factor, v, values)
+    return run(kernel, (rows // TILE,), [SMEM, at, stack], (at, squares), shapes, operands, moved)
 
 
 def spread_only(mine, center, radius_total, worker_count):
@@ -216,20 +246,15 @@
             swap = [(i, i ^ step) for i in range(workers)]
             sent = send(sent, swap, "worker")
         held.append(sent)
-    edges = [(0, AHEAD), (AHEAD, cut)]
-    spread = []
-    for low, high in edges:
-        spread.append(
-            lax.all_to_all(
-                mine[:, low:high], ("worker", "outer"), split_axis=0, concat_axis=0, tiled=True
-            )
-        )
+    spread = lax.all_to_all(
+        mine[:, :cut], ("worker", "outer"), split_axis=0, concat_axis=0, tiled=True
+    )
     first = (o % 2) == 0
     near = jnp.where(first, jnp.stack([tail, pair]), jnp.stack([pair, tail]))
     crossed = send(near, ACROSS)
     far = jnp.where(is_end, send(crossed, TO_ENDS), crossed)
     line_v = jnp.where(is_low, jnp.concatenate([near, far]), jnp.concatenate([far, near]))
-    spread_v = [center[low:high] for low, high in edges]
+    spread_v, share = center[:cut], 1 / worker_count
 
     places = jnp.stack([(w ^ step) * outers + o for step in steps])
     hit = places[:, None] == jnp.arange(worker_count)[None]
@@ -241,42 +266,31 @@
         norm_sq = sum_over_devices(both)
         factor = jnp.minimum(1.0, radius_total * lax.rsqrt(norm_sq + epsilon))
         return factor, jnp.sum(jnp.where(hit, factor[None], 0.0), axis=1)
-
-    def spread_norms(values):
-        return [
-            jnp.sum(jnp.square(part - v[None]), axis=(1, 2)) for part, v in zip(spread, values)
-        ]
-
-    def spread_update(values, factor):
-        weight = factor[:, None, None]
-        return [
-            v + jnp.sum(weight * (part - v[None]), axis=0) / worker_count
-            for part, v in zip(spread, values)
-        ]
 
     line_sq, v = jnp.zeros((worker_count,), jnp.float32), line_v
     for place in reversed(range(workers)):
         square = jnp.sum(jnp.square(held[place] - v))
         line_sq = lax.optimization_barrier(line_sq + jnp.where(hit[place], square, 0.0))
         v = tie(v, line_sq)
-    ahead, last = spread_norms(spread_v)
-    factor, line_factor = factors(last + lax.optimization_barrier(line_sq + ahead))
+    spread_sq = jnp.sum(jnp.square(spread - spread_v[None]), axis=(1, 2))
+    factor, line_factor = factors(spread_sq + line_sq)
 
     flat = [value.reshape(outers * rest, columns) for value in held]
     flat_v = line_v.reshape(outers * rest, columns)
     end_flag = is_end.astype(jnp.int32).reshape(1)
-    next_spread_v = spread_update(spread_v, factor)
-    spread_sq = sum(spread_norms(next_spread_v))
-    early = {1: next_spread_v, 2: spread_sq}
+    next_spread_v, spread_sq = move_spread(share, factor, spread, spread_v)
+    early = {2: next_spread_v}
     count, places = len(sizes), begins(sizes)
-    own = step_chunks(line_factor, flat, flat_v, 0, sizes[:2])
-    own += step_chunks(line_factor, flat, tie(flat_v, own[0]), places[2], sizes[2:])
-    groups = [slice(0, count - 5), slice(count - 5, count - 2), slice(count - 2, count)]
+    own = step_chunks(line_factor, flat, flat_v, 0, sizes[:1])
+    own += step_chunks(line_factor, flat, tie(flat_v, own[0]), places[1], sizes[1:2])
+    own += step_chunks(line_factor, flat, tie(flat_v, own[1]), places[2], sizes[2:])
+    cuts = [0, count - 6, count - 4, count - 2, count]
+    groups = [slice(*pair) for pair in zip(cuts, cuts[1:])]
     totals, backs, carried = [], [], ()
 
     def move(part, carried):
         return move_chunks(
-            end_flag, 1 / worker_count, totals[part], backs[part], flat, flat_v,
+            end_flag, share, totals[part], backs[part], flat, flat_v,
             places[part.start], sizes[part], carried,
         )
 
@@ -288,28 +302,30 @@
         total = total + send(total, ACROSS)
         if chunk in early:
             total = tie(total, early[chunk])
-        if chunk == count - 2:
-            carried = move(groups[0], carried)
+        if chunk in (count - 4, count - 1):
+            carried = move(groups[chunk == count - 1], carried)
             total = tie(total, carried[1])
         totals.append(total)
         backs.append(send(total, TO_ENDS))
-    for part in groups[1:]:
+    for part in groups[2:]:
         carried = move(part, carried)
     spread_v = next_spread_v
     flat_v = carried[0]
     line_v = flat_v.reshape(line_v.shape)
+    spread_sq = lax.optimization_barrier(jnp.sum(spread_sq, axis=(1, 2)))
     factor, line_factor = factors(spread_sq + placed(jnp.sum(carried[1], axis=(1, 2))))
 
     order = [jnp.where(is_low, LINE - 1 - place, place) for place in range(LINE)]
-    block = step_blocks(order[:1], line_factor, flat, flat_v, rest)
-    block += step_blocks(order[1:], line_factor, flat, tie(flat_v, block[0]), rest)
+    block = step_blocks(order[:1], line_factor, held, line_v)
+    block += step_blocks(order[1:], line_factor, held, tie(line_v, block[0]))
     arrived = [send(block[place], TO_MIDS) for place in range(3)]
     passed = [send(block[place] + arrived[place], ACROSS) for place in range(2)]
     end_sum = block[3] + send(block[3] + passed[0], TO_ENDS)
     mid_sum = block[2] + arrived[2] + passed[1]
     own_v = lax.dynamic_index_in_dim(line_v, o, 0, keepdims=False)
-    own_v = own_v + jnp.where(is_end, end_sum, mid_sum) / worker_count
-    return jnp.concatenate([*spread_update(spread_v, factor), own_v])
+    own_v = own_v + jnp.where(is_end, end_sum, mid_sum) * share
+    step = jnp.sum(factor[:, None, None] * (spread - spread_v[None]), axis=0)
+    return jnp.concatenate([spread_v + step * share, own_v])
 
 
 def solution(mesh):

time: 781 us -> 797 us (1.020)
  Pallas kernels: 52 us -> 66.8 us
  other arithmetic: 69.8 us -> 58.9 us
  starting transfers between devices: 101 us -> 110 us
    ppermute x36 -> x42, waiting for transfers between devices: 457 us -> 500 us  [send(): return lax.ppermute(value, axis, pairs)]
    all_to_all x2 -> x1, waiting for transfers between devices: 39.8 us -> 0.01 us  [on_device(): lax.all_to_all(mine[:, :cut], ('worker', 'outer'), split_axis=0, concat_a...]
    pallas_call x7 -> x10, Pallas kernels: 52 us -> 66.8 us  [run(): pl.pallas_call(kernel, grid_spec=pltpu.PrefetchScalarGridSpec(num_scalar_...]
    ppermute x36 -> x42, starting transfers between devices: 82.1 us -> 96.1 us  [send(): return lax.ppermute(value, axis, pairs)]
    reduce_sum x8 -> x3, other arithmetic: 22.7 us -> 11.8 us  [the longest x1 6 us: on_device(): step = jnp.sum(factor[:, None, None] * (spread - spread_v[None]), axis=0)]
  transfers between devices with their start and end apart: 48 -> 53, of which waited for: 24 -> 22; matrix products, arithmetic and copies ran while one was open for 11% -> 8% of each run, Pallas kernels for 5% -> 7%
where the time goes in v5:
time: 797 us; the launch traced here: 794 us
  waiting for transfers between devices  526 us (66%)
  starting transfers between devices  110 us (14%)
  Pallas kernels  66.8 us (8%)
  other arithmetic  58.9 us (7%)
  local copies, waits for them, and re-layouts  30.2 us (4%)
    ppermute x42, waiting for transfers between devices, send(): return lax.ppermute(value, axis, pairs)  500 us
    ppermute x42, starting transfers between devices, send(): return lax.ppermute(value, axis, pairs)  96.1 us
    pallas_call x10, Pallas kernels, run(): pl.pallas_call(kernel, grid_spec=pltpu.PrefetchScalarGridSpec(num_scalar_...  66.8 us
    ppermute x10, waiting for transfers between devices, sum_over_devices(): lax.ppermute(value, axis, [(i, i ^ step) for i in range(size)])  25.7 us
    reduce_sum x4, other arithmetic, on_device(): square = jnp.sum(jnp.square(held[place] - v))  19 us
  transfers between devices with their start and end apart: 53, of which 22 were waited for; matrix products, arithmetic and copies ran while one was open for 8% of the time, Pallas kernels for 7%

profile of v5, /device:TPU:0, one launch (start us, length us, event | category | flops | bytes accessed | tf_op | source)
XLA Modules:
  0.0 793.5 jit_solution(2043894035162406568)
XLA Ops:
  0.0 10.4 %slice.28 = f32[16,88,2048]{2,1,0:T(8,128)} slice(f32[16,224,2048]{2,1,0:T(8,128)} %bitcast.53), slice={[0:16], [0:88], [0:2048]} | slice | bytes 23068672 | tf_op jit(solution)/shard_map/slice | solution.py:250
  10.4 7.6 all-to-all-start
  19.3 1.9 collective-permute-start
  21.2 207.4 %collective-permute-done = f32[136,2048]{1,0:T(8,128)S(1)} collective-permute-done((f32[136,2048]{1,0:T(8,128)}, f32[136,2048]{1,0:T(8,128)S(1)}, u32[]{:S(2)}, u32[]{:S(2)}) %collective-permute-start) | collective-permute-done | bytes 1114144 | tf_op jit(solution)/shard_map/ppermute | solution.py:35
  229.6 1.9 maximum_select_fusion.1
  231.4 2.0 collective-permute-start.1
  233.4 4.8 constant_dynamic-slice_fusion.3
  238.3 4.9 constant_dynamic-slice_fusion.2
  243.2 4.9 constant_dynamic-slice_fusion.1
  248.1 1.7 collective-permute-start.4
  252.9 114.4 %collective-permute-done.2 = f32[2,136,2048]{2,1,0:T(8,128)} collective-permute-done((f32[2,136,2048]{2,1,0:T(8,128)}, f32[2,136,2048]{2,1,0:T(8,128)}, u32[]{:S(2)}, u32[]{:S(2)}) %collective-permute-start.2) | collective-permute-done | bytes 2228256 | tf_op jit(solution)/shard_map/ppermute | solution.py:35
  367.3 2.0 broadcast_select_fusion
  369.3 6.0 multiply_reduce_fusion.5
  376.0 4.9 multiply_reduce_fusion.4
  381.6 4.0 multiply_reduce_fusion.3
  386.3 63.8 %collective-permute-done.5.refs_0_ = f32[4,136,2048]{2,1,0:T(8,128)} collective-permute-done((f32[4,136,2048]{2,1,0:T(8,128)}, f32[4,136,2048]{2,1,0:T(8,128)}, u32[]{:S(2)}, u32[]{:S(2)}) %collective-permute-start.5) | collective-permute-done | bytes 4456480 | tf_op jit(solution)/shard_map/ppermute | solution.py:35
  450.1 4.0 multiply_reduce_fusion.2
  454.8 5.6 multiply_reduce_fusion.1
  461.6 1.6 collective-permute-start.7
  463.2 1.9 collective-permute-done.7
  465.2 3.6 collective-permute-done.8
  469.4 3.8 collective-permute-done.9
  473.2 1.5 collective-permute-start.10
  474.7 2.0 collective-permute-done.10
  477.5 2.1 shard_map.38
  479.6 2.6 shard_map.39
  482.2 2.1 collective-permute-start.20
  484.3 13.9 %shard_map.40 = (f32[96,2048]{1,0:T(8,128)}, f32[96,2048]{1,0:T(8,128)}, f32[32,2048]{1,0:T(8,128)}, f32[64,2048]{1,0:T(8,128)}, f32[64,2048]{1,0:T(8,128)}, /*i...) custom-call(f32[4]{0:T(128)} %select_reduce_fusion.2.factor, f32[544,2048]{1,0:T(8,128)} %bitcast.14.refs_0_, ...), custom_call_target="tpu_custom_call" | custom-call | flops 22020096 | bytes 22020096 | tf_op jit(solution)/shard_map/pallas_call | solution.py:62
  498.2 1.5 collective-permute-start.14
  503.2 32.0 %collective-permute-done.15 = f32[32,2048]{1,0:T(8,128)S(1)} collective-permute-done((f32[32,2048]{1,0:T(8,128)S(1)}, f32[32,2048]{1,0:T(8,128)S(1)}, u32[]{:S(2)}, u32[]{:S(2)}) %collective-permute-start.15) | collective-permute-done | bytes 262176 | tf_op jit(solution)/shard_map/ppermute | solution.py:35
  536.2 1.7 collective-permute-start.17
  538.0 1.6 collective-permute-start.23
  539.6 17.0 %collective-permute-start.31 = (f32[64,2048]{1,0:T(8,128)}, f32[64,2048]{1,0:T(8,128)}, u32[]{:S(2)}, u32[]{:S(2)}) collective-permute-start(f32[64,2048]{1,0:T(8,128)} %get-tuple-element.71), channel_id=1, source_target_pairs={{0,2},{6,4},{1,3},{7,5},{8,10},{14,12},{9,11},{15,13},{16,18},{22,... | collective-permute-start | bytes 1572872 | tf_op jit(solution)/shard_map/ppermute | solution.py:35
  556.7 2.0 collective-permute-start.13
  558.7 2.1 collective-permute-start.12
  560.7 9.9 %shard_map.37 = (f32[88,2048]{1,0:T(8,128)}, f32[16,8,128]{2,1,0:T(8,128)}) custom-call(f32[16]{0:T(128)} %copy-done.35, f32[88,2048]{1,0:T(8,128)} %copy-done.1, f32[16,88,2048]{2,1,0:T(8,128)} %all-to-all-done.values), custom_call_target="tpu_custom_call" | custom-call | flops 12976128 | bytes 12976128 | tf_op jit(solution)/shard_map/pallas_call | solution.py:62
  572.0 1.5 add.197.refs_7_
  573.5 1.5 add.200
  577.5 14.7 %collective-permute-start.29 = (f32[32,2048]{1,0:T(8,128)S(1)}, f32[32,2048]{1,0:T(8,128)}, u32[]{:S(2)}, u32[]{:S(2)}) collective-permute-start(f32[32,2048]{1,0:T(8,128)S(1)} %copy-done.31), channel_id=1, source_target_pairs={{0,2},{6,4},{1,3},{7,5},{8,10},{14,12},{9,11},{15,13},{16,18},{22,... | collective-permute-start | bytes 786440 | tf_op jit(solution)/shard_map/ppermute | solution.py:35
  601.5 36.8 %collective-permute-done.24.refs_8_ = f32[32,2048]{1,0:T(8,128)S(1)} collective-permute-done((f32[32,2048]{1,0:T(8,128)S(1)}, f32[32,2048]{1,0:T(8,128)S(1)}, u32[]{:S(2)}, u32[]{:S(2)}) %collective-permute-start.24) | collective-permute-done | bytes 262176 | tf_op jit(solution)/shard_map/ppermute | solution.py:35
  640.4 10.2 %collective-permute-start.11 = (f32[32,2048]{1,0:T(8,128)}, f32[32,2048]{1,0:T(8,128)}, u32[]{:S(2)}, u32[]{:S(2)}) collective-permute-start(f32[32,2048]{1,0:T(8,128)} %get-tuple-element.56), channel_id=1, source_target_pairs={{0,2},{6,4},{1,3},{7,5},{8,10},{14,12},{9,11},{15,13},{16,18},{22,... | collective-permute-start | bytes 786440 | tf_op jit(solution)/shard_map/ppermute | solution.py:35
  656.3 9.6 %shard_map.41 = (f32[544,2048]{1,0:T(8,128)}, f32[4,8,128]{2,1,0:T(8,128)}) custom-call(s32[1]{0:T(128)} %bitcast.12.is_end, f32[544,2048]{1,0:T(8,128)} %bitcast.39, f32[544,2048]{1,0:T(8,128)} %bitcast.14.refs_0_, f32[544,2048]{1,0:T(8,128)} %bitcast.15.refs_1_, f32[544,2048]{1,0:T(8,128)} %bitcast.16.refs_2_, f32[544,2048]{1,0:T(8,128)} %bitcast.46, ...), custom_call_target="tpu_custom_call" | custom-call | flops 18874368 | bytes 18874368 | tf_op jit(solution)/shard_map/pallas_call | solution.py:62
  670.4 4.3 shard_map.42
  677.6 4.9 collective-permute-done.40.refs_7_
  683.3 4.2 shard_map.43
  688.3 2.8 collective-permute-done.38.refs_7_
  691.8 2.8 shard_map.44
  696.7 1.6 collective-permute-start.42
  698.4 1.9 collective-permute-done.42
  700.3 3.6 collective-permute-done.43
  703.9 4.5 collective-permute-done.44
  708.3 1.5 collective-permute-start.45
  709.9 2.0 collective-permute-done.45
  712.6 4.4 shard_map.45
  717.0 2.0 collective-permute-start.46
  719.7 12.9 %shard_map.46 = (f32[136,2048]{1,0:T(8,128)}, f32[136,2048]{1,0:T(8,128)}, f32[136,2048]{1,0:T(8,128)}) custom-call(s32[3]{0:T(128)} %pad_add_fusion.1.places, f32[4]{0:T(128)} %select_reduce_fusion.factor, f32[4,136,2048]{2,1,0:T(8,128)} %collective-permute-done.5.refs_0_, f32[4,136,2048]{2,1,0:T(8,128)} %collective-permute-done.4.refs_1_, ...), custom_call_target="tpu_custom_call" | custom-call | flops 20054016 | bytes 20054016 | tf_op jit(solution)/shard_map/pallas_call | solution.py:62
  732.5 2.4 collective-permute-start.50
  734.9 9.2 %collective-permute-done.46 = f32[136,2048]{1,0:T(8,128)S(1)} collective-permute-done((f32[136,2048]{1,0:T(8,128)}, f32[136,2048]{1,0:T(8,128)S(1)}, u32[]{:S(2)}, u32[]{:S(2)}) %collective-permute-start.46) | collective-permute-done | bytes 1114144 | tf_op jit(solution)/shard_map/ppermute | solution.py:35
  746.1 6.1 collective-permute-start.49
  752.2 15.8 %collective-permute-done.50 = f32[136,2048]{1,0:T(8,128)} collective-permute-done((f32[136,2048]{1,0:T(8,128)}, f32[136,2048]{1,0:T(8,128)}, u32[]{:S(2)}, u32[]{:S(2)}) %collective-permute-start.50) | collective-permute-done | bytes 1114144 | tf_op jit(solution)/shard_map/ppermute | solution.py:35
  771.8 6.0 multiply_reduce_fusion
  777.9 8.9 %collective-permute-done.49 = f32[136,2048]{1,0:T(8,128)S(1)} collective-permute-done((f32[136,2048]{1,0:T(8,128)}, f32[136,2048]{1,0:T(8,128)S(1)}, u32[]{:S(2)}, u32[]{:S(2)}) %collective-permute-start.49) | collective-permute-done | bytes 1114144 | tf_op jit(solution)/shard_map/ppermute | solution.py:35
  786.8 3.5 collective-permute-done.48
  790.3 1.9 bitcast_add_fusion
  (188 shorter events, 54.9 us)
Async XLA Ops:
  10.4 444.3 %all-to-all-start = ((f32[16,88,2048]{2,1,0:T(8,128)}), f32[16,88,2048]{2,1,0:T(8,128)}, u32[]{:S(2)}, u32[]{:S(2)}) async-start(f32[16,88,2048]{2,1,0:T(8,128)} %slice.28), calls=%async_computation | async-start | bytes 23068672 | tf_op jit(solution)/shard_map/all_to_all | solution.py:249
  19.3 209.3 %collective-permute-start = (f32[136,2048]{1,0:T(8,128)}, f32[136,2048]{1,0:T(8,128)S(1)}, u32[]{:S(2)}, u32[]{:S(2)}) collective-permute-start(f32[136,2048]{1,0:T(8,128)} %get-tuple-element.91), channel_id=1, source_target_pairs={{0,2},{2,0},{4,6},{6,4},{1,3},{3,1},{5,7},{7,5},{8,10},{10,8},{12,... | collective-permute-start | bytes 3342344 | tf_op jit(solution)/shard_map/ppermute | solution.py:35
  231.4 18.4 %collective-permute-start.1 = (f32[2,136,2048]{2,1,0:T(8,128)S(1)}, f32[2,136,2048]{2,1,0:T(8,128)}, u32[]{:S(2)}, u32[]{:S(2)}) collective-permute-start(f32[2,136,2048]{2,1,0:T(8,128)S(1)} %maximum_select_fusion.1), channel_id=1, source_target_pairs={{2,4},{4,2},{3,5},{5,3},{10,12},{12,10},{11,13},{13,11},{18,20},{2... | collective-permute-start | bytes 6684680 | tf_op jit(solution)/shard_map/ppermute | solution.py:35
  248.0 128.0 %collective-permute-start.3 = (f32[4,136,2048]{2,1,0:T(8,128)}, f32[4,136,2048]{2,1,0:T(8,128)}, u32[]{:S(2)}, u32[]{:S(2)}) collective-permute-start(f32[4,136,2048]{2,1,0:T(8,128)} %constant_dynamic-slice_fusion.1), channel_id=1, source_target_pairs={{0,8},{8,0},{16,24},{24,16},{1,9},{9,1},{17,25},{25,17},{2,10},{10... | collective-permute-start | bytes 13369352 | tf_op jit(solution)/shard_map/ppermute | solution.py:35
  248.1 133.6 %collective-permute-start.4 = (f32[4,136,2048]{2,1,0:T(8,128)}, f32[4,136,2048]{2,1,0:T(8,128)}, u32[]{:S(2)}, u32[]{:S(2)}) collective-permute-start(f32[4,136,2048]{2,1,0:T(8,128)} %constant_dynamic-slice_fusion.2), channel_id=1, source_target_pairs={{0,24},{8,16},{16,8},{24,0},{1,25},{9,17},{17,9},{25,1},{2,26},{10... | collective-permute-start | bytes 13369352 | tf_op jit(solution)/shard_map/ppermute | solution.py:35
  249.8 117.5 %collective-permute-start.2 = (f32[2,136,2048]{2,1,0:T(8,128)}, f32[2,136,2048]{2,1,0:T(8,128)}, u32[]{:S(2)}, u32[]{:S(2)}) collective-permute-start(f32[2,136,2048]{2,1,0:T(8,128)} %collective-permute-done.1), channel_id=1, source_target_pairs={{2,0},{4,6},{3,1},{5,7},{10,8},{12,14},{11,9},{13,15},{18,16},{20,... | collective-permute-start | bytes 6684680 | tf_op jit(solution)/shard_map/ppermute | solution.py:35
  251.1 199.0 %collective-permute-start.5 = (f32[4,136,2048]{2,1,0:T(8,128)}, f32[4,136,2048]{2,1,0:T(8,128)}, u32[]{:S(2)}, u32[]{:S(2)}) collective-permute-start(f32[4,136,2048]{2,1,0:T(8,128)} %constant_dynamic-slice_fusion.3), channel_id=1, source_target_pairs={{0,16},{8,24},{16,0},{24,8},{1,17},{9,25},{17,1},{25,9},{2,18},{10... | collective-permute-start | bytes 13369352 | tf_op jit(solution)/shard_map/ppermute | solution.py:35
  252.7 202.1 %copy-start.1 = (f32[88,2048]{1,0:T(8,128)}, f32[88,2048]{1,0:T(8,128)S(1)}, u32[]{:S(2)}) copy-start(f32[88,2048]{1,0:T(8,128)S(1)} %slice.22.v) | copy-start | bytes 2162692
  375.4 74.7 %copy-start = (f32[4,136,2048]{2,1,0:T(8,128)}, f32[4,136,2048]{2,1,0:T(8,128)S(1)}, u32[]{:S(2)}) copy-start(f32[4,136,2048]{2,1,0:T(8,128)S(1)} %get-tuple-element.51) | copy-start | bytes 13369348
  460.4 1.2 collective-permute-start.6
  461.6 3.6 collective-permute-start.7
  465.2 3.6 collective-permute-start.8
  468.7 4.5 collective-permute-start.9
  473.2 3.6 collective-permute-start.10
  482.2 20.2 %collective-permute-start.20 = (f32[64,2048]{1,0:T(8,128)}, f32[64,2048]{1,0:T(8,128)S(1)}, u32[]{:S(2)}, u32[]{:S(2)}) collective-permute-start(f32[64,2048]{1,0:T(8,128)} %shard_map.39), channel_id=1, source_target_pairs={{0,2},{6,4},{1,3},{7,5},{8,10},{14,12},{9,11},{15,13},{16,18},{22,... | collective-permute-start | bytes 1572872 | tf_op jit(solution)/shard_map/ppermute | solution.py:35
  498.2 37.9 %copy-start.23 = (f32[96,2048]{1,0:T(8,128)S(1)}, f32[96,2048]{1,0:T(8,128)}, u32[]{:S(2)}) copy-start(f32[96,2048]{1,0:T(8,128)} %get-tuple-element.59) | copy-start | bytes 2359300
  498.2 37.8 %collective-permute-start.14 = (f32[96,2048]{1,0:T(8,128)}, f32[96,2048]{1,0:T(8,128)S(1)}, u32[]{:S(2)}, u32[]{:S(2)}) collective-permute-start(f32[96,2048]{1,0:T(8,128)} %get-tuple-element.59), channel_id=1, source_target_pairs={{0,2},{6,4},{1,3},{7,5},{8,10},{14,12},{9,11},{15,13},{16,18},{22,... | collective-permute-start | bytes 2359304 | tf_op jit(solution)/shard_map/ppermute | solution.py:35
  499.7 38.2 %collective-permute-start.22 = (f32[96,2048]{1,0:T(8,128)}, f32[96,2048]{1,0:T(8,128)S(1)}, u32[]{:S(2)}, u32[]{:S(2)}) collective-permute-start(f32[96,2048]{1,0:T(8,128)} %get-tuple-element.64), channel_id=1, source_target_pairs={{0,2},{6,4},{1,3},{7,5},{8,10},{14,12},{9,11},{15,13},{16,18},{22,... | collective-permute-start | bytes 2359304 | tf_op jit(solution)/shard_map/ppermute | solution.py:35
  501.1 34.1 %collective-permute-start.15 = (f32[32,2048]{1,0:T(8,128)S(1)}, f32[32,2048]{1,0:T(8,128)S(1)}, u32[]{:S(2)}, u32[]{:S(2)}) collective-permute-start(f32[32,2048]{1,0:T(8,128)S(1)} %copy-done.20), channel_id=1, source_target_pairs={{0,2},{6,4},{1,3},{7,5},{8,10},{14,12},{9,11},{15,13},{16,18},{22,... | collective-permute-start | bytes 786440 | tf_op jit(solution)/shard_map/ppermute | solution.py:35
  502.5 35.4 %collective-permute-start.21 = (f32[64,2048]{1,0:T(8,128)S(1)}, f32[64,2048]{1,0:T(8,128)S(1)}, u32[]{:S(2)}, u32[]{:S(2)}) collective-permute-start(f32[64,2048]{1,0:T(8,128)S(1)} %add.194), channel_id=1, source_target_pairs={{2,4},{4,2},{3,5},{5,3},{10,12},{12,10},{11,13},{13,11},{18,20},{2... | collective-permute-start | bytes 1572872 | tf_op jit(solution)/shard_map/ppermute | solution.py:35
  535.2 0.8 collective-permute-start.16
  536.0 62.7 %copy-start.16 = (f32[32,2048]{1,0:T(8,128)}, f32[32,2048]{1,0:T(8,128)S(1)}, u32[]{:S(2)}) copy-start(f32[32,2048]{1,0:T(8,128)S(1)} %add.187.refs_4_) | copy-start | bytes 786436
  536.2 34.5 %collective-permute-start.17 = (f32[96,2048]{1,0:T(8,128)S(1)}, f32[96,2048]{1,0:T(8,128)}, u32[]{:S(2)}, u32[]{:S(2)}) collective-permute-start(f32[96,2048]{1,0:T(8,128)S(1)} %add.188), channel_id=1, source_target_pairs={{2,4},{4,2},{3,5},{5,3},{10,12},{12,10},{11,13},{13,11},{18,20},{2... | collective-permute-start | bytes 2359304 | tf_op jit(solution)/shard_map/ppermute | solution.py:35
  537.9 62.1 %copy-start.9 = (f32[64,2048]{1,0:T(8,128)}, f32[64,2048]{1,0:T(8,128)S(1)}, u32[]{:S(2)}) copy-start(f32[64,2048]{1,0:T(8,128)S(1)} %add.195.refs_5_) | copy-start | bytes 1572868
  538.0 33.9 %collective-permute-start.23 = (f32[96,2048]{1,0:T(8,128)S(1)}, f32[96,2048]{1,0:T(8,128)}, u32[]{:S(2)}, u32[]{:S(2)}) collective-permute-start(f32[96,2048]{1,0:T(8,128)S(1)} %add.196), channel_id=1, source_target_pairs={{2,4},{4,2},{3,5},{5,3},{10,12},{12,10},{11,13},{13,11},{18,20},{2... | collective-permute-start | bytes 2359304 | tf_op jit(solution)/shard_map/ppermute | solution.py:35
  539.6 33.9 %collective-permute-start.31 = (f32[64,2048]{1,0:T(8,128)}, f32[64,2048]{1,0:T(8,128)}, u32[]{:S(2)}, u32[]{:S(2)}) collective-permute-start(f32[64,2048]{1,0:T(8,128)} %get-tuple-element.71), channel_id=1, source_target_pairs={{0,2},{6,4},{1,3},{7,5},{8,10},{14,12},{9,11},{15,13},{16,18},{22,... | collective-permute-start | bytes 1572872 | tf_op jit(solution)/shard_map/ppermute | solution.py:35
  556.7 15.3 %collective-permute-start.13 = (f32[32,2048]{1,0:T(8,128)}, f32[32,2048]{1,0:T(8,128)}, u32[]{:S(2)}, u32[]{:S(2)}) collective-permute-start(f32[32,2048]{1,0:T(8,128)} %get-tuple-element.58), channel_id=1, source_target_pairs={{0,2},{6,4},{1,3},{7,5},{8,10},{14,12},{9,11},{15,13},{16,18},{22,... | collective-permute-start | bytes 786440 | tf_op jit(solution)/shard_map/ppermute | solution.py:35
  558.7 34.9 %collective-permute-start.12 = (f32[64,2048]{1,0:T(8,128)S(1)}, f32[64,2048]{1,0:T(8,128)}, u32[]{:S(2)}, u32[]{:S(2)}) collective-permute-start(f32[64,2048]{1,0:T(8,128)S(1)} %copy-done.25), channel_id=1, source_target_pairs={{0,2},{6,4},{1,3},{7,5},{8,10},{14,12},{9,11},{15,13},{16,18},{22,... | collective-permute-start | bytes 1572872 | tf_op jit(solution)/shard_map/ppermute | solution.py:35
  575.1 25.0 %collective-permute-start.32 = (f32[64,2048]{1,0:T(8,128)S(1)}, f32[64,2048]{1,0:T(8,128)S(1)}, u32[]{:S(2)}, u32[]{:S(2)}) collective-permute-start(f32[64,2048]{1,0:T(8,128)S(1)} %add.200), channel_id=1, source_target_pairs={{2,4},{4,2},{3,5},{5,3},{10,12},{12,10},{11,13},{13,11},{18,20},{2... | collective-permute-start | bytes 1572872 | tf_op jit(solution)/shard_map/ppermute | solution.py:35
  576.8 18.0 %collective-permute-start.18 = (f32[32,2048]{1,0:T(8,128)S(1)}, f32[32,2048]{1,0:T(8,128)S(1)}, u32[]{:S(2)}, u32[]{:S(2)}) collective-permute-start(f32[32,2048]{1,0:T(8,128)S(1)} %add.190), channel_id=1, source_target_pairs={{2,4},{4,2},{3,5},{5,3},{10,12},{12,10},{11,13},{13,11},{18,20},{2... | collective-permute-start | bytes 786440 | tf_op jit(solution)/shard_map/ppermute | solution.py:35
  577.5 20.5 %collective-permute-start.29 = (f32[32,2048]{1,0:T(8,128)S(1)}, f32[32,2048]{1,0:T(8,128)}, u32[]{:S(2)}, u32[]{:S(2)}) collective-permute-start(f32[32,2048]{1,0:T(8,128)S(1)} %copy-done.31), channel_id=1, source_target_pairs={{0,2},{6,4},{1,3},{7,5},{8,10},{14,12},{9,11},{15,13},{16,18},{22,... | collective-permute-start | bytes 786440 | tf_op jit(solution)/shard_map/ppermute | solution.py:35
  592.2 6.5 collective-permute-start.30
  593.5 62.0 %collective-permute-start.26 = (f32[96,2048]{1,0:T(8,128)S(1)}, f32[96,2048]{1,0:T(8,128)}, u32[]{:S(2)}, u32[]{:S(2)}) collective-permute-start(f32[96,2048]{1,0:T(8,128)S(1)} %add.189.refs_6_), channel_id=1, source_target_pairs={{2,0},{4,6},{3,1},{5,7},{10,8},{12,14},{11,9},{13,15},{18,16},{20,... | collective-permute-start | bytes 2359304 | tf_op jit(solution)/shard_map/ppermute | solution.py:35
  594.8 61.4 %collective-permute-start.27 = (f32[96,2048]{1,0:T(8,128)S(1)}, f32[96,2048]{1,0:T(8,128)}, u32[]{:S(2)}, u32[]{:S(2)}) collective-permute-start(f32[96,2048]{1,0:T(8,128)S(1)} %add.197.refs_7_), channel_id=1, source_target_pairs={{2,0},{4,6},{3,1},{5,7},{10,8},{12,14},{11,9},{13,15},{18,16},{20,... | collective-permute-start | bytes 2359304 | tf_op jit(solution)/shard_map/ppermute | solution.py:35
  598.0 41.0 %copy-start.10 = (f32[64,2048]{1,0:T(8,128)}, f32[64,2048]{1,0:T(8,128)S(1)}, u32[]{:S(2)}) copy-start(f32[64,2048]{1,0:T(8,128)S(1)} %add.192) | copy-start | bytes 1572868
  598.0 41.0 %collective-permute-start.19 = (f32[64,2048]{1,0:T(8,128)S(1)}, f32[64,2048]{1,0:T(8,128)S(1)}, u32[]{:S(2)}, u32[]{:S(2)}) collective-permute-start(f32[64,2048]{1,0:T(8,128)S(1)} %add.192), channel_id=1, source_target_pairs={{2,4},{4,2},{3,5},{5,3},{10,12},{12,10},{11,13},{13,11},{18,20},{2... | collective-permute-start | bytes 1572872 | tf_op jit(solution)/shard_map/ppermute | solution.py:35
  598.7 39.6 %collective-permute-start.24 = (f32[32,2048]{1,0:T(8,128)S(1)}, f32[32,2048]{1,0:T(8,128)S(1)}, u32[]{:S(2)}, u32[]{:S(2)}) collective-permute-start(f32[32,2048]{1,0:T(8,128)S(1)} %add.187.refs_4_), channel_id=1, source_target_pairs={{2,0},{4,6},{3,1},{5,7},{10,8},{12,14},{11,9},{13,15},{18,16},{20,... | collective-permute-start | bytes 786440 | tf_op jit(solution)/shard_map/ppermute | solution.py:35
  600.1 54.2 %collective-permute-start.25 = (f32[64,2048]{1,0:T(8,128)S(1)}, f32[64,2048]{1,0:T(8,128)}, u32[]{:S(2)}, u32[]{:S(2)}) collective-permute-start(f32[64,2048]{1,0:T(8,128)S(1)} %add.195.refs_5_), channel_id=1, source_target_pairs={{2,0},{4,6},{3,1},{5,7},{10,8},{12,14},{11,9},{13,15},{18,16},{20,... | collective-permute-start | bytes 1572872 | tf_op jit(solution)/shard_map/ppermute | solution.py:35
  601.5 64.4 %copy-start.8 = (f32[64,2048]{1,0:T(8,128)}, f32[64,2048]{1,0:T(8,128)S(1)}, u32[]{:S(2)}) copy-start(f32[64,2048]{1,0:T(8,128)S(1)} %add.201.refs_5_) | copy-start | bytes 1572868
  601.5 49.0 %copy-start.21 = (f32[32,2048]{1,0:T(8,128)}, f32[32,2048]{1,0:T(8,128)S(1)}, u32[]{:S(2)}) copy-start(f32[32,2048]{1,0:T(8,128)S(1)} %add.202) | copy-start | bytes 786436
  638.3 2.0 collective-permute-start.33
  639.0 31.3 %collective-permute-start.36 = (f32[64,2048]{1,0:T(8,128)S(1)}, f32[64,2048]{1,0:T(8,128)}, u32[]{:S(2)}, u32[]{:S(2)}) collective-permute-start(f32[64,2048]{1,0:T(8,128)S(1)} %add.201.refs_5_), channel_id=1, source_target_pairs={{2,0},{4,6},{3,1},{5,7},{10,8},{12,14},{11,9},{13,15},{18,16},{20,... | collective-permute-start | bytes 1572872 | tf_op jit(solution)/shard_map/ppermute | solution.py:35
  640.4 26.9 %collective-permute-start.11 = (f32[32,2048]{1,0:T(8,128)}, f32[32,2048]{1,0:T(8,128)}, u32[]{:S(2)}, u32[]{:S(2)}) collective-permute-start(f32[32,2048]{1,0:T(8,128)} %get-tuple-element.56), channel_id=1, source_target_pairs={{0,2},{6,4},{1,3},{7,5},{8,10},{14,12},{9,11},{15,13},{16,18},{22,... | collective-permute-start | bytes 786440 | tf_op jit(solution)/shard_map/ppermute | solution.py:35
  654.3 16.1 %collective-permute-start.35 = (f32[32,2048]{1,0:T(8,128)}, f32[32,2048]{1,0:T(8,128)}, u32[]{:S(2)}, u32[]{:S(2)}) collective-permute-start(f32[32,2048]{1,0:T(8,128)} %add.191.refs_4_), channel_id=1, source_target_pairs={{2,0},{4,6},{3,1},{5,7},{10,8},{12,14},{11,9},{13,15},{18,16},{20,... | collective-permute-start | bytes 786440 | tf_op jit(solution)/shard_map/ppermute | solution.py:35
  655.6 13.4 %collective-permute-start.34 = (f32[32,2048]{1,0:T(8,128)S(1)}, f32[32,2048]{1,0:T(8,128)S(1)}, u32[]{:S(2)}, u32[]{:S(2)}) collective-permute-start(f32[32,2048]{1,0:T(8,128)S(1)} %add.204), channel_id=1, source_target_pairs={{2,4},{4,2},{3,5},{5,3},{10,12},{12,10},{11,13},{13,11},{18,20},{2... | collective-permute-start | bytes 786440 | tf_op jit(solution)/shard_map/ppermute | solution.py:35
  665.9 16.6 %collective-permute-start.39 = (f32[64,2048]{1,0:T(8,128)S(1)}, f32[64,2048]{1,0:T(8,128)S(1)}, u32[]{:S(2)}, u32[]{:S(2)}) collective-permute-start(f32[64,2048]{1,0:T(8,128)S(1)} %add.193.refs_4_), channel_id=1, source_target_pairs={{2,0},{4,6},{3,1},{5,7},{10,8},{12,14},{11,9},{13,15},{18,16},{20,... | collective-permute-start | bytes 1572872 | tf_op jit(solution)/shard_map/ppermute | solution.py:35
  668.3 6.4 collective-permute-start.28
  669.0 13.5 %collective-permute-start.40 = (f32[32,2048]{1,0:T(8,128)S(1)}, f32[32,2048]{1,0:T(8,128)S(1)}, u32[]{:S(2)}, u32[]{:S(2)}) collective-permute-start(f32[32,2048]{1,0:T(8,128)S(1)} %add.203.refs_5_), channel_id=1, source_target_pairs={{2,0},{4,6},{3,1},{5,7},{10,8},{12,14},{11,9},{13,15},{18,16},{20,... | collective-permute-start | bytes 786440 | tf_op jit(solution)/shard_map/ppermute | solution.py:35
  674.8 13.5 %collective-permute-start.37 = (f32[32,2048]{1,0:T(8,128)S(1)}, f32[32,2048]{1,0:T(8,128)S(1)}, u32[]{:S(2)}, u32[]{:S(2)}) collective-permute-start(f32[32,2048]{1,0:T(8,128)S(1)} %add.199.refs_4_), channel_id=1, source_target_pairs={{2,0},{4,6},{3,1},{5,7},{10,8},{12,14},{11,9},{13,15},{18,16},{20,... | collective-permute-start | bytes 786440 | tf_op jit(solution)/shard_map/ppermute | solution.py:35
  676.1 15.0 %collective-permute-start.38 = (f32[32,2048]{1,0:T(8,128)S(1)}, f32[32,2048]{1,0:T(8,128)S(1)}, u32[]{:S(2)}, u32[]{:S(2)}) collective-permute-start(f32[32,2048]{1,0:T(8,128)S(1)} %add.205.refs_5_), channel_id=1, source_target_pairs={{2,0},{4,6},{3,1},{5,7},{10,8},{12,14},{11,9},{13,15},{18,16},{20,... | collective-permute-start | bytes 786440 | tf_op jit(solution)/shard_map/ppermute | solution.py:35
  695.5 1.2 collective-permute-start.41
  696.7 3.6 collective-permute-start.42
  700.3 3.6 collective-permute-start.43
  703.9 4.5 collective-permute-start.44
  708.3 3.6 collective-permute-start.45
  717.0 27.2 %collective-permute-start.46 = (f32[136,2048]{1,0:T(8,128)}, f32[136,2048]{1,0:T(8,128)S(1)}, u32[]{:S(2)}, u32[]{:S(2)}) collective-permute-start(f32[136,2048]{1,0:T(8,128)} %shard_map.45), channel_id=1, source_target_pairs={{0,2},{6,4},{1,3},{7,5},{8,10},{14,12},{9,11},{15,13},{16,18},{22,... | collective-permute-start | bytes 3342344 | tf_op jit(solution)/shard_map/ppermute | solution.py:35
  719.7 24.5 %copy-start.2 = (f32[136,2048]{1,0:T(8,128)S(1)}, f32[136,2048]{1,0:T(8,128)}, u32[]{:S(2)}) copy-start(f32[136,2048]{1,0:T(8,128)} %shard_map.45) | copy-start | bytes 3342340
  732.5 35.5 %copy-start.13 = (f32[136,2048]{1,0:T(8,128)S(1)}, f32[136,2048]{1,0:T(8,128)}, u32[]{:S(2)}) copy-start(f32[136,2048]{1,0:T(8,128)} %get-tuple-element.86) | copy-start | bytes 3342340
  732.5 35.5 %collective-permute-start.50 = (f32[136,2048]{1,0:T(8,128)}, f32[136,2048]{1,0:T(8,128)}, u32[]{:S(2)}, u32[]{:S(2)}) collective-permute-start(f32[136,2048]{1,0:T(8,128)} %get-tuple-element.86), channel_id=1, source_target_pairs={{0,2},{6,4},{1,3},{7,5},{8,10},{14,12},{9,11},{15,13},{16,18},{22,... | collective-permute-start | bytes 3342344 | tf_op jit(solution)/shard_map/ppermute | solution.py:35
  745.3 25.0 %copy-start.3 = (f32[136,2048]{1,0:T(8,128)S(1)}, f32[136,2048]{1,0:T(8,128)}, u32[]{:S(2)}) copy-start(f32[136,2048]{1,0:T(8,128)} %get-tuple-element.84) | copy-start | bytes 3342340
  745.3 25.0 %collective-permute-start.47 = (f32[136,2048]{1,0:T(8,128)}, f32[136,2048]{1,0:T(8,128)S(1)}, u32[]{:S(2)}, u32[]{:S(2)}) collective-permute-start(f32[136,2048]{1,0:T(8,128)} %add.215), channel_id=1, source_target_pairs={{2,4},{4,2},{3,5},{5,3},{10,12},{12,10},{11,13},{13,11},{18,20},{2... | collective-permute-start | bytes 3342344 | tf_op jit(solution)/shard_map/ppermute | solution.py:35
  746.1 40.7 %collective-permute-start.49 = (f32[136,2048]{1,0:T(8,128)}, f32[136,2048]{1,0:T(8,128)S(1)}, u32[]{:S(2)}, u32[]{:S(2)}) collective-permute-start(f32[136,2048]{1,0:T(8,128)} %get-tuple-element.85), channel_id=1, source_target_pairs={{0,2},{6,4},{1,3},{7,5},{8,10},{14,12},{9,11},{15,13},{16,18},{22,... | collective-permute-start | bytes 3342344 | tf_op jit(solution)/shard_map/ppermute | solution.py:35
  769.4 17.4 %collective-permute-start.51 = (f32[136,2048]{1,0:T(8,128)S(1)}, f32[136,2048]{1,0:T(8,128)S(1)}, u32[]{:S(2)}, u32[]{:S(2)}) collective-permute-start(f32[136,2048]{1,0:T(8,128)S(1)} %add.219), channel_id=1, source_target_pairs={{2,4},{4,2},{3,5},{5,3},{10,12},{12,10},{11,13},{13,11},{18,20},{2... | collective-permute-start | bytes 3342344 | tf_op jit(solution)/shard_map/ppermute | solution.py:35
  770.5 19.8 %collective-permute-start.48 = (f32[136,2048]{1,0:T(8,128)S(1)}, f32[136,2048]{1,0:T(8,128)S(1)}, u32[]{:S(2)}, u32[]{:S(2)}) collective-permute-start(f32[136,2048]{1,0:T(8,128)S(1)} %add.216), channel_id=1, source_target_pairs={{2,0},{4,6},{3,1},{5,7},{10,8},{12,14},{11,9},{13,15},{18,16},{20,... | collective-permute-start | bytes 3342344 | tf_op jit(solution)/shard_map/ppermute | solution.py:35
  (25 other events, 236.8 us)

commit v6 on v5

--- a/solution.py
+++ b/solution.py
@@ -14,7 +14,7 @@
 AXES = ("worker", "outer", "mp")
 LINE = 4
 TILE = 8
-SPREAD = 0.4
+SPREAD = 3 / 7
 
 GRANT = 60 << 20
 
@@ -51,7 +51,7 @@
     if outers != LINE or rest % TILE or tiles < 13 or not cut:
         return None
     body = tiles - 10
-    sizes = [1, 2] + [3] * (body // 3) + [body % 3] * (body % 3 > 0) + [2, 2, 1, 1, 1]
+    sizes = [1, 2, 2] + [3] * (body // 3) + [body % 3] * (body % 3 > 0) + [2, 2, 1]
     return cut, sizes
 
 
@@ -179,6 +179,7 @@
 
 def move_spread(share, factor, values, v):
     (rows, columns), count = v.shape, values.shape[0]
+    tile = 2 * TILE if rows % (2 * TILE) == 0 else TILE
 
     def kernel(factor, v, values, v_out, sq_out):
         base = v[...]
@@ -191,10 +192,11 @@
 
         for k in range(count):
             square = jnp.square(values[k] - moved)
-            sq_out[k] += sum(square[:, j : j + 128] for j in range(0, columns, 128))
-
-    at = pl.BlockSpec((TILE, columns), lambda i: (i, 0))
-    stack = pl.BlockSpec((count, TILE, columns), lambda i: (0, i, 0))
+            folded = sum(square[j : j + TILE] for j in range(0, tile, TILE))
+            sq_out[k] += sum(folded[:, j : j + 128] for j in range(0, columns, 128))
+
+    at = pl.BlockSpec((tile, columns), lambda i: (i, 0))
+    stack = pl.BlockSpec((count, tile, columns), lambda i: (0, i, 0))
     squares = pl.BlockSpec((count, TILE, 128), lambda i: (0, 0, 0))
     shapes = (
         jax.ShapeDtypeStruct(v.shape, v.dtype),
@@ -202,7 +204,7 @@
     )
     moved = (count + 2) * rows * columns
     operands = (factor, v, values)
-    return run(kernel, (rows // TILE,), [SMEM, at, stack], (at, squares), shapes, operands, moved)
+    return run(kernel, (rows // tile,), [SMEM, at, stack], (at, squares), shapes, operands, moved)
 
 
 def spread_only(mine, center, radius_total, worker_count):
@@ -250,10 +252,13 @@
         mine[:, :cut], ("worker", "outer"), split_axis=0, concat_axis=0, tiled=True
     )
     first = (o % 2) == 0
-    near = jnp.where(first, jnp.stack([tail, pair]), jnp.stack([pair, tail]))
-    crossed = send(near, ACROSS)
-    far = jnp.where(is_end, send(crossed, TO_ENDS), crossed)
-    line_v = jnp.where(is_low, jnp.concatenate([near, far]), jnp.concatenate([far, near]))
+    near = [jnp.where(first, tail, pair), jnp.where(first, pair, tail)]
+    far = []
+    for part in (tail, pair):
+        crossed = send(part, ACROSS)
+        far.append(jnp.where(is_end, send(crossed, TO_ENDS), crossed))
+    low, high = near + far, far[::-1] + near
+    line_v = jnp.stack([jnp.where(is_low, *parts) for parts in zip(low, high)])
     spread_v, share = center[:cut], 1 / worker_count
 
     places = jnp.stack([(w ^ step) * outers + o for step in steps])
@@ -283,8 +288,9 @@
     count, places = len(sizes), begins(sizes)
     own = step_chunks(line_factor, flat, flat_v, 0, sizes[:1])
     own += step_chunks(line_factor, flat, tie(flat_v, own[0]), places[1], sizes[1:2])
-    own += step_chunks(line_factor, flat, tie(flat_v, own[1]), places[2], sizes[2:])
-    cuts = [0, count - 6, count - 4, count - 2, count]
+    own += step_chunks(line_factor, flat, tie(flat_v, own[1]), places[2], sizes[2:4])
+    own += step_chunks(line_factor, flat, tie(flat_v, own[2]), places[4], sizes[4:])
+    cuts = [0, count - 5, count - 3, count - 1, count]
     groups = [slice(*pair) for pair in zip(cuts, cuts[1:])]
     totals, backs, carried = [], [], ()
 
@@ -302,7 +308,7 @@
         total = total + send(total, ACROSS)
         if chunk in early:
             total = tie(total, early[chunk])
-        if chunk in (count - 4, count - 1):
+        if chunk in (count - 3, count - 1):
             carried = move(groups[chunk == count - 1], carried)
             total = tie(total, carried[1])
         totals.append(total)

time: 797 us -> 675 us (0.85)
  waiting for transfers between devices: 526 us -> 435 us
  starting transfers between devices: 110 us -> 90 us
    ppermute x42 -> x38, waiting for transfers between devices: 500 us -> 411 us  [send(): return lax.ppermute(value, axis, pairs)]
    ppermute x42 -> x38, starting transfers between devices: 96.1 us -> 75.4 us  [send(): return lax.ppermute(value, axis, pairs)]
    pallas_call x10 -> x11, Pallas kernels: 66.8 us -> 63.7 us  [run(): pl.pallas_call(kernel, grid_spec=pltpu.PrefetchScalarGridSpec(num_scalar_...]
  transfers between devices with their start and end apart: 53 -> 49, of which waited for: 22 -> 26; matrix products, arithmetic and copies ran while one was open for 8% -> 9% of each run, Pallas kernels for 7% -> 8%
where the time goes in v6:
time: 675 us; the launch traced here: 673 us
  waiting for transfers between devices  435 us (64%)
  starting transfers between devices  90 us (13%)
  Pallas kernels  63.7 us (9%)
  other arithmetic  55.4 us (8%)
  local copies, waits for them, and re-layouts  26.5 us (4%)
    ppermute x38, waiting for transfers between devices, send(): return lax.ppermute(value, axis, pairs)  411 us
    ppermute x38, starting transfers between devices, send(): return lax.ppermute(value, axis, pairs)  75.4 us
    pallas_call x11, Pallas kernels, run(): pl.pallas_call(kernel, grid_spec=pltpu.PrefetchScalarGridSpec(num_scalar_...  63.7 us
    ppermute x10, waiting for transfers between devices, sum_over_devices(): lax.ppermute(value, axis, [(i, i ^ step) for i in range(size)])  24.9 us
    reduce_sum x4, other arithmetic, on_device(): square = jnp.sum(jnp.square(held[place] - v))  17.5 us
    dynamic_slice x3, local copies, waits for them, and re-layouts, line_rows(): lax.dynamic_slice(source, (worker * outers, cut, 0), (outers, rest, colum...  14.1 us
  transfers between devices with their start and end apart: 49, of which 26 were waited for; matrix products, arithmetic and copies ran while one was open for 9% of the time, Pallas kernels for 8%

profile of v6, /device:TPU:0, one launch (start us, length us, event | category | flops | bytes accessed | tf_op | source)
XLA Modules:
  0.0 672.6 jit_solution(13290151889952745040)
XLA Ops:
  0.0 11.5 %slice.28 = f32[16,96,2048]{2,1,0:T(8,128)} slice(f32[16,224,2048]{2,1,0:T(8,128)} %bitcast.60), slice={[0:16], [0:96], [0:2048]} | slice | bytes 25165824 | tf_op jit(solution)/shard_map/slice | solution.py:252
  11.5 7.6 %all-to-all-start = ((f32[16,96,2048]{2,1,0:T(8,128)}), f32[16,96,2048]{2,1,0:T(8,128)}, u32[]{:S(2)}, u32[]{:S(2)}) async-start(f32[16,96,2048]{2,1,0:T(8,128)} %slice.28), calls=%async_computation | async-start | bytes 25165824 | tf_op jit(solution)/shard_map/all_to_all | solution.py:251
  19.2 1.9 collective-permute-start
  21.1 4.6 constant_dynamic-slice_fusion.3
  25.7 4.8 constant_dynamic-slice_fusion.2
  30.5 4.7 constant_dynamic-slice_fusion.1
  35.2 1.6 collective-permute-start.6
  36.8 1.6 collective-permute-start.3
  38.4 206.6 %collective-permute-done = f32[128,2048]{1,0:T(8,128)} collective-permute-done((f32[128,2048]{1,0:T(8,128)S(1)}, f32[128,2048]{1,0:T(8,128)}, u32[]{:S(2)}, u32[]{:S(2)}) %collective-permute-start) | collective-permute-done | bytes 1048608 | tf_op jit(solution)/shard_map/ppermute | solution.py:35
  245.0 1.7 collective-permute-start.1
  246.7 1.6 collective-permute-start.7
  251.2 89.2 %collective-permute-done.4 = f32[128,2048]{1,0:T(8,128)} collective-permute-done((f32[128,2048]{1,0:T(8,128)}, f32[128,2048]{1,0:T(8,128)}, u32[]{:S(2)}, u32[]{:S(2)}) %collective-permute-start.4) | collective-permute-done | bytes 1048608 | tf_op jit(solution)/shard_map/ppermute | solution.py:35
  340.3 22.5 %collective-permute-done.2 = f32[128,2048]{1,0:T(8,128)} collective-permute-done((f32[128,2048]{1,0:T(8,128)}, f32[128,2048]{1,0:T(8,128)}, u32[]{:S(2)}, u32[]{:S(2)}) %collective-permute-start.2) | collective-permute-done | bytes 1048608 | tf_op jit(solution)/shard_map/ppermute | solution.py:35
  362.8 2.5 select_bitcast_fusion.3
  365.3 4.9 multiply_reduce_fusion.5
  370.9 4.7 multiply_reduce_fusion.4
  376.1 4.0 multiply_reduce_fusion.3
  380.8 3.9 multiply_reduce_fusion.2
  385.4 6.0 multiply_reduce_fusion.1
  394.1 2.1 collective-permute-done.9
  396.2 3.6 collective-permute-done.10
  400.8 3.4 collective-permute-done.11
  404.2 1.5 collective-permute-start.12
  405.7 2.0 collective-permute-done.12
  408.5 2.1 shard_map.38
  410.6 2.7 shard_map.39
  413.3 1.9 collective-permute-start.16
  416.6 5.8 shard_map.40
  425.0 8.3 %collective-permute-done.20 = f32[32,2048]{1,0:T(8,128)S(1)} collective-permute-done((f32[32,2048]{1,0:T(8,128)S(1)}, f32[32,2048]{1,0:T(8,128)S(1)}, u32[]{:S(2)}, u32[]{:S(2)}) %collective-permute-start.20) | collective-permute-done | bytes 262176 | tf_op jit(solution)/shard_map/ppermute | solution.py:35
  434.2 8.3 %shard_map.41 = (f32[96,2048]{1,0:T(8,128)}, f32[64,2048]{1,0:T(8,128)}, f32[64,2048]{1,0:T(8,128)}, f32[32,2048]{1,0:T(8,128)}) custom-call(f32[4]{0:T(128)} %select_reduce_fusion.2.factor, f32[512,2048]{1,0:T(8,128)} %bitcast.16.refs_0_, f32[512,2048]{1,0:T(8,128)} %bitcast.17.refs_1_, f32[512,2048]{1,0:T(8,128)} %bitcast.18.refs_2_, ...), custom_call_target="tpu_custom_call" | custom-call | flops 12582912 | bytes 12582912 | tf_op jit(solution)/shard_map/pallas_call | solution.py:62
  442.6 7.8 %collective-permute-start.28 = (f32[96,2048]{1,0:T(8,128)}, f32[96,2048]{1,0:T(8,128)}, u32[]{:S(2)}, u32[]{:S(2)}) collective-permute-start(f32[96,2048]{1,0:T(8,128)} %get-tuple-element.65), channel_id=1, source_target_pairs={{0,2},{6,4},{1,3},{7,5},{8,10},{14,12},{9,11},{15,13},{16,18},{22,... | collective-permute-start | bytes 2359304 | tf_op jit(solution)/shard_map/ppermute | solution.py:35
  452.9 8.6 %collective-permute-done.15 = f32[96,2048]{1,0:T(8,128)S(1)} collective-permute-done((f32[96,2048]{1,0:T(8,128)}, f32[96,2048]{1,0:T(8,128)S(1)}, u32[]{:S(2)}, u32[]{:S(2)}) %collective-permute-start.15) | collective-permute-done | bytes 786464 | tf_op jit(solution)/shard_map/ppermute | solution.py:35
  461.6 1.8 collective-permute-start.18
  463.4 7.9 %shard_map.37 = (f32[96,2048]{1,0:T(8,128)}, f32[16,8,128]{2,1,0:T(8,128)}) custom-call(f32[16]{0:T(128)} %copy-done.28, f32[96,2048]{1,0:T(8,128)} %copy-done.1, f32[16,96,2048]{2,1,0:T(8,128)} %all-to-all-done.values), custom_call_target="tpu_custom_call" | custom-call | flops 14155776 | bytes 14155776 | tf_op jit(solution)/shard_map/pallas_call | solution.py:62
  475.2 7.3 %collective-permute-start.14 = (f32[64,2048]{1,0:T(8,128)S(1)}, f32[64,2048]{1,0:T(8,128)S(1)}, u32[]{:S(2)}, u32[]{:S(2)}) collective-permute-start(f32[64,2048]{1,0:T(8,128)S(1)} %copy-done.19), channel_id=1, source_target_pairs={{0,2},{6,4},{1,3},{7,5},{8,10},{14,12},{9,11},{15,13},{16,18},{22,... | collective-permute-start | bytes 1572872 | tf_op jit(solution)/shard_map/ppermute | solution.py:35
  485.1 8.3 %collective-permute-done.14 = f32[64,2048]{1,0:T(8,128)S(1)} collective-permute-done((f32[64,2048]{1,0:T(8,128)S(1)}, f32[64,2048]{1,0:T(8,128)S(1)}, u32[]{:S(2)}, u32[]{:S(2)}) %collective-permute-start.14) | collective-permute-done | bytes 524320 | tf_op jit(solution)/shard_map/ppermute | solution.py:35
  500.4 16.9 %collective-permute-done.24.refs_7_ = f32[32,2048]{1,0:T(8,128)S(1)} collective-permute-done((f32[32,2048]{1,0:T(8,128)S(1)}, f32[32,2048]{1,0:T(8,128)S(1)}, u32[]{:S(2)}, u32[]{:S(2)}) %collective-permute-start.24) | collective-permute-done | bytes 262176 | tf_op jit(solution)/shard_map/ppermute | solution.py:35
  518.7 1.9 add.188
  522.0 7.7 %collective-permute-start.13 = (f32[32,2048]{1,0:T(8,128)}, f32[32,2048]{1,0:T(8,128)}, u32[]{:S(2)}, u32[]{:S(2)}) collective-permute-start(f32[32,2048]{1,0:T(8,128)} %get-tuple-element.55), channel_id=1, source_target_pairs={{0,2},{6,4},{1,3},{7,5},{8,10},{14,12},{9,11},{15,13},{16,18},{22,... | collective-permute-start | bytes 786440 | tf_op jit(solution)/shard_map/ppermute | solution.py:35
  529.8 6.1 shard_map.42
  543.0 8.2 %collective-permute-done.31.refs_7_ = f32[96,2048]{1,0:T(8,128)} collective-permute-done((f32[96,2048]{1,0:T(8,128)S(1)}, f32[96,2048]{1,0:T(8,128)}, u32[]{:S(2)}, u32[]{:S(2)}) %collective-permute-start.31) | collective-permute-done | bytes 786464 | tf_op jit(solution)/shard_map/ppermute | solution.py:35
  551.2 6.7 %shard_map.43 = (f32[512,2048]{1,0:T(8,128)}, f32[4,8,128]{2,1,0:T(8,128)}) custom-call(s32[1]{0:T(128)} %bitcast.14.is_end, f32[512,2048]{1,0:T(8,128)} %bitcast.46, f32[512,2048]{1,0:T(8,128)} %bitcast.16.refs_0_, f32[512,2048]{1,0:T(8,128)} %bitcast.17.refs_1_, f32[512,2048]{1,0:T(8,128)} %bitcast.18.refs_2_, ...), custom_call_target="tpu_custom_call", output_to_operand_aliasing={{0}: (10, {}), {1}: (11, {})} | custom-call | flops 12582912 | bytes 12582912 | tf_op jit(solution)/shard_map/pallas_call | solution.py:62
  559.5 2.9 collective-permute-done.35.refs_6_
  562.3 6.9 %collective-permute-done.36.refs_7_ = f32[64,2048]{1,0:T(8,128)} collective-permute-done((f32[64,2048]{1,0:T(8,128)S(1)}, f32[64,2048]{1,0:T(8,128)}, u32[]{:S(2)}, u32[]{:S(2)}) %collective-permute-start.36) | collective-permute-done | bytes 524320 | tf_op jit(solution)/shard_map/ppermute | solution.py:35
  569.2 4.9 shard_map.44
  574.9 2.2 shard_map.45
  579.2 1.6 collective-permute-start.38
  580.9 1.9 collective-permute-done.38
  582.8 3.6 collective-permute-done.39
  586.9 4.0 collective-permute-done.40
  592.4 2.0 collective-permute-done.41
  595.2 4.3 shard_map.46
  599.5 2.9 collective-permute-start.42
  603.0 12.5 %shard_map.47 = (f32[128,2048]{1,0:T(8,128)}, f32[128,2048]{1,0:T(8,128)}, f32[128,2048]{1,0:T(8,128)}) custom-call(s32[3]{0:T(128)} %pad_add_fusion.1.places, f32[4]{0:T(128)} %select_reduce_fusion.factor, f32[4,128,2048]{2,1,0:T(8,128)} %collective-permute-done.7.refs_0_, f32[4,128,2048]{2,1,0:T(8,128)} %collective-permute-done.6.refs_1_, ...), custom_call_target="tpu_custom_call" | custom-call | flops 18874368 | bytes 18874368 | tf_op jit(solution)/shard_map/pallas_call | solution.py:62
  615.6 2.4 collective-permute-start.46
  618.0 7.3 %collective-permute-done.42 = f32[128,2048]{1,0:T(8,128)} collective-permute-done((f32[128,2048]{1,0:T(8,128)}, f32[128,2048]{1,0:T(8,128)}, u32[]{:S(2)}, u32[]{:S(2)}) %collective-permute-start.42) | collective-permute-done | bytes 1048608 | tf_op jit(solution)/shard_map/ppermute | solution.py:35
  625.3 2.3 add.199
  628.3 6.7 %collective-permute-start.45 = (f32[128,2048]{1,0:T(8,128)}, f32[128,2048]{1,0:T(8,128)S(1)}, u32[]{:S(2)}, u32[]{:S(2)}) collective-permute-start(f32[128,2048]{1,0:T(8,128)} %get-tuple-element.79), channel_id=1, source_target_pairs={{0,2},{6,4},{1,3},{7,5},{8,10},{14,12},{9,11},{15,13},{16,18},{22,... | collective-permute-start | bytes 3145736 | tf_op jit(solution)/shard_map/ppermute | solution.py:35
  635.1 12.7 %collective-permute-done.46 = f32[128,2048]{1,0:T(8,128)} collective-permute-done((f32[128,2048]{1,0:T(8,128)}, f32[128,2048]{1,0:T(8,128)}, u32[]{:S(2)}, u32[]{:S(2)}) %collective-permute-start.46) | collective-permute-done | bytes 1048608 | tf_op jit(solution)/shard_map/ppermute | solution.py:35
  647.7 1.7 add.203
  651.7 6.4 multiply_reduce_fusion
  658.3 6.8 %collective-permute-done.45 = f32[128,2048]{1,0:T(8,128)S(1)} collective-permute-done((f32[128,2048]{1,0:T(8,128)}, f32[128,2048]{1,0:T(8,128)S(1)}, u32[]{:S(2)}, u32[]{:S(2)}) %collective-permute-start.45) | collective-permute-done | bytes 1048608 | tf_op jit(solution)/shard_map/ppermute | solution.py:35
  665.1 4.3 collective-permute-done.44
  669.4 1.8 bitcast_add_fusion
  (162 shorter events, 51.8 us)
Async XLA Ops:
  11.5 373.9 %all-to-all-start = ((f32[16,96,2048]{2,1,0:T(8,128)}), f32[16,96,2048]{2,1,0:T(8,128)}, u32[]{:S(2)}, u32[]{:S(2)}) async-start(f32[16,96,2048]{2,1,0:T(8,128)} %slice.28), calls=%async_computation | async-start | bytes 25165824 | tf_op jit(solution)/shard_map/all_to_all | solution.py:251
  19.2 225.8 %collective-permute-start = (f32[128,2048]{1,0:T(8,128)S(1)}, f32[128,2048]{1,0:T(8,128)}, u32[]{:S(2)}, u32[]{:S(2)}) collective-permute-start(f32[128,2048]{1,0:T(8,128)S(1)} %slice.24), channel_id=1, source_target_pairs={{0,2},{2,0},{4,6},{6,4},{1,3},{3,1},{5,7},{7,5},{8,10},{10,8},{12,... | collective-permute-start | bytes 3145736 | tf_op jit(solution)/shard_map/ppermute | solution.py:35
  35.2 335.7 %collective-permute-start.5 = (f32[4,128,2048]{2,1,0:T(8,128)}, f32[4,128,2048]{2,1,0:T(8,128)}, u32[]{:S(2)}, u32[]{:S(2)}) collective-permute-start(f32[4,128,2048]{2,1,0:T(8,128)} %constant_dynamic-slice_fusion.1), channel_id=1, source_target_pairs={{0,8},{8,0},{16,24},{24,16},{1,9},{9,1},{17,25},{25,17},{2,10},{10... | collective-permute-start | bytes 12582920 | tf_op jit(solution)/shard_map/ppermute | solution.py:35
  35.2 340.9 %collective-permute-start.6 = (f32[4,128,2048]{2,1,0:T(8,128)}, f32[4,128,2048]{2,1,0:T(8,128)}, u32[]{:S(2)}, u32[]{:S(2)}) collective-permute-start(f32[4,128,2048]{2,1,0:T(8,128)} %constant_dynamic-slice_fusion.2), channel_id=1, source_target_pairs={{0,24},{8,16},{16,8},{24,0},{1,25},{9,17},{17,9},{25,1},{2,26},{10... | collective-permute-start | bytes 12582920 | tf_op jit(solution)/shard_map/ppermute | solution.py:35
  36.8 211.5 %collective-permute-start.3 = (f32[128,2048]{1,0:T(8,128)S(1)}, f32[128,2048]{1,0:T(8,128)}, u32[]{:S(2)}, u32[]{:S(2)}) collective-permute-start(f32[128,2048]{1,0:T(8,128)S(1)} %slice.24), channel_id=1, source_target_pairs={{2,4},{4,2},{3,5},{5,3},{10,12},{12,10},{11,13},{13,11},{18,20},{2... | collective-permute-start | bytes 3145736 | tf_op jit(solution)/shard_map/ppermute | solution.py:35
  245.0 4.6 collective-permute-start.1
  246.7 134.1 %collective-permute-start.7 = (f32[4,128,2048]{2,1,0:T(8,128)}, f32[4,128,2048]{2,1,0:T(8,128)}, u32[]{:S(2)}, u32[]{:S(2)}) collective-permute-start(f32[4,128,2048]{2,1,0:T(8,128)} %constant_dynamic-slice_fusion.3), channel_id=1, source_target_pairs={{0,16},{8,24},{16,0},{24,8},{1,17},{9,25},{17,1},{25,9},{2,18},{10... | collective-permute-start | bytes 12582920 | tf_op jit(solution)/shard_map/ppermute | solution.py:35
  248.3 92.0 %collective-permute-start.4 = (f32[128,2048]{1,0:T(8,128)}, f32[128,2048]{1,0:T(8,128)}, u32[]{:S(2)}, u32[]{:S(2)}) collective-permute-start(f32[128,2048]{1,0:T(8,128)} %collective-permute-done.3), channel_id=1, source_target_pairs={{2,0},{4,6},{3,1},{5,7},{10,8},{12,14},{11,9},{13,15},{18,16},{20,... | collective-permute-start | bytes 3145736 | tf_op jit(solution)/shard_map/ppermute | solution.py:35
  249.6 113.2 %collective-permute-start.2 = (f32[128,2048]{1,0:T(8,128)}, f32[128,2048]{1,0:T(8,128)}, u32[]{:S(2)}, u32[]{:S(2)}) collective-permute-start(f32[128,2048]{1,0:T(8,128)} %collective-permute-done.1), channel_id=1, source_target_pairs={{2,0},{4,6},{3,1},{5,7},{10,8},{12,14},{11,9},{13,15},{18,16},{20,... | collective-permute-start | bytes 3145736 | tf_op jit(solution)/shard_map/ppermute | solution.py:35
  251.0 134.4 %copy-start.1 = (f32[96,2048]{1,0:T(8,128)}, f32[96,2048]{1,0:T(8,128)S(1)}, u32[]{:S(2)}) copy-start(f32[96,2048]{1,0:T(8,128)S(1)} %slice.22.v) | copy-start | bytes 2359300
  391.4 1.2 collective-permute-start.8
  392.6 3.6 collective-permute-start.9
  396.2 3.6 collective-permute-start.10
  399.7 4.5 collective-permute-start.11
  404.2 3.6 collective-permute-start.12
  413.3 37.1 %collective-permute-start.16 = (f32[64,2048]{1,0:T(8,128)}, f32[64,2048]{1,0:T(8,128)S(1)}, u32[]{:S(2)}, u32[]{:S(2)}) collective-permute-start(f32[64,2048]{1,0:T(8,128)} %shard_map.39), channel_id=1, source_target_pairs={{0,2},{6,4},{1,3},{7,5},{8,10},{14,12},{9,11},{15,13},{16,18},{22,... | collective-permute-start | bytes 1572872 | tf_op jit(solution)/shard_map/ppermute | solution.py:35
  415.2 18.1 %collective-permute-start.20 = (f32[32,2048]{1,0:T(8,128)S(1)}, f32[32,2048]{1,0:T(8,128)S(1)}, u32[]{:S(2)}, u32[]{:S(2)}) collective-permute-start(f32[32,2048]{1,0:T(8,128)S(1)} %copy-done.15), channel_id=1, source_target_pairs={{0,2},{6,4},{1,3},{7,5},{8,10},{14,12},{9,11},{15,13},{16,18},{22,... | collective-permute-start | bytes 786440 | tf_op jit(solution)/shard_map/ppermute | solution.py:35
  422.3 28.9 %collective-permute-start.22 = (f32[64,2048]{1,0:T(8,128)}, f32[64,2048]{1,0:T(8,128)S(1)}, u32[]{:S(2)}, u32[]{:S(2)}) collective-permute-start(f32[64,2048]{1,0:T(8,128)} %get-tuple-element.53), channel_id=1, source_target_pairs={{0,2},{6,4},{1,3},{7,5},{8,10},{14,12},{9,11},{15,13},{16,18},{22,... | collective-permute-start | bytes 1572872 | tf_op jit(solution)/shard_map/ppermute | solution.py:35
  423.6 37.9 %collective-permute-start.15 = (f32[96,2048]{1,0:T(8,128)}, f32[96,2048]{1,0:T(8,128)S(1)}, u32[]{:S(2)}, u32[]{:S(2)}) collective-permute-start(f32[96,2048]{1,0:T(8,128)} %get-tuple-element.57), channel_id=1, source_target_pairs={{0,2},{6,4},{1,3},{7,5},{8,10},{14,12},{9,11},{15,13},{16,18},{22,... | collective-permute-start | bytes 2359304 | tf_op jit(solution)/shard_map/ppermute | solution.py:35
  433.4 17.0 %copy-start.10 = (f32[64,2048]{1,0:T(8,128)S(1)}, f32[64,2048]{1,0:T(8,128)}, u32[]{:S(2)}) copy-start(f32[64,2048]{1,0:T(8,128)} %shard_map.39) | copy-start | bytes 1572868
  433.4 17.9 %copy-start.23 = (f32[64,2048]{1,0:T(8,128)S(1)}, f32[64,2048]{1,0:T(8,128)}, u32[]{:S(2)}) copy-start(f32[64,2048]{1,0:T(8,128)} %get-tuple-element.53) | copy-start | bytes 1572868
  433.4 17.8 %collective-permute-start.21 = (f32[32,2048]{1,0:T(8,128)S(1)}, f32[32,2048]{1,0:T(8,128)S(1)}, u32[]{:S(2)}, u32[]{:S(2)}) collective-permute-start(f32[32,2048]{1,0:T(8,128)S(1)} %add.180), channel_id=1, source_target_pairs={{2,4},{4,2},{3,5},{5,3},{10,12},{12,10},{11,13},{13,11},{18,20},{2... | collective-permute-start | bytes 786440 | tf_op jit(solution)/shard_map/ppermute | solution.py:35
  442.5 19.0 %copy-start.18 = (f32[96,2048]{1,0:T(8,128)S(1)}, f32[96,2048]{1,0:T(8,128)}, u32[]{:S(2)}) copy-start(f32[96,2048]{1,0:T(8,128)} %get-tuple-element.57) | copy-start | bytes 2359300
  442.6 30.7 %collective-permute-start.28 = (f32[96,2048]{1,0:T(8,128)}, f32[96,2048]{1,0:T(8,128)}, u32[]{:S(2)}, u32[]{:S(2)}) collective-permute-start(f32[96,2048]{1,0:T(8,128)} %get-tuple-element.65), channel_id=1, source_target_pairs={{0,2},{6,4},{1,3},{7,5},{8,10},{14,12},{9,11},{15,13},{16,18},{22,... | collective-permute-start | bytes 2359304 | tf_op jit(solution)/shard_map/ppermute | solution.py:35
  450.5 2.3 collective-permute-start.17
  451.2 43.5 %copy-start.13 = (f32[32,2048]{1,0:T(8,128)}, f32[32,2048]{1,0:T(8,128)S(1)}, u32[]{:S(2)}) copy-start(f32[32,2048]{1,0:T(8,128)S(1)} %add.181.refs_4_) | copy-start | bytes 786436
  451.3 20.0 %collective-permute-start.23 = (f32[64,2048]{1,0:T(8,128)S(1)}, f32[64,2048]{1,0:T(8,128)}, u32[]{:S(2)}, u32[]{:S(2)}) collective-permute-start(f32[64,2048]{1,0:T(8,128)S(1)} %add.182), channel_id=1, source_target_pairs={{2,4},{4,2},{3,5},{5,3},{10,12},{12,10},{11,13},{13,11},{18,20},{2... | collective-permute-start | bytes 1572872 | tf_op jit(solution)/shard_map/ppermute | solution.py:35
  452.9 31.0 %copy-start.8 = (f32[64,2048]{1,0:T(8,128)}, f32[64,2048]{1,0:T(8,128)S(1)}, u32[]{:S(2)}) copy-start(f32[64,2048]{1,0:T(8,128)S(1)} %add.175.refs_5_) | copy-start | bytes 1572868
  461.6 33.1 %collective-permute-start.18 = (f32[96,2048]{1,0:T(8,128)S(1)}, f32[96,2048]{1,0:T(8,128)}, u32[]{:S(2)}, u32[]{:S(2)}) collective-permute-start(f32[96,2048]{1,0:T(8,128)S(1)} %add.176), channel_id=1, source_target_pairs={{2,4},{4,2},{3,5},{5,3},{10,12},{12,10},{11,13},{13,11},{18,20},{2... | collective-permute-start | bytes 2359304 | tf_op jit(solution)/shard_map/ppermute | solution.py:35
  471.3 25.9 %copy-start.20 = (f32[64,2048]{1,0:T(8,128)S(1)}, f32[64,2048]{1,0:T(8,128)}, u32[]{:S(2)}) copy-start(f32[64,2048]{1,0:T(8,128)} %get-tuple-element.56) | copy-start | bytes 1572868
  472.5 26.4 %copy-start.9 = (f32[64,2048]{1,0:T(8,128)}, f32[64,2048]{1,0:T(8,128)S(1)}, u32[]{:S(2)}) copy-start(f32[64,2048]{1,0:T(8,128)S(1)} %add.183.refs_6_) | copy-start | bytes 1572868
  474.5 22.9 %collective-permute-start.29 = (f32[96,2048]{1,0:T(8,128)S(1)}, f32[96,2048]{1,0:T(8,128)S(1)}, u32[]{:S(2)}, u32[]{:S(2)}) collective-permute-start(f32[96,2048]{1,0:T(8,128)S(1)} %add.186), channel_id=1, source_target_pairs={{2,4},{4,2},{3,5},{5,3},{10,12},{12,10},{11,13},{13,11},{18,20},{2... | collective-permute-start | bytes 2359304 | tf_op jit(solution)/shard_map/ppermute | solution.py:35
  475.2 18.2 %collective-permute-start.14 = (f32[64,2048]{1,0:T(8,128)S(1)}, f32[64,2048]{1,0:T(8,128)S(1)}, u32[]{:S(2)}, u32[]{:S(2)}) collective-permute-start(f32[64,2048]{1,0:T(8,128)S(1)} %copy-done.19), channel_id=1, source_target_pairs={{0,2},{6,4},{1,3},{7,5},{8,10},{14,12},{9,11},{15,13},{16,18},{22,... | collective-permute-start | bytes 1572872 | tf_op jit(solution)/shard_map/ppermute | solution.py:35
  482.5 16.6 %collective-permute-start.33 = (f32[64,2048]{1,0:T(8,128)}, f32[64,2048]{1,0:T(8,128)S(1)}, u32[]{:S(2)}, u32[]{:S(2)}) collective-permute-start(f32[64,2048]{1,0:T(8,128)} %get-tuple-element.70), channel_id=1, source_target_pairs={{0,2},{6,4},{1,3},{7,5},{8,10},{14,12},{9,11},{15,13},{16,18},{22,... | collective-permute-start | bytes 1572872 | tf_op jit(solution)/shard_map/ppermute | solution.py:35
  483.8 36.7 %collective-permute-start.25 = (f32[64,2048]{1,0:T(8,128)S(1)}, f32[64,2048]{1,0:T(8,128)S(1)}, u32[]{:S(2)}, u32[]{:S(2)}) collective-permute-start(f32[64,2048]{1,0:T(8,128)S(1)} %add.175.refs_5_), channel_id=1, source_target_pairs={{2,0},{4,6},{3,1},{5,7},{10,8},{12,14},{11,9},{13,15},{18,16},{20,... | collective-permute-start | bytes 1572872 | tf_op jit(solution)/shard_map/ppermute | solution.py:35
  493.4 28.6 %collective-permute-start.26 = (f32[64,2048]{1,0:T(8,128)S(1)}, f32[64,2048]{1,0:T(8,128)S(1)}, u32[]{:S(2)}, u32[]{:S(2)}) collective-permute-start(f32[64,2048]{1,0:T(8,128)S(1)} %add.183.refs_6_), channel_id=1, source_target_pairs={{2,0},{4,6},{3,1},{5,7},{10,8},{12,14},{11,9},{13,15},{18,16},{20,... | collective-permute-start | bytes 1572872 | tf_op jit(solution)/shard_map/ppermute | solution.py:35
  494.7 22.6 %collective-permute-start.24 = (f32[32,2048]{1,0:T(8,128)S(1)}, f32[32,2048]{1,0:T(8,128)S(1)}, u32[]{:S(2)}, u32[]{:S(2)}) collective-permute-start(f32[32,2048]{1,0:T(8,128)S(1)} %add.181.refs_4_), channel_id=1, source_target_pairs={{2,0},{4,6},{3,1},{5,7},{10,8},{12,14},{11,9},{13,15},{18,16},{20,... | collective-permute-start | bytes 786440 | tf_op jit(solution)/shard_map/ppermute | solution.py:35
  497.3 38.7 %copy-start.5 = (f32[96,2048]{1,0:T(8,128)}, f32[96,2048]{1,0:T(8,128)S(1)}, u32[]{:S(2)}) copy-start(f32[96,2048]{1,0:T(8,128)S(1)} %add.177.refs_4_) | copy-start | bytes 2359300
  497.4 38.6 %collective-permute-start.19 = (f32[64,2048]{1,0:T(8,128)S(1)}, f32[64,2048]{1,0:T(8,128)}, u32[]{:S(2)}, u32[]{:S(2)}) collective-permute-start(f32[64,2048]{1,0:T(8,128)S(1)} %add.178), channel_id=1, source_target_pairs={{2,4},{4,2},{3,5},{5,3},{10,12},{12,10},{11,13},{13,11},{18,20},{2... | collective-permute-start | bytes 1572872 | tf_op jit(solution)/shard_map/ppermute | solution.py:35
  498.9 37.0 %copy-start.6 = (f32[96,2048]{1,0:T(8,128)}, f32[96,2048]{1,0:T(8,128)S(1)}, u32[]{:S(2)}) copy-start(f32[96,2048]{1,0:T(8,128)S(1)} %add.187.refs_5_) | copy-start | bytes 2359300
  499.2 43.8 %collective-permute-start.30 = (f32[96,2048]{1,0:T(8,128)S(1)}, f32[96,2048]{1,0:T(8,128)}, u32[]{:S(2)}, u32[]{:S(2)}) collective-permute-start(f32[96,2048]{1,0:T(8,128)S(1)} %add.177.refs_4_), channel_id=1, source_target_pairs={{2,0},{4,6},{3,1},{5,7},{10,8},{12,14},{11,9},{13,15},{18,16},{20,... | collective-permute-start | bytes 2359304 | tf_op jit(solution)/shard_map/ppermute | solution.py:35
  517.4 33.8 %collective-permute-start.31 = (f32[96,2048]{1,0:T(8,128)S(1)}, f32[96,2048]{1,0:T(8,128)}, u32[]{:S(2)}, u32[]{:S(2)}) collective-permute-start(f32[96,2048]{1,0:T(8,128)S(1)} %add.187.refs_5_), channel_id=1, source_target_pairs={{2,0},{4,6},{3,1},{5,7},{10,8},{12,14},{11,9},{13,15},{18,16},{20,... | collective-permute-start | bytes 2359304 | tf_op jit(solution)/shard_map/ppermute | solution.py:35
  520.6 19.7 %collective-permute-start.34 = (f32[64,2048]{1,0:T(8,128)}, f32[64,2048]{1,0:T(8,128)}, u32[]{:S(2)}, u32[]{:S(2)}) collective-permute-start(f32[64,2048]{1,0:T(8,128)} %add.188), channel_id=1, source_target_pairs={{2,4},{4,2},{3,5},{5,3},{10,12},{12,10},{11,13},{13,11},{18,20},{2... | collective-permute-start | bytes 1572872 | tf_op jit(solution)/shard_map/ppermute | solution.py:35
  522.0 15.0 %collective-permute-start.13 = (f32[32,2048]{1,0:T(8,128)}, f32[32,2048]{1,0:T(8,128)}, u32[]{:S(2)}, u32[]{:S(2)}) collective-permute-start(f32[32,2048]{1,0:T(8,128)} %get-tuple-element.55), channel_id=1, source_target_pairs={{0,2},{6,4},{1,3},{7,5},{8,10},{14,12},{9,11},{15,13},{16,18},{22,... | collective-permute-start | bytes 786440 | tf_op jit(solution)/shard_map/ppermute | solution.py:35
  537.1 20.9 %copy-start.11 = (f32[64,2048]{1,0:T(8,128)}, f32[64,2048]{1,0:T(8,128)S(1)}, u32[]{:S(2)}) copy-start(f32[64,2048]{1,0:T(8,128)S(1)} %add.179.refs_4_) | copy-start | bytes 1572868
  538.3 4.6 collective-permute-start.27
  539.0 23.3 %collective-permute-start.35 = (f32[64,2048]{1,0:T(8,128)S(1)}, f32[64,2048]{1,0:T(8,128)S(1)}, u32[]{:S(2)}, u32[]{:S(2)}) collective-permute-start(f32[64,2048]{1,0:T(8,128)S(1)} %add.179.refs_4_), channel_id=1, source_target_pairs={{2,0},{4,6},{3,1},{5,7},{10,8},{12,14},{11,9},{13,15},{18,16},{20,... | collective-permute-start | bytes 1572872 | tf_op jit(solution)/shard_map/ppermute | solution.py:35
  541.6 27.6 %collective-permute-start.36 = (f32[64,2048]{1,0:T(8,128)S(1)}, f32[64,2048]{1,0:T(8,128)}, u32[]{:S(2)}, u32[]{:S(2)}) collective-permute-start(f32[64,2048]{1,0:T(8,128)S(1)} %add.189.refs_5_), channel_id=1, source_target_pairs={{2,0},{4,6},{3,1},{5,7},{10,8},{12,14},{11,9},{13,15},{18,16},{20,... | collective-permute-start | bytes 1572872 | tf_op jit(solution)/shard_map/ppermute | solution.py:35
  558.0 16.2 %collective-permute-start.32 = (f32[32,2048]{1,0:T(8,128)S(1)}, f32[32,2048]{1,0:T(8,128)S(1)}, u32[]{:S(2)}, u32[]{:S(2)}) collective-permute-start(f32[32,2048]{1,0:T(8,128)S(1)} %add.185.refs_4_), channel_id=1, source_target_pairs={{2,0},{4,6},{3,1},{5,7},{10,8},{12,14},{11,9},{13,15},{18,16},{20,... | collective-permute-start | bytes 786440 | tf_op jit(solution)/shard_map/ppermute | solution.py:35
  578.0 1.2 collective-permute-start.37
  579.2 3.6 collective-permute-start.38
  582.8 3.6 collective-permute-start.39
  586.4 4.5 collective-permute-start.40
  590.9 3.6 collective-permute-start.41
  599.5 25.8 %collective-permute-start.42 = (f32[128,2048]{1,0:T(8,128)}, f32[128,2048]{1,0:T(8,128)}, u32[]{:S(2)}, u32[]{:S(2)}) collective-permute-start(f32[128,2048]{1,0:T(8,128)} %shard_map.46), channel_id=1, source_target_pairs={{0,2},{6,4},{1,3},{7,5},{8,10},{14,12},{9,11},{15,13},{16,18},{22,... | collective-permute-start | bytes 3145736 | tf_op jit(solution)/shard_map/ppermute | solution.py:35
  603.0 22.2 %copy-start.3 = (f32[128,2048]{1,0:T(8,128)S(1)}, f32[128,2048]{1,0:T(8,128)}, u32[]{:S(2)}) copy-start(f32[128,2048]{1,0:T(8,128)} %shard_map.46) | copy-start | bytes 3145732
  615.5 34.6 %copy-start.4 = (f32[128,2048]{1,0:T(8,128)S(1)}, f32[128,2048]{1,0:T(8,128)}, u32[]{:S(2)}) copy-start(f32[128,2048]{1,0:T(8,128)} %get-tuple-element.78) | copy-start | bytes 3145732
  615.5 36.2 %copy-start.7 = (f32[96,2048]{1,0:T(8,128)S(1)}, f32[96,2048]{1,0:T(8,128)}, u32[]{:S(2)}) copy-start(f32[96,2048]{1,0:T(8,128)} %get-tuple-element.49) | copy-start | bytes 2359300
  615.6 32.2 %collective-permute-start.46 = (f32[128,2048]{1,0:T(8,128)}, f32[128,2048]{1,0:T(8,128)}, u32[]{:S(2)}, u32[]{:S(2)}) collective-permute-start(f32[128,2048]{1,0:T(8,128)} %get-tuple-element.80), channel_id=1, source_target_pairs={{0,2},{6,4},{1,3},{7,5},{8,10},{14,12},{9,11},{15,13},{16,18},{22,... | collective-permute-start | bytes 3145736 | tf_op jit(solution)/shard_map/ppermute | solution.py:35
  627.6 22.5 %collective-permute-start.43 = (f32[128,2048]{1,0:T(8,128)}, f32[128,2048]{1,0:T(8,128)S(1)}, u32[]{:S(2)}, u32[]{:S(2)}) collective-permute-start(f32[128,2048]{1,0:T(8,128)} %add.199), channel_id=1, source_target_pairs={{2,4},{4,2},{3,5},{5,3},{10,12},{12,10},{11,13},{13,11},{18,20},{2... | collective-permute-start | bytes 3145736 | tf_op jit(solution)/shard_map/ppermute | solution.py:35
  628.3 36.8 %collective-permute-start.45 = (f32[128,2048]{1,0:T(8,128)}, f32[128,2048]{1,0:T(8,128)S(1)}, u32[]{:S(2)}, u32[]{:S(2)}) collective-permute-start(f32[128,2048]{1,0:T(8,128)} %get-tuple-element.79), channel_id=1, source_target_pairs={{0,2},{6,4},{1,3},{7,5},{8,10},{14,12},{9,11},{15,13},{16,18},{22,... | collective-permute-start | bytes 3145736 | tf_op jit(solution)/shard_map/ppermute | solution.py:35
  649.4 15.7 %collective-permute-start.47 = (f32[128,2048]{1,0:T(8,128)S(1)}, f32[128,2048]{1,0:T(8,128)S(1)}, u32[]{:S(2)}, u32[]{:S(2)}) collective-permute-start(f32[128,2048]{1,0:T(8,128)S(1)} %add.203), channel_id=1, source_target_pairs={{2,4},{4,2},{3,5},{5,3},{10,12},{12,10},{11,13},{13,11},{18,20},{2... | collective-permute-start | bytes 3145736 | tf_op jit(solution)/shard_map/ppermute | solution.py:35
  650.3 19.1 %copy-start.16 = (f32[128,2048]{1,0:T(8,128)S(1)}, f32[128,2048]{1,0:T(8,128)}, u32[]{:S(2)}) copy-start(f32[128,2048]{1,0:T(8,128)} %get-tuple-element.79) | copy-start | bytes 3145732
  650.3 19.1 %collective-permute-start.44 = (f32[128,2048]{1,0:T(8,128)S(1)}, f32[128,2048]{1,0:T(8,128)S(1)}, u32[]{:S(2)}, u32[]{:S(2)}) collective-permute-start(f32[128,2048]{1,0:T(8,128)S(1)} %add.200), channel_id=1, source_target_pairs={{2,0},{4,6},{3,1},{5,7},{10,8},{12,14},{11,9},{13,15},{18,16},{20,... | collective-permute-start | bytes 3145736 | tf_op jit(solution)/shard_map/ppermute | solution.py:35
  (14 other events, 119.5 us)

commit v7 on v6

--- a/solution.py
+++ b/solution.py
@@ -50,8 +50,7 @@
     tiles = rest // TILE
     if outers != LINE or rest % TILE or tiles < 13 or not cut:
         return None
-    body = tiles - 10
-    sizes = [1, 2, 2] + [3] * (body // 3) + [body % 3] * (body % 3 > 0) + [2, 2, 1]
+    sizes = [1] + [2] * ((tiles - 2) // 2) + [1] * (tiles % 2) + [1]
     return cut, sizes
 
 
@@ -284,7 +283,7 @@
     flat_v = line_v.reshape(outers * rest, columns)
     end_flag = is_end.astype(jnp.int32).reshape(1)
     next_spread_v, spread_sq = move_spread(share, factor, spread, spread_v)
-    early = {2: next_spread_v}
+    early = {4: next_spread_v}
     count, places = len(sizes), begins(sizes)
     own = step_chunks(line_factor, flat, flat_v, 0, sizes[:1])
     own += step_chunks(line_factor, flat, tie(flat_v, own[0]), places[1], sizes[1:2])
@@ -331,7 +330,8 @@
     own_v = lax.dynamic_index_in_dim(line_v, o, 0, keepdims=False)
     own_v = own_v + jnp.where(is_end, end_sum, mid_sum) * share
     step = jnp.sum(factor[:, None, None] * (spread - spread_v[None]), axis=0)
-    return jnp.concatenate([spread_v + step * share, own_v])
+    buffer = lax.optimization_barrier(jnp.pad(spread_v + step * share, ((0, rest), (0, 0))))
+    return lax.dynamic_update_slice(buffer, own_v, (cut, 0))
 
 
 def solution(mesh):

time: 675 us -> 677 us (level)
  waiting for transfers between devices: 435 us -> 423 us
  starting transfers between devices: 90 us -> 97.9 us
    ppermute x38 -> x41, waiting for transfers between devices: 411 us -> 398 us  [send(): return lax.ppermute(value, axis, pairs)]
    ppermute x38 -> x41, starting transfers between devices: 75.4 us -> 83.4 us  [send(): return lax.ppermute(value, axis, pairs)]
  transfers between devices with their start and end apart: 49 -> 52, of which waited for: 26 -> 26; matrix products, arithmetic and copies ran while one was open for 9% -> 9% of each run, Pallas kernels for 8% -> 8%
where the time goes in v7:
time: 677 us; the launch traced here: 674 us
  waiting for transfers between devices  423 us (62%)
  starting transfers between devices  97.9 us (14%)
  Pallas kernels  63.9 us (9%)
  other arithmetic  58.3 us (9%)
  local copies, waits for them, and re-layouts  29.5 us (4%)
    ppermute x41, waiting for transfers between devices, send(): return lax.ppermute(value, axis, pairs)  398 us
    ppermute x41, starting transfers between devices, send(): return lax.ppermute(value, axis, pairs)  83.4 us
    pallas_call x11, Pallas kernels, run(): pl.pallas_call(kernel, grid_spec=pltpu.PrefetchScalarGridSpec(num_scalar_...  63.9 us
    ppermute x10, waiting for transfers between devices, sum_over_devices(): lax.ppermute(value, axis, [(i, i ^ step) for i in range(size)])  25.1 us
    reduce_sum x4, other arithmetic, on_device(): square = jnp.sum(jnp.square(held[place] - v))  17.5 us
    dynamic_slice x3, local copies, waits for them, and re-layouts, line_rows(): lax.dynamic_slice(source, (worker * outers, cut, 0), (outers, rest, colum...  14.1 us
  transfers between devices with their start and end apart: 52, of which 26 were waited for; matrix products, arithmetic and copies ran while one was open for 9% of the time, Pallas kernels for 8%

profile of v7, /device:TPU:0, one launch (start us, length us, event | category | flops | bytes accessed | tf_op | source)
XLA Modules:
  0.0 674.3 jit_solution(5262089908515823798)
XLA Ops:
  0.0 11.5 %slice.28 = f32[16,96,2048]{2,1,0:T(8,128)} slice(f32[16,224,2048]{2,1,0:T(8,128)} %bitcast.62), slice={[0:16], [0:96], [0:2048]} | slice | bytes 25165824 | tf_op jit(solution)/shard_map/slice | solution.py:251
  11.5 7.6 %all-to-all-start = ((f32[16,96,2048]{2,1,0:T(8,128)}), f32[16,96,2048]{2,1,0:T(8,128)}, u32[]{:S(2)}, u32[]{:S(2)}) async-start(f32[16,96,2048]{2,1,0:T(8,128)} %slice.28), calls=%async_computation | async-start | bytes 25165824 | tf_op jit(solution)/shard_map/all_to_all | solution.py:250
  19.2 1.9 collective-permute-start
  21.1 4.6 constant_dynamic-slice_fusion.3
  25.7 4.8 constant_dynamic-slice_fusion.2
  30.5 4.7 constant_dynamic-slice_fusion.1
  35.2 1.6 collective-permute-start.6
  36.7 1.6 collective-permute-start.3
  38.4 206.6 %collective-permute-done = f32[128,2048]{1,0:T(8,128)} collective-permute-done((f32[128,2048]{1,0:T(8,128)S(1)}, f32[128,2048]{1,0:T(8,128)}, u32[]{:S(2)}, u32[]{:S(2)}) %collective-permute-start) | collective-permute-done | bytes 1048608 | tf_op jit(solution)/shard_map/ppermute | solution.py:35
  245.0 1.7 collective-permute-start.1
  246.7 1.6 collective-permute-start.7
  251.2 89.2 %collective-permute-done.4 = f32[128,2048]{1,0:T(8,128)} collective-permute-done((f32[128,2048]{1,0:T(8,128)}, f32[128,2048]{1,0:T(8,128)}, u32[]{:S(2)}, u32[]{:S(2)}) %collective-permute-start.4) | collective-permute-done | bytes 1048608 | tf_op jit(solution)/shard_map/ppermute | solution.py:35
  340.3 22.5 %collective-permute-done.2 = f32[128,2048]{1,0:T(8,128)} collective-permute-done((f32[128,2048]{1,0:T(8,128)}, f32[128,2048]{1,0:T(8,128)}, u32[]{:S(2)}, u32[]{:S(2)}) %collective-permute-start.2) | collective-permute-done | bytes 1048608 | tf_op jit(solution)/shard_map/ppermute | solution.py:35
  362.8 2.5 select_bitcast_fusion.3
  365.3 4.9 multiply_reduce_fusion.5
  370.8 4.8 multiply_reduce_fusion.4
  376.3 3.9 multiply_reduce_fusion.3
  380.9 3.9 multiply_reduce_fusion.2
  385.4 6.0 multiply_reduce_fusion.1
  394.1 2.1 collective-permute-done.9
  396.2 3.6 collective-permute-done.10
  400.8 3.4 collective-permute-done.11
  405.7 2.0 collective-permute-done.12
  408.5 2.1 shard_map.38
  410.6 2.7 shard_map.39
  413.3 2.1 collective-permute-start.22
  416.6 4.7 shard_map.40
  421.3 2.1 collective-permute-start.16
  423.4 4.5 collective-permute-done.22
  429.4 6.5 collective-permute-start.24
  437.0 9.6 %shard_map.41 = (f32[64,2048]{1,0:T(8,128)}, f32[64,2048]{1,0:T(8,128)}, f32[64,2048]{1,0:T(8,128)}, f32[64,2048]{1,0:T(8,128)}, f32[32,2048]{1,0:T(8,128)}) custom-call(f32[4]{0:T(128)} %select_reduce_fusion.2.factor, f32[512,2048]{1,0:T(8,128)} %bitcast.16.refs_0_, f32[512,2048]{1,0:T(8,128)} %bitcast.17.refs_1_, f32[512,2048]{1,0:T(8,128)} %bitcast.18.refs_2_, ...), custom_call_target="tpu_custom_call" | custom-call | flops 14155776 | bytes 14155776 | tf_op jit(solution)/shard_map/pallas_call | solution.py:61
  448.6 6.4 collective-permute-start.15
  458.1 6.3 collective-permute-start.31
  464.5 3.0 collective-permute-done.15
  469.1 6.5 collective-permute-start.14
  475.6 2.1 collective-permute-start.36
  480.2 7.9 %shard_map.37 = (f32[96,2048]{1,0:T(8,128)}, f32[16,8,128]{2,1,0:T(8,128)}) custom-call(f32[16]{0:T(128)} %copy-done.30, f32[96,2048]{1,0:T(8,128)} %copy-done.1, f32[16,96,2048]{2,1,0:T(8,128)} %all-to-all-done.values), custom_call_target="tpu_custom_call" | custom-call | flops 14155776 | bytes 14155776 | tf_op jit(solution)/shard_map/pallas_call | solution.py:61
  500.8 22.3 %collective-permute-done.26.refs_8_ = f32[32,2048]{1,0:T(8,128)S(1)} collective-permute-done((f32[32,2048]{1,0:T(8,128)S(1)}, f32[32,2048]{1,0:T(8,128)S(1)}, u32[]{:S(2)}, u32[]{:S(2)}) %collective-permute-start.26) | collective-permute-done | bytes 262176 | tf_op jit(solution)/shard_map/ppermute | solution.py:35
  524.5 3.0 collective-permute-start.13
  531.0 1.9 add.189.refs_4_
  534.4 8.1 %shard_map.42 = (f32[512,2048]{1,0:T(8,128)}, f32[4,8,128]{2,1,0:T(8,128)}) custom-call(s32[1]{0:T(128)} %bitcast.14.is_end, f32[512,2048]{1,0:T(8,128)} %bitcast.47, f32[512,2048]{1,0:T(8,128)} %bitcast.16.refs_0_, f32[512,2048]{1,0:T(8,128)} %bitcast.17.refs_1_, f32[512,2048]{1,0:T(8,128)} %bitcast.18.refs_2_, f32[512,2048]{1,0:T(8,128)} %bitcast.55, ...), custom_call_target="tpu_custom_call" | custom-call | flops 14680064 | bytes 14680064 | tf_op jit(solution)/shard_map/pallas_call | solution.py:61
  548.0 8.9 %collective-permute-done.34.refs_7_ = f32[64,2048]{1,0:T(8,128)} collective-permute-done((f32[64,2048]{1,0:T(8,128)S(1)}, f32[64,2048]{1,0:T(8,128)}, u32[]{:S(2)}, u32[]{:S(2)}) %collective-permute-start.34) | collective-permute-done | bytes 524320 | tf_op jit(solution)/shard_map/ppermute | solution.py:35
  556.9 5.0 shard_map.43
  563.4 2.0 collective-permute-done.38.refs_6_
  565.4 5.5 collective-permute-done.39.refs_7_
  571.7 4.9 shard_map.44
  577.3 2.2 shard_map.45
  583.2 2.1 collective-permute-done.41
  585.3 3.6 collective-permute-done.42
  589.3 4.0 collective-permute-done.43
  594.8 2.0 collective-permute-done.44
  597.6 4.3 shard_map.46
  601.9 2.9 collective-permute-start.45
  605.5 12.5 %shard_map.47 = (f32[128,2048]{1,0:T(8,128)}, f32[128,2048]{1,0:T(8,128)}, f32[128,2048]{1,0:T(8,128)}) custom-call(s32[3]{0:T(128)} %pad_add_fusion.1.places, f32[4]{0:T(128)} %select_reduce_fusion.factor, f32[4,128,2048]{2,1,0:T(8,128)} %collective-permute-done.7.refs_0_, f32[4,128,2048]{2,1,0:T(8,128)} %collective-permute-done.6.refs_1_, ...), custom_call_target="tpu_custom_call" | custom-call | flops 18874368 | bytes 18874368 | tf_op jit(solution)/shard_map/pallas_call | solution.py:61
  618.0 2.4 collective-permute-start.49
  620.5 7.2 %collective-permute-done.45 = f32[128,2048]{1,0:T(8,128)} collective-permute-done((f32[128,2048]{1,0:T(8,128)}, f32[128,2048]{1,0:T(8,128)}, u32[]{:S(2)}, u32[]{:S(2)}) %collective-permute-start.45) | collective-permute-done | bytes 1048608 | tf_op jit(solution)/shard_map/ppermute | solution.py:35
  627.7 2.3 add.209
  630.7 6.7 collective-permute-start.48
  637.4 12.8 %collective-permute-done.49 = f32[128,2048]{1,0:T(8,128)} collective-permute-done((f32[128,2048]{1,0:T(8,128)}, f32[128,2048]{1,0:T(8,128)}, u32[]{:S(2)}, u32[]{:S(2)}) %collective-permute-start.49) | collective-permute-done | bytes 1048608 | tf_op jit(solution)/shard_map/ppermute | solution.py:35
  650.2 1.7 add.213
  654.0 6.4 multiply_reduce_fusion
  662.0 5.5 collective-permute-done.48
  667.5 4.1 collective-permute-done.47
  671.6 2.7 fusion
  (174 shorter events, 62.4 us)
Async XLA Ops:
  11.5 373.9 %all-to-all-start = ((f32[16,96,2048]{2,1,0:T(8,128)}), f32[16,96,2048]{2,1,0:T(8,128)}, u32[]{:S(2)}, u32[]{:S(2)}) async-start(f32[16,96,2048]{2,1,0:T(8,128)} %slice.28), calls=%async_computation | async-start | bytes 25165824 | tf_op jit(solution)/shard_map/all_to_all | solution.py:250
  19.2 225.8 %collective-permute-start = (f32[128,2048]{1,0:T(8,128)S(1)}, f32[128,2048]{1,0:T(8,128)}, u32[]{:S(2)}, u32[]{:S(2)}) collective-permute-start(f32[128,2048]{1,0:T(8,128)S(1)} %slice.24), channel_id=1, source_target_pairs={{0,2},{2,0},{4,6},{6,4},{1,3},{3,1},{5,7},{7,5},{8,10},{10,8},{12,... | collective-permute-start | bytes 3145736 | tf_op jit(solution)/shard_map/ppermute | solution.py:35
  35.2 335.6 %collective-permute-start.5 = (f32[4,128,2048]{2,1,0:T(8,128)}, f32[4,128,2048]{2,1,0:T(8,128)}, u32[]{:S(2)}, u32[]{:S(2)}) collective-permute-start(f32[4,128,2048]{2,1,0:T(8,128)} %constant_dynamic-slice_fusion.1), channel_id=1, source_target_pairs={{0,8},{8,0},{16,24},{24,16},{1,9},{9,1},{17,25},{25,17},{2,10},{10... | collective-permute-start | bytes 12582920 | tf_op jit(solution)/shard_map/ppermute | solution.py:35
  35.2 341.1 %collective-permute-start.6 = (f32[4,128,2048]{2,1,0:T(8,128)}, f32[4,128,2048]{2,1,0:T(8,128)}, u32[]{:S(2)}, u32[]{:S(2)}) collective-permute-start(f32[4,128,2048]{2,1,0:T(8,128)} %constant_dynamic-slice_fusion.2), channel_id=1, source_target_pairs={{0,24},{8,16},{16,8},{24,0},{1,25},{9,17},{17,9},{25,1},{2,26},{10... | collective-permute-start | bytes 12582920 | tf_op jit(solution)/shard_map/ppermute | solution.py:35
  36.7 211.5 %collective-permute-start.3 = (f32[128,2048]{1,0:T(8,128)S(1)}, f32[128,2048]{1,0:T(8,128)}, u32[]{:S(2)}, u32[]{:S(2)}) collective-permute-start(f32[128,2048]{1,0:T(8,128)S(1)} %slice.24), channel_id=1, source_target_pairs={{2,4},{4,2},{3,5},{5,3},{10,12},{12,10},{11,13},{13,11},{18,20},{2... | collective-permute-start | bytes 3145736 | tf_op jit(solution)/shard_map/ppermute | solution.py:35
  245.0 4.6 collective-permute-start.1
  246.7 134.2 %collective-permute-start.7 = (f32[4,128,2048]{2,1,0:T(8,128)}, f32[4,128,2048]{2,1,0:T(8,128)}, u32[]{:S(2)}, u32[]{:S(2)}) collective-permute-start(f32[4,128,2048]{2,1,0:T(8,128)} %constant_dynamic-slice_fusion.3), channel_id=1, source_target_pairs={{0,16},{8,24},{16,0},{24,8},{1,17},{9,25},{17,1},{25,9},{2,18},{10... | collective-permute-start | bytes 12582920 | tf_op jit(solution)/shard_map/ppermute | solution.py:35
  248.3 92.0 %collective-permute-start.4 = (f32[128,2048]{1,0:T(8,128)}, f32[128,2048]{1,0:T(8,128)}, u32[]{:S(2)}, u32[]{:S(2)}) collective-permute-start(f32[128,2048]{1,0:T(8,128)} %collective-permute-done.3), channel_id=1, source_target_pairs={{2,0},{4,6},{3,1},{5,7},{10,8},{12,14},{11,9},{13,15},{18,16},{20,... | collective-permute-start | bytes 3145736 | tf_op jit(solution)/shard_map/ppermute | solution.py:35
  249.6 113.2 %collective-permute-start.2 = (f32[128,2048]{1,0:T(8,128)}, f32[128,2048]{1,0:T(8,128)}, u32[]{:S(2)}, u32[]{:S(2)}) collective-permute-start(f32[128,2048]{1,0:T(8,128)} %collective-permute-done.1), channel_id=1, source_target_pairs={{2,0},{4,6},{3,1},{5,7},{10,8},{12,14},{11,9},{13,15},{18,16},{20,... | collective-permute-start | bytes 3145736 | tf_op jit(solution)/shard_map/ppermute | solution.py:35
  250.9 134.5 %copy-start.1 = (f32[96,2048]{1,0:T(8,128)}, f32[96,2048]{1,0:T(8,128)S(1)}, u32[]{:S(2)}) copy-start(f32[96,2048]{1,0:T(8,128)S(1)} %slice.22.v) | copy-start | bytes 2359300
  391.4 1.2 collective-permute-start.8
  392.6 3.6 collective-permute-start.9
  396.2 3.6 collective-permute-start.10
  399.8 4.5 collective-permute-start.11
  404.2 3.6 collective-permute-start.12
  413.3 14.6 %collective-permute-start.22 = (f32[64,2048]{1,0:T(8,128)}, f32[64,2048]{1,0:T(8,128)S(1)}, u32[]{:S(2)}, u32[]{:S(2)}) collective-permute-start(f32[64,2048]{1,0:T(8,128)} %shard_map.39), channel_id=1, source_target_pairs={{0,2},{6,4},{1,3},{7,5},{8,10},{14,12},{9,11},{15,13},{16,18},{22,... | collective-permute-start | bytes 1572872 | tf_op jit(solution)/shard_map/ppermute | solution.py:35
  415.3 20.6 %collective-permute-start.17 = (f32[32,2048]{1,0:T(8,128)S(1)}, f32[32,2048]{1,0:T(8,128)S(1)}, u32[]{:S(2)}, u32[]{:S(2)}) collective-permute-start(f32[32,2048]{1,0:T(8,128)S(1)} %copy-done.15), channel_id=1, source_target_pairs={{0,2},{6,4},{1,3},{7,5},{8,10},{14,12},{9,11},{15,13},{16,18},{22,... | collective-permute-start | bytes 786440 | tf_op jit(solution)/shard_map/ppermute | solution.py:35
  421.3 25.3 %collective-permute-start.16 = (f32[64,2048]{1,0:T(8,128)}, f32[64,2048]{1,0:T(8,128)}, u32[]{:S(2)}, u32[]{:S(2)}) collective-permute-start(f32[64,2048]{1,0:T(8,128)} %get-tuple-element.55), channel_id=1, source_target_pairs={{0,2},{6,4},{1,3},{7,5},{8,10},{14,12},{9,11},{15,13},{16,18},{22,... | collective-permute-start | bytes 1572872 | tf_op jit(solution)/shard_map/ppermute | solution.py:35
  428.0 27.0 %collective-permute-start.23 = (f32[64,2048]{1,0:T(8,128)S(1)}, f32[64,2048]{1,0:T(8,128)}, u32[]{:S(2)}, u32[]{:S(2)}) collective-permute-start(f32[64,2048]{1,0:T(8,128)S(1)} %add.190), channel_id=1, source_target_pairs={{2,4},{4,2},{3,5},{5,3},{10,12},{12,10},{11,13},{13,11},{18,20},{2... | collective-permute-start | bytes 1572872 | tf_op jit(solution)/shard_map/ppermute | solution.py:35
  429.4 26.6 %collective-permute-start.24 = (f32[64,2048]{1,0:T(8,128)}, f32[64,2048]{1,0:T(8,128)}, u32[]{:S(2)}, u32[]{:S(2)}) collective-permute-start(f32[64,2048]{1,0:T(8,128)} %get-tuple-element.64), channel_id=1, source_target_pairs={{0,2},{6,4},{1,3},{7,5},{8,10},{14,12},{9,11},{15,13},{16,18},{22,... | collective-permute-start | bytes 1572872 | tf_op jit(solution)/shard_map/ppermute | solution.py:35
  436.0 10.6 %collective-permute-start.18 = (f32[32,2048]{1,0:T(8,128)S(1)}, f32[32,2048]{1,0:T(8,128)S(1)}, u32[]{:S(2)}, u32[]{:S(2)}) collective-permute-start(f32[32,2048]{1,0:T(8,128)S(1)} %add.182), channel_id=1, source_target_pairs={{2,4},{4,2},{3,5},{5,3},{10,12},{12,10},{11,13},{13,11},{18,20},{2... | collective-permute-start | bytes 786440 | tf_op jit(solution)/shard_map/ppermute | solution.py:35
  446.6 21.0 %copy-start.23 = (f32[64,2048]{1,0:T(8,128)S(1)}, f32[64,2048]{1,0:T(8,128)}, u32[]{:S(2)}) copy-start(f32[64,2048]{1,0:T(8,128)} %get-tuple-element.59) | copy-start | bytes 1572868
  446.6 29.0 %copy-start.17 = (f32[64,2048]{1,0:T(8,128)S(1)}, f32[64,2048]{1,0:T(8,128)}, u32[]{:S(2)}) copy-start(f32[64,2048]{1,0:T(8,128)} %get-tuple-element.74) | copy-start | bytes 1572868
  446.6 49.1 %copy-start.13 = (f32[32,2048]{1,0:T(8,128)}, f32[32,2048]{1,0:T(8,128)S(1)}, u32[]{:S(2)}) copy-start(f32[32,2048]{1,0:T(8,128)S(1)} %add.183.refs_4_) | copy-start | bytes 786436
  447.9 16.5 %collective-permute-start.19 = (f32[64,2048]{1,0:T(8,128)S(1)}, f32[64,2048]{1,0:T(8,128)S(1)}, u32[]{:S(2)}, u32[]{:S(2)}) collective-permute-start(f32[64,2048]{1,0:T(8,128)S(1)} %add.184), channel_id=1, source_target_pairs={{2,4},{4,2},{3,5},{5,3},{10,12},{12,10},{11,13},{13,11},{18,20},{2... | collective-permute-start | bytes 1572872 | tf_op jit(solution)/shard_map/ppermute | solution.py:35
  448.6 18.9 %collective-permute-start.15 = (f32[64,2048]{1,0:T(8,128)}, f32[64,2048]{1,0:T(8,128)S(1)}, u32[]{:S(2)}, u32[]{:S(2)}) collective-permute-start(f32[64,2048]{1,0:T(8,128)} %get-tuple-element.59), channel_id=1, source_target_pairs={{0,2},{6,4},{1,3},{7,5},{8,10},{14,12},{9,11},{15,13},{16,18},{22,... | collective-permute-start | bytes 1572872 | tf_op jit(solution)/shard_map/ppermute | solution.py:35
  456.1 32.1 %copy-start.6 = (f32[64,2048]{1,0:T(8,128)}, f32[64,2048]{1,0:T(8,128)S(1)}, u32[]{:S(2)}) copy-start(f32[64,2048]{1,0:T(8,128)S(1)} %add.191.refs_5_) | copy-start | bytes 1572868
  457.4 20.3 %collective-permute-start.25 = (f32[64,2048]{1,0:T(8,128)S(1)}, f32[64,2048]{1,0:T(8,128)S(1)}, u32[]{:S(2)}, u32[]{:S(2)}) collective-permute-start(f32[64,2048]{1,0:T(8,128)S(1)} %add.192), channel_id=1, source_target_pairs={{2,4},{4,2},{3,5},{5,3},{10,12},{12,10},{11,13},{13,11},{18,20},{2... | collective-permute-start | bytes 1572872 | tf_op jit(solution)/shard_map/ppermute | solution.py:35
  458.1 20.6 %collective-permute-start.31 = (f32[64,2048]{1,0:T(8,128)S(1)}, f32[64,2048]{1,0:T(8,128)S(1)}, u32[]{:S(2)}, u32[]{:S(2)}) collective-permute-start(f32[64,2048]{1,0:T(8,128)S(1)} %copy-done.20), channel_id=1, source_target_pairs={{0,2},{6,4},{1,3},{7,5},{8,10},{14,12},{9,11},{15,13},{16,18},{22,... | collective-permute-start | bytes 1572872 | tf_op jit(solution)/shard_map/ppermute | solution.py:35
  464.5 25.1 %copy-start.7 = (f32[64,2048]{1,0:T(8,128)}, f32[64,2048]{1,0:T(8,128)S(1)}, u32[]{:S(2)}) copy-start(f32[64,2048]{1,0:T(8,128)S(1)} %add.185.refs_6_) | copy-start | bytes 1572868
  467.6 22.0 %collective-permute-start.20 = (f32[64,2048]{1,0:T(8,128)S(1)}, f32[64,2048]{1,0:T(8,128)}, u32[]{:S(2)}, u32[]{:S(2)}) collective-permute-start(f32[64,2048]{1,0:T(8,128)S(1)} %add.186), channel_id=1, source_target_pairs={{2,4},{4,2},{3,5},{5,3},{10,12},{12,10},{11,13},{13,11},{18,20},{2... | collective-permute-start | bytes 1572872 | tf_op jit(solution)/shard_map/ppermute | solution.py:35
  469.1 22.9 %collective-permute-start.14 = (f32[64,2048]{1,0:T(8,128)}, f32[64,2048]{1,0:T(8,128)}, u32[]{:S(2)}, u32[]{:S(2)}) collective-permute-start(f32[64,2048]{1,0:T(8,128)} %get-tuple-element.58), channel_id=1, source_target_pairs={{0,2},{6,4},{1,3},{7,5},{8,10},{14,12},{9,11},{15,13},{16,18},{22,... | collective-permute-start | bytes 1572872 | tf_op jit(solution)/shard_map/ppermute | solution.py:35
  475.6 20.1 %collective-permute-start.36 = (f32[64,2048]{1,0:T(8,128)S(1)}, f32[64,2048]{1,0:T(8,128)}, u32[]{:S(2)}, u32[]{:S(2)}) collective-permute-start(f32[64,2048]{1,0:T(8,128)S(1)} %copy-done.17), channel_id=1, source_target_pairs={{0,2},{6,4},{1,3},{7,5},{8,10},{14,12},{9,11},{15,13},{16,18},{22,... | collective-permute-start | bytes 1572872 | tf_op jit(solution)/shard_map/ppermute | solution.py:35
  477.8 19.2 %copy-start.8 = (f32[64,2048]{1,0:T(8,128)}, f32[64,2048]{1,0:T(8,128)S(1)}, u32[]{:S(2)}) copy-start(f32[64,2048]{1,0:T(8,128)S(1)} %add.193.refs_7_) | copy-start | bytes 1572868
  478.8 18.2 %collective-permute-start.32 = (f32[64,2048]{1,0:T(8,128)S(1)}, f32[64,2048]{1,0:T(8,128)}, u32[]{:S(2)}, u32[]{:S(2)}) collective-permute-start(f32[64,2048]{1,0:T(8,128)S(1)} %add.196), channel_id=1, source_target_pairs={{2,4},{4,2},{3,5},{5,3},{10,12},{12,10},{11,13},{13,11},{18,20},{2... | collective-permute-start | bytes 1572872 | tf_op jit(solution)/shard_map/ppermute | solution.py:35
  488.2 36.4 %collective-permute-start.27 = (f32[64,2048]{1,0:T(8,128)S(1)}, f32[64,2048]{1,0:T(8,128)S(1)}, u32[]{:S(2)}, u32[]{:S(2)}) collective-permute-start(f32[64,2048]{1,0:T(8,128)S(1)} %add.191.refs_5_), channel_id=1, source_target_pairs={{2,0},{4,6},{3,1},{5,7},{10,8},{12,14},{11,9},{13,15},{18,16},{20,... | collective-permute-start | bytes 1572872 | tf_op jit(solution)/shard_map/ppermute | solution.py:35
  489.6 38.0 %collective-permute-start.28 = (f32[64,2048]{1,0:T(8,128)S(1)}, f32[64,2048]{1,0:T(8,128)S(1)}, u32[]{:S(2)}, u32[]{:S(2)}) collective-permute-start(f32[64,2048]{1,0:T(8,128)S(1)} %add.185.refs_6_), channel_id=1, source_target_pairs={{2,0},{4,6},{3,1},{5,7},{10,8},{12,14},{11,9},{13,15},{18,16},{20,... | collective-permute-start | bytes 1572872 | tf_op jit(solution)/shard_map/ppermute | solution.py:35
  492.0 50.5 %copy-start.10 = (f32[64,2048]{1,0:T(8,128)}, f32[64,2048]{1,0:T(8,128)S(1)}, u32[]{:S(2)}) copy-start(f32[64,2048]{1,0:T(8,128)S(1)} %add.187.refs_4_) | copy-start | bytes 1572868
  493.5 35.4 %collective-permute-start.21 = (f32[64,2048]{1,0:T(8,128)S(1)}, f32[64,2048]{1,0:T(8,128)S(1)}, u32[]{:S(2)}, u32[]{:S(2)}) collective-permute-start(f32[64,2048]{1,0:T(8,128)S(1)} %add.188), channel_id=1, source_target_pairs={{2,4},{4,2},{3,5},{5,3},{10,12},{12,10},{11,13},{13,11},{18,20},{2... | collective-permute-start | bytes 1572872 | tf_op jit(solution)/shard_map/ppermute | solution.py:35
  495.7 27.4 %collective-permute-start.26 = (f32[32,2048]{1,0:T(8,128)S(1)}, f32[32,2048]{1,0:T(8,128)S(1)}, u32[]{:S(2)}, u32[]{:S(2)}) collective-permute-start(f32[32,2048]{1,0:T(8,128)S(1)} %add.183.refs_4_), channel_id=1, source_target_pairs={{2,0},{4,6},{3,1},{5,7},{10,8},{12,14},{11,9},{13,15},{18,16},{20,... | collective-permute-start | bytes 786440 | tf_op jit(solution)/shard_map/ppermute | solution.py:35
  497.0 37.4 %collective-permute-start.29 = (f32[64,2048]{1,0:T(8,128)S(1)}, f32[64,2048]{1,0:T(8,128)}, u32[]{:S(2)}, u32[]{:S(2)}) collective-permute-start(f32[64,2048]{1,0:T(8,128)S(1)} %add.193.refs_7_), channel_id=1, source_target_pairs={{2,0},{4,6},{3,1},{5,7},{10,8},{12,14},{11,9},{13,15},{18,16},{20,... | collective-permute-start | bytes 1572872 | tf_op jit(solution)/shard_map/ppermute | solution.py:35
  499.4 43.0 %copy-start.11 = (f32[64,2048]{1,0:T(8,128)}, f32[64,2048]{1,0:T(8,128)S(1)}, u32[]{:S(2)}) copy-start(f32[64,2048]{1,0:T(8,128)S(1)} %add.197.refs_5_) | copy-start | bytes 1572868
  523.1 22.4 %collective-permute-start.37 = (f32[64,2048]{1,0:T(8,128)S(1)}, f32[64,2048]{1,0:T(8,128)}, u32[]{:S(2)}, u32[]{:S(2)}) collective-permute-start(f32[64,2048]{1,0:T(8,128)S(1)} %add.198), channel_id=1, source_target_pairs={{2,4},{4,2},{3,5},{5,3},{10,12},{12,10},{11,13},{13,11},{18,20},{2... | collective-permute-start | bytes 1572872 | tf_op jit(solution)/shard_map/ppermute | solution.py:35
  524.5 17.9 %collective-permute-start.13 = (f32[32,2048]{1,0:T(8,128)}, f32[32,2048]{1,0:T(8,128)S(1)}, u32[]{:S(2)}, u32[]{:S(2)}) collective-permute-start(f32[32,2048]{1,0:T(8,128)} %get-tuple-element.57), channel_id=1, source_target_pairs={{0,2},{6,4},{1,3},{7,5},{8,10},{14,12},{9,11},{15,13},{16,18},{22,... | collective-permute-start | bytes 786440 | tf_op jit(solution)/shard_map/ppermute | solution.py:35
  527.6 20.4 %collective-permute-start.33 = (f32[64,2048]{1,0:T(8,128)S(1)}, f32[64,2048]{1,0:T(8,128)}, u32[]{:S(2)}, u32[]{:S(2)}) collective-permute-start(f32[64,2048]{1,0:T(8,128)S(1)} %add.187.refs_4_), channel_id=1, source_target_pairs={{2,0},{4,6},{3,1},{5,7},{10,8},{12,14},{11,9},{13,15},{18,16},{20,... | collective-permute-start | bytes 1572872 | tf_op jit(solution)/shard_map/ppermute | solution.py:35
  529.7 27.1 %collective-permute-start.34 = (f32[64,2048]{1,0:T(8,128)S(1)}, f32[64,2048]{1,0:T(8,128)}, u32[]{:S(2)}, u32[]{:S(2)}) collective-permute-start(f32[64,2048]{1,0:T(8,128)S(1)} %add.197.refs_5_), channel_id=1, source_target_pairs={{2,0},{4,6},{3,1},{5,7},{10,8},{12,14},{11,9},{13,15},{18,16},{20,... | collective-permute-start | bytes 1572872 | tf_op jit(solution)/shard_map/ppermute | solution.py:35
  543.5 4.4 collective-permute-start.30
  544.2 21.2 %collective-permute-start.38 = (f32[64,2048]{1,0:T(8,128)}, f32[64,2048]{1,0:T(8,128)}, u32[]{:S(2)}, u32[]{:S(2)}) collective-permute-start(f32[64,2048]{1,0:T(8,128)} %add.189.refs_4_), channel_id=1, source_target_pairs={{2,0},{4,6},{3,1},{5,7},{10,8},{12,14},{11,9},{13,15},{18,16},{20,... | collective-permute-start | bytes 1572872 | tf_op jit(solution)/shard_map/ppermute | solution.py:35
  546.6 24.3 %collective-permute-start.39 = (f32[64,2048]{1,0:T(8,128)S(1)}, f32[64,2048]{1,0:T(8,128)S(1)}, u32[]{:S(2)}, u32[]{:S(2)}) collective-permute-start(f32[64,2048]{1,0:T(8,128)S(1)} %add.199.refs_5_), channel_id=1, source_target_pairs={{2,0},{4,6},{3,1},{5,7},{10,8},{12,14},{11,9},{13,15},{18,16},{20,... | collective-permute-start | bytes 1572872 | tf_op jit(solution)/shard_map/ppermute | solution.py:35
  561.9 14.7 %collective-permute-start.35 = (f32[32,2048]{1,0:T(8,128)S(1)}, f32[32,2048]{1,0:T(8,128)S(1)}, u32[]{:S(2)}, u32[]{:S(2)}) collective-permute-start(f32[32,2048]{1,0:T(8,128)S(1)} %add.195.refs_4_), channel_id=1, source_target_pairs={{2,0},{4,6},{3,1},{5,7},{10,8},{12,14},{11,9},{13,15},{18,16},{20,... | collective-permute-start | bytes 786440 | tf_op jit(solution)/shard_map/ppermute | solution.py:35
  580.5 1.2 collective-permute-start.40
  581.7 3.6 collective-permute-start.41
  585.3 3.6 collective-permute-start.42
  588.8 4.5 collective-permute-start.43
  593.3 3.6 collective-permute-start.44
  601.9 25.8 %collective-permute-start.45 = (f32[128,2048]{1,0:T(8,128)}, f32[128,2048]{1,0:T(8,128)}, u32[]{:S(2)}, u32[]{:S(2)}) collective-permute-start(f32[128,2048]{1,0:T(8,128)} %shard_map.46), channel_id=1, source_target_pairs={{0,2},{6,4},{1,3},{7,5},{8,10},{14,12},{9,11},{15,13},{16,18},{22,... | collective-permute-start | bytes 3145736 | tf_op jit(solution)/shard_map/ppermute | solution.py:35
  605.5 22.2 %copy-start.3 = (f32[128,2048]{1,0:T(8,128)S(1)}, f32[128,2048]{1,0:T(8,128)}, u32[]{:S(2)}) copy-start(f32[128,2048]{1,0:T(8,128)} %shard_map.46) | copy-start | bytes 3145732
  618.0 34.5 %copy-start.4 = (f32[128,2048]{1,0:T(8,128)S(1)}, f32[128,2048]{1,0:T(8,128)}, u32[]{:S(2)}) copy-start(f32[128,2048]{1,0:T(8,128)} %get-tuple-element.82) | copy-start | bytes 3145732
  618.0 36.0 %copy-start.5 = (f32[96,2048]{1,0:T(8,128)S(1)}, f32[96,2048]{1,0:T(8,128)}, u32[]{:S(2)}) copy-start(f32[96,2048]{1,0:T(8,128)} %get-tuple-element.51) | copy-start | bytes 2359300
  618.0 32.1 %collective-permute-start.49 = (f32[128,2048]{1,0:T(8,128)}, f32[128,2048]{1,0:T(8,128)}, u32[]{:S(2)}, u32[]{:S(2)}) collective-permute-start(f32[128,2048]{1,0:T(8,128)} %get-tuple-element.84), channel_id=1, source_target_pairs={{0,2},{6,4},{1,3},{7,5},{8,10},{14,12},{9,11},{15,13},{16,18},{22,... | collective-permute-start | bytes 3145736 | tf_op jit(solution)/shard_map/ppermute | solution.py:35
  630.0 22.5 %collective-permute-start.46 = (f32[128,2048]{1,0:T(8,128)}, f32[128,2048]{1,0:T(8,128)S(1)}, u32[]{:S(2)}, u32[]{:S(2)}) collective-permute-start(f32[128,2048]{1,0:T(8,128)} %add.209), channel_id=1, source_target_pairs={{2,4},{4,2},{3,5},{5,3},{10,12},{12,10},{11,13},{13,11},{18,20},{2... | collective-permute-start | bytes 3145736 | tf_op jit(solution)/shard_map/ppermute | solution.py:35
  630.7 36.8 %collective-permute-start.48 = (f32[128,2048]{1,0:T(8,128)}, f32[128,2048]{1,0:T(8,128)S(1)}, u32[]{:S(2)}, u32[]{:S(2)}) collective-permute-start(f32[128,2048]{1,0:T(8,128)} %get-tuple-element.83), channel_id=1, source_target_pairs={{0,2},{6,4},{1,3},{7,5},{8,10},{14,12},{9,11},{15,13},{16,18},{22,... | collective-permute-start | bytes 3145736 | tf_op jit(solution)/shard_map/ppermute | solution.py:35
  651.8 15.7 %collective-permute-start.50 = (f32[128,2048]{1,0:T(8,128)S(1)}, f32[128,2048]{1,0:T(8,128)S(1)}, u32[]{:S(2)}, u32[]{:S(2)}) collective-permute-start(f32[128,2048]{1,0:T(8,128)S(1)} %add.213), channel_id=1, source_target_pairs={{2,4},{4,2},{3,5},{5,3},{10,12},{12,10},{11,13},{13,11},{18,20},{2... | collective-permute-start | bytes 3145736 | tf_op jit(solution)/shard_map/ppermute | solution.py:35
  652.7 18.9 %collective-permute-start.47 = (f32[128,2048]{1,0:T(8,128)S(1)}, f32[128,2048]{1,0:T(8,128)S(1)}, u32[]{:S(2)}, u32[]{:S(2)}) collective-permute-start(f32[128,2048]{1,0:T(8,128)S(1)} %add.210), channel_id=1, source_target_pairs={{2,0},{4,6},{3,1},{5,7},{10,8},{12,14},{11,9},{13,15},{18,16},{20,... | collective-permute-start | bytes 3145736 | tf_op jit(solution)/shard_map/ppermute | solution.py:35
  (19 other events, 143.9 us)

commit v8 on v7

--- a/solution.py
+++ b/solution.py
@@ -283,7 +283,7 @@
     flat_v = line_v.reshape(outers * rest, columns)
     end_flag = is_end.astype(jnp.int32).reshape(1)
     next_spread_v, spread_sq = move_spread(share, factor, spread, spread_v)
-    early = {4: next_spread_v}
+    early = {2: next_spread_v}
     count, places = len(sizes), begins(sizes)
     own = step_chunks(line_factor, flat, flat_v, 0, sizes[:1])
     own += step_chunks(line_factor, flat, tie(flat_v, own[0]), places[1], sizes[1:2])
@@ -307,12 +307,10 @@
         total = total + send(total, ACROSS)
         if chunk in early:
             total = tie(total, early[chunk])
-        if chunk in (count - 3, count - 1):
-            carried = move(groups[chunk == count - 1], carried)
-            total = tie(total, carried[1])
         totals.append(total)
         backs.append(send(total, TO_ENDS))
-    for part in groups[2:]:
+    carried = move(groups[0], carried)
+    for part in groups[1:]:
         carried = move(part, carried)
     spread_v = next_spread_v
     flat_v = carried[0]

time: 677 us -> 688 us (1.016)
  waiting for transfers between devices: 423 us -> 440 us
    ppermute x41, waiting for transfers between devices: 398 us -> 415 us  [send(): return lax.ppermute(value, axis, pairs)]
  transfers between devices with their start and end apart: 52 -> 52, of which waited for: 26 -> 28; matrix products, arithmetic and copies ran while one was open for 9% -> 8% of each run, Pallas kernels for 8% -> 8%
where the time goes in v8:
time: 688 us; the launch traced here: 685 us
  waiting for transfers between devices  440 us (64%)
  starting transfers between devices  98.9 us (14%)
  Pallas kernels  63.8 us (9%)
  other arithmetic  52.1 us (8%)
  local copies, waits for them, and re-layouts  28.7 us (4%)
    ppermute x41, waiting for transfers between devices, send(): return lax.ppermute(value, axis, pairs)  415 us
    ppermute x41, starting transfers between devices, send(): return lax.ppermute(value, axis, pairs)  84.5 us
    pallas_call x11, Pallas kernels, run(): pl.pallas_call(kernel, grid_spec=pltpu.PrefetchScalarGridSpec(num_scalar_...  63.8 us
    ppermute x10, waiting for transfers between devices, sum_over_devices(): lax.ppermute(value, axis, [(i, i ^ step) for i in range(size)])  25.2 us
    reduce_sum x4, other arithmetic, on_device(): square = jnp.sum(jnp.square(held[place] - v))  17.6 us
    dynamic_slice x3, local copies, waits for them, and re-layouts, line_rows(): lax.dynamic_slice(source, (worker * outers, cut, 0), (outers, rest, colum...  14.1 us
  transfers between devices with their start and end apart: 52, of which 28 were waited for; matrix products, arithmetic and copies ran while one was open for 8% of the time, Pallas kernels for 8%

profile of v8, /device:TPU:0, one launch (start us, length us, event | category | flops | bytes accessed | tf_op | source)
XLA Modules:
  0.0 685.0 jit_solution(14073150531378173080)
XLA Ops:
  0.0 11.5 %slice.28 = f32[16,96,2048]{2,1,0:T(8,128)} slice(f32[16,224,2048]{2,1,0:T(8,128)} %bitcast.62), slice={[0:16], [0:96], [0:2048]} | slice | bytes 25165824 | tf_op jit(solution)/shard_map/slice | solution.py:251
  11.5 7.6 %all-to-all-start = ((f32[16,96,2048]{2,1,0:T(8,128)}), f32[16,96,2048]{2,1,0:T(8,128)}, u32[]{:S(2)}, u32[]{:S(2)}) async-start(f32[16,96,2048]{2,1,0:T(8,128)} %slice.28), calls=%async_computation | async-start | bytes 25165824 | tf_op jit(solution)/shard_map/all_to_all | solution.py:250
  19.2 1.9 collective-permute-start
  21.1 4.6 constant_dynamic-slice_fusion.3
  25.7 4.7 constant_dynamic-slice_fusion.2
  30.5 4.7 constant_dynamic-slice_fusion.1
  36.7 1.6 collective-permute-start.3
  38.4 206.6 %collective-permute-done = f32[128,2048]{1,0:T(8,128)} collective-permute-done((f32[128,2048]{1,0:T(8,128)S(1)}, f32[128,2048]{1,0:T(8,128)}, u32[]{:S(2)}, u32[]{:S(2)}) %collective-permute-start) | collective-permute-done | bytes 1048608 | tf_op jit(solution)/shard_map/ppermute | solution.py:35
  245.0 1.7 collective-permute-start.1
  246.7 1.6 collective-permute-start.7
  251.2 89.2 %collective-permute-done.4 = f32[128,2048]{1,0:T(8,128)} collective-permute-done((f32[128,2048]{1,0:T(8,128)}, f32[128,2048]{1,0:T(8,128)}, u32[]{:S(2)}, u32[]{:S(2)}) %collective-permute-start.4) | collective-permute-done | bytes 1048608 | tf_op jit(solution)/shard_map/ppermute | solution.py:35
  340.3 22.5 %collective-permute-done.2 = f32[128,2048]{1,0:T(8,128)} collective-permute-done((f32[128,2048]{1,0:T(8,128)}, f32[128,2048]{1,0:T(8,128)}, u32[]{:S(2)}, u32[]{:S(2)}) %collective-permute-start.2) | collective-permute-done | bytes 1048608 | tf_op jit(solution)/shard_map/ppermute | solution.py:35
  362.8 2.5 select_bitcast_fusion.3
  365.3 4.9 multiply_reduce_fusion.5
  370.8 4.8 multiply_reduce_fusion.4
  376.3 3.9 multiply_reduce_fusion.3
  380.9 3.9 multiply_reduce_fusion.2
  385.5 6.0 multiply_reduce_fusion.1
  394.1 2.1 collective-permute-done.9
  396.2 3.6 collective-permute-done.10
  400.9 3.4 collective-permute-done.11
  405.8 2.0 collective-permute-done.12
  408.6 2.1 shard_map.38
  410.7 2.6 shard_map.39
  413.4 2.1 collective-permute-start.27
  416.7 4.7 shard_map.40
  422.7 10.8 %collective-permute-done.17 = f32[32,2048]{1,0:T(8,128)S(1)} collective-permute-done((f32[32,2048]{1,0:T(8,128)S(1)}, f32[32,2048]{1,0:T(8,128)S(1)}, u32[]{:S(2)}, u32[]{:S(2)}) %collective-permute-start.17) | collective-permute-done | bytes 262176 | tf_op jit(solution)/shard_map/ppermute | solution.py:35
  435.0 8.9 %collective-permute-start.26 = (f32[64,2048]{1,0:T(8,128)}, f32[64,2048]{1,0:T(8,128)S(1)}, u32[]{:S(2)}, u32[]{:S(2)}) collective-permute-start(f32[64,2048]{1,0:T(8,128)} %get-tuple-element.65), channel_id=1, source_target_pairs={{0,2},{6,4},{1,3},{7,5},{8,10},{14,12},{9,11},{15,13},{16,18},{22,... | collective-permute-start | bytes 1572872 | tf_op jit(solution)/shard_map/ppermute | solution.py:35
  446.0 1.7 collective-permute-start.19
  447.6 9.4 %shard_map.41 = (f32[64,2048]{1,0:T(8,128)}, f32[64,2048]{1,0:T(8,128)}, f32[64,2048]{1,0:T(8,128)}, f32[64,2048]{1,0:T(8,128)}, f32[32,2048]{1,0:T(8,128)}) custom-call(f32[4]{0:T(128)} %select_reduce_fusion.2.factor, f32[512,2048]{1,0:T(8,128)} %bitcast.16.refs_0_, f32[512,2048]{1,0:T(8,128)} %bitcast.17.refs_1_, f32[512,2048]{1,0:T(8,128)} %bitcast.18.refs_2_, ...), custom_call_target="tpu_custom_call" | custom-call | flops 14155776 | bytes 14155776 | tf_op jit(solution)/shard_map/pallas_call | solution.py:61
  457.0 6.7 collective-permute-start.15
  465.3 2.9 collective-permute-start.25
  468.3 7.9 %shard_map.37 = (f32[96,2048]{1,0:T(8,128)}, f32[16,8,128]{2,1,0:T(8,128)}) custom-call(f32[16]{0:T(128)} %copy-done.29, f32[96,2048]{1,0:T(8,128)} %copy-done.1, f32[16,96,2048]{2,1,0:T(8,128)} %all-to-all-done.values), custom_call_target="tpu_custom_call" | custom-call | flops 14155776 | bytes 14155776 | tf_op jit(solution)/shard_map/pallas_call | solution.py:61
  479.4 2.7 collective-permute-start.14
  485.3 3.6 collective-permute-start.24
  489.0 3.2 collective-permute-done.14
  494.6 3.7 collective-permute-done.24
  499.1 9.7 %collective-permute-start.13 = (f32[32,2048]{1,0:T(8,128)S(1)}, f32[32,2048]{1,0:T(8,128)S(1)}, u32[]{:S(2)}, u32[]{:S(2)}) collective-permute-start(f32[32,2048]{1,0:T(8,128)S(1)} %copy-done.27), channel_id=1, source_target_pairs={{0,2},{6,4},{1,3},{7,5},{8,10},{14,12},{9,11},{15,13},{16,18},{22,... | collective-permute-start | bytes 786440 | tf_op jit(solution)/shard_map/ppermute | solution.py:35
  513.3 13.3 %collective-permute-done.36.refs_8_ = f32[32,2048]{1,0:T(8,128)} collective-permute-done((f32[32,2048]{1,0:T(8,128)S(1)}, f32[32,2048]{1,0:T(8,128)}, u32[]{:S(2)}, u32[]{:S(2)}) %collective-permute-start.36) | collective-permute-done | bytes 262176 | tf_op jit(solution)/shard_map/ppermute | solution.py:35
  533.3 10.0 %collective-permute-done.39.refs_11_ = f32[64,2048]{1,0:T(8,128)S(1)} collective-permute-done((f32[64,2048]{1,0:T(8,128)S(1)}, f32[64,2048]{1,0:T(8,128)S(1)}, u32[]{:S(2)}, u32[]{:S(2)}) %collective-permute-start.39) | collective-permute-done | bytes 524320 | tf_op jit(solution)/shard_map/ppermute | solution.py:35
  545.6 8.1 %shard_map.42 = (f32[512,2048]{1,0:T(8,128)}, f32[4,8,128]{2,1,0:T(8,128)}) custom-call(s32[1]{0:T(128)} %bitcast.14.is_end, f32[512,2048]{1,0:T(8,128)} %bitcast.47, f32[512,2048]{1,0:T(8,128)} %bitcast.16.refs_0_, f32[512,2048]{1,0:T(8,128)} %bitcast.17.refs_1_, f32[512,2048]{1,0:T(8,128)} %bitcast.18.refs_2_, f32[512,2048]{1,0:T(8,128)} %bitcast.55, ...), custom_call_target="tpu_custom_call" | custom-call | flops 14680064 | bytes 14680064 | tf_op jit(solution)/shard_map/pallas_call | solution.py:61
  554.6 11.2 %collective-permute-done.35.refs_7_ = f32[64,2048]{1,0:T(8,128)} collective-permute-done((f32[64,2048]{1,0:T(8,128)S(1)}, f32[64,2048]{1,0:T(8,128)}, u32[]{:S(2)}, u32[]{:S(2)}) %collective-permute-start.35) | collective-permute-done | bytes 524320 | tf_op jit(solution)/shard_map/ppermute | solution.py:35
  565.8 4.9 shard_map.43
  570.8 5.9 collective-permute-done.32.refs_6_
  576.7 5.6 collective-permute-done.33.refs_7_
  582.3 4.9 shard_map.44
  588.0 2.2 shard_map.45
  593.8 2.1 collective-permute-done.41
  595.9 3.6 collective-permute-done.42
  599.9 4.1 collective-permute-done.43
  605.5 2.0 collective-permute-done.44
  608.3 4.4 shard_map.46
  612.6 2.9 collective-permute-start.45
  616.1 12.5 %shard_map.47 = (f32[128,2048]{1,0:T(8,128)}, f32[128,2048]{1,0:T(8,128)}, f32[128,2048]{1,0:T(8,128)}) custom-call(s32[3]{0:T(128)} %pad_add_fusion.1.places, f32[4]{0:T(128)} %select_reduce_fusion.factor, f32[4,128,2048]{2,1,0:T(8,128)} %collective-permute-done.7.refs_0_, f32[4,128,2048]{2,1,0:T(8,128)} %collective-permute-done.6.refs_1_, ...), custom_call_target="tpu_custom_call" | custom-call | flops 18874368 | bytes 18874368 | tf_op jit(solution)/shard_map/pallas_call | solution.py:61
  628.7 2.4 collective-permute-start.49
  631.1 7.3 %collective-permute-done.45 = f32[128,2048]{1,0:T(8,128)} collective-permute-done((f32[128,2048]{1,0:T(8,128)}, f32[128,2048]{1,0:T(8,128)}, u32[]{:S(2)}, u32[]{:S(2)}) %collective-permute-start.45) | collective-permute-done | bytes 1048608 | tf_op jit(solution)/shard_map/ppermute | solution.py:35
  638.4 2.3 add.209
  641.4 6.6 collective-permute-start.48
  648.0 12.8 %collective-permute-done.49 = f32[128,2048]{1,0:T(8,128)} collective-permute-done((f32[128,2048]{1,0:T(8,128)}, f32[128,2048]{1,0:T(8,128)}, u32[]{:S(2)}, u32[]{:S(2)}) %collective-permute-start.49) | collective-permute-done | bytes 1048608 | tf_op jit(solution)/shard_map/ppermute | solution.py:35
  660.9 1.7 add.213
  664.7 6.4 multiply_reduce_fusion
  672.7 5.5 collective-permute-done.48
  678.2 4.0 collective-permute-done.47
  682.2 2.7 fusion
  (172 shorter events, 55.7 us)
Async XLA Ops:
  11.5 374.0 %all-to-all-start = ((f32[16,96,2048]{2,1,0:T(8,128)}), f32[16,96,2048]{2,1,0:T(8,128)}, u32[]{:S(2)}, u32[]{:S(2)}) async-start(f32[16,96,2048]{2,1,0:T(8,128)} %slice.28), calls=%async_computation | async-start | bytes 25165824 | tf_op jit(solution)/shard_map/all_to_all | solution.py:250
  19.2 225.8 %collective-permute-start = (f32[128,2048]{1,0:T(8,128)S(1)}, f32[128,2048]{1,0:T(8,128)}, u32[]{:S(2)}, u32[]{:S(2)}) collective-permute-start(f32[128,2048]{1,0:T(8,128)S(1)} %slice.24), channel_id=1, source_target_pairs={{0,2},{2,0},{4,6},{6,4},{1,3},{3,1},{5,7},{7,5},{8,10},{10,8},{12,... | collective-permute-start | bytes 3145736 | tf_op jit(solution)/shard_map/ppermute | solution.py:35
  35.2 335.7 %collective-permute-start.5 = (f32[4,128,2048]{2,1,0:T(8,128)}, f32[4,128,2048]{2,1,0:T(8,128)}, u32[]{:S(2)}, u32[]{:S(2)}) collective-permute-start(f32[4,128,2048]{2,1,0:T(8,128)} %constant_dynamic-slice_fusion.1), channel_id=1, source_target_pairs={{0,8},{8,0},{16,24},{24,16},{1,9},{9,1},{17,25},{25,17},{2,10},{10... | collective-permute-start | bytes 12582920 | tf_op jit(solution)/shard_map/ppermute | solution.py:35
  35.2 341.2 %collective-permute-start.6 = (f32[4,128,2048]{2,1,0:T(8,128)}, f32[4,128,2048]{2,1,0:T(8,128)}, u32[]{:S(2)}, u32[]{:S(2)}) collective-permute-start(f32[4,128,2048]{2,1,0:T(8,128)} %constant_dynamic-slice_fusion.2), channel_id=1, source_target_pairs={{0,24},{8,16},{16,8},{24,0},{1,25},{9,17},{17,9},{25,1},{2,26},{10... | collective-permute-start | bytes 12582920 | tf_op jit(solution)/shard_map/ppermute | solution.py:35
  36.7 211.6 %collective-permute-start.3 = (f32[128,2048]{1,0:T(8,128)S(1)}, f32[128,2048]{1,0:T(8,128)}, u32[]{:S(2)}, u32[]{:S(2)}) collective-permute-start(f32[128,2048]{1,0:T(8,128)S(1)} %slice.24), channel_id=1, source_target_pairs={{2,4},{4,2},{3,5},{5,3},{10,12},{12,10},{11,13},{13,11},{18,20},{2... | collective-permute-start | bytes 3145736 | tf_op jit(solution)/shard_map/ppermute | solution.py:35
  245.0 4.6 collective-permute-start.1
  246.7 134.2 %collective-permute-start.7 = (f32[4,128,2048]{2,1,0:T(8,128)}, f32[4,128,2048]{2,1,0:T(8,128)}, u32[]{:S(2)}, u32[]{:S(2)}) collective-permute-start(f32[4,128,2048]{2,1,0:T(8,128)} %constant_dynamic-slice_fusion.3), channel_id=1, source_target_pairs={{0,16},{8,24},{16,0},{24,8},{1,17},{9,25},{17,1},{25,9},{2,18},{10... | collective-permute-start | bytes 12582920 | tf_op jit(solution)/shard_map/ppermute | solution.py:35
  248.3 92.0 %collective-permute-start.4 = (f32[128,2048]{1,0:T(8,128)}, f32[128,2048]{1,0:T(8,128)}, u32[]{:S(2)}, u32[]{:S(2)}) collective-permute-start(f32[128,2048]{1,0:T(8,128)} %collective-permute-done.3), channel_id=1, source_target_pairs={{2,0},{4,6},{3,1},{5,7},{10,8},{12,14},{11,9},{13,15},{18,16},{20,... | collective-permute-start | bytes 3145736 | tf_op jit(solution)/shard_map/ppermute | solution.py:35
  249.6 113.2 %collective-permute-start.2 = (f32[128,2048]{1,0:T(8,128)}, f32[128,2048]{1,0:T(8,128)}, u32[]{:S(2)}, u32[]{:S(2)}) collective-permute-start(f32[128,2048]{1,0:T(8,128)} %collective-permute-done.1), channel_id=1, source_target_pairs={{2,0},{4,6},{3,1},{5,7},{10,8},{12,14},{11,9},{13,15},{18,16},{20,... | collective-permute-start | bytes 3145736 | tf_op jit(solution)/shard_map/ppermute | solution.py:35
  251.0 134.5 %copy-start.1 = (f32[96,2048]{1,0:T(8,128)}, f32[96,2048]{1,0:T(8,128)S(1)}, u32[]{:S(2)}) copy-start(f32[96,2048]{1,0:T(8,128)S(1)} %slice.22.v) | copy-start | bytes 2359300
  391.5 1.2 collective-permute-start.8
  392.7 3.6 collective-permute-start.9
  396.2 3.6 collective-permute-start.10
  399.8 4.5 collective-permute-start.11
  404.3 3.6 collective-permute-start.12
  413.4 20.9 %collective-permute-start.27 = (f32[64,2048]{1,0:T(8,128)}, f32[64,2048]{1,0:T(8,128)S(1)}, u32[]{:S(2)}, u32[]{:S(2)}) collective-permute-start(f32[64,2048]{1,0:T(8,128)} %shard_map.39), channel_id=1, source_target_pairs={{0,2},{6,4},{1,3},{7,5},{8,10},{14,12},{9,11},{15,13},{16,18},{22,... | collective-permute-start | bytes 1572872 | tf_op jit(solution)/shard_map/ppermute | solution.py:35
  415.4 18.1 %collective-permute-start.17 = (f32[32,2048]{1,0:T(8,128)S(1)}, f32[32,2048]{1,0:T(8,128)S(1)}, u32[]{:S(2)}, u32[]{:S(2)}) collective-permute-start(f32[32,2048]{1,0:T(8,128)S(1)} %copy-done.16), channel_id=1, source_target_pairs={{0,2},{6,4},{1,3},{7,5},{8,10},{14,12},{9,11},{15,13},{16,18},{22,... | collective-permute-start | bytes 786440 | tf_op jit(solution)/shard_map/ppermute | solution.py:35
  421.4 23.4 %collective-permute-start.16 = (f32[64,2048]{1,0:T(8,128)}, f32[64,2048]{1,0:T(8,128)S(1)}, u32[]{:S(2)}, u32[]{:S(2)}) collective-permute-start(f32[64,2048]{1,0:T(8,128)} %get-tuple-element.53), channel_id=1, source_target_pairs={{0,2},{6,4},{1,3},{7,5},{8,10},{14,12},{9,11},{15,13},{16,18},{22,... | collective-permute-start | bytes 1572872 | tf_op jit(solution)/shard_map/ppermute | solution.py:35
  433.6 10.4 %collective-permute-start.18 = (f32[32,2048]{1,0:T(8,128)S(1)}, f32[32,2048]{1,0:T(8,128)S(1)}, u32[]{:S(2)}, u32[]{:S(2)}) collective-permute-start(f32[32,2048]{1,0:T(8,128)S(1)} %add.182), channel_id=1, source_target_pairs={{2,4},{4,2},{3,5},{5,3},{10,12},{12,10},{11,13},{13,11},{18,20},{2... | collective-permute-start | bytes 786440 | tf_op jit(solution)/shard_map/ppermute | solution.py:35
  434.3 29.4 %collective-permute-start.28 = (f32[64,2048]{1,0:T(8,128)S(1)}, f32[64,2048]{1,0:T(8,128)S(1)}, u32[]{:S(2)}, u32[]{:S(2)}) collective-permute-start(f32[64,2048]{1,0:T(8,128)S(1)} %add.192), channel_id=1, source_target_pairs={{2,4},{4,2},{3,5},{5,3},{10,12},{12,10},{11,13},{13,11},{18,20},{2... | collective-permute-start | bytes 1572872 | tf_op jit(solution)/shard_map/ppermute | solution.py:35
  435.0 28.8 %collective-permute-start.26 = (f32[64,2048]{1,0:T(8,128)}, f32[64,2048]{1,0:T(8,128)S(1)}, u32[]{:S(2)}, u32[]{:S(2)}) collective-permute-start(f32[64,2048]{1,0:T(8,128)} %get-tuple-element.65), channel_id=1, source_target_pairs={{0,2},{6,4},{1,3},{7,5},{8,10},{14,12},{9,11},{15,13},{16,18},{22,... | collective-permute-start | bytes 1572872 | tf_op jit(solution)/shard_map/ppermute | solution.py:35
  444.0 66.1 %copy-start.14 = (f32[32,2048]{1,0:T(8,128)}, f32[32,2048]{1,0:T(8,128)S(1)}, u32[]{:S(2)}) copy-start(f32[32,2048]{1,0:T(8,128)S(1)} %add.183.refs_4_) | copy-start | bytes 786436
  446.0 30.2 %collective-permute-start.19 = (f32[64,2048]{1,0:T(8,128)S(1)}, f32[64,2048]{1,0:T(8,128)}, u32[]{:S(2)}, u32[]{:S(2)}) collective-permute-start(f32[64,2048]{1,0:T(8,128)S(1)} %add.184), channel_id=1, source_target_pairs={{2,4},{4,2},{3,5},{5,3},{10,12},{12,10},{11,13},{13,11},{18,20},{2... | collective-permute-start | bytes 1572872 | tf_op jit(solution)/shard_map/ppermute | solution.py:35
  457.0 20.4 %collective-permute-start.15 = (f32[64,2048]{1,0:T(8,128)}, f32[64,2048]{1,0:T(8,128)}, u32[]{:S(2)}, u32[]{:S(2)}) collective-permute-start(f32[64,2048]{1,0:T(8,128)} %get-tuple-element.57), channel_id=1, source_target_pairs={{0,2},{6,4},{1,3},{7,5},{8,10},{14,12},{9,11},{15,13},{16,18},{22,... | collective-permute-start | bytes 1572872 | tf_op jit(solution)/shard_map/ppermute | solution.py:35
  463.8 29.4 %copy-start.6 = (f32[64,2048]{1,0:T(8,128)}, f32[64,2048]{1,0:T(8,128)S(1)}, u32[]{:S(2)}) copy-start(f32[64,2048]{1,0:T(8,128)S(1)} %add.193.refs_5_) | copy-start | bytes 1572868
  463.9 18.3 %collective-permute-start.29 = (f32[64,2048]{1,0:T(8,128)S(1)}, f32[64,2048]{1,0:T(8,128)}, u32[]{:S(2)}, u32[]{:S(2)}) collective-permute-start(f32[64,2048]{1,0:T(8,128)S(1)} %add.194), channel_id=1, source_target_pairs={{2,4},{4,2},{3,5},{5,3},{10,12},{12,10},{11,13},{13,11},{18,20},{2... | collective-permute-start | bytes 1572872 | tf_op jit(solution)/shard_map/ppermute | solution.py:35
  465.3 18.0 %collective-permute-start.25 = (f32[64,2048]{1,0:T(8,128)}, f32[64,2048]{1,0:T(8,128)}, u32[]{:S(2)}, u32[]{:S(2)}) collective-permute-start(f32[64,2048]{1,0:T(8,128)} %get-tuple-element.64), channel_id=1, source_target_pairs={{0,2},{6,4},{1,3},{7,5},{8,10},{14,12},{9,11},{15,13},{16,18},{22,... | collective-permute-start | bytes 1572872 | tf_op jit(solution)/shard_map/ppermute | solution.py:35
  477.4 31.3 %copy-start.7 = (f32[64,2048]{1,0:T(8,128)}, f32[64,2048]{1,0:T(8,128)S(1)}, u32[]{:S(2)}) copy-start(f32[64,2048]{1,0:T(8,128)S(1)} %add.185.refs_6_) | copy-start | bytes 1572868
  478.7 10.2 %collective-permute-start.20 = (f32[64,2048]{1,0:T(8,128)S(1)}, f32[64,2048]{1,0:T(8,128)S(1)}, u32[]{:S(2)}, u32[]{:S(2)}) collective-permute-start(f32[64,2048]{1,0:T(8,128)S(1)} %add.186), channel_id=1, source_target_pairs={{2,4},{4,2},{3,5},{5,3},{10,12},{12,10},{11,13},{13,11},{18,20},{2... | collective-permute-start | bytes 1572872 | tf_op jit(solution)/shard_map/ppermute | solution.py:35
  479.4 12.8 %collective-permute-start.14 = (f32[64,2048]{1,0:T(8,128)S(1)}, f32[64,2048]{1,0:T(8,128)S(1)}, u32[]{:S(2)}, u32[]{:S(2)}) collective-permute-start(f32[64,2048]{1,0:T(8,128)S(1)} %copy-done.20), channel_id=1, source_target_pairs={{0,2},{6,4},{1,3},{7,5},{8,10},{14,12},{9,11},{15,13},{16,18},{22,... | collective-permute-start | bytes 1572872 | tf_op jit(solution)/shard_map/ppermute | solution.py:35
  483.3 43.3 %copy-start.8 = (f32[64,2048]{1,0:T(8,128)}, f32[64,2048]{1,0:T(8,128)S(1)}, u32[]{:S(2)}) copy-start(f32[64,2048]{1,0:T(8,128)S(1)} %add.195.refs_7_) | copy-start | bytes 1572868
  484.6 9.9 %collective-permute-start.30 = (f32[64,2048]{1,0:T(8,128)S(1)}, f32[64,2048]{1,0:T(8,128)S(1)}, u32[]{:S(2)}, u32[]{:S(2)}) collective-permute-start(f32[64,2048]{1,0:T(8,128)S(1)} %add.196), channel_id=1, source_target_pairs={{2,4},{4,2},{3,5},{5,3},{10,12},{12,10},{11,13},{13,11},{18,20},{2... | collective-permute-start | bytes 1572872 | tf_op jit(solution)/shard_map/ppermute | solution.py:35
  485.3 12.9 %collective-permute-start.24 = (f32[64,2048]{1,0:T(8,128)S(1)}, f32[64,2048]{1,0:T(8,128)S(1)}, u32[]{:S(2)}, u32[]{:S(2)}) collective-permute-start(f32[64,2048]{1,0:T(8,128)S(1)} %copy-done.19), channel_id=1, source_target_pairs={{0,2},{6,4},{1,3},{7,5},{8,10},{14,12},{9,11},{15,13},{16,18},{22,... | collective-permute-start | bytes 1572872 | tf_op jit(solution)/shard_map/ppermute | solution.py:35
  489.0 41.5 %copy-start.10 = (f32[64,2048]{1,0:T(8,128)}, f32[64,2048]{1,0:T(8,128)S(1)}, u32[]{:S(2)}) copy-start(f32[64,2048]{1,0:T(8,128)S(1)} %add.187.refs_4_) | copy-start | bytes 1572868
  492.3 53.0 %copy-start.28 = (f32[16,8,128]{2,1,0:T(8,128)S(1)}, f32[16,8,128]{2,1,0:T(8,128)}, u32[]{:S(2)}) copy-start(f32[16,8,128]{2,1,0:T(8,128)} %get-tuple-element.50) | copy-start | bytes 196612
  492.4 17.7 %collective-permute-start.21 = (f32[64,2048]{1,0:T(8,128)S(1)}, f32[64,2048]{1,0:T(8,128)S(1)}, u32[]{:S(2)}, u32[]{:S(2)}) collective-permute-start(f32[64,2048]{1,0:T(8,128)S(1)} %add.188), channel_id=1, source_target_pairs={{2,4},{4,2},{3,5},{5,3},{10,12},{12,10},{11,13},{13,11},{18,20},{2... | collective-permute-start | bytes 1572872 | tf_op jit(solution)/shard_map/ppermute | solution.py:35
  493.2 34.7 %collective-permute-start.37 = (f32[64,2048]{1,0:T(8,128)S(1)}, f32[64,2048]{1,0:T(8,128)S(1)}, u32[]{:S(2)}, u32[]{:S(2)}) collective-permute-start(f32[64,2048]{1,0:T(8,128)S(1)} %add.193.refs_5_), channel_id=1, source_target_pairs={{2,0},{4,6},{3,1},{5,7},{10,8},{12,14},{11,9},{13,15},{18,16},{20,... | collective-permute-start | bytes 1572872 | tf_op jit(solution)/shard_map/ppermute | solution.py:35
  494.6 59.1 %copy-start.11 = (f32[64,2048]{1,0:T(8,128)}, f32[64,2048]{1,0:T(8,128)S(1)}, u32[]{:S(2)}) copy-start(f32[64,2048]{1,0:T(8,128)S(1)} %add.197.refs_5_) | copy-start | bytes 1572868
  498.4 30.8 %collective-permute-start.31 = (f32[64,2048]{1,0:T(8,128)S(1)}, f32[64,2048]{1,0:T(8,128)S(1)}, u32[]{:S(2)}, u32[]{:S(2)}) collective-permute-start(f32[64,2048]{1,0:T(8,128)S(1)} %add.198), channel_id=1, source_target_pairs={{2,4},{4,2},{3,5},{5,3},{10,12},{12,10},{11,13},{13,11},{18,20},{2... | collective-permute-start | bytes 1572872 | tf_op jit(solution)/shard_map/ppermute | solution.py:35
  499.1 13.5 %collective-permute-start.13 = (f32[32,2048]{1,0:T(8,128)S(1)}, f32[32,2048]{1,0:T(8,128)S(1)}, u32[]{:S(2)}, u32[]{:S(2)}) collective-permute-start(f32[32,2048]{1,0:T(8,128)S(1)} %copy-done.27), channel_id=1, source_target_pairs={{0,2},{6,4},{1,3},{7,5},{8,10},{14,12},{9,11},{15,13},{16,18},{22,... | collective-permute-start | bytes 786440 | tf_op jit(solution)/shard_map/ppermute | solution.py:35
  508.8 21.8 %collective-permute-start.38 = (f32[64,2048]{1,0:T(8,128)S(1)}, f32[64,2048]{1,0:T(8,128)S(1)}, u32[]{:S(2)}, u32[]{:S(2)}) collective-permute-start(f32[64,2048]{1,0:T(8,128)S(1)} %add.185.refs_6_), channel_id=1, source_target_pairs={{2,0},{4,6},{3,1},{5,7},{10,8},{12,14},{11,9},{13,15},{18,16},{20,... | collective-permute-start | bytes 1572872 | tf_op jit(solution)/shard_map/ppermute | solution.py:35
  510.1 16.5 %collective-permute-start.36 = (f32[32,2048]{1,0:T(8,128)S(1)}, f32[32,2048]{1,0:T(8,128)}, u32[]{:S(2)}, u32[]{:S(2)}) collective-permute-start(f32[32,2048]{1,0:T(8,128)S(1)} %add.183.refs_4_), channel_id=1, source_target_pairs={{2,0},{4,6},{3,1},{5,7},{10,8},{12,14},{11,9},{13,15},{18,16},{20,... | collective-permute-start | bytes 786440 | tf_op jit(solution)/shard_map/ppermute | solution.py:35
  511.5 42.2 %copy-start.12 = (f32[64,2048]{1,0:T(8,128)}, f32[64,2048]{1,0:T(8,128)S(1)}, u32[]{:S(2)}) copy-start(f32[64,2048]{1,0:T(8,128)S(1)} %add.189.refs_4_) | copy-start | bytes 1572868
  512.6 19.3 %collective-permute-start.22 = (f32[32,2048]{1,0:T(8,128)S(1)}, f32[32,2048]{1,0:T(8,128)S(1)}, u32[]{:S(2)}, u32[]{:S(2)}) collective-permute-start(f32[32,2048]{1,0:T(8,128)S(1)} %add.190), channel_id=1, source_target_pairs={{2,4},{4,2},{3,5},{5,3},{10,12},{12,10},{11,13},{13,11},{18,20},{2... | collective-permute-start | bytes 786440 | tf_op jit(solution)/shard_map/ppermute | solution.py:35
  526.6 16.7 %collective-permute-start.39 = (f32[64,2048]{1,0:T(8,128)S(1)}, f32[64,2048]{1,0:T(8,128)S(1)}, u32[]{:S(2)}, u32[]{:S(2)}) collective-permute-start(f32[64,2048]{1,0:T(8,128)S(1)} %add.195.refs_7_), channel_id=1, source_target_pairs={{2,0},{4,6},{3,1},{5,7},{10,8},{12,14},{11,9},{13,15},{18,16},{20,... | collective-permute-start | bytes 1572872 | tf_op jit(solution)/shard_map/ppermute | solution.py:35
  527.9 26.7 %collective-permute-start.34 = (f32[64,2048]{1,0:T(8,128)S(1)}, f32[64,2048]{1,0:T(8,128)}, u32[]{:S(2)}, u32[]{:S(2)}) collective-permute-start(f32[64,2048]{1,0:T(8,128)S(1)} %add.187.refs_4_), channel_id=1, source_target_pairs={{2,0},{4,6},{3,1},{5,7},{10,8},{12,14},{11,9},{13,15},{18,16},{20,... | collective-permute-start | bytes 1572872 | tf_op jit(solution)/shard_map/ppermute | solution.py:35
  529.2 36.6 %collective-permute-start.35 = (f32[64,2048]{1,0:T(8,128)S(1)}, f32[64,2048]{1,0:T(8,128)}, u32[]{:S(2)}, u32[]{:S(2)}) collective-permute-start(f32[64,2048]{1,0:T(8,128)S(1)} %add.197.refs_5_), channel_id=1, source_target_pairs={{2,0},{4,6},{3,1},{5,7},{10,8},{12,14},{11,9},{13,15},{18,16},{20,... | collective-permute-start | bytes 1572872 | tf_op jit(solution)/shard_map/ppermute | solution.py:35
  530.6 23.1 %copy-start.13 = (f32[64,2048]{1,0:T(8,128)}, f32[64,2048]{1,0:T(8,128)S(1)}, u32[]{:S(2)}) copy-start(f32[64,2048]{1,0:T(8,128)S(1)} %add.199.refs_5_) | copy-start | bytes 1572868
  530.6 46.1 %collective-permute-start.32 = (f32[64,2048]{1,0:T(8,128)S(1)}, f32[64,2048]{1,0:T(8,128)}, u32[]{:S(2)}, u32[]{:S(2)}) collective-permute-start(f32[64,2048]{1,0:T(8,128)S(1)} %add.189.refs_4_), channel_id=1, source_target_pairs={{2,0},{4,6},{3,1},{5,7},{10,8},{12,14},{11,9},{13,15},{18,16},{20,... | collective-permute-start | bytes 1572872 | tf_op jit(solution)/shard_map/ppermute | solution.py:35
  531.9 50.4 %collective-permute-start.33 = (f32[64,2048]{1,0:T(8,128)S(1)}, f32[64,2048]{1,0:T(8,128)}, u32[]{:S(2)}, u32[]{:S(2)}) collective-permute-start(f32[64,2048]{1,0:T(8,128)S(1)} %add.199.refs_5_), channel_id=1, source_target_pairs={{2,0},{4,6},{3,1},{5,7},{10,8},{12,14},{11,9},{13,15},{18,16},{20,... | collective-permute-start | bytes 1572872 | tf_op jit(solution)/shard_map/ppermute | solution.py:35
  544.1 43.2 %collective-permute-start.23 = (f32[32,2048]{1,0:T(8,128)S(1)}, f32[32,2048]{1,0:T(8,128)S(1)}, u32[]{:S(2)}, u32[]{:S(2)}) collective-permute-start(f32[32,2048]{1,0:T(8,128)S(1)} %add.191.refs_4_), channel_id=1, source_target_pairs={{2,0},{4,6},{3,1},{5,7},{10,8},{12,14},{11,9},{13,15},{18,16},{20,... | collective-permute-start | bytes 786440 | tf_op jit(solution)/shard_map/ppermute | solution.py:35
  591.1 1.2 collective-permute-start.40
  592.4 3.6 collective-permute-start.41
  595.9 3.6 collective-permute-start.42
  599.5 4.5 collective-permute-start.43
  604.0 3.6 collective-permute-start.44
  612.6 25.8 %collective-permute-start.45 = (f32[128,2048]{1,0:T(8,128)}, f32[128,2048]{1,0:T(8,128)}, u32[]{:S(2)}, u32[]{:S(2)}) collective-permute-start(f32[128,2048]{1,0:T(8,128)} %shard_map.46), channel_id=1, source_target_pairs={{0,2},{6,4},{1,3},{7,5},{8,10},{14,12},{9,11},{15,13},{16,18},{22,... | collective-permute-start | bytes 3145736 | tf_op jit(solution)/shard_map/ppermute | solution.py:35
  628.7 34.6 %copy-start.4 = (f32[128,2048]{1,0:T(8,128)S(1)}, f32[128,2048]{1,0:T(8,128)}, u32[]{:S(2)}) copy-start(f32[128,2048]{1,0:T(8,128)} %get-tuple-element.78) | copy-start | bytes 3145732
  628.7 36.0 %copy-start.5 = (f32[96,2048]{1,0:T(8,128)S(1)}, f32[96,2048]{1,0:T(8,128)}, u32[]{:S(2)}) copy-start(f32[96,2048]{1,0:T(8,128)} %get-tuple-element.49) | copy-start | bytes 2359300
  628.7 32.2 %collective-permute-start.49 = (f32[128,2048]{1,0:T(8,128)}, f32[128,2048]{1,0:T(8,128)}, u32[]{:S(2)}, u32[]{:S(2)}) collective-permute-start(f32[128,2048]{1,0:T(8,128)} %get-tuple-element.80), channel_id=1, source_target_pairs={{0,2},{6,4},{1,3},{7,5},{8,10},{14,12},{9,11},{15,13},{16,18},{22,... | collective-permute-start | bytes 3145736 | tf_op jit(solution)/shard_map/ppermute | solution.py:35
  640.7 22.5 %collective-permute-start.46 = (f32[128,2048]{1,0:T(8,128)}, f32[128,2048]{1,0:T(8,128)S(1)}, u32[]{:S(2)}, u32[]{:S(2)}) collective-permute-start(f32[128,2048]{1,0:T(8,128)} %add.209), channel_id=1, source_target_pairs={{2,4},{4,2},{3,5},{5,3},{10,12},{12,10},{11,13},{13,11},{18,20},{2... | collective-permute-start | bytes 3145736 | tf_op jit(solution)/shard_map/ppermute | solution.py:35
  641.4 36.8 %collective-permute-start.48 = (f32[128,2048]{1,0:T(8,128)}, f32[128,2048]{1,0:T(8,128)S(1)}, u32[]{:S(2)}, u32[]{:S(2)}) collective-permute-start(f32[128,2048]{1,0:T(8,128)} %get-tuple-element.79), channel_id=1, source_target_pairs={{0,2},{6,4},{1,3},{7,5},{8,10},{14,12},{9,11},{15,13},{16,18},{22,... | collective-permute-start | bytes 3145736 | tf_op jit(solution)/shard_map/ppermute | solution.py:35
  662.5 15.7 %collective-permute-start.50 = (f32[128,2048]{1,0:T(8,128)S(1)}, f32[128,2048]{1,0:T(8,128)S(1)}, u32[]{:S(2)}, u32[]{:S(2)}) collective-permute-start(f32[128,2048]{1,0:T(8,128)S(1)} %add.213), channel_id=1, source_target_pairs={{2,4},{4,2},{3,5},{5,3},{10,12},{12,10},{11,13},{13,11},{18,20},{2... | collective-permute-start | bytes 3145736 | tf_op jit(solution)/shard_map/ppermute | solution.py:35
  663.4 18.8 %collective-permute-start.47 = (f32[128,2048]{1,0:T(8,128)S(1)}, f32[128,2048]{1,0:T(8,128)S(1)}, u32[]{:S(2)}, u32[]{:S(2)}) collective-permute-start(f32[128,2048]{1,0:T(8,128)S(1)} %add.210), channel_id=1, source_target_pairs={{2,0},{4,6},{3,1},{5,7},{10,8},{12,14},{11,9},{13,15},{18,16},{20,... | collective-permute-start | bytes 3145736 | tf_op jit(solution)/shard_map/ppermute | solution.py:35
  (18 other events, 196.9 us)

commit v9 on v7

--- a/solution.py
+++ b/solution.py
@@ -288,8 +288,9 @@
     own = step_chunks(line_factor, flat, flat_v, 0, sizes[:1])
     own += step_chunks(line_factor, flat, tie(flat_v, own[0]), places[1], sizes[1:2])
     own += step_chunks(line_factor, flat, tie(flat_v, own[1]), places[2], sizes[2:4])
-    own += step_chunks(line_factor, flat, tie(flat_v, own[2]), places[4], sizes[4:])
-    cuts = [0, count - 5, count - 3, count - 1, count]
+    own += step_chunks(line_factor, flat, tie(flat_v, own[2]), places[4], sizes[4:6])
+    own += step_chunks(line_factor, flat, tie(flat_v, own[4]), places[6], sizes[6:])
+    cuts = [0, count - 6, count - 4, count - 2, count]
     groups = [slice(*pair) for pair in zip(cuts, cuts[1:])]
     totals, backs, carried = [], [], ()
 
@@ -307,11 +308,12 @@
         total = total + send(total, ACROSS)
         if chunk in early:
             total = tie(total, early[chunk])
-        if chunk in (count - 3, count - 1):
-            carried = move(groups[chunk == count - 1], carried)
+        if chunk == count - 3:
+            carried = move(groups[0], carried)
             total = tie(total, carried[1])
         totals.append(total)
         backs.append(send(total, TO_ENDS))
+    carried = move(groups[1], carried)
     for part in groups[2:]:
         carried = move(part, carried)
     spread_v = next_spread_v

time: 677 us -> 683 us (level)
    pallas_call x11 -> x12, Pallas kernels: 63.9 us -> 65 us  [run(): pl.pallas_call(kernel, grid_spec=pltpu.PrefetchScalarGridSpec(num_scalar_...]
where the time goes in v9:
time: 683 us; the launch traced here: 680 us
  waiting for transfers between devices  425 us (62%)
  starting transfers between devices  98.6 us (14%)
  Pallas kernels  65 us (10%)
  other arithmetic  59.9 us (9%)
  local copies, waits for them, and re-layouts  29.4 us (4%)
    ppermute x41, waiting for transfers between devices, send(): return lax.ppermute(value, axis, pairs)  401 us
    ppermute x41, starting transfers between devices, send(): return lax.ppermute(value, axis, pairs)  83.7 us
    pallas_call x12, Pallas kernels, run(): pl.pallas_call(kernel, grid_spec=pltpu.PrefetchScalarGridSpec(num_scalar_...  65 us
    ppermute x10, waiting for transfers between devices, sum_over_devices(): lax.ppermute(value, axis, [(i, i ^ step) for i in range(size)])  24.7 us
    reduce_sum x4, other arithmetic, on_device(): square = jnp.sum(jnp.square(held[place] - v))  17.5 us
    dynamic_slice x3, local copies, waits for them, and re-layouts, line_rows(): lax.dynamic_slice(source, (worker * outers, cut, 0), (outers, rest, colum...  14.1 us
  transfers between devices with their start and end apart: 52, of which 26 were waited for; matrix products, arithmetic and copies ran while one was open for 9% of the time, Pallas kernels for 8%

profile of v9, /device:TPU:0, one launch (start us, length us, event | category | flops | bytes accessed | tf_op | source)
XLA Modules:
  0.0 679.8 jit_solution(9652418959422173806)
XLA Ops:
  0.0 11.5 %slice.28 = f32[16,96,2048]{2,1,0:T(8,128)} slice(f32[16,224,2048]{2,1,0:T(8,128)} %bitcast.64), slice={[0:16], [0:96], [0:2048]} | slice | bytes 25165824 | tf_op jit(solution)/shard_map/slice | solution.py:251
  11.5 7.6 %all-to-all-start = ((f32[16,96,2048]{2,1,0:T(8,128)}), f32[16,96,2048]{2,1,0:T(8,128)}, u32[]{:S(2)}, u32[]{:S(2)}) async-start(f32[16,96,2048]{2,1,0:T(8,128)} %slice.28), calls=%async_computation | async-start | bytes 25165824 | tf_op jit(solution)/shard_map/all_to_all | solution.py:250
  19.2 1.9 collective-permute-start
  21.1 4.6 constant_dynamic-slice_fusion.3
  25.7 4.8 constant_dynamic-slice_fusion.2
  30.5 4.7 constant_dynamic-slice_fusion.1
  38.4 206.6 %collective-permute-done = f32[128,2048]{1,0:T(8,128)} collective-permute-done((f32[128,2048]{1,0:T(8,128)S(1)}, f32[128,2048]{1,0:T(8,128)}, u32[]{:S(2)}, u32[]{:S(2)}) %collective-permute-start) | collective-permute-done | bytes 1048608 | tf_op jit(solution)/shard_map/ppermute | solution.py:35
  251.2 89.2 %collective-permute-done.4 = f32[128,2048]{1,0:T(8,128)} collective-permute-done((f32[128,2048]{1,0:T(8,128)}, f32[128,2048]{1,0:T(8,128)}, u32[]{:S(2)}, u32[]{:S(2)}) %collective-permute-start.4) | collective-permute-done | bytes 1048608 | tf_op jit(solution)/shard_map/ppermute | solution.py:35
  340.3 22.5 %collective-permute-done.2 = f32[128,2048]{1,0:T(8,128)} collective-permute-done((f32[128,2048]{1,0:T(8,128)}, f32[128,2048]{1,0:T(8,128)}, u32[]{:S(2)}, u32[]{:S(2)}) %collective-permute-start.2) | collective-permute-done | bytes 1048608 | tf_op jit(solution)/shard_map/ppermute | solution.py:35
  362.8 2.5 select_bitcast_fusion.3
  365.3 5.0 multiply_reduce_fusion.5
  371.0 4.7 multiply_reduce_fusion.4
  376.3 3.9 multiply_reduce_fusion.3
  380.8 3.9 multiply_reduce_fusion.2
  385.3 6.0 multiply_reduce_fusion.1
  394.0 2.1 collective-permute-done.9
  396.1 3.6 collective-permute-done.10
  400.8 3.4 collective-permute-done.11
  405.7 2.0 collective-permute-done.12
  408.4 2.1 shard_map.38
  410.5 2.6 shard_map.39
  413.2 2.1 collective-permute-start.16
  416.6 4.7 shard_map.40
  421.2 2.1 collective-permute-start.24
  423.3 4.5 collective-permute-done.16
  429.3 5.7 collective-permute-start.15
  436.1 4.7 shard_map.41
  440.9 3.8 collective-permute-done.24
  446.5 6.6 collective-permute-start.23
  454.2 1.7 collective-permute-done.15
  457.4 6.5 collective-permute-start.14
  464.0 3.1 collective-permute-done.23
  467.9 5.9 shard_map.42
  473.8 7.3 %collective-permute-start.22 = (f32[64,2048]{1,0:T(8,128)}, f32[64,2048]{1,0:T(8,128)}, u32[]{:S(2)}, u32[]{:S(2)}) collective-permute-start(f32[64,2048]{1,0:T(8,128)} %get-tuple-element.66), channel_id=1, source_target_pairs={{0,2},{6,4},{1,3},{7,5},{8,10},{14,12},{9,11},{15,13},{16,18},{22,... | collective-permute-start | bytes 1572872 | tf_op jit(solution)/shard_map/ppermute | solution.py:35
  485.0 2.8 collective-permute-start.13
  490.4 7.9 %shard_map.37 = (f32[96,2048]{1,0:T(8,128)}, f32[16,8,128]{2,1,0:T(8,128)}) custom-call(f32[16]{0:T(128)} %copy-done.27, f32[96,2048]{1,0:T(8,128)} %copy-done.1, f32[16,96,2048]{2,1,0:T(8,128)} %all-to-all-done.values), custom_call_target="tpu_custom_call" | custom-call | flops 14155776 | bytes 14155776 | tf_op jit(solution)/shard_map/pallas_call | solution.py:61
  503.7 2.0 add.187.refs_4_
  508.3 7.9 %collective-permute-done.30.refs_7_ = f32[32,2048]{1,0:T(8,128)S(1)} collective-permute-done((f32[32,2048]{1,0:T(8,128)S(1)}, f32[32,2048]{1,0:T(8,128)S(1)}, u32[]{:S(2)}, u32[]{:S(2)}) %collective-permute-start.30) | collective-permute-done | bytes 262176 | tf_op jit(solution)/shard_map/ppermute | solution.py:35
  519.7 6.2 shard_map.43
  525.9 2.0 add.197.refs_5_
  538.3 10.5 %collective-permute-done.38.refs_6_ = f32[64,2048]{1,0:T(8,128)} collective-permute-done((f32[64,2048]{1,0:T(8,128)S(1)}, f32[64,2048]{1,0:T(8,128)}, u32[]{:S(2)}, u32[]{:S(2)}) %collective-permute-start.38) | collective-permute-done | bytes 524320 | tf_op jit(solution)/shard_map/ppermute | solution.py:35
  548.8 4.9 shard_map.44
  553.7 6.3 collective-permute-done.37.refs_7_
  560.0 11.2 %collective-permute-done.36.refs_6_ = f32[64,2048]{1,0:T(8,128)} collective-permute-done((f32[64,2048]{1,0:T(8,128)S(1)}, f32[64,2048]{1,0:T(8,128)}, u32[]{:S(2)}, u32[]{:S(2)}) %collective-permute-start.36) | collective-permute-done | bytes 524320 | tf_op jit(solution)/shard_map/ppermute | solution.py:35
  571.2 4.9 shard_map.45
  576.2 3.8 collective-permute-done.35.refs_7_
  580.7 4.2 shard_map.46
  587.0 1.8 collective-permute-start.41
  588.8 1.8 collective-permute-done.41
  590.6 3.6 collective-permute-done.42
  594.8 3.9 collective-permute-done.43
  600.2 2.0 collective-permute-done.44
  603.0 4.3 shard_map.47
  607.3 2.9 collective-permute-start.45
  610.8 12.5 %shard_map.48 = (f32[128,2048]{1,0:T(8,128)}, f32[128,2048]{1,0:T(8,128)}, f32[128,2048]{1,0:T(8,128)}) custom-call(s32[3]{0:T(128)} %pad_add_fusion.1.places, f32[4]{0:T(128)} %select_reduce_fusion.factor, f32[4,128,2048]{2,1,0:T(8,128)} %collective-permute-done.7.refs_0_, f32[4,128,2048]{2,1,0:T(8,128)} %collective-permute-done.6.refs_1_, ...), custom_call_target="tpu_custom_call" | custom-call | flops 18874368 | bytes 18874368 | tf_op jit(solution)/shard_map/pallas_call | solution.py:61
  623.4 2.4 collective-permute-start.49
  625.8 7.3 %collective-permute-done.45 = f32[128,2048]{1,0:T(8,128)} collective-permute-done((f32[128,2048]{1,0:T(8,128)}, f32[128,2048]{1,0:T(8,128)}, u32[]{:S(2)}, u32[]{:S(2)}) %collective-permute-start.45) | collective-permute-done | bytes 1048608 | tf_op jit(solution)/shard_map/ppermute | solution.py:35
  633.1 2.3 add.209
  636.1 6.8 collective-permute-start.48
  642.9 12.6 %collective-permute-done.49 = f32[128,2048]{1,0:T(8,128)} collective-permute-done((f32[128,2048]{1,0:T(8,128)}, f32[128,2048]{1,0:T(8,128)}, u32[]{:S(2)}, u32[]{:S(2)}) %collective-permute-start.49) | collective-permute-done | bytes 1048608 | tf_op jit(solution)/shard_map/ppermute | solution.py:35
  659.4 6.4 multiply_reduce_fusion
  667.4 5.6 collective-permute-done.48
  672.9 4.1 collective-permute-done.47
  677.1 2.7 fusion
  (169 shorter events, 66.9 us)
Async XLA Ops:
  11.5 373.9 %all-to-all-start = ((f32[16,96,2048]{2,1,0:T(8,128)}), f32[16,96,2048]{2,1,0:T(8,128)}, u32[]{:S(2)}, u32[]{:S(2)}) async-start(f32[16,96,2048]{2,1,0:T(8,128)} %slice.28), calls=%async_computation | async-start | bytes 25165824 | tf_op jit(solution)/shard_map/all_to_all | solution.py:250
  19.2 225.8 %collective-permute-start = (f32[128,2048]{1,0:T(8,128)S(1)}, f32[128,2048]{1,0:T(8,128)}, u32[]{:S(2)}, u32[]{:S(2)}) collective-permute-start(f32[128,2048]{1,0:T(8,128)S(1)} %slice.24), channel_id=1, source_target_pairs={{0,2},{2,0},{4,6},{6,4},{1,3},{3,1},{5,7},{7,5},{8,10},{10,8},{12,... | collective-permute-start | bytes 3145736 | tf_op jit(solution)/shard_map/ppermute | solution.py:35
  35.1 335.8 %collective-permute-start.5 = (f32[4,128,2048]{2,1,0:T(8,128)}, f32[4,128,2048]{2,1,0:T(8,128)}, u32[]{:S(2)}, u32[]{:S(2)}) collective-permute-start(f32[4,128,2048]{2,1,0:T(8,128)} %constant_dynamic-slice_fusion.1), channel_id=1, source_target_pairs={{0,8},{8,0},{16,24},{24,16},{1,9},{9,1},{17,25},{25,17},{2,10},{10... | collective-permute-start | bytes 12582920 | tf_op jit(solution)/shard_map/ppermute | solution.py:35
  35.2 341.2 %collective-permute-start.6 = (f32[4,128,2048]{2,1,0:T(8,128)}, f32[4,128,2048]{2,1,0:T(8,128)}, u32[]{:S(2)}, u32[]{:S(2)}) collective-permute-start(f32[4,128,2048]{2,1,0:T(8,128)} %constant_dynamic-slice_fusion.2), channel_id=1, source_target_pairs={{0,24},{8,16},{16,8},{24,0},{1,25},{9,17},{17,9},{25,1},{2,26},{10... | collective-permute-start | bytes 12582920 | tf_op jit(solution)/shard_map/ppermute | solution.py:35
  36.7 211.6 %collective-permute-start.3 = (f32[128,2048]{1,0:T(8,128)S(1)}, f32[128,2048]{1,0:T(8,128)}, u32[]{:S(2)}, u32[]{:S(2)}) collective-permute-start(f32[128,2048]{1,0:T(8,128)S(1)} %slice.24), channel_id=1, source_target_pairs={{2,4},{4,2},{3,5},{5,3},{10,12},{12,10},{11,13},{13,11},{18,20},{2... | collective-permute-start | bytes 3145736 | tf_op jit(solution)/shard_map/ppermute | solution.py:35
  245.0 4.6 collective-permute-start.1
  246.7 134.1 %collective-permute-start.7 = (f32[4,128,2048]{2,1,0:T(8,128)}, f32[4,128,2048]{2,1,0:T(8,128)}, u32[]{:S(2)}, u32[]{:S(2)}) collective-permute-start(f32[4,128,2048]{2,1,0:T(8,128)} %constant_dynamic-slice_fusion.3), channel_id=1, source_target_pairs={{0,16},{8,24},{16,0},{24,8},{1,17},{9,25},{17,1},{25,9},{2,18},{10... | collective-permute-start | bytes 12582920 | tf_op jit(solution)/shard_map/ppermute | solution.py:35
  248.3 92.0 %collective-permute-start.4 = (f32[128,2048]{1,0:T(8,128)}, f32[128,2048]{1,0:T(8,128)}, u32[]{:S(2)}, u32[]{:S(2)}) collective-permute-start(f32[128,2048]{1,0:T(8,128)} %collective-permute-done.3), channel_id=1, source_target_pairs={{2,0},{4,6},{3,1},{5,7},{10,8},{12,14},{11,9},{13,15},{18,16},{20,... | collective-permute-start | bytes 3145736 | tf_op jit(solution)/shard_map/ppermute | solution.py:35
  249.6 113.2 %collective-permute-start.2 = (f32[128,2048]{1,0:T(8,128)}, f32[128,2048]{1,0:T(8,128)}, u32[]{:S(2)}, u32[]{:S(2)}) collective-permute-start(f32[128,2048]{1,0:T(8,128)} %collective-permute-done.1), channel_id=1, source_target_pairs={{2,0},{4,6},{3,1},{5,7},{10,8},{12,14},{11,9},{13,15},{18,16},{20,... | collective-permute-start | bytes 3145736 | tf_op jit(solution)/shard_map/ppermute | solution.py:35
  251.0 134.4 %copy-start.1 = (f32[96,2048]{1,0:T(8,128)}, f32[96,2048]{1,0:T(8,128)S(1)}, u32[]{:S(2)}) copy-start(f32[96,2048]{1,0:T(8,128)S(1)} %slice.22.v) | copy-start | bytes 2359300
  391.4 1.2 collective-permute-start.8
  392.5 3.6 collective-permute-start.9
  396.1 3.6 collective-permute-start.10
  399.7 4.5 collective-permute-start.11
  404.2 3.6 collective-permute-start.12
  413.2 14.6 %collective-permute-start.16 = (f32[64,2048]{1,0:T(8,128)}, f32[64,2048]{1,0:T(8,128)S(1)}, u32[]{:S(2)}, u32[]{:S(2)}) collective-permute-start(f32[64,2048]{1,0:T(8,128)} %shard_map.39), channel_id=1, source_target_pairs={{0,2},{6,4},{1,3},{7,5},{8,10},{14,12},{9,11},{15,13},{16,18},{22,... | collective-permute-start | bytes 1572872 | tf_op jit(solution)/shard_map/ppermute | solution.py:35
  415.2 19.8 %collective-permute-start.25 = (f32[32,2048]{1,0:T(8,128)S(1)}, f32[32,2048]{1,0:T(8,128)S(1)}, u32[]{:S(2)}, u32[]{:S(2)}) collective-permute-start(f32[32,2048]{1,0:T(8,128)S(1)} %copy-done.15), channel_id=1, source_target_pairs={{0,2},{6,4},{1,3},{7,5},{8,10},{14,12},{9,11},{15,13},{16,18},{22,... | collective-permute-start | bytes 786440 | tf_op jit(solution)/shard_map/ppermute | solution.py:35
  421.2 23.4 %collective-permute-start.24 = (f32[64,2048]{1,0:T(8,128)}, f32[64,2048]{1,0:T(8,128)}, u32[]{:S(2)}, u32[]{:S(2)}) collective-permute-start(f32[64,2048]{1,0:T(8,128)} %get-tuple-element.55), channel_id=1, source_target_pairs={{0,2},{6,4},{1,3},{7,5},{8,10},{14,12},{9,11},{15,13},{16,18},{22,... | collective-permute-start | bytes 1572872 | tf_op jit(solution)/shard_map/ppermute | solution.py:35
  427.9 25.2 %collective-permute-start.17 = (f32[64,2048]{1,0:T(8,128)S(1)}, f32[64,2048]{1,0:T(8,128)}, u32[]{:S(2)}, u32[]{:S(2)}) collective-permute-start(f32[64,2048]{1,0:T(8,128)S(1)} %add.182), channel_id=1, source_target_pairs={{2,4},{4,2},{3,5},{5,3},{10,12},{12,10},{11,13},{13,11},{18,20},{2... | collective-permute-start | bytes 1572872 | tf_op jit(solution)/shard_map/ppermute | solution.py:35
  429.3 26.6 %collective-permute-start.15 = (f32[64,2048]{1,0:T(8,128)}, f32[64,2048]{1,0:T(8,128)S(1)}, u32[]{:S(2)}, u32[]{:S(2)}) collective-permute-start(f32[64,2048]{1,0:T(8,128)} %get-tuple-element.61), channel_id=1, source_target_pairs={{0,2},{6,4},{1,3},{7,5},{8,10},{14,12},{9,11},{15,13},{16,18},{22,... | collective-permute-start | bytes 1572872 | tf_op jit(solution)/shard_map/ppermute | solution.py:35
  435.1 5.7 collective-permute-start.26
  440.8 26.3 %copy-start.20 = (f32[64,2048]{1,0:T(8,128)S(1)}, f32[64,2048]{1,0:T(8,128)}, u32[]{:S(2)}) copy-start(f32[64,2048]{1,0:T(8,128)} %get-tuple-element.57) | copy-start | bytes 1572868
  440.9 61.6 %copy-start.13 = (f32[32,2048]{1,0:T(8,128)}, f32[32,2048]{1,0:T(8,128)S(1)}, u32[]{:S(2)}) copy-start(f32[32,2048]{1,0:T(8,128)S(1)} %add.191.refs_4_) | copy-start | bytes 786436
  445.8 18.2 %collective-permute-start.27 = (f32[64,2048]{1,0:T(8,128)S(1)}, f32[64,2048]{1,0:T(8,128)S(1)}, u32[]{:S(2)}, u32[]{:S(2)}) collective-permute-start(f32[64,2048]{1,0:T(8,128)S(1)} %add.192), channel_id=1, source_target_pairs={{2,4},{4,2},{3,5},{5,3},{10,12},{12,10},{11,13},{13,11},{18,20},{2... | collective-permute-start | bytes 1572872 | tf_op jit(solution)/shard_map/ppermute | solution.py:35
  446.5 20.7 %collective-permute-start.23 = (f32[64,2048]{1,0:T(8,128)}, f32[64,2048]{1,0:T(8,128)S(1)}, u32[]{:S(2)}, u32[]{:S(2)}) collective-permute-start(f32[64,2048]{1,0:T(8,128)} %get-tuple-element.57), channel_id=1, source_target_pairs={{0,2},{6,4},{1,3},{7,5},{8,10},{14,12},{9,11},{15,13},{16,18},{22,... | collective-permute-start | bytes 1572872 | tf_op jit(solution)/shard_map/ppermute | solution.py:35
  454.2 34.9 %copy-start.6 = (f32[64,2048]{1,0:T(8,128)}, f32[64,2048]{1,0:T(8,128)S(1)}, u32[]{:S(2)}) copy-start(f32[64,2048]{1,0:T(8,128)S(1)} %add.183.refs_5_) | copy-start | bytes 1572868
  456.0 25.1 %collective-permute-start.18 = (f32[64,2048]{1,0:T(8,128)S(1)}, f32[64,2048]{1,0:T(8,128)}, u32[]{:S(2)}, u32[]{:S(2)}) collective-permute-start(f32[64,2048]{1,0:T(8,128)S(1)} %add.184), channel_id=1, source_target_pairs={{2,4},{4,2},{3,5},{5,3},{10,12},{12,10},{11,13},{13,11},{18,20},{2... | collective-permute-start | bytes 1572872 | tf_op jit(solution)/shard_map/ppermute | solution.py:35
  457.4 24.8 %collective-permute-start.14 = (f32[64,2048]{1,0:T(8,128)S(1)}, f32[64,2048]{1,0:T(8,128)}, u32[]{:S(2)}, u32[]{:S(2)}) collective-permute-start(f32[64,2048]{1,0:T(8,128)S(1)} %copy-done.17), channel_id=1, source_target_pairs={{0,2},{6,4},{1,3},{7,5},{8,10},{14,12},{9,11},{15,13},{16,18},{22,... | collective-permute-start | bytes 1572872 | tf_op jit(solution)/shard_map/ppermute | solution.py:35
  464.0 23.7 %copy-start.7 = (f32[64,2048]{1,0:T(8,128)}, f32[64,2048]{1,0:T(8,128)S(1)}, u32[]{:S(2)}) copy-start(f32[64,2048]{1,0:T(8,128)S(1)} %add.193.refs_6_) | copy-start | bytes 1572868
  467.2 21.8 %collective-permute-start.28 = (f32[64,2048]{1,0:T(8,128)S(1)}, f32[64,2048]{1,0:T(8,128)S(1)}, u32[]{:S(2)}, u32[]{:S(2)}) collective-permute-start(f32[64,2048]{1,0:T(8,128)S(1)} %add.194), channel_id=1, source_target_pairs={{2,4},{4,2},{3,5},{5,3},{10,12},{12,10},{11,13},{13,11},{18,20},{2... | collective-permute-start | bytes 1572872 | tf_op jit(solution)/shard_map/ppermute | solution.py:35
  473.8 25.7 %collective-permute-start.22 = (f32[64,2048]{1,0:T(8,128)}, f32[64,2048]{1,0:T(8,128)}, u32[]{:S(2)}, u32[]{:S(2)}) collective-permute-start(f32[64,2048]{1,0:T(8,128)} %get-tuple-element.66), channel_id=1, source_target_pairs={{0,2},{6,4},{1,3},{7,5},{8,10},{14,12},{9,11},{15,13},{16,18},{22,... | collective-permute-start | bytes 1572872 | tf_op jit(solution)/shard_map/ppermute | solution.py:35
  482.2 47.4 %copy-start.10 = (f32[64,2048]{1,0:T(8,128)}, f32[64,2048]{1,0:T(8,128)S(1)}, u32[]{:S(2)}) copy-start(f32[64,2048]{1,0:T(8,128)S(1)} %add.185.refs_4_) | copy-start | bytes 1572868
  483.5 18.9 %collective-permute-start.19 = (f32[64,2048]{1,0:T(8,128)S(1)}, f32[64,2048]{1,0:T(8,128)}, u32[]{:S(2)}, u32[]{:S(2)}) collective-permute-start(f32[64,2048]{1,0:T(8,128)S(1)} %add.186), channel_id=1, source_target_pairs={{2,4},{4,2},{3,5},{5,3},{10,12},{12,10},{11,13},{13,11},{18,20},{2... | collective-permute-start | bytes 1572872 | tf_op jit(solution)/shard_map/ppermute | solution.py:35
  485.0 20.7 %collective-permute-start.13 = (f32[64,2048]{1,0:T(8,128)}, f32[64,2048]{1,0:T(8,128)}, u32[]{:S(2)}, u32[]{:S(2)}) collective-permute-start(f32[64,2048]{1,0:T(8,128)} %get-tuple-element.59), channel_id=1, source_target_pairs={{0,2},{6,4},{1,3},{7,5},{8,10},{14,12},{9,11},{15,13},{16,18},{22,... | collective-permute-start | bytes 1572872 | tf_op jit(solution)/shard_map/ppermute | solution.py:35
  487.8 30.6 %collective-permute-start.32 = (f32[64,2048]{1,0:T(8,128)S(1)}, f32[64,2048]{1,0:T(8,128)}, u32[]{:S(2)}, u32[]{:S(2)}) collective-permute-start(f32[64,2048]{1,0:T(8,128)S(1)} %add.193.refs_6_), channel_id=1, source_target_pairs={{2,0},{4,6},{3,1},{5,7},{10,8},{12,14},{11,9},{13,15},{18,16},{20,... | collective-permute-start | bytes 1572872 | tf_op jit(solution)/shard_map/ppermute | solution.py:35
  489.1 30.6 %collective-permute-start.31 = (f32[64,2048]{1,0:T(8,128)S(1)}, f32[64,2048]{1,0:T(8,128)}, u32[]{:S(2)}, u32[]{:S(2)}) collective-permute-start(f32[64,2048]{1,0:T(8,128)S(1)} %add.183.refs_5_), channel_id=1, source_target_pairs={{2,0},{4,6},{3,1},{5,7},{10,8},{12,14},{11,9},{13,15},{18,16},{20,... | collective-permute-start | bytes 1572872 | tf_op jit(solution)/shard_map/ppermute | solution.py:35
  499.5 26.4 %copy-start.11 = (f32[64,2048]{1,0:T(8,128)}, f32[64,2048]{1,0:T(8,128)S(1)}, u32[]{:S(2)}) copy-start(f32[64,2048]{1,0:T(8,128)S(1)} %add.195.refs_5_) | copy-start | bytes 1572868
  501.0 25.0 %collective-permute-start.29 = (f32[64,2048]{1,0:T(8,128)S(1)}, f32[64,2048]{1,0:T(8,128)}, u32[]{:S(2)}, u32[]{:S(2)}) collective-permute-start(f32[64,2048]{1,0:T(8,128)S(1)} %add.196), channel_id=1, source_target_pairs={{2,4},{4,2},{3,5},{5,3},{10,12},{12,10},{11,13},{13,11},{18,20},{2... | collective-permute-start | bytes 1572872 | tf_op jit(solution)/shard_map/ppermute | solution.py:35
  502.4 13.8 %collective-permute-start.30 = (f32[32,2048]{1,0:T(8,128)S(1)}, f32[32,2048]{1,0:T(8,128)S(1)}, u32[]{:S(2)}, u32[]{:S(2)}) collective-permute-start(f32[32,2048]{1,0:T(8,128)S(1)} %add.191.refs_4_), channel_id=1, source_target_pairs={{2,0},{4,6},{3,1},{5,7},{10,8},{12,14},{11,9},{13,15},{18,16},{20,... | collective-permute-start | bytes 786440 | tf_op jit(solution)/shard_map/ppermute | solution.py:35
  506.8 25.4 %collective-permute-start.20 = (f32[64,2048]{1,0:T(8,128)S(1)}, f32[64,2048]{1,0:T(8,128)}, u32[]{:S(2)}, u32[]{:S(2)}) collective-permute-start(f32[64,2048]{1,0:T(8,128)S(1)} %add.188), channel_id=1, source_target_pairs={{2,4},{4,2},{3,5},{5,3},{10,12},{12,10},{11,13},{13,11},{18,20},{2... | collective-permute-start | bytes 1572872 | tf_op jit(solution)/shard_map/ppermute | solution.py:35
  516.9 11.0 %collective-permute-start.21 = (f32[32,2048]{1,0:T(8,128)}, f32[32,2048]{1,0:T(8,128)S(1)}, u32[]{:S(2)}, u32[]{:S(2)}) collective-permute-start(f32[32,2048]{1,0:T(8,128)} %get-tuple-element.65), channel_id=1, source_target_pairs={{0,2},{6,4},{1,3},{7,5},{8,10},{14,12},{9,11},{15,13},{16,18},{22,... | collective-permute-start | bytes 786440 | tf_op jit(solution)/shard_map/ppermute | solution.py:35
  518.4 17.6 %collective-permute-start.39 = (f32[64,2048]{1,0:T(8,128)S(1)}, f32[64,2048]{1,0:T(8,128)S(1)}, u32[]{:S(2)}, u32[]{:S(2)}) collective-permute-start(f32[64,2048]{1,0:T(8,128)S(1)} %add.195.refs_5_), channel_id=1, source_target_pairs={{2,0},{4,6},{3,1},{5,7},{10,8},{12,14},{11,9},{13,15},{18,16},{20,... | collective-permute-start | bytes 1572872 | tf_op jit(solution)/shard_map/ppermute | solution.py:35
  528.9 5.7 collective-permute-start.33
  529.6 19.2 %collective-permute-start.38 = (f32[64,2048]{1,0:T(8,128)S(1)}, f32[64,2048]{1,0:T(8,128)}, u32[]{:S(2)}, u32[]{:S(2)}) collective-permute-start(f32[64,2048]{1,0:T(8,128)S(1)} %add.185.refs_4_), channel_id=1, source_target_pairs={{2,0},{4,6},{3,1},{5,7},{10,8},{12,14},{11,9},{13,15},{18,16},{20,... | collective-permute-start | bytes 1572872 | tf_op jit(solution)/shard_map/ppermute | solution.py:35
  530.9 29.1 %collective-permute-start.37 = (f32[64,2048]{1,0:T(8,128)}, f32[64,2048]{1,0:T(8,128)}, u32[]{:S(2)}, u32[]{:S(2)}) collective-permute-start(f32[64,2048]{1,0:T(8,128)} %add.197.refs_5_), channel_id=1, source_target_pairs={{2,0},{4,6},{3,1},{5,7},{10,8},{12,14},{11,9},{13,15},{18,16},{20,... | collective-permute-start | bytes 1572872 | tf_op jit(solution)/shard_map/ppermute | solution.py:35
  532.2 39.1 %collective-permute-start.36 = (f32[64,2048]{1,0:T(8,128)S(1)}, f32[64,2048]{1,0:T(8,128)}, u32[]{:S(2)}, u32[]{:S(2)}) collective-permute-start(f32[64,2048]{1,0:T(8,128)S(1)} %copy-done.12), channel_id=1, source_target_pairs={{2,0},{4,6},{3,1},{5,7},{10,8},{12,14},{11,9},{13,15},{18,16},{20,... | collective-permute-start | bytes 1572872 | tf_op jit(solution)/shard_map/ppermute | solution.py:35
  534.6 19.1 %copy-start.8 = (f32[64,2048]{1,0:T(8,128)}, f32[64,2048]{1,0:T(8,128)S(1)}, u32[]{:S(2)}) copy-start(f32[64,2048]{1,0:T(8,128)S(1)} %add.189.refs_4_) | copy-start | bytes 1572868
  534.6 45.4 %collective-permute-start.34 = (f32[64,2048]{1,0:T(8,128)S(1)}, f32[64,2048]{1,0:T(8,128)}, u32[]{:S(2)}, u32[]{:S(2)}) collective-permute-start(f32[64,2048]{1,0:T(8,128)S(1)} %add.189.refs_4_), channel_id=1, source_target_pairs={{2,0},{4,6},{3,1},{5,7},{10,8},{12,14},{11,9},{13,15},{18,16},{20,... | collective-permute-start | bytes 1572872 | tf_op jit(solution)/shard_map/ppermute | solution.py:35
  535.9 17.8 %copy-start.14 = (f32[32,2048]{1,0:T(8,128)}, f32[32,2048]{1,0:T(8,128)S(1)}, u32[]{:S(2)}) copy-start(f32[32,2048]{1,0:T(8,128)S(1)} %add.199.refs_5_) | copy-start | bytes 786436
  536.8 43.2 %collective-permute-start.35 = (f32[32,2048]{1,0:T(8,128)S(1)}, f32[32,2048]{1,0:T(8,128)S(1)}, u32[]{:S(2)}, u32[]{:S(2)}) collective-permute-start(f32[32,2048]{1,0:T(8,128)S(1)} %add.199.refs_5_), channel_id=1, source_target_pairs={{2,0},{4,6},{3,1},{5,7},{10,8},{12,14},{11,9},{13,15},{18,16},{20,... | collective-permute-start | bytes 786440 | tf_op jit(solution)/shard_map/ppermute | solution.py:35
  585.8 1.2 collective-permute-start.40
  587.0 3.6 collective-permute-start.41
  590.6 3.6 collective-permute-start.42
  594.2 4.5 collective-permute-start.43
  598.7 3.6 collective-permute-start.44
  607.3 25.8 %collective-permute-start.45 = (f32[128,2048]{1,0:T(8,128)}, f32[128,2048]{1,0:T(8,128)}, u32[]{:S(2)}, u32[]{:S(2)}) collective-permute-start(f32[128,2048]{1,0:T(8,128)} %shard_map.47), channel_id=1, source_target_pairs={{0,2},{6,4},{1,3},{7,5},{8,10},{14,12},{9,11},{15,13},{16,18},{22,... | collective-permute-start | bytes 3145736 | tf_op jit(solution)/shard_map/ppermute | solution.py:35
  610.8 22.2 %copy-start.3 = (f32[128,2048]{1,0:T(8,128)S(1)}, f32[128,2048]{1,0:T(8,128)}, u32[]{:S(2)}) copy-start(f32[128,2048]{1,0:T(8,128)} %shard_map.47) | copy-start | bytes 3145732
  623.4 34.6 %copy-start.4 = (f32[128,2048]{1,0:T(8,128)S(1)}, f32[128,2048]{1,0:T(8,128)}, u32[]{:S(2)}) copy-start(f32[128,2048]{1,0:T(8,128)} %get-tuple-element.82) | copy-start | bytes 3145732
  623.4 36.0 %copy-start.5 = (f32[96,2048]{1,0:T(8,128)S(1)}, f32[96,2048]{1,0:T(8,128)}, u32[]{:S(2)}) copy-start(f32[96,2048]{1,0:T(8,128)} %get-tuple-element.51) | copy-start | bytes 2359300
  623.4 32.2 %collective-permute-start.49 = (f32[128,2048]{1,0:T(8,128)}, f32[128,2048]{1,0:T(8,128)}, u32[]{:S(2)}, u32[]{:S(2)}) collective-permute-start(f32[128,2048]{1,0:T(8,128)} %get-tuple-element.84), channel_id=1, source_target_pairs={{0,2},{6,4},{1,3},{7,5},{8,10},{14,12},{9,11},{15,13},{16,18},{22,... | collective-permute-start | bytes 3145736 | tf_op jit(solution)/shard_map/ppermute | solution.py:35
  635.4 22.6 %collective-permute-start.46 = (f32[128,2048]{1,0:T(8,128)}, f32[128,2048]{1,0:T(8,128)S(1)}, u32[]{:S(2)}, u32[]{:S(2)}) collective-permute-start(f32[128,2048]{1,0:T(8,128)} %add.209), channel_id=1, source_target_pairs={{2,4},{4,2},{3,5},{5,3},{10,12},{12,10},{11,13},{13,11},{18,20},{2... | collective-permute-start | bytes 3145736 | tf_op jit(solution)/shard_map/ppermute | solution.py:35
  636.1 36.8 %collective-permute-start.48 = (f32[128,2048]{1,0:T(8,128)}, f32[128,2048]{1,0:T(8,128)S(1)}, u32[]{:S(2)}, u32[]{:S(2)}) collective-permute-start(f32[128,2048]{1,0:T(8,128)} %get-tuple-element.83), channel_id=1, source_target_pairs={{0,2},{6,4},{1,3},{7,5},{8,10},{14,12},{9,11},{15,13},{16,18},{22,... | collective-permute-start | bytes 3145736 | tf_op jit(solution)/shard_map/ppermute | solution.py:35
  657.2 15.8 %collective-permute-start.50 = (f32[128,2048]{1,0:T(8,128)S(1)}, f32[128,2048]{1,0:T(8,128)S(1)}, u32[]{:S(2)}, u32[]{:S(2)}) collective-permute-start(f32[128,2048]{1,0:T(8,128)S(1)} %add.213), channel_id=1, source_target_pairs={{2,4},{4,2},{3,5},{5,3},{10,12},{12,10},{11,13},{13,11},{18,20},{2... | collective-permute-start | bytes 3145736 | tf_op jit(solution)/shard_map/ppermute | solution.py:35
  658.1 19.0 %collective-permute-start.47 = (f32[128,2048]{1,0:T(8,128)S(1)}, f32[128,2048]{1,0:T(8,128)S(1)}, u32[]{:S(2)}, u32[]{:S(2)}) collective-permute-start(f32[128,2048]{1,0:T(8,128)S(1)} %add.210), channel_id=1, source_target_pairs={{2,0},{4,6},{3,1},{5,7},{10,8},{12,14},{11,9},{13,15},{18,16},{20,... | collective-permute-start | bytes 3145736 | tf_op jit(solution)/shard_map/ppermute | solution.py:35
  (16 other events, 128.3 us)

commit v10 on v7

--- a/solution.py
+++ b/solution.py
@@ -14,6 +14,7 @@
 AXES = ("worker", "outer", "mp")
 LINE = 4
 TILE = 8
+UNIT = 16
 SPREAD = 3 / 7
 
 GRANT = 60 << 20
@@ -47,10 +48,11 @@
 def split(rows, outers):
     cut = int(rows * SPREAD) // TILE * TILE
     rest = rows - cut
-    tiles = rest // TILE
-    if outers != LINE or rest % TILE or tiles < 13 or not cut:
+    units = rest * outers // UNIT
+    if outers != LINE or rest % TILE or units < 22 or not cut:
         return None
-    sizes = [1] + [2] * ((tiles - 2) // 2) + [1] * (tiles % 2) + [1]
+    body = units - 7
+    sizes = [3] + [5] * (body // 5) + [body % 5] * (body % 5 > 0) + [4]
     return cut, sizes
 
 
@@ -83,7 +85,7 @@
 
 
 def step_chunks(factor, values, v, start, sizes):
-    columns, tile, count = v.shape[1], TILE * LINE, len(values)
+    columns, tile, count = v.shape[1], UNIT, len(values)
     places = begins(sizes)
 
     def kernel(factor, *refs):
@@ -105,7 +107,7 @@
 
 
 def move_chunks(is_end, share, totals, backs, values, v, start, sizes, carried):
-    columns, tile, count, chunks = v.shape[1], TILE * LINE, len(values), len(sizes)
+    columns, tile, count, chunks = v.shape[1], UNIT, len(values), len(sizes)
     places = begins(sizes)
 
     def kernel(is_end, v, *refs):
@@ -283,7 +285,7 @@
     flat_v = line_v.reshape(outers * rest, columns)
     end_flag = is_end.astype(jnp.int32).reshape(1)
     next_spread_v, spread_sq = move_spread(share, factor, spread, spread_v)
-    early = {4: next_spread_v}
+    early = {3: next_spread_v}
     count, places = len(sizes), begins(sizes)
     own = step_chunks(line_factor, flat, flat_v, 0, sizes[:1])
     own += step_chunks(line_factor, flat, tie(flat_v, own[0]), places[1], sizes[1:2])
@@ -307,11 +309,12 @@
         total = total + send(total, ACROSS)
         if chunk in early:
             total = tie(total, early[chunk])
-        if chunk in (count - 3, count - 1):
-            carried = move(groups[chunk == count - 1], carried)
+        if chunk == count - 2:
+            carried = move(groups[0], carried)
             total = tie(total, carried[1])
         totals.append(total)
         backs.append(send(total, TO_ENDS))
+    carried = move(groups[1], carried)
     for part in groups[2:]:
         carried = move(part, carried)
     spread_v = next_spread_v

time: 677 us -> 687 us (1.015)
  Pallas kernels: 63.9 us -> 76.8 us
  starting transfers between devices: 97.9 us -> 88.2 us
  waiting for transfers between devices: 423 us -> 432 us
    pallas_call x11, Pallas kernels: 63.9 us -> 76.8 us  [run(): pl.pallas_call(kernel, grid_spec=pltpu.PrefetchScalarGridSpec(num_scalar_...]
    ppermute x41 -> x35, starting transfers between devices: 83.4 us -> 73.5 us  [send(): return lax.ppermute(value, axis, pairs)]
    ppermute x41 -> x35, waiting for transfers between devices: 398 us -> 407 us  [send(): return lax.ppermute(value, axis, pairs)]
  transfers between devices with their start and end apart: 52 -> 46, of which waited for: 26 -> 24; matrix products, arithmetic and copies ran while one was open for 9% -> 9% of each run, Pallas kernels for 8% -> 9%
where the time goes in v10:
time: 687 us; the launch traced here: 683 us
  waiting for transfers between devices  432 us (63%)
  starting transfers between devices  88.2 us (13%)
  Pallas kernels  76.8 us (11%)
  other arithmetic  58.4 us (9%)
  local copies, waits for them, and re-layouts  27.2 us (4%)
    ppermute x35, waiting for transfers between devices, send(): return lax.ppermute(value, axis, pairs)  407 us
    pallas_call x11, Pallas kernels, run(): pl.pallas_call(kernel, grid_spec=pltpu.PrefetchScalarGridSpec(num_scalar_...  76.8 us
    ppermute x35, starting transfers between devices, send(): return lax.ppermute(value, axis, pairs)  73.5 us
    ppermute x10, waiting for transfers between devices, sum_over_devices(): lax.ppermute(value, axis, [(i, i ^ step) for i in range(size)])  24.9 us
    reduce_sum x4, other arithmetic, on_device(): square = jnp.sum(jnp.square(held[place] - v))  17.5 us
    dynamic_slice x3, local copies, waits for them, and re-layouts, line_rows(): lax.dynamic_slice(source, (worker * outers, cut, 0), (outers, rest, colum...  14.1 us
  transfers between devices with their start and end apart: 46, of which 24 were waited for; matrix products, arithmetic and copies ran while one was open for 9% of the time, Pallas kernels for 9%

profile of v10, /device:TPU:0, one launch (start us, length us, event | category | flops | bytes accessed | tf_op | source)
XLA Modules:
  0.0 683.5 jit_solution(9736150508566783395)
XLA Ops:
  0.0 11.5 %slice.28 = f32[16,96,2048]{2,1,0:T(8,128)} slice(f32[16,224,2048]{2,1,0:T(8,128)} %bitcast.62), slice={[0:16], [0:96], [0:2048]} | slice | bytes 25165824 | tf_op jit(solution)/shard_map/slice | solution.py:253
  11.5 7.6 %all-to-all-start = ((f32[16,96,2048]{2,1,0:T(8,128)}), f32[16,96,2048]{2,1,0:T(8,128)}, u32[]{:S(2)}, u32[]{:S(2)}) async-start(f32[16,96,2048]{2,1,0:T(8,128)} %slice.28), calls=%async_computation | async-start | bytes 25165824 | tf_op jit(solution)/shard_map/all_to_all | solution.py:252
  19.1 1.9 collective-permute-start
  21.1 4.7 constant_dynamic-slice_fusion.3
  25.7 4.7 constant_dynamic-slice_fusion.2
  30.5 4.7 constant_dynamic-slice_fusion.1
  35.2 1.6 collective-permute-start.6
  36.7 1.6 collective-permute-start.3
  38.4 206.6 %collective-permute-done = f32[128,2048]{1,0:T(8,128)} collective-permute-done((f32[128,2048]{1,0:T(8,128)S(1)}, f32[128,2048]{1,0:T(8,128)}, u32[]{:S(2)}, u32[]{:S(2)}) %collective-permute-start) | collective-permute-done | bytes 1048608 | tf_op jit(solution)/shard_map/ppermute | solution.py:36
  245.0 1.7 collective-permute-start.1
  246.6 1.6 collective-permute-start.7
  251.1 89.2 %collective-permute-done.4 = f32[128,2048]{1,0:T(8,128)} collective-permute-done((f32[128,2048]{1,0:T(8,128)}, f32[128,2048]{1,0:T(8,128)}, u32[]{:S(2)}, u32[]{:S(2)}) %collective-permute-start.4) | collective-permute-done | bytes 1048608 | tf_op jit(solution)/shard_map/ppermute | solution.py:36
  340.3 22.5 %collective-permute-done.2 = f32[128,2048]{1,0:T(8,128)} collective-permute-done((f32[128,2048]{1,0:T(8,128)}, f32[128,2048]{1,0:T(8,128)}, u32[]{:S(2)}, u32[]{:S(2)}) %collective-permute-start.2) | collective-permute-done | bytes 1048608 | tf_op jit(solution)/shard_map/ppermute | solution.py:36
  362.8 2.5 select_bitcast_fusion.3
  365.3 4.9 multiply_reduce_fusion.5
  370.8 4.8 multiply_reduce_fusion.4
  376.2 4.0 multiply_reduce_fusion.3
  380.9 3.9 multiply_reduce_fusion.2
  385.4 6.0 multiply_reduce_fusion.1
  394.1 2.1 collective-permute-done.9
  396.2 3.6 collective-permute-done.10
  400.8 3.4 collective-permute-done.11
  405.7 2.0 collective-permute-done.12
  408.6 3.2 shard_map.38
  411.8 4.5 shard_map.39
  416.3 2.1 collective-permute-start.24
  419.7 7.7 %shard_map.40 = (f32[80,2048]{1,0:T(8,128)}, f32[80,2048]{1,0:T(8,128)}) custom-call(f32[4]{0:T(128)} %select_reduce_fusion.2.factor, f32[512,2048]{1,0:T(8,128)} %bitcast.16.refs_0_, f32[512,2048]{1,0:T(8,128)} %bitcast.17.refs_1_, f32[512,2048]{1,0:T(8,128)} %bitcast.18.refs_2_, f32[512,2048]{1,0:T(8,128)} %bitcast.53, f32[512,2048]{1,0:T(8,128)} %bitcast.45), custom_call_target="tpu_custom_call" | custom-call | flops 7864320 | bytes 7864320 | tf_op jit(solution)/shard_map/pallas_call | solution.py:63
  428.8 13.3 %collective-permute-done.16 = f32[48,2048]{1,0:T(8,128)S(1)} collective-permute-done((f32[48,2048]{1,0:T(8,128)S(1)}, f32[48,2048]{1,0:T(8,128)S(1)}, u32[]{:S(2)}, u32[]{:S(2)}) %collective-permute-start.16) | collective-permute-done | bytes 393248 | tf_op jit(solution)/shard_map/ppermute | solution.py:36
  442.9 1.5 collective-permute-start.25
  444.5 9.0 %collective-permute-start.23 = (f32[80,2048]{1,0:T(8,128)}, f32[80,2048]{1,0:T(8,128)}, u32[]{:S(2)}, u32[]{:S(2)}) collective-permute-start(f32[80,2048]{1,0:T(8,128)} %get-tuple-element.58), channel_id=1, source_target_pairs={{0,2},{6,4},{1,3},{7,5},{8,10},{14,12},{9,11},{15,13},{16,18},{22,... | collective-permute-start | bytes 1966088 | tf_op jit(solution)/shard_map/ppermute | solution.py:36
  453.5 10.3 %shard_map.41 = (f32[80,2048]{1,0:T(8,128)}, f32[80,2048]{1,0:T(8,128)}, f32[64,2048]{1,0:T(8,128)}) custom-call(f32[4]{0:T(128)} %select_reduce_fusion.2.factor, f32[512,2048]{1,0:T(8,128)} %bitcast.16.refs_0_, f32[512,2048]{1,0:T(8,128)} %bitcast.17.refs_1_, f32[512,2048]{1,0:T(8,128)} %bitcast.18.refs_2_, f32[512,2048]{1,0:T(8,128)} %bitcast.54, ...), custom_call_target="tpu_custom_call" | custom-call | flops 11010048 | bytes 11010048 | tf_op jit(solution)/shard_map/pallas_call | solution.py:63
  465.5 2.9 collective-permute-start.14
  473.0 6.6 collective-permute-start.22
  479.7 4.7 collective-permute-done.14
  486.8 6.5 collective-permute-start.13
  494.5 7.9 %shard_map.37 = (f32[96,2048]{1,0:T(8,128)}, f32[16,8,128]{2,1,0:T(8,128)}) custom-call(f32[16]{0:T(128)} %copy-done.21, f32[96,2048]{1,0:T(8,128)} %copy-done.1, f32[16,96,2048]{2,1,0:T(8,128)} %all-to-all-done.values), custom_call_target="tpu_custom_call" | custom-call | flops 14155776 | bytes 14155776 | tf_op jit(solution)/shard_map/pallas_call | solution.py:63
  503.7 1.6 add.182
  509.5 2.1 add.176
  514.3 8.9 %collective-permute-done.28.refs_6_ = f32[48,2048]{1,0:T(8,128)} collective-permute-done((f32[48,2048]{1,0:T(8,128)}, f32[48,2048]{1,0:T(8,128)}, u32[]{:S(2)}, u32[]{:S(2)}) %collective-permute-start.28) | collective-permute-done | bytes 393248 | tf_op jit(solution)/shard_map/ppermute | solution.py:36
  524.6 6.6 shard_map.42
  537.8 13.6 %collective-permute-done.33.refs_7_ = f32[80,2048]{1,0:T(8,128)} collective-permute-done((f32[80,2048]{1,0:T(8,128)S(1)}, f32[80,2048]{1,0:T(8,128)}, u32[]{:S(2)}, u32[]{:S(2)}) %collective-permute-start.33) | collective-permute-done | bytes 655392 | tf_op jit(solution)/shard_map/ppermute | solution.py:36
  551.4 7.9 %shard_map.43 = (f32[512,2048]{1,0:T(8,128)}, f32[4,8,128]{2,1,0:T(8,128)}) custom-call(s32[1]{0:T(128)} %bitcast.14.is_end, f32[512,2048]{1,0:T(8,128)} %bitcast.48, f32[512,2048]{1,0:T(8,128)} %bitcast.16.refs_0_, f32[512,2048]{1,0:T(8,128)} %bitcast.17.refs_1_, f32[512,2048]{1,0:T(8,128)} %bitcast.18.refs_2_, ...), custom_call_target="tpu_custom_call", output_to_operand_aliasing={{0}: (10, {}), {1}: (11, {})} | custom-call | flops 10485760 | bytes 10485760 | tf_op jit(solution)/shard_map/pallas_call | solution.py:63
  559.3 6.1 collective-permute-done.30.refs_6_
  565.4 11.5 %collective-permute-done.31.refs_7_ = f32[80,2048]{1,0:T(8,128)} collective-permute-done((f32[80,2048]{1,0:T(8,128)S(1)}, f32[80,2048]{1,0:T(8,128)}, u32[]{:S(2)}, u32[]{:S(2)}) %collective-permute-start.31) | collective-permute-done | bytes 655392 | tf_op jit(solution)/shard_map/ppermute | solution.py:36
  576.9 7.9 %shard_map.44 = (f32[512,2048]{1,0:T(8,128)}, f32[4,8,128]{2,1,0:T(8,128)}) custom-call(s32[1]{0:T(128)} %bitcast.14.is_end, f32[512,2048]{1,0:T(8,128)} %bitcast.49, f32[512,2048]{1,0:T(8,128)} %bitcast.16.refs_0_, f32[512,2048]{1,0:T(8,128)} %bitcast.17.refs_1_, f32[512,2048]{1,0:T(8,128)} %bitcast.18.refs_2_, ...), custom_call_target="tpu_custom_call", output_to_operand_aliasing={{0}: (10, {}), {1}: (11, {})} | custom-call | flops 10485760 | bytes 10485760 | tf_op jit(solution)/shard_map/pallas_call | solution.py:63
  584.8 3.9 shard_map.45
  590.8 1.6 collective-permute-start.35
  592.5 1.9 collective-permute-done.35
  594.4 3.6 collective-permute-done.36
  598.5 4.0 collective-permute-done.37
  604.0 2.0 collective-permute-done.38
  606.7 4.3 shard_map.46
  611.0 2.9 collective-permute-start.39
  614.6 12.5 %shard_map.47 = (f32[128,2048]{1,0:T(8,128)}, f32[128,2048]{1,0:T(8,128)}, f32[128,2048]{1,0:T(8,128)}) custom-call(s32[3]{0:T(128)} %pad_add_fusion.1.places, f32[4]{0:T(128)} %select_reduce_fusion.factor, f32[4,128,2048]{2,1,0:T(8,128)} %collective-permute-done.7.refs_0_, f32[4,128,2048]{2,1,0:T(8,128)} %collective-permute-done.6.refs_1_, ...), custom_call_target="tpu_custom_call" | custom-call | flops 18874368 | bytes 18874368 | tf_op jit(solution)/shard_map/pallas_call | solution.py:63
  627.1 2.5 collective-permute-start.43
  629.6 7.2 %collective-permute-done.39 = f32[128,2048]{1,0:T(8,128)} collective-permute-done((f32[128,2048]{1,0:T(8,128)}, f32[128,2048]{1,0:T(8,128)}, u32[]{:S(2)}, u32[]{:S(2)}) %collective-permute-start.39) | collective-permute-done | bytes 1048608 | tf_op jit(solution)/shard_map/ppermute | solution.py:36
  636.8 2.3 add.193
  639.8 6.7 collective-permute-start.42
  646.5 12.7 %collective-permute-done.43 = f32[128,2048]{1,0:T(8,128)} collective-permute-done((f32[128,2048]{1,0:T(8,128)}, f32[128,2048]{1,0:T(8,128)}, u32[]{:S(2)}, u32[]{:S(2)}) %collective-permute-start.43) | collective-permute-done | bytes 1048608 | tf_op jit(solution)/shard_map/ppermute | solution.py:36
  659.2 1.7 add.197
  663.1 6.4 multiply_reduce_fusion
  671.1 5.5 collective-permute-done.42
  676.6 4.1 collective-permute-done.41
  680.7 2.7 fusion
  (140 shorter events, 50.0 us)
Async XLA Ops:
  11.5 373.9 %all-to-all-start = ((f32[16,96,2048]{2,1,0:T(8,128)}), f32[16,96,2048]{2,1,0:T(8,128)}, u32[]{:S(2)}, u32[]{:S(2)}) async-start(f32[16,96,2048]{2,1,0:T(8,128)} %slice.28), calls=%async_computation | async-start | bytes 25165824 | tf_op jit(solution)/shard_map/all_to_all | solution.py:252
  19.1 225.8 %collective-permute-start = (f32[128,2048]{1,0:T(8,128)S(1)}, f32[128,2048]{1,0:T(8,128)}, u32[]{:S(2)}, u32[]{:S(2)}) collective-permute-start(f32[128,2048]{1,0:T(8,128)S(1)} %slice.24), channel_id=1, source_target_pairs={{0,2},{2,0},{4,6},{6,4},{1,3},{3,1},{5,7},{7,5},{8,10},{10,8},{12,... | collective-permute-start | bytes 3145736 | tf_op jit(solution)/shard_map/ppermute | solution.py:36
  35.2 335.6 %collective-permute-start.5 = (f32[4,128,2048]{2,1,0:T(8,128)}, f32[4,128,2048]{2,1,0:T(8,128)}, u32[]{:S(2)}, u32[]{:S(2)}) collective-permute-start(f32[4,128,2048]{2,1,0:T(8,128)} %constant_dynamic-slice_fusion.1), channel_id=1, source_target_pairs={{0,8},{8,0},{16,24},{24,16},{1,9},{9,1},{17,25},{25,17},{2,10},{10... | collective-permute-start | bytes 12582920 | tf_op jit(solution)/shard_map/ppermute | solution.py:36
  35.2 341.0 %collective-permute-start.6 = (f32[4,128,2048]{2,1,0:T(8,128)}, f32[4,128,2048]{2,1,0:T(8,128)}, u32[]{:S(2)}, u32[]{:S(2)}) collective-permute-start(f32[4,128,2048]{2,1,0:T(8,128)} %constant_dynamic-slice_fusion.2), channel_id=1, source_target_pairs={{0,24},{8,16},{16,8},{24,0},{1,25},{9,17},{17,9},{25,1},{2,26},{10... | collective-permute-start | bytes 12582920 | tf_op jit(solution)/shard_map/ppermute | solution.py:36
  36.7 211.5 %collective-permute-start.3 = (f32[128,2048]{1,0:T(8,128)S(1)}, f32[128,2048]{1,0:T(8,128)}, u32[]{:S(2)}, u32[]{:S(2)}) collective-permute-start(f32[128,2048]{1,0:T(8,128)S(1)} %slice.24), channel_id=1, source_target_pairs={{2,4},{4,2},{3,5},{5,3},{10,12},{12,10},{11,13},{13,11},{18,20},{2... | collective-permute-start | bytes 3145736 | tf_op jit(solution)/shard_map/ppermute | solution.py:36
  245.0 4.6 collective-permute-start.1
  246.6 134.2 %collective-permute-start.7 = (f32[4,128,2048]{2,1,0:T(8,128)}, f32[4,128,2048]{2,1,0:T(8,128)}, u32[]{:S(2)}, u32[]{:S(2)}) collective-permute-start(f32[4,128,2048]{2,1,0:T(8,128)} %constant_dynamic-slice_fusion.3), channel_id=1, source_target_pairs={{0,16},{8,24},{16,0},{24,8},{1,17},{9,25},{17,1},{25,9},{2,18},{10... | collective-permute-start | bytes 12582920 | tf_op jit(solution)/shard_map/ppermute | solution.py:36
  248.3 92.0 %collective-permute-start.4 = (f32[128,2048]{1,0:T(8,128)}, f32[128,2048]{1,0:T(8,128)}, u32[]{:S(2)}, u32[]{:S(2)}) collective-permute-start(f32[128,2048]{1,0:T(8,128)} %collective-permute-done.3), channel_id=1, source_target_pairs={{2,0},{4,6},{3,1},{5,7},{10,8},{12,14},{11,9},{13,15},{18,16},{20,... | collective-permute-start | bytes 3145736 | tf_op jit(solution)/shard_map/ppermute | solution.py:36
  249.6 113.2 %collective-permute-start.2 = (f32[128,2048]{1,0:T(8,128)}, f32[128,2048]{1,0:T(8,128)}, u32[]{:S(2)}, u32[]{:S(2)}) collective-permute-start(f32[128,2048]{1,0:T(8,128)} %collective-permute-done.1), channel_id=1, source_target_pairs={{2,0},{4,6},{3,1},{5,7},{10,8},{12,14},{11,9},{13,15},{18,16},{20,... | collective-permute-start | bytes 3145736 | tf_op jit(solution)/shard_map/ppermute | solution.py:36
  250.9 134.4 %copy-start.1 = (f32[96,2048]{1,0:T(8,128)}, f32[96,2048]{1,0:T(8,128)S(1)}, u32[]{:S(2)}) copy-start(f32[96,2048]{1,0:T(8,128)S(1)} %slice.22.v) | copy-start | bytes 2359300
  370.2 10.7 %copy-start = (f32[4,128,2048]{2,1,0:T(8,128)}, f32[4,128,2048]{2,1,0:T(8,128)S(1)}, u32[]{:S(2)}) copy-start(f32[4,128,2048]{2,1,0:T(8,128)S(1)} %get-tuple-element.45) | copy-start | bytes 12582916
  391.4 1.2 collective-permute-start.8
  392.6 3.6 collective-permute-start.9
  396.2 3.6 collective-permute-start.10
  399.8 4.5 collective-permute-start.11
  404.2 3.6 collective-permute-start.12
  416.3 26.5 %copy-start.11 = (f32[80,2048]{1,0:T(8,128)S(1)}, f32[80,2048]{1,0:T(8,128)}, u32[]{:S(2)}) copy-start(f32[80,2048]{1,0:T(8,128)} %shard_map.39) | copy-start | bytes 1966084
  416.3 26.5 %collective-permute-start.24 = (f32[80,2048]{1,0:T(8,128)}, f32[80,2048]{1,0:T(8,128)S(1)}, u32[]{:S(2)}, u32[]{:S(2)}) collective-permute-start(f32[80,2048]{1,0:T(8,128)} %shard_map.39), channel_id=1, source_target_pairs={{0,2},{6,4},{1,3},{7,5},{8,10},{14,12},{9,11},{15,13},{16,18},{22,... | collective-permute-start | bytes 1966088 | tf_op jit(solution)/shard_map/ppermute | solution.py:36
  418.4 23.7 %collective-permute-start.16 = (f32[48,2048]{1,0:T(8,128)S(1)}, f32[48,2048]{1,0:T(8,128)S(1)}, u32[]{:S(2)}, u32[]{:S(2)}) collective-permute-start(f32[48,2048]{1,0:T(8,128)S(1)} %copy-done.13), channel_id=1, source_target_pairs={{0,2},{6,4},{1,3},{7,5},{8,10},{14,12},{9,11},{15,13},{16,18},{22,... | collective-permute-start | bytes 1179656 | tf_op jit(solution)/shard_map/ppermute | solution.py:36
  427.4 37.2 %collective-permute-start.15 = (f32[80,2048]{1,0:T(8,128)}, f32[80,2048]{1,0:T(8,128)S(1)}, u32[]{:S(2)}, u32[]{:S(2)}) collective-permute-start(f32[80,2048]{1,0:T(8,128)} %get-tuple-element.50), channel_id=1, source_target_pairs={{0,2},{6,4},{1,3},{7,5},{8,10},{14,12},{9,11},{15,13},{16,18},{22,... | collective-permute-start | bytes 1966088 | tf_op jit(solution)/shard_map/ppermute | solution.py:36
  442.1 21.7 %collective-permute-start.17 = (f32[48,2048]{1,0:T(8,128)S(1)}, f32[48,2048]{1,0:T(8,128)S(1)}, u32[]{:S(2)}, u32[]{:S(2)}) collective-permute-start(f32[48,2048]{1,0:T(8,128)S(1)} %add.170), channel_id=1, source_target_pairs={{2,4},{4,2},{3,5},{5,3},{10,12},{12,10},{11,13},{13,11},{18,20},{2... | collective-permute-start | bytes 1179656 | tf_op jit(solution)/shard_map/ppermute | solution.py:36
  442.9 25.5 %collective-permute-start.25 = (f32[80,2048]{1,0:T(8,128)S(1)}, f32[80,2048]{1,0:T(8,128)}, u32[]{:S(2)}, u32[]{:S(2)}) collective-permute-start(f32[80,2048]{1,0:T(8,128)S(1)} %add.178), channel_id=1, source_target_pairs={{2,4},{4,2},{3,5},{5,3},{10,12},{12,10},{11,13},{13,11},{18,20},{2... | collective-permute-start | bytes 1966088 | tf_op jit(solution)/shard_map/ppermute | solution.py:36
  444.5 20.2 %copy-start.18 = (f32[80,2048]{1,0:T(8,128)S(1)}, f32[80,2048]{1,0:T(8,128)}, u32[]{:S(2)}) copy-start(f32[80,2048]{1,0:T(8,128)} %get-tuple-element.50) | copy-start | bytes 1966084
  444.5 25.8 %collective-permute-start.23 = (f32[80,2048]{1,0:T(8,128)}, f32[80,2048]{1,0:T(8,128)}, u32[]{:S(2)}, u32[]{:S(2)}) collective-permute-start(f32[80,2048]{1,0:T(8,128)} %get-tuple-element.58), channel_id=1, source_target_pairs={{0,2},{6,4},{1,3},{7,5},{8,10},{14,12},{9,11},{15,13},{16,18},{22,... | collective-permute-start | bytes 1966088 | tf_op jit(solution)/shard_map/ppermute | solution.py:36
  463.8 9.2 %copy-start.15 = (f32[80,2048]{1,0:T(8,128)S(1)}, f32[80,2048]{1,0:T(8,128)}, u32[]{:S(2)}) copy-start(f32[80,2048]{1,0:T(8,128)} %get-tuple-element.57) | copy-start | bytes 1966084
  464.6 19.7 %copy-start.17 = (f32[80,2048]{1,0:T(8,128)S(1)}, f32[80,2048]{1,0:T(8,128)}, u32[]{:S(2)}) copy-start(f32[80,2048]{1,0:T(8,128)} %get-tuple-element.53) | copy-start | bytes 1966084
  464.7 22.1 %copy-start.19 = (f32[64,2048]{1,0:T(8,128)S(1)}, f32[64,2048]{1,0:T(8,128)}, u32[]{:S(2)}) copy-start(f32[64,2048]{1,0:T(8,128)} %get-tuple-element.52) | copy-start | bytes 1572868
  464.7 14.9 %collective-permute-start.18 = (f32[80,2048]{1,0:T(8,128)S(1)}, f32[80,2048]{1,0:T(8,128)S(1)}, u32[]{:S(2)}, u32[]{:S(2)}) collective-permute-start(f32[80,2048]{1,0:T(8,128)S(1)} %add.172), channel_id=1, source_target_pairs={{2,4},{4,2},{3,5},{5,3},{10,12},{12,10},{11,13},{13,11},{18,20},{2... | collective-permute-start | bytes 1966088 | tf_op jit(solution)/shard_map/ppermute | solution.py:36
  465.5 18.8 %collective-permute-start.14 = (f32[80,2048]{1,0:T(8,128)}, f32[80,2048]{1,0:T(8,128)S(1)}, u32[]{:S(2)}, u32[]{:S(2)}) collective-permute-start(f32[80,2048]{1,0:T(8,128)} %get-tuple-element.53), channel_id=1, source_target_pairs={{0,2},{6,4},{1,3},{7,5},{8,10},{14,12},{9,11},{15,13},{16,18},{22,... | collective-permute-start | bytes 1966088 | tf_op jit(solution)/shard_map/ppermute | solution.py:36
  469.6 32.9 %copy-start.7 = (f32[80,2048]{1,0:T(8,128)}, f32[80,2048]{1,0:T(8,128)S(1)}, u32[]{:S(2)}) copy-start(f32[80,2048]{1,0:T(8,128)S(1)} %add.179.refs_5_) | copy-start | bytes 1966084
  471.4 31.0 %collective-permute-start.26 = (f32[80,2048]{1,0:T(8,128)S(1)}, f32[80,2048]{1,0:T(8,128)}, u32[]{:S(2)}, u32[]{:S(2)}) collective-permute-start(f32[80,2048]{1,0:T(8,128)S(1)} %add.180), channel_id=1, source_target_pairs={{2,4},{4,2},{3,5},{5,3},{10,12},{12,10},{11,13},{13,11},{18,20},{2... | collective-permute-start | bytes 1966088 | tf_op jit(solution)/shard_map/ppermute | solution.py:36
  473.0 30.7 %collective-permute-start.22 = (f32[80,2048]{1,0:T(8,128)S(1)}, f32[80,2048]{1,0:T(8,128)}, u32[]{:S(2)}, u32[]{:S(2)}) collective-permute-start(f32[80,2048]{1,0:T(8,128)S(1)} %copy-done.15), channel_id=1, source_target_pairs={{0,2},{6,4},{1,3},{7,5},{8,10},{14,12},{9,11},{15,13},{16,18},{22,... | collective-permute-start | bytes 1966088 | tf_op jit(solution)/shard_map/ppermute | solution.py:36
  479.7 33.4 %copy-start.6 = (f32[80,2048]{1,0:T(8,128)}, f32[80,2048]{1,0:T(8,128)S(1)}, u32[]{:S(2)}) copy-start(f32[80,2048]{1,0:T(8,128)S(1)} %add.173.refs_4_) | copy-start | bytes 1966084
  485.3 22.8 %collective-permute-start.19 = (f32[80,2048]{1,0:T(8,128)}, f32[80,2048]{1,0:T(8,128)}, u32[]{:S(2)}, u32[]{:S(2)}) collective-permute-start(f32[80,2048]{1,0:T(8,128)} %add.174), channel_id=1, source_target_pairs={{2,4},{4,2},{3,5},{5,3},{10,12},{12,10},{11,13},{13,11},{18,20},{2... | collective-permute-start | bytes 1966088 | tf_op jit(solution)/shard_map/ppermute | solution.py:36
  486.8 22.7 %collective-permute-start.13 = (f32[64,2048]{1,0:T(8,128)S(1)}, f32[64,2048]{1,0:T(8,128)}, u32[]{:S(2)}, u32[]{:S(2)}) collective-permute-start(f32[64,2048]{1,0:T(8,128)S(1)} %copy-done.19), channel_id=1, source_target_pairs={{0,2},{6,4},{1,3},{7,5},{8,10},{14,12},{9,11},{15,13},{16,18},{22,... | collective-permute-start | bytes 1572872 | tf_op jit(solution)/shard_map/ppermute | solution.py:36
  493.3 31.3 %collective-permute-start.29 = (f32[80,2048]{1,0:T(8,128)S(1)}, f32[80,2048]{1,0:T(8,128)}, u32[]{:S(2)}, u32[]{:S(2)}) collective-permute-start(f32[80,2048]{1,0:T(8,128)S(1)} %add.179.refs_5_), channel_id=1, source_target_pairs={{2,0},{4,6},{3,1},{5,7},{10,8},{12,14},{11,9},{13,15},{18,16},{20,... | collective-permute-start | bytes 1966088 | tf_op jit(solution)/shard_map/ppermute | solution.py:36
  503.7 27.5 %copy-start.8 = (f32[80,2048]{1,0:T(8,128)}, f32[80,2048]{1,0:T(8,128)S(1)}, u32[]{:S(2)}) copy-start(f32[80,2048]{1,0:T(8,128)S(1)} %add.181.refs_5_) | copy-start | bytes 1966084
  505.3 27.2 %collective-permute-start.27 = (f32[80,2048]{1,0:T(8,128)S(1)}, f32[80,2048]{1,0:T(8,128)}, u32[]{:S(2)}, u32[]{:S(2)}) collective-permute-start(f32[80,2048]{1,0:T(8,128)S(1)} %add.182), channel_id=1, source_target_pairs={{2,4},{4,2},{3,5},{5,3},{10,12},{12,10},{11,13},{13,11},{18,20},{2... | collective-permute-start | bytes 1966088 | tf_op jit(solution)/shard_map/ppermute | solution.py:36
  506.8 16.5 %collective-permute-start.28 = (f32[48,2048]{1,0:T(8,128)}, f32[48,2048]{1,0:T(8,128)}, u32[]{:S(2)}, u32[]{:S(2)}) collective-permute-start(f32[48,2048]{1,0:T(8,128)} %add.171.refs_4_), channel_id=1, source_target_pairs={{2,0},{4,6},{3,1},{5,7},{10,8},{12,14},{11,9},{13,15},{18,16},{20,... | collective-permute-start | bytes 1179656 | tf_op jit(solution)/shard_map/ppermute | solution.py:36
  509.4 21.7 %copy-start.9 = (f32[80,2048]{1,0:T(8,128)}, f32[80,2048]{1,0:T(8,128)S(1)}, u32[]{:S(2)}) copy-start(f32[80,2048]{1,0:T(8,128)S(1)} %add.175.refs_4_) | copy-start | bytes 1966084
  511.6 23.4 %collective-permute-start.20 = (f32[64,2048]{1,0:T(8,128)}, f32[64,2048]{1,0:T(8,128)}, u32[]{:S(2)}, u32[]{:S(2)}) collective-permute-start(f32[64,2048]{1,0:T(8,128)} %add.176), channel_id=1, source_target_pairs={{2,4},{4,2},{3,5},{5,3},{10,12},{12,10},{11,13},{13,11},{18,20},{2... | collective-permute-start | bytes 1572872 | tf_op jit(solution)/shard_map/ppermute | solution.py:36
  513.1 24.7 %collective-permute-start.32 = (f32[80,2048]{1,0:T(8,128)S(1)}, f32[80,2048]{1,0:T(8,128)}, u32[]{:S(2)}, u32[]{:S(2)}) collective-permute-start(f32[80,2048]{1,0:T(8,128)S(1)} %add.173.refs_4_), channel_id=1, source_target_pairs={{2,0},{4,6},{3,1},{5,7},{10,8},{12,14},{11,9},{13,15},{18,16},{20,... | collective-permute-start | bytes 1966088 | tf_op jit(solution)/shard_map/ppermute | solution.py:36
  523.3 28.1 %collective-permute-start.33 = (f32[80,2048]{1,0:T(8,128)S(1)}, f32[80,2048]{1,0:T(8,128)}, u32[]{:S(2)}, u32[]{:S(2)}) collective-permute-start(f32[80,2048]{1,0:T(8,128)S(1)} %add.181.refs_5_), channel_id=1, source_target_pairs={{2,0},{4,6},{3,1},{5,7},{10,8},{12,14},{11,9},{13,15},{18,16},{20,... | collective-permute-start | bytes 1966088 | tf_op jit(solution)/shard_map/ppermute | solution.py:36
  524.6 13.0 %copy-start.20 = (f32[16,8,128]{2,1,0:T(8,128)S(1)}, f32[16,8,128]{2,1,0:T(8,128)}, u32[]{:S(2)}) copy-start(f32[16,8,128]{2,1,0:T(8,128)} %get-tuple-element.47) | copy-start | bytes 196612
  531.2 34.2 %collective-permute-start.30 = (f32[80,2048]{1,0:T(8,128)S(1)}, f32[80,2048]{1,0:T(8,128)}, u32[]{:S(2)}, u32[]{:S(2)}) collective-permute-start(f32[80,2048]{1,0:T(8,128)S(1)} %add.175.refs_4_), channel_id=1, source_target_pairs={{2,0},{4,6},{3,1},{5,7},{10,8},{12,14},{11,9},{13,15},{18,16},{20,... | collective-permute-start | bytes 1966088 | tf_op jit(solution)/shard_map/ppermute | solution.py:36
  533.7 25.6 %copy-start.10 = (f32[80,2048]{1,0:T(8,128)}, f32[80,2048]{1,0:T(8,128)S(1)}, u32[]{:S(2)}) copy-start(f32[80,2048]{1,0:T(8,128)S(1)} %add.183.refs_5_) | copy-start | bytes 1966084
  533.7 43.2 %collective-permute-start.31 = (f32[80,2048]{1,0:T(8,128)S(1)}, f32[80,2048]{1,0:T(8,128)}, u32[]{:S(2)}, u32[]{:S(2)}) collective-permute-start(f32[80,2048]{1,0:T(8,128)S(1)} %add.183.refs_5_), channel_id=1, source_target_pairs={{2,0},{4,6},{3,1},{5,7},{10,8},{12,14},{11,9},{13,15},{18,16},{20,... | collective-permute-start | bytes 1966088 | tf_op jit(solution)/shard_map/ppermute | solution.py:36
  536.3 23.0 %copy-start.12 = (f32[64,2048]{1,0:T(8,128)}, f32[64,2048]{1,0:T(8,128)S(1)}, u32[]{:S(2)}) copy-start(f32[64,2048]{1,0:T(8,128)S(1)} %add.177.refs_4_) | copy-start | bytes 1572868
  536.3 48.5 %collective-permute-start.21 = (f32[64,2048]{1,0:T(8,128)S(1)}, f32[64,2048]{1,0:T(8,128)}, u32[]{:S(2)}, u32[]{:S(2)}) collective-permute-start(f32[64,2048]{1,0:T(8,128)S(1)} %add.177.refs_4_), channel_id=1, source_target_pairs={{2,0},{4,6},{3,1},{5,7},{10,8},{12,14},{11,9},{13,15},{18,16},{20,... | collective-permute-start | bytes 1572872 | tf_op jit(solution)/shard_map/ppermute | solution.py:36
  589.6 1.2 collective-permute-start.34
  590.8 3.6 collective-permute-start.35
  594.4 3.6 collective-permute-start.36
  598.0 4.5 collective-permute-start.37
  602.4 3.6 collective-permute-start.38
  611.0 25.8 %collective-permute-start.39 = (f32[128,2048]{1,0:T(8,128)}, f32[128,2048]{1,0:T(8,128)}, u32[]{:S(2)}, u32[]{:S(2)}) collective-permute-start(f32[128,2048]{1,0:T(8,128)} %shard_map.46), channel_id=1, source_target_pairs={{0,2},{6,4},{1,3},{7,5},{8,10},{14,12},{9,11},{15,13},{16,18},{22,... | collective-permute-start | bytes 3145736 | tf_op jit(solution)/shard_map/ppermute | solution.py:36
  614.6 22.2 %copy-start.3 = (f32[128,2048]{1,0:T(8,128)S(1)}, f32[128,2048]{1,0:T(8,128)}, u32[]{:S(2)}) copy-start(f32[128,2048]{1,0:T(8,128)} %shard_map.46) | copy-start | bytes 3145732
  627.1 34.5 %copy-start.4 = (f32[128,2048]{1,0:T(8,128)S(1)}, f32[128,2048]{1,0:T(8,128)}, u32[]{:S(2)}) copy-start(f32[128,2048]{1,0:T(8,128)} %get-tuple-element.72) | copy-start | bytes 3145732
  627.1 36.0 %copy-start.5 = (f32[96,2048]{1,0:T(8,128)S(1)}, f32[96,2048]{1,0:T(8,128)}, u32[]{:S(2)}) copy-start(f32[96,2048]{1,0:T(8,128)} %get-tuple-element.46) | copy-start | bytes 2359300
  627.1 32.1 %collective-permute-start.43 = (f32[128,2048]{1,0:T(8,128)}, f32[128,2048]{1,0:T(8,128)}, u32[]{:S(2)}, u32[]{:S(2)}) collective-permute-start(f32[128,2048]{1,0:T(8,128)} %get-tuple-element.74), channel_id=1, source_target_pairs={{0,2},{6,4},{1,3},{7,5},{8,10},{14,12},{9,11},{15,13},{16,18},{22,... | collective-permute-start | bytes 3145736 | tf_op jit(solution)/shard_map/ppermute | solution.py:36
  639.1 22.6 %collective-permute-start.40 = (f32[128,2048]{1,0:T(8,128)}, f32[128,2048]{1,0:T(8,128)S(1)}, u32[]{:S(2)}, u32[]{:S(2)}) collective-permute-start(f32[128,2048]{1,0:T(8,128)} %add.193), channel_id=1, source_target_pairs={{2,4},{4,2},{3,5},{5,3},{10,12},{12,10},{11,13},{13,11},{18,20},{2... | collective-permute-start | bytes 3145736 | tf_op jit(solution)/shard_map/ppermute | solution.py:36
  639.8 36.8 %collective-permute-start.42 = (f32[128,2048]{1,0:T(8,128)}, f32[128,2048]{1,0:T(8,128)S(1)}, u32[]{:S(2)}, u32[]{:S(2)}) collective-permute-start(f32[128,2048]{1,0:T(8,128)} %get-tuple-element.73), channel_id=1, source_target_pairs={{0,2},{6,4},{1,3},{7,5},{8,10},{14,12},{9,11},{15,13},{16,18},{22,... | collective-permute-start | bytes 3145736 | tf_op jit(solution)/shard_map/ppermute | solution.py:36
  660.9 15.7 %collective-permute-start.44 = (f32[128,2048]{1,0:T(8,128)S(1)}, f32[128,2048]{1,0:T(8,128)S(1)}, u32[]{:S(2)}, u32[]{:S(2)}) collective-permute-start(f32[128,2048]{1,0:T(8,128)S(1)} %add.197), channel_id=1, source_target_pairs={{2,4},{4,2},{3,5},{5,3},{10,12},{12,10},{11,13},{13,11},{18,20},{2... | collective-permute-start | bytes 3145736 | tf_op jit(solution)/shard_map/ppermute | solution.py:36
  661.8 18.9 %collective-permute-start.41 = (f32[128,2048]{1,0:T(8,128)S(1)}, f32[128,2048]{1,0:T(8,128)S(1)}, u32[]{:S(2)}, u32[]{:S(2)}) collective-permute-start(f32[128,2048]{1,0:T(8,128)S(1)} %add.194), channel_id=1, source_target_pairs={{2,0},{4,6},{3,1},{5,7},{10,8},{12,14},{11,9},{13,15},{18,16},{20,... | collective-permute-start | bytes 3145736 | tf_op jit(solution)/shard_map/ppermute | solution.py:36
  669.6 11.2 %copy-start.14 = (f32[128,2048]{1,0:T(8,128)S(1)}, f32[128,2048]{1,0:T(8,128)}, u32[]{:S(2)}) copy-start(f32[128,2048]{1,0:T(8,128)} %get-tuple-element.73) | copy-start | bytes 3145732
  (4 other events, 24.7 us)

commit v11 on v10

--- a/solution.py
+++ b/solution.py
@@ -17,7 +17,7 @@
 UNIT = 16
 SPREAD = 3 / 7
 
-GRANT = 60 << 20
+GRANT = 8 << 20
 
 epsilon = 1e-06
 
@@ -51,8 +51,8 @@
     units = rest * outers // UNIT
     if outers != LINE or rest % TILE or units < 22 or not cut:
         return None
-    body = units - 7
-    sizes = [3] + [5] * (body // 5) + [body % 5] * (body % 5 > 0) + [4]
+    body = units - 12
+    sizes = [2, 4] + [5] * (body // 5) + [body % 5] * (body % 5 > 0) + [4, 2]
     return cut, sizes
 
 
@@ -132,10 +132,17 @@
             folded = sum(square[j : j + 8] for j in range(0, tile, 8))
             sq_out[k] += sum(folded[:, j : j + 128] for j in range(0, columns, 128))
 
-    at = pl.BlockSpec((tile, columns), lambda i: (start + i, 0))
-    squares = pl.BlockSpec((count, 8, 128), lambda i: (0, 0, 0))
-    parts = [group_spec(begin, size, tile, columns) for begin, size in zip(places, sizes)]
-    in_specs = [SMEM] + [at] * (count + 1) + parts + parts
+    at = pl.BlockSpec((tile, columns), lambda i, _: (start + i, 0))
+    squares = pl.BlockSpec((count, 8, 128), lambda i, _: (0, 0, 0))
+
+    def part(begin, size, wanted):
+        def index(i, is_end):
+            return (jnp.where(is_end[0] == wanted, jnp.clip(i - begin, 0, size - 1), 0), 0)
+
+        return pl.BlockSpec((tile, columns), index)
+
+    parts = [part(*place, wanted) for wanted in (0, 1) for place in zip(places, sizes)]
+    in_specs = [at] * (count + 1) + parts
     operands = (is_end, v, *values, *totals, *backs)
     aliases = {}
     if carried:
@@ -147,7 +154,7 @@
         jax.ShapeDtypeStruct((count, 8, 128), v.dtype),
     )
     moved = (count + 4) * sum(sizes) * tile * columns
-    return run(kernel, (sum(sizes),), in_specs, (at, squares), shapes, operands, moved, aliases)
+    return run(kernel, (sum(sizes),), in_specs, (at, squares), shapes, operands, moved, aliases, prefetch=1)
 
 
 def step_blocks(places, factor, values, v):
@@ -291,7 +298,7 @@
     own += step_chunks(line_factor, flat, tie(flat_v, own[0]), places[1], sizes[1:2])
     own += step_chunks(line_factor, flat, tie(flat_v, own[1]), places[2], sizes[2:4])
     own += step_chunks(line_factor, flat, tie(flat_v, own[2]), places[4], sizes[4:])
-    cuts = [0, count - 5, count - 3, count - 1, count]
+    cuts = [0, count - 4, count - 2, count]
     groups = [slice(*pair) for pair in zip(cuts, cuts[1:])]
     totals, backs, carried = [], [], ()
 
@@ -309,13 +316,10 @@
         total = total + send(total, ACROSS)
         if chunk in early:
             total = tie(total, early[chunk])
-        if chunk == count - 2:
-            carried = move(groups[0], carried)
-            total = tie(total, carried[1])
         totals.append(total)
         backs.append(send(total, TO_ENDS))
-    carried = move(groups[1], carried)
-    for part in groups[2:]:
+    carried = move(groups[0], carried)
+    for part in groups[1:]:
         carried = move(part, carried)
     spread_v = next_spread_v
     flat_v = carried[0]
@@ -328,10 +332,10 @@
     block += step_blocks(order[1:], line_factor, held, tie(line_v, block[0]))
     arrived = [send(block[place], TO_MIDS) for place in range(3)]
     passed = [send(block[place] + arrived[place], ACROSS) for place in range(2)]
-    end_sum = block[3] + send(block[3] + passed[0], TO_ENDS)
-    mid_sum = block[2] + arrived[2] + passed[1]
+    last = send(block[3] + passed[0], TO_ENDS)
     own_v = lax.dynamic_index_in_dim(line_v, o, 0, keepdims=False)
-    own_v = own_v + jnp.where(is_end, end_sum, mid_sum) * share
+    own_v = lax.optimization_barrier(own_v + jnp.where(is_end, block[3], block[2]) * share)
+    own_v = own_v + jnp.where(is_end, last, arrived[2] + passed[1]) * share
     step = jnp.sum(factor[:, None, None] * (spread - spread_v[None]), axis=0)
     buffer = lax.optimization_barrier(jnp.pad(spread_v + step * share, ((0, rest), (0, 0))))
     return lax.dynamic_update_slice(buffer, own_v, (cut, 0))

time: 687 us -> 694 us (1.010)
  local copies, waits for them, and re-layouts: 27.2 us -> 47.2 us
  Pallas kernels: 76.8 us -> 59.1 us
  other arithmetic: 58.4 us -> 45.9 us
  starting transfers between devices: 88.2 us -> 99 us
  waiting for transfers between devices: 432 us -> 439 us
    unnamed x44 -> x42, local copies, waits for them, and re-layouts: 0.09 us -> 20.1 us
    pallas_call x11 -> x10, Pallas kernels: 76.8 us -> 59.1 us  [run(): pl.pallas_call(kernel, grid_spec=pltpu.PrefetchScalarGridSpec(num_scalar_...]
    ppermute x35 -> x38, starting transfers between devices: 73.5 us -> 84.1 us  [send(): return lax.ppermute(value, axis, pairs)]
    ppermute x35 -> x38, waiting for transfers between devices: 407 us -> 414 us  [send(): return lax.ppermute(value, axis, pairs)]
  transfers between devices with their start and end apart: 46 -> 49, of which waited for: 24 -> 25; matrix products, arithmetic and copies ran while one was open for 9% -> 8% of each run, Pallas kernels for 9% -> 7%
where the time goes in v11:
time: 694 us; the launch traced here: 691 us
  waiting for transfers between devices  439 us (63%)
  starting transfers between devices  99 us (14%)
  Pallas kernels  59.1 us (9%)
  local copies, waits for them, and re-layouts  47.2 us (7%)
  other arithmetic  45.9 us (7%)
    ppermute x38, waiting for transfers between devices, send(): return lax.ppermute(value, axis, pairs)  414 us
    ppermute x38, starting transfers between devices, send(): return lax.ppermute(value, axis, pairs)  84.1 us
    pallas_call x10, Pallas kernels, run(): pl.pallas_call(kernel, grid_spec=pltpu.PrefetchScalarGridSpec(num_scalar_...  59.1 us
    ppermute x10, waiting for transfers between devices, sum_over_devices(): lax.ppermute(value, axis, [(i, i ^ step) for i in range(size)])  24.7 us
    unnamed x42, local copies, waits for them, and re-layouts  20.1 us
    reduce_sum x4, other arithmetic, on_device(): square = jnp.sum(jnp.square(held[place] - v))  17.4 us
    dynamic_slice x3, local copies, waits for them, and re-layouts, line_rows(): lax.dynamic_slice(source, (worker * outers, cut, 0), (outers, rest, colum...  14.1 us
  transfers between devices with their start and end apart: 49, of which 25 were waited for; matrix products, arithmetic and copies ran while one was open for 8% of the time, Pallas kernels for 7%

profile of v11, /device:TPU:0, one launch (start us, length us, event | category | flops | bytes accessed | tf_op | source)
XLA Modules:
  0.0 691.3 jit_solution(14348949663514775451)
XLA Ops:
  0.0 11.5 %slice.28 = f32[16,96,2048]{2,1,0:T(8,128)} slice(f32[16,224,2048]{2,1,0:T(8,128)} %bitcast.58), slice={[0:16], [0:96], [0:2048]} | slice | bytes 25165824 | tf_op jit(solution)/shard_map/slice | solution.py:260
  11.5 7.6 %all-to-all-start = ((f32[16,96,2048]{2,1,0:T(8,128)}), f32[16,96,2048]{2,1,0:T(8,128)}, u32[]{:S(2)}, u32[]{:S(2)}) async-start(f32[16,96,2048]{2,1,0:T(8,128)} %slice.28), calls=%async_computation | async-start | bytes 25165824 | tf_op jit(solution)/shard_map/all_to_all | solution.py:259
  19.1 1.9 collective-permute-start
  21.1 4.7 constant_dynamic-slice_fusion.3
  25.8 4.7 constant_dynamic-slice_fusion.2
  30.4 4.7 constant_dynamic-slice_fusion.1
  38.4 206.6 %collective-permute-done = f32[128,2048]{1,0:T(8,128)} collective-permute-done((f32[128,2048]{1,0:T(8,128)S(1)}, f32[128,2048]{1,0:T(8,128)}, u32[]{:S(2)}, u32[]{:S(2)}) %collective-permute-start) | collective-permute-done | bytes 1048608 | tf_op jit(solution)/shard_map/ppermute | solution.py:36
  245.0 1.7 collective-permute-start.1
  251.1 89.2 %collective-permute-done.4 = f32[128,2048]{1,0:T(8,128)} collective-permute-done((f32[128,2048]{1,0:T(8,128)}, f32[128,2048]{1,0:T(8,128)}, u32[]{:S(2)}, u32[]{:S(2)}) %collective-permute-start.4) | collective-permute-done | bytes 1048608 | tf_op jit(solution)/shard_map/ppermute | solution.py:36
  340.3 22.5 %collective-permute-done.2 = f32[128,2048]{1,0:T(8,128)} collective-permute-done((f32[128,2048]{1,0:T(8,128)}, f32[128,2048]{1,0:T(8,128)}, u32[]{:S(2)}, u32[]{:S(2)}) %collective-permute-start.2) | collective-permute-done | bytes 1048608 | tf_op jit(solution)/shard_map/ppermute | solution.py:36
  362.8 2.5 select_bitcast_fusion.3
  365.3 4.9 multiply_reduce_fusion.5
  370.9 4.7 multiply_reduce_fusion.4
  376.2 3.9 multiply_reduce_fusion.3
  380.8 3.9 multiply_reduce_fusion.2
  385.3 6.2 multiply_reduce_fusion.1
  394.2 2.1 collective-permute-done.9
  396.3 3.6 collective-permute-done.10
  400.9 3.4 collective-permute-done.11
  405.8 2.0 collective-permute-done.12
  409.4 2.5 shard_map.39
  411.9 1.9 collective-permute-start.24
  413.8 5.9 shard_map.40
  423.8 20.8 %collective-permute-done.16 = f32[32,2048]{1,0:T(8,128)S(1)} collective-permute-done((f32[32,2048]{1,0:T(8,128)S(1)}, f32[32,2048]{1,0:T(8,128)S(1)}, u32[]{:S(2)}, u32[]{:S(2)}) %collective-permute-start.16) | collective-permute-done | bytes 262176 | tf_op jit(solution)/shard_map/ppermute | solution.py:36
  446.1 9.6 %shard_map.41 = (f32[80,2048]{1,0:T(8,128)S(1)}, f32[80,2048]{1,0:T(8,128)S(1)}, f32[64,2048]{1,0:T(8,128)S(1)}, f32[32,2048]{1,0:T(8,128)S(1)}) custom-call(f32[4]{0:T(128)S(1)} %select_reduce_fusion.2.factor, f32[512,2048]{1,0:T(8,128)} %bitcast.16.refs_0_, f32[512,2048]{1,0:T(8,128)} %bitcast.17.refs_1_, f32[512,2048]{1,0:T(8,128)} %bitcast.18.refs_2_, ...), custom_call_target="tpu_custom_call" | custom-call | flops 12582912 | bytes 12582912 | tf_op jit(solution)/shard_map/pallas_call | solution.py:63
  456.5 11.3 %collective-permute-start.14 = (f32[80,2048]{1,0:T(8,128)S(1)}, f32[80,2048]{1,0:T(8,128)S(1)}, u32[]{:S(2)}, u32[]{:S(2)}) collective-permute-start(f32[80,2048]{1,0:T(8,128)S(1)} %get-tuple-element.52), channel_id=1, source_target_pairs={{0,2},{6,4},{1,3},{7,5},{8,10},{14,12},{9,11},{15,13},{16,18},{22,... | collective-permute-start | bytes 1966088 | tf_op jit(solution)/shard_map/ppermute | solution.py:36
  468.7 3.6 collective-permute-start.22
  472.3 10.3 %collective-permute-done.14 = f32[80,2048]{1,0:T(8,128)S(1)} collective-permute-done((f32[80,2048]{1,0:T(8,128)S(1)}, f32[80,2048]{1,0:T(8,128)S(1)}, u32[]{:S(2)}, u32[]{:S(2)}) %collective-permute-start.14) | collective-permute-done | bytes 655392 | tf_op jit(solution)/shard_map/ppermute | solution.py:36
  483.5 6.7 collective-permute-start.13
  490.1 7.1 %shard_map.37 = (f32[96,2048]{1,0:T(8,128)S(1)}, f32[16,8,128]{2,1,0:T(8,128)S(1)}) custom-call(f32[16]{0:T(128)S(1)} %multiply_minimum_fusion.1.factor, f32[96,2048]{1,0:T(8,128)S(1)} %slice.22.v, f32[16,96,2048]{2,1,0:T(8,128)} %all-to-all-done.values), custom_call_target="tpu_custom_call" | custom-call | flops 14155776 | bytes 14155776 | tf_op jit(solution)/shard_map/pallas_call | solution.py:63
  500.3 15.0 %collective-permute-start.21 = (f32[32,2048]{1,0:T(8,128)S(1)}, f32[32,2048]{1,0:T(8,128)S(1)}, u32[]{:S(2)}, u32[]{:S(2)}) collective-permute-start(f32[32,2048]{1,0:T(8,128)S(1)} %get-tuple-element.56), channel_id=1, source_target_pairs={{0,2},{6,4},{1,3},{7,5},{8,10},{14,12},{9,11},{15,13},{16,18},{22,... | collective-permute-start | bytes 786440 | tf_op jit(solution)/shard_map/ppermute | solution.py:36
  519.9 6.5 collective-permute-done.33.refs_8_
  532.5 8.7 %collective-permute-done.35.refs_10_ = f32[80,2048]{1,0:T(8,128)S(1)} collective-permute-done((f32[80,2048]{1,0:T(8,128)S(1)}, f32[80,2048]{1,0:T(8,128)S(1)}, u32[]{:S(2)}, u32[]{:S(2)}) %collective-permute-start.35) | collective-permute-done | bytes 655392 | tf_op jit(solution)/shard_map/ppermute | solution.py:36
  543.6 11.8 %collective-permute-done.36.refs_11_ = f32[80,2048]{1,0:T(8,128)} collective-permute-done((f32[80,2048]{1,0:T(8,128)S(1)}, f32[80,2048]{1,0:T(8,128)}, u32[]{:S(2)}, u32[]{:S(2)}) %collective-permute-start.36) | collective-permute-done | bytes 655392 | tf_op jit(solution)/shard_map/ppermute | solution.py:36
  555.4 2.2 copy-done.2
  557.6 2.2 copy-done.4
  563.9 9.5 %shard_map.42 = (f32[512,2048]{1,0:T(8,128)S(1)}, f32[4,8,128]{2,1,0:T(8,128)S(1)}) custom-call(s32[1]{0:T(128)} %bitcast.14.is_end, f32[512,2048]{1,0:T(8,128)S(1)} %bitcast.45, f32[512,2048]{1,0:T(8,128)} %bitcast.16.refs_0_, f32[512,2048]{1,0:T(8,128)} %bitcast.17.refs_1_, f32[512,2048]{1,0:T(8,128)} %bitcast.18.refs_2_, f32[512,2048]{1,0:T(8,128)S(1)} %bitcast.52, ...), custom_call_target="tpu_custom_call" | custom-call | flops 16777216 | bytes 16777216 | tf_op jit(solution)/shard_map/pallas_call | solution.py:63
  573.4 6.6 collective-permute-done.32.refs_7_
  580.0 6.3 shard_map.43
  586.3 2.2 collective-permute-done.30.refs_7_
  588.5 3.9 shard_map.44
  592.4 1.9 copy-done.7
  595.7 1.8 collective-permute-start.38
  597.5 1.8 collective-permute-done.38
  599.3 3.6 collective-permute-done.39
  603.5 3.9 collective-permute-done.40
  608.9 2.0 collective-permute-done.41
  611.1 2.2 copy-done.5
  613.3 2.2 copy-done.8
  615.5 2.9 shard_map.45
  618.4 2.9 collective-permute-start.42
  621.4 2.2 copy-done.6
  623.6 2.2 copy-done.9
  625.8 10.2 %shard_map.46 = (f32[128,2048]{1,0:T(8,128)S(1)}, f32[128,2048]{1,0:T(8,128)S(1)}, f32[128,2048]{1,0:T(8,128)S(1)}) custom-call(s32[3]{0:T(128)S(1)} %pad_add_fusion.1.places, f32[4]{0:T(128)S(1)} %select_reduce_fusion.factor, f32[4,128,2048]{2,1,0:T(8,128)} %collective-permute-done.7.refs_0_, f32[4,128,2048]{2,1,0:T(8,128)} %collective-permute-done.6.refs_1_, ...), custom_call_target="tpu_custom_call" | custom-call | flops 18874368 | bytes 18874368 | tf_op jit(solution)/shard_map/pallas_call | solution.py:63
  636.0 2.3 collective-permute-start.46
  638.3 5.6 collective-permute-done.42
  643.9 2.3 add.199
  646.2 1.7 collective-permute-start.43
  647.8 6.0 collective-permute-start.45
  653.8 12.5 %collective-permute-done.46 = f32[128,2048]{1,0:T(8,128)} collective-permute-done((f32[128,2048]{1,0:T(8,128)S(1)}, f32[128,2048]{1,0:T(8,128)}, u32[]{:S(2)}, u32[]{:S(2)}) %collective-permute-start.46) | collective-permute-done | bytes 1048608 | tf_op jit(solution)/shard_map/ppermute | solution.py:36
  668.4 2.2 fusion.7
  671.9 6.4 multiply_reduce_fusion
  679.9 4.0 collective-permute-done.45
  683.8 6.2 collective-permute-done.44
  (145 shorter events, 54.4 us)
Async XLA Ops:
  11.5 7.6 %copy-start.20 = (f32[224,2048]{1,0:T(8,128)S(1)}, f32[224,2048]{1,0:T(8,128)}, u32[]{:S(2)}) copy-start(f32[224,2048]{1,0:T(8,128)} %param.4) | copy-start | bytes 5505028
  11.5 373.8 %all-to-all-start = ((f32[16,96,2048]{2,1,0:T(8,128)}), f32[16,96,2048]{2,1,0:T(8,128)}, u32[]{:S(2)}, u32[]{:S(2)}) async-start(f32[16,96,2048]{2,1,0:T(8,128)} %slice.28), calls=%async_computation | async-start | bytes 25165824 | tf_op jit(solution)/shard_map/all_to_all | solution.py:259
  19.1 225.8 %collective-permute-start = (f32[128,2048]{1,0:T(8,128)S(1)}, f32[128,2048]{1,0:T(8,128)}, u32[]{:S(2)}, u32[]{:S(2)}) collective-permute-start(f32[128,2048]{1,0:T(8,128)S(1)} %slice.24), channel_id=1, source_target_pairs={{0,2},{2,0},{4,6},{6,4},{1,3},{3,1},{5,7},{7,5},{8,10},{10,8},{12,... | collective-permute-start | bytes 3145736 | tf_op jit(solution)/shard_map/ppermute | solution.py:36
  35.2 335.7 %collective-permute-start.5 = (f32[4,128,2048]{2,1,0:T(8,128)}, f32[4,128,2048]{2,1,0:T(8,128)}, u32[]{:S(2)}, u32[]{:S(2)}) collective-permute-start(f32[4,128,2048]{2,1,0:T(8,128)} %constant_dynamic-slice_fusion.1), channel_id=1, source_target_pairs={{0,8},{8,0},{16,24},{24,16},{1,9},{9,1},{17,25},{25,17},{2,10},{10... | collective-permute-start | bytes 12582920 | tf_op jit(solution)/shard_map/ppermute | solution.py:36
  35.2 341.0 %collective-permute-start.6 = (f32[4,128,2048]{2,1,0:T(8,128)}, f32[4,128,2048]{2,1,0:T(8,128)}, u32[]{:S(2)}, u32[]{:S(2)}) collective-permute-start(f32[4,128,2048]{2,1,0:T(8,128)} %constant_dynamic-slice_fusion.2), channel_id=1, source_target_pairs={{0,24},{8,16},{16,8},{24,0},{1,25},{9,17},{17,9},{25,1},{2,26},{10... | collective-permute-start | bytes 12582920 | tf_op jit(solution)/shard_map/ppermute | solution.py:36
  36.8 211.5 %collective-permute-start.3 = (f32[128,2048]{1,0:T(8,128)S(1)}, f32[128,2048]{1,0:T(8,128)}, u32[]{:S(2)}, u32[]{:S(2)}) collective-permute-start(f32[128,2048]{1,0:T(8,128)S(1)} %slice.24), channel_id=1, source_target_pairs={{2,4},{4,2},{3,5},{5,3},{10,12},{12,10},{11,13},{13,11},{18,20},{2... | collective-permute-start | bytes 3145736 | tf_op jit(solution)/shard_map/ppermute | solution.py:36
  245.0 4.6 collective-permute-start.1
  246.6 134.1 %collective-permute-start.7 = (f32[4,128,2048]{2,1,0:T(8,128)}, f32[4,128,2048]{2,1,0:T(8,128)}, u32[]{:S(2)}, u32[]{:S(2)}) collective-permute-start(f32[4,128,2048]{2,1,0:T(8,128)} %constant_dynamic-slice_fusion.3), channel_id=1, source_target_pairs={{0,16},{8,24},{16,0},{24,8},{1,17},{9,25},{17,1},{25,9},{2,18},{10... | collective-permute-start | bytes 12582920 | tf_op jit(solution)/shard_map/ppermute | solution.py:36
  248.3 92.0 %collective-permute-start.4 = (f32[128,2048]{1,0:T(8,128)}, f32[128,2048]{1,0:T(8,128)}, u32[]{:S(2)}, u32[]{:S(2)}) collective-permute-start(f32[128,2048]{1,0:T(8,128)} %collective-permute-done.3), channel_id=1, source_target_pairs={{2,0},{4,6},{3,1},{5,7},{10,8},{12,14},{11,9},{13,15},{18,16},{20,... | collective-permute-start | bytes 3145736 | tf_op jit(solution)/shard_map/ppermute | solution.py:36
  249.6 113.2 %collective-permute-start.2 = (f32[128,2048]{1,0:T(8,128)}, f32[128,2048]{1,0:T(8,128)}, u32[]{:S(2)}, u32[]{:S(2)}) collective-permute-start(f32[128,2048]{1,0:T(8,128)} %collective-permute-done.1), channel_id=1, source_target_pairs={{2,0},{4,6},{3,1},{5,7},{10,8},{12,14},{11,9},{13,15},{18,16},{20,... | collective-permute-start | bytes 3145736 | tf_op jit(solution)/shard_map/ppermute | solution.py:36
  370.2 10.6 %copy-start = (f32[4,128,2048]{2,1,0:T(8,128)}, f32[4,128,2048]{2,1,0:T(8,128)S(1)}, u32[]{:S(2)}) copy-start(f32[4,128,2048]{2,1,0:T(8,128)S(1)} %get-tuple-element.44) | copy-start | bytes 12582916
  385.3 22.8 %copy-start.1 = (f32[4,128,2048]{2,1,0:T(8,128)S(1)}, f32[4,128,2048]{2,1,0:T(8,128)}, u32[]{:S(2)}) copy-start(f32[4,128,2048]{2,1,0:T(8,128)} %copy-done) | copy-start | bytes 12582916
  385.3 22.7 %copy-start.3 = (f32[4,128,2048]{2,1,0:T(8,128)S(1)}, f32[4,128,2048]{2,1,0:T(8,128)}, u32[]{:S(2)}) copy-start(f32[4,128,2048]{2,1,0:T(8,128)} %get-tuple-element.74.refs_3_) | copy-start | bytes 12582916
  391.5 1.2 collective-permute-start.8
  392.7 3.6 collective-permute-start.9
  396.3 3.6 collective-permute-start.10
  399.8 4.5 collective-permute-start.11
  404.3 3.6 collective-permute-start.12
  411.9 33.4 %collective-permute-start.24 = (f32[64,2048]{1,0:T(8,128)S(1)}, f32[64,2048]{1,0:T(8,128)S(1)}, u32[]{:S(2)}, u32[]{:S(2)}) collective-permute-start(f32[64,2048]{1,0:T(8,128)S(1)} %shard_map.39), channel_id=1, source_target_pairs={{0,2},{6,4},{1,3},{7,5},{8,10},{14,12},{9,11},{15,13},{16,18},{22,... | collective-permute-start | bytes 1572872 | tf_op jit(solution)/shard_map/ppermute | solution.py:36
  419.8 36.0 %collective-permute-start.15 = (f32[80,2048]{1,0:T(8,128)S(1)}, f32[80,2048]{1,0:T(8,128)S(1)}, u32[]{:S(2)}, u32[]{:S(2)}) collective-permute-start(f32[80,2048]{1,0:T(8,128)S(1)} %get-tuple-element.49), channel_id=1, source_target_pairs={{0,2},{6,4},{1,3},{7,5},{8,10},{14,12},{9,11},{15,13},{16,18},{22,... | collective-permute-start | bytes 1966088 | tf_op jit(solution)/shard_map/ppermute | solution.py:36
  421.1 23.5 %collective-permute-start.16 = (f32[32,2048]{1,0:T(8,128)S(1)}, f32[32,2048]{1,0:T(8,128)S(1)}, u32[]{:S(2)}, u32[]{:S(2)}) collective-permute-start(f32[32,2048]{1,0:T(8,128)S(1)} %shard_map.38), channel_id=1, source_target_pairs={{0,2},{6,4},{1,3},{7,5},{8,10},{14,12},{9,11},{15,13},{16,18},{22,... | collective-permute-start | bytes 786440 | tf_op jit(solution)/shard_map/ppermute | solution.py:36
  422.4 45.4 %collective-permute-start.23 = (f32[80,2048]{1,0:T(8,128)S(1)}, f32[80,2048]{1,0:T(8,128)S(1)}, u32[]{:S(2)}, u32[]{:S(2)}) collective-permute-start(f32[80,2048]{1,0:T(8,128)S(1)} %get-tuple-element.58), channel_id=1, source_target_pairs={{0,2},{6,4},{1,3},{7,5},{8,10},{14,12},{9,11},{15,13},{16,18},{22,... | collective-permute-start | bytes 1966088 | tf_op jit(solution)/shard_map/ppermute | solution.py:36
  444.7 11.0 %collective-permute-start.17 = (f32[32,2048]{1,0:T(8,128)S(1)}, f32[32,2048]{1,0:T(8,128)S(1)}, u32[]{:S(2)}, u32[]{:S(2)}) collective-permute-start(f32[32,2048]{1,0:T(8,128)S(1)} %add.173), channel_id=1, source_target_pairs={{2,4},{4,2},{3,5},{5,3},{10,12},{12,10},{11,13},{13,11},{18,20},{2... | collective-permute-start | bytes 786440 | tf_op jit(solution)/shard_map/ppermute | solution.py:36
  445.4 22.4 %collective-permute-start.25 = (f32[64,2048]{1,0:T(8,128)S(1)}, f32[64,2048]{1,0:T(8,128)S(1)}, u32[]{:S(2)}, u32[]{:S(2)}) collective-permute-start(f32[64,2048]{1,0:T(8,128)S(1)} %add.181), channel_id=1, source_target_pairs={{2,4},{4,2},{3,5},{5,3},{10,12},{12,10},{11,13},{13,11},{18,20},{2... | collective-permute-start | bytes 1572872 | tf_op jit(solution)/shard_map/ppermute | solution.py:36
  455.8 16.4 %collective-permute-start.18 = (f32[80,2048]{1,0:T(8,128)S(1)}, f32[80,2048]{1,0:T(8,128)S(1)}, u32[]{:S(2)}, u32[]{:S(2)}) collective-permute-start(f32[80,2048]{1,0:T(8,128)S(1)} %add.175), channel_id=1, source_target_pairs={{2,4},{4,2},{3,5},{5,3},{10,12},{12,10},{11,13},{13,11},{18,20},{2... | collective-permute-start | bytes 1966088 | tf_op jit(solution)/shard_map/ppermute | solution.py:36
  456.5 26.1 %collective-permute-start.14 = (f32[80,2048]{1,0:T(8,128)S(1)}, f32[80,2048]{1,0:T(8,128)S(1)}, u32[]{:S(2)}, u32[]{:S(2)}) collective-permute-start(f32[80,2048]{1,0:T(8,128)S(1)} %get-tuple-element.52), channel_id=1, source_target_pairs={{0,2},{6,4},{1,3},{7,5},{8,10},{14,12},{9,11},{15,13},{16,18},{22,... | collective-permute-start | bytes 1966088 | tf_op jit(solution)/shard_map/ppermute | solution.py:36
  467.9 30.3 %copy-start.10 = (f32[64,2048]{1,0:T(8,128)}, f32[64,2048]{1,0:T(8,128)S(1)}, u32[]{:S(2)}) copy-start(f32[64,2048]{1,0:T(8,128)S(1)} %add.182.refs_5_) | copy-start | bytes 1572868
  468.0 29.3 %collective-permute-start.26 = (f32[80,2048]{1,0:T(8,128)S(1)}, f32[80,2048]{1,0:T(8,128)S(1)}, u32[]{:S(2)}, u32[]{:S(2)}) collective-permute-start(f32[80,2048]{1,0:T(8,128)S(1)} %add.183), channel_id=1, source_target_pairs={{2,4},{4,2},{3,5},{5,3},{10,12},{12,10},{11,13},{13,11},{18,20},{2... | collective-permute-start | bytes 1966088 | tf_op jit(solution)/shard_map/ppermute | solution.py:36
  468.7 28.7 %collective-permute-start.22 = (f32[80,2048]{1,0:T(8,128)S(1)}, f32[80,2048]{1,0:T(8,128)S(1)}, u32[]{:S(2)}, u32[]{:S(2)}) collective-permute-start(f32[80,2048]{1,0:T(8,128)S(1)} %get-tuple-element.57), channel_id=1, source_target_pairs={{0,2},{6,4},{1,3},{7,5},{8,10},{14,12},{9,11},{15,13},{16,18},{22,... | collective-permute-start | bytes 1966088 | tf_op jit(solution)/shard_map/ppermute | solution.py:36
  482.7 16.7 %collective-permute-start.19 = (f32[80,2048]{1,0:T(8,128)S(1)}, f32[80,2048]{1,0:T(8,128)S(1)}, u32[]{:S(2)}, u32[]{:S(2)}) collective-permute-start(f32[80,2048]{1,0:T(8,128)S(1)} %add.177), channel_id=1, source_target_pairs={{2,4},{4,2},{3,5},{5,3},{10,12},{12,10},{11,13},{13,11},{18,20},{2... | collective-permute-start | bytes 1966088 | tf_op jit(solution)/shard_map/ppermute | solution.py:36
  483.5 16.1 %collective-permute-start.13 = (f32[64,2048]{1,0:T(8,128)S(1)}, f32[64,2048]{1,0:T(8,128)S(1)}, u32[]{:S(2)}, u32[]{:S(2)}) collective-permute-start(f32[64,2048]{1,0:T(8,128)S(1)} %get-tuple-element.51), channel_id=1, source_target_pairs={{0,2},{6,4},{1,3},{7,5},{8,10},{14,12},{9,11},{15,13},{16,18},{22,... | collective-permute-start | bytes 1572872 | tf_op jit(solution)/shard_map/ppermute | solution.py:36
  497.4 19.2 %collective-permute-start.27 = (f32[80,2048]{1,0:T(8,128)S(1)}, f32[80,2048]{1,0:T(8,128)S(1)}, u32[]{:S(2)}, u32[]{:S(2)}) collective-permute-start(f32[80,2048]{1,0:T(8,128)S(1)} %add.185), channel_id=1, source_target_pairs={{2,4},{4,2},{3,5},{5,3},{10,12},{12,10},{11,13},{13,11},{18,20},{2... | collective-permute-start | bytes 1966088 | tf_op jit(solution)/shard_map/ppermute | solution.py:36
  498.2 29.5 %collective-permute-start.34 = (f32[64,2048]{1,0:T(8,128)S(1)}, f32[64,2048]{1,0:T(8,128)S(1)}, u32[]{:S(2)}, u32[]{:S(2)}) collective-permute-start(f32[64,2048]{1,0:T(8,128)S(1)} %add.182.refs_5_), channel_id=1, source_target_pairs={{2,0},{4,6},{3,1},{5,7},{10,8},{12,14},{11,9},{13,15},{18,16},{20,... | collective-permute-start | bytes 1572872 | tf_op jit(solution)/shard_map/ppermute | solution.py:36
  499.6 29.4 %collective-permute-start.20 = (f32[64,2048]{1,0:T(8,128)S(1)}, f32[64,2048]{1,0:T(8,128)S(1)}, u32[]{:S(2)}, u32[]{:S(2)}) collective-permute-start(f32[64,2048]{1,0:T(8,128)S(1)} %add.179), channel_id=1, source_target_pairs={{2,4},{4,2},{3,5},{5,3},{10,12},{12,10},{11,13},{13,11},{18,20},{2... | collective-permute-start | bytes 1572872 | tf_op jit(solution)/shard_map/ppermute | solution.py:36
  500.3 18.8 %collective-permute-start.21 = (f32[32,2048]{1,0:T(8,128)S(1)}, f32[32,2048]{1,0:T(8,128)S(1)}, u32[]{:S(2)}, u32[]{:S(2)}) collective-permute-start(f32[32,2048]{1,0:T(8,128)S(1)} %get-tuple-element.56), channel_id=1, source_target_pairs={{0,2},{6,4},{1,3},{7,5},{8,10},{14,12},{9,11},{15,13},{16,18},{22,... | collective-permute-start | bytes 786440 | tf_op jit(solution)/shard_map/ppermute | solution.py:36
  515.3 11.1 %collective-permute-start.33 = (f32[32,2048]{1,0:T(8,128)S(1)}, f32[32,2048]{1,0:T(8,128)S(1)}, u32[]{:S(2)}, u32[]{:S(2)}) collective-permute-start(f32[32,2048]{1,0:T(8,128)S(1)} %add.174.refs_4_), channel_id=1, source_target_pairs={{2,0},{4,6},{3,1},{5,7},{10,8},{12,14},{11,9},{13,15},{18,16},{20,... | collective-permute-start | bytes 786440 | tf_op jit(solution)/shard_map/ppermute | solution.py:36
  516.6 24.6 %collective-permute-start.35 = (f32[80,2048]{1,0:T(8,128)S(1)}, f32[80,2048]{1,0:T(8,128)S(1)}, u32[]{:S(2)}, u32[]{:S(2)}) collective-permute-start(f32[80,2048]{1,0:T(8,128)S(1)} %add.176.refs_6_), channel_id=1, source_target_pairs={{2,0},{4,6},{3,1},{5,7},{10,8},{12,14},{11,9},{13,15},{18,16},{20,... | collective-permute-start | bytes 1966088 | tf_op jit(solution)/shard_map/ppermute | solution.py:36
  519.2 12.0 %collective-permute-start.28 = (f32[32,2048]{1,0:T(8,128)S(1)}, f32[32,2048]{1,0:T(8,128)S(1)}, u32[]{:S(2)}, u32[]{:S(2)}) collective-permute-start(f32[32,2048]{1,0:T(8,128)S(1)} %add.187), channel_id=1, source_target_pairs={{2,4},{4,2},{3,5},{5,3},{10,12},{12,10},{11,13},{13,11},{18,20},{2... | collective-permute-start | bytes 786440 | tf_op jit(solution)/shard_map/ppermute | solution.py:36
  526.4 14.9 %copy-start.18 = (f32[32,2048]{1,0:T(8,128)}, f32[32,2048]{1,0:T(8,128)S(1)}, u32[]{:S(2)}) copy-start(f32[32,2048]{1,0:T(8,128)S(1)} %collective-permute-done.33.refs_8_) | copy-start | bytes 786436
  526.4 29.0 %collective-permute-start.36 = (f32[80,2048]{1,0:T(8,128)S(1)}, f32[80,2048]{1,0:T(8,128)}, u32[]{:S(2)}, u32[]{:S(2)}) collective-permute-start(f32[80,2048]{1,0:T(8,128)S(1)} %add.184.refs_7_), channel_id=1, source_target_pairs={{2,0},{4,6},{3,1},{5,7},{10,8},{12,14},{11,9},{13,15},{18,16},{20,... | collective-permute-start | bytes 1966088 | tf_op jit(solution)/shard_map/ppermute | solution.py:36
  527.7 13.6 %copy-start.16 = (f32[64,2048]{1,0:T(8,128)}, f32[64,2048]{1,0:T(8,128)S(1)}, u32[]{:S(2)}) copy-start(f32[64,2048]{1,0:T(8,128)S(1)} %collective-permute-done.34.refs_9_) | copy-start | bytes 1572868
  527.7 45.7 %collective-permute-start.31 = (f32[80,2048]{1,0:T(8,128)S(1)}, f32[80,2048]{1,0:T(8,128)}, u32[]{:S(2)}, u32[]{:S(2)}) collective-permute-start(f32[80,2048]{1,0:T(8,128)S(1)} %add.178.refs_4_), channel_id=1, source_target_pairs={{2,0},{4,6},{3,1},{5,7},{10,8},{12,14},{11,9},{13,15},{18,16},{20,... | collective-permute-start | bytes 1966088 | tf_op jit(solution)/shard_map/ppermute | solution.py:36
  529.0 51.0 %collective-permute-start.32 = (f32[80,2048]{1,0:T(8,128)}, f32[80,2048]{1,0:T(8,128)}, u32[]{:S(2)}, u32[]{:S(2)}) collective-permute-start(f32[80,2048]{1,0:T(8,128)} %add.186.refs_5_), channel_id=1, source_target_pairs={{2,0},{4,6},{3,1},{5,7},{10,8},{12,14},{11,9},{13,15},{18,16},{20,... | collective-permute-start | bytes 1966088 | tf_op jit(solution)/shard_map/ppermute | solution.py:36
  531.2 57.3 %collective-permute-start.29 = (f32[64,2048]{1,0:T(8,128)}, f32[64,2048]{1,0:T(8,128)}, u32[]{:S(2)}, u32[]{:S(2)}) collective-permute-start(f32[64,2048]{1,0:T(8,128)} %add.180.refs_4_), channel_id=1, source_target_pairs={{2,0},{4,6},{3,1},{5,7},{10,8},{12,14},{11,9},{13,15},{18,16},{20,... | collective-permute-start | bytes 1572872 | tf_op jit(solution)/shard_map/ppermute | solution.py:36
  542.1 46.3 %collective-permute-start.30 = (f32[32,2048]{1,0:T(8,128)S(1)}, f32[32,2048]{1,0:T(8,128)}, u32[]{:S(2)}, u32[]{:S(2)}) collective-permute-start(f32[32,2048]{1,0:T(8,128)S(1)} %add.188.refs_5_), channel_id=1, source_target_pairs={{2,0},{4,6},{3,1},{5,7},{10,8},{12,14},{11,9},{13,15},{18,16},{20,... | collective-permute-start | bytes 786440 | tf_op jit(solution)/shard_map/ppermute | solution.py:36
  555.4 2.2 copy-start.2
  557.6 2.2 copy-start.4
  594.5 1.2 collective-permute-start.37
  595.7 3.6 collective-permute-start.38
  599.3 3.6 collective-permute-start.39
  602.9 4.5 collective-permute-start.40
  607.4 3.6 collective-permute-start.41
  611.1 2.2 copy-start.5
  613.3 2.2 copy-start.8
  618.4 25.4 %collective-permute-start.42 = (f32[128,2048]{1,0:T(8,128)S(1)}, f32[128,2048]{1,0:T(8,128)}, u32[]{:S(2)}, u32[]{:S(2)}) collective-permute-start(f32[128,2048]{1,0:T(8,128)S(1)} %shard_map.45), channel_id=1, source_target_pairs={{0,2},{6,4},{1,3},{7,5},{8,10},{14,12},{9,11},{15,13},{16,18},{22,... | collective-permute-start | bytes 3145736 | tf_op jit(solution)/shard_map/ppermute | solution.py:36
  621.4 2.2 copy-start.6
  623.6 2.2 copy-start.9
  636.0 10.2 %copy-start.12 = (f32[128,2048]{1,0:T(8,128)}, f32[128,2048]{1,0:T(8,128)S(1)}, u32[]{:S(2)}) copy-start(f32[128,2048]{1,0:T(8,128)S(1)} %get-tuple-element.71) | copy-start | bytes 3145732
  636.0 10.2 %copy-start.13 = (f32[128,2048]{1,0:T(8,128)}, f32[128,2048]{1,0:T(8,128)S(1)}, u32[]{:S(2)}) copy-start(f32[128,2048]{1,0:T(8,128)S(1)} %get-tuple-element.70) | copy-start | bytes 3145732
  636.0 30.3 %collective-permute-start.46 = (f32[128,2048]{1,0:T(8,128)S(1)}, f32[128,2048]{1,0:T(8,128)}, u32[]{:S(2)}, u32[]{:S(2)}) collective-permute-start(f32[128,2048]{1,0:T(8,128)S(1)} %get-tuple-element.72), channel_id=1, source_target_pairs={{0,2},{6,4},{1,3},{7,5},{8,10},{14,12},{9,11},{15,13},{16,18},{22,... | collective-permute-start | bytes 3145736 | tf_op jit(solution)/shard_map/ppermute | solution.py:36
  646.2 22.3 %collective-permute-start.43 = (f32[128,2048]{1,0:T(8,128)}, f32[128,2048]{1,0:T(8,128)}, u32[]{:S(2)}, u32[]{:S(2)}) collective-permute-start(f32[128,2048]{1,0:T(8,128)} %add.199), channel_id=1, source_target_pairs={{2,4},{4,2},{3,5},{5,3},{10,12},{12,10},{11,13},{13,11},{18,20},{2... | collective-permute-start | bytes 3145736 | tf_op jit(solution)/shard_map/ppermute | solution.py:36
  647.8 36.0 %collective-permute-start.45 = (f32[128,2048]{1,0:T(8,128)}, f32[128,2048]{1,0:T(8,128)S(1)}, u32[]{:S(2)}, u32[]{:S(2)}) collective-permute-start(f32[128,2048]{1,0:T(8,128)} %copy-done.12), channel_id=1, source_target_pairs={{0,2},{6,4},{1,3},{7,5},{8,10},{14,12},{9,11},{15,13},{16,18},{22,... | collective-permute-start | bytes 3145736 | tf_op jit(solution)/shard_map/ppermute | solution.py:36
  667.7 16.1 %collective-permute-start.47 = (f32[128,2048]{1,0:T(8,128)S(1)}, f32[128,2048]{1,0:T(8,128)S(1)}, u32[]{:S(2)}, u32[]{:S(2)}) collective-permute-start(f32[128,2048]{1,0:T(8,128)S(1)} %add.201), channel_id=1, source_target_pairs={{2,4},{4,2},{3,5},{5,3},{10,12},{12,10},{11,13},{13,11},{18,20},{2... | collective-permute-start | bytes 3145736 | tf_op jit(solution)/shard_map/ppermute | solution.py:36
  670.6 19.4 %collective-permute-start.44 = (f32[128,2048]{1,0:T(8,128)S(1)}, f32[128,2048]{1,0:T(8,128)S(1)}, u32[]{:S(2)}, u32[]{:S(2)}) collective-permute-start(f32[128,2048]{1,0:T(8,128)S(1)} %get-tuple-element.82), channel_id=1, source_target_pairs={{2,0},{4,6},{3,1},{5,7},{10,8},{12,14},{11,9},{13,15},{18,16},{20,... | collective-permute-start | bytes 3145736 | tf_op jit(solution)/shard_map/ppermute | solution.py:36
  (6 other events, 6.9 us)

commit v12 on v11

--- a/solution.py
+++ b/solution.py
@@ -17,7 +17,8 @@
 UNIT = 16
 SPREAD = 3 / 7
 
-GRANT = 8 << 20
+GRANT = 60 << 20
+SMALL_GRANT = 8 << 20
 
 epsilon = 1e-06
 
@@ -51,15 +52,17 @@
     units = rest * outers // UNIT
     if outers != LINE or rest % TILE or units < 22 or not cut:
         return None
-    body = units - 12
-    sizes = [2, 4] + [5] * (body // 5) + [body % 5] * (body % 5 > 0) + [4, 2]
+    body = units - 4
+    sizes = [2] + [4] * (body // 4) + [body % 4] * (body % 4 > 0) + [2]
     return cut, sizes
 
 
 SMEM = pl.BlockSpec(memory_space=pltpu.SMEM)
 
 
-def run(kernel, grid, in_specs, out_specs, out_shape, operands, moved, aliases={}, prefetch=0):
+def run(
+    kernel, grid, in_specs, out_specs, out_shape, operands, moved, aliases={}, prefetch=0, grant=GRANT
+):
     return pl.pallas_call(
         kernel,
         grid_spec=pltpu.PrefetchScalarGridSpec(
@@ -67,7 +70,7 @@
         ),
         out_shape=out_shape,
         input_output_aliases=aliases,
-        compiler_params=pltpu.CompilerParams(vmem_limit_bytes=GRANT),
+        compiler_params=pltpu.CompilerParams(vmem_limit_bytes=grant),
         cost_estimate=pl.CostEstimate(flops=4 * moved, bytes_accessed=4 * moved, transcendentals=0),
     )(*operands)
 
@@ -103,7 +106,7 @@
     shapes = [jax.ShapeDtypeStruct((size * tile, columns), v.dtype) for size in sizes]
     moved = (count + 2) * sum(sizes) * tile * columns
     in_specs = [SMEM] + [at] * (count + 1)
-    return run(kernel, (sum(sizes),), in_specs, outs, shapes, (factor, *values, v), moved)
+    return run(kernel, (sum(sizes),), in_specs, outs, shapes, (factor, *values, v), moved, grant=SMALL_GRANT)
 
 
 def move_chunks(is_end, share, totals, backs, values, v, start, sizes, carried):
@@ -212,7 +215,8 @@
     )
     moved = (count + 2) * rows * columns
     operands = (factor, v, values)
-    return run(kernel, (rows // tile,), [SMEM, at, stack], (at, squares), shapes, operands, moved)
+    specs = [SMEM, at, stack], (at, squares)
+    return run(kernel, (rows // tile,), *specs, shapes, operands, moved, grant=SMALL_GRANT + (8 << 20))
 
 
 def spread_only(mine, center, radius_total, worker_count):
@@ -292,13 +296,13 @@
     flat_v = line_v.reshape(outers * rest, columns)
     end_flag = is_end.astype(jnp.int32).reshape(1)
     next_spread_v, spread_sq = move_spread(share, factor, spread, spread_v)
-    early = {3: next_spread_v}
+    early = {2: next_spread_v}
     count, places = len(sizes), begins(sizes)
     own = step_chunks(line_factor, flat, flat_v, 0, sizes[:1])
     own += step_chunks(line_factor, flat, tie(flat_v, own[0]), places[1], sizes[1:2])
     own += step_chunks(line_factor, flat, tie(flat_v, own[1]), places[2], sizes[2:4])
     own += step_chunks(line_factor, flat, tie(flat_v, own[2]), places[4], sizes[4:])
-    cuts = [0, count - 4, count - 2, count]
+    cuts = [0, count - 5, count - 3, count - 2, count - 1, count]
     groups = [slice(*pair) for pair in zip(cuts, cuts[1:])]
     totals, backs, carried = [], [], ()
 
@@ -316,10 +320,13 @@
         total = total + send(total, ACROSS)
         if chunk in early:
             total = tie(total, early[chunk])
+        if chunk == count - 3:
+            carried = move(groups[0], carried)
+            total = tie(total, carried[1])
         totals.append(total)
         backs.append(send(total, TO_ENDS))
-    carried = move(groups[0], carried)
-    for part in groups[1:]:
+    carried = move(groups[1], carried)
+    for part in groups[2:]:
         carried = move(part, carried)
     spread_v = next_spread_v
     flat_v = carried[0]

time: 694 us -> 680 us (0.980)
  local copies, waits for them, and re-layouts: 47.2 us -> 30.3 us
  waiting for transfers between devices: 439 us -> 427 us
  Pallas kernels: 59.1 us -> 70.4 us
    unnamed x42 -> x34, local copies, waits for them, and re-layouts: 20.1 us -> 3.17 us
    pallas_call x10 -> x12, Pallas kernels: 59.1 us -> 70.4 us  [run(): pl.pallas_call(kernel, grid_spec=pltpu.PrefetchScalarGridSpec(num_scalar_...]
    ppermute x38 -> x41, starting transfers between devices: 84.1 us -> 74 us  [send(): return lax.ppermute(value, axis, pairs)]
    ppermute x10, starting transfers between devices: 7.37 us -> 16.2 us  [sum_over_devices(): lax.ppermute(value, axis, [(i, i ^ step) for i in range(size)])]
    ppermute x38 -> x41, waiting for transfers between devices: 414 us -> 406 us  [send(): return lax.ppermute(value, axis, pairs)]
  transfers between devices with their start and end apart: 49 -> 52, of which waited for: 25 -> 28; matrix products, arithmetic and copies ran while one was open for 8% -> 8% of each run, Pallas kernels for 7% -> 9%
where the time goes in v12:
time: 680 us; the launch traced here: 678 us
  waiting for transfers between devices  427 us (63%)
  starting transfers between devices  97.8 us (14%)
  Pallas kernels  70.4 us (10%)
  other arithmetic  50.6 us (7%)
  local copies, waits for them, and re-layouts  30.3 us (4%)
    ppermute x41, waiting for transfers between devices, send(): return lax.ppermute(value, axis, pairs)  406 us
    ppermute x41, starting transfers between devices, send(): return lax.ppermute(value, axis, pairs)  74 us
    pallas_call x12, Pallas kernels, run(): pl.pallas_call(kernel, grid_spec=pltpu.PrefetchScalarGridSpec(num_scalar_...  70.4 us
    ppermute x10, waiting for transfers between devices, sum_over_devices(): lax.ppermute(value, axis, [(i, i ^ step) for i in range(size)])  21 us
    reduce_sum x4, other arithmetic, on_device(): square = jnp.sum(jnp.square(held[place] - v))  17.4 us
    ppermute x10, starting transfers between devices, sum_over_devices(): lax.ppermute(value, axis, [(i, i ^ step) for i in range(size)])  16.2 us
    dynamic_slice x3, local copies, waits for them, and re-layouts, line_rows(): lax.dynamic_slice(source, (worker * outers, cut, 0), (outers, rest, colum...  14.1 us
  transfers between devices with their start and end apart: 52, of which 28 were waited for; matrix products, arithmetic and copies ran while one was open for 8% of the time, Pallas kernels for 9%

profile of v12, /device:TPU:0, one launch (start us, length us, event | category | flops | bytes accessed | tf_op | source)
XLA Modules:
  0.0 677.5 jit_solution(13610683631684102334)
XLA Ops:
  0.0 11.5 %slice.28 = f32[16,96,2048]{2,1,0:T(8,128)} slice(f32[16,224,2048]{2,1,0:T(8,128)} %bitcast.62), slice={[0:16], [0:96], [0:2048]} | slice | bytes 25165824 | tf_op jit(solution)/shard_map/slice | solution.py:264
  11.5 7.6 %all-to-all-start = ((f32[16,96,2048]{2,1,0:T(8,128)}), f32[16,96,2048]{2,1,0:T(8,128)}, u32[]{:S(2)}, u32[]{:S(2)}) async-start(f32[16,96,2048]{2,1,0:T(8,128)} %slice.28), calls=%async_computation | async-start | bytes 25165824 | tf_op jit(solution)/shard_map/all_to_all | solution.py:263
  19.1 1.9 collective-permute-start
  21.1 4.7 constant_dynamic-slice_fusion.3
  25.8 4.7 constant_dynamic-slice_fusion.2
  30.5 4.7 constant_dynamic-slice_fusion.1
  35.2 1.6 collective-permute-start.6
  36.8 1.6 collective-permute-start.3
  38.4 206.6 %collective-permute-done = f32[128,2048]{1,0:T(8,128)} collective-permute-done((f32[128,2048]{1,0:T(8,128)S(1)}, f32[128,2048]{1,0:T(8,128)}, u32[]{:S(2)}, u32[]{:S(2)}) %collective-permute-start) | collective-permute-done | bytes 1048608 | tf_op jit(solution)/shard_map/ppermute | solution.py:37
  245.0 1.7 collective-permute-start.1
  246.6 1.6 collective-permute-start.7
  251.1 89.2 %collective-permute-done.4 = f32[128,2048]{1,0:T(8,128)} collective-permute-done((f32[128,2048]{1,0:T(8,128)}, f32[128,2048]{1,0:T(8,128)}, u32[]{:S(2)}, u32[]{:S(2)}) %collective-permute-start.4) | collective-permute-done | bytes 1048608 | tf_op jit(solution)/shard_map/ppermute | solution.py:37
  340.3 22.5 %collective-permute-done.2 = f32[128,2048]{1,0:T(8,128)} collective-permute-done((f32[128,2048]{1,0:T(8,128)}, f32[128,2048]{1,0:T(8,128)}, u32[]{:S(2)}, u32[]{:S(2)}) %collective-permute-start.2) | collective-permute-done | bytes 1048608 | tf_op jit(solution)/shard_map/ppermute | solution.py:37
  362.8 2.5 select_bitcast_fusion.3
  365.3 4.9 multiply_reduce_fusion.5
  370.9 4.7 multiply_reduce_fusion.4
  376.2 3.9 multiply_reduce_fusion.3
  380.8 3.9 multiply_reduce_fusion.2
  385.3 6.2 multiply_reduce_fusion.1
  394.1 2.1 collective-permute-done.9
  396.2 3.6 collective-permute-done.10
  400.9 3.4 collective-permute-done.11
  405.8 2.0 collective-permute-done.12
  409.4 2.5 shard_map.39
  411.9 1.9 collective-permute-start.22
  415.1 4.8 shard_map.40
  421.3 4.8 collective-permute-done.22
  426.9 6.6 collective-permute-start.24
  434.3 8.7 %collective-permute-done.16 = f32[64,2048]{1,0:T(8,128)S(1)} collective-permute-done((f32[64,2048]{1,0:T(8,128)S(1)}, f32[64,2048]{1,0:T(8,128)S(1)}, u32[]{:S(2)}, u32[]{:S(2)}) %collective-permute-start.16) | collective-permute-done | bytes 524320 | tf_op jit(solution)/shard_map/ppermute | solution.py:37
  443.7 10.9 %shard_map.41 = (f32[64,2048]{1,0:T(8,128)S(1)}, f32[64,2048]{1,0:T(8,128)S(1)}, f32[64,2048]{1,0:T(8,128)S(1)}, f32[64,2048]{1,0:T(8,128)S(1)}, f32[32,2048]{1,0:T(8,128)S(1)}) custom-call(f32[4]{0:T(128)S(1)} %select_reduce_fusion.2.factor, f32[512,2048]{1,0:T(8,128)} %bitcast.16.refs_0_, f32[512,2048]{1,0:T(8,128)} %bitcast.17.refs_1_, ...), custom_call_target="tpu_custom_call" | custom-call | flops 14155776 | bytes 14155776 | tf_op jit(solution)/shard_map/pallas_call | solution.py:66
  454.6 6.8 %collective-permute-start.15 = (f32[64,2048]{1,0:T(8,128)S(1)}, f32[64,2048]{1,0:T(8,128)S(1)}, u32[]{:S(2)}, u32[]{:S(2)}) collective-permute-start(f32[64,2048]{1,0:T(8,128)S(1)} %get-tuple-element.60), channel_id=1, source_target_pairs={{0,2},{6,4},{1,3},{7,5},{8,10},{14,12},{9,11},{15,13},{16,18},{22,... | collective-permute-start | bytes 1572872 | tf_op jit(solution)/shard_map/ppermute | solution.py:37
  462.2 3.6 collective-permute-start.33
  467.1 7.1 %shard_map.37 = (f32[96,2048]{1,0:T(8,128)S(1)}, f32[16,8,128]{2,1,0:T(8,128)S(1)}) custom-call(f32[16]{0:T(128)S(1)} %multiply_minimum_fusion.1.factor, f32[96,2048]{1,0:T(8,128)S(1)} %slice.22.v, f32[16,96,2048]{2,1,0:T(8,128)} %all-to-all-done.values), custom_call_target="tpu_custom_call" | custom-call | flops 14155776 | bytes 14155776 | tf_op jit(solution)/shard_map/pallas_call | solution.py:66
  476.6 8.0 %collective-permute-done.33 = f32[64,2048]{1,0:T(8,128)S(1)} collective-permute-done((f32[64,2048]{1,0:T(8,128)S(1)}, f32[64,2048]{1,0:T(8,128)S(1)}, u32[]{:S(2)}, u32[]{:S(2)}) %collective-permute-start.33) | collective-permute-done | bytes 524320 | tf_op jit(solution)/shard_map/ppermute | solution.py:37
  486.6 3.5 collective-permute-done.14
  491.5 4.3 collective-permute-done.32
  504.0 5.8 collective-permute-done.27.refs_9_
  510.6 4.0 collective-permute-start.13
  514.6 6.5 collective-permute-done.28.refs_10_
  522.4 9.9 %collective-permute-done.29.refs_11_ = f32[64,2048]{1,0:T(8,128)} collective-permute-done((f32[64,2048]{1,0:T(8,128)S(1)}, f32[64,2048]{1,0:T(8,128)}, u32[]{:S(2)}, u32[]{:S(2)}) %collective-permute-start.29) | collective-permute-done | bytes 524320 | tf_op jit(solution)/shard_map/ppermute | solution.py:37
  533.6 10.8 %shard_map.42 = (f32[512,2048]{1,0:T(8,128)}, f32[4,8,128]{2,1,0:T(8,128)}) custom-call(s32[1]{0:T(128)} %bitcast.14.is_end, f32[512,2048]{1,0:T(8,128)} %bitcast.41, f32[512,2048]{1,0:T(8,128)} %bitcast.16.refs_0_, f32[512,2048]{1,0:T(8,128)} %bitcast.17.refs_1_, f32[512,2048]{1,0:T(8,128)} %bitcast.18.refs_2_, f32[512,2048]{1,0:T(8,128)} %bitcast.50, ...), custom_call_target="tpu_custom_call" | custom-call | flops 14680064 | bytes 14680064 | tf_op jit(solution)/shard_map/pallas_call | solution.py:66
  552.7 2.1 collective-permute-done.39.refs_7_
  554.8 6.4 shard_map.43
  563.0 3.8 shard_map.44
  568.6 3.8 shard_map.45
  573.1 2.2 shard_map.46
  577.4 1.6 collective-permute-start.41
  579.0 1.9 collective-permute-done.41
  581.0 7.1 %collective-permute-start.42 = (f32[16]{0:T(128)S(1)}, f32[16]{0:T(128)S(1)}, u32[]{:S(2)}, u32[]{:S(2)}) collective-permute-start(f32[16]{0:T(128)S(1)} %add.199), channel_id=1, source_target_pairs={{0,2},{2,0},{4,6},{6,4},{1,3},{3,1},{5,7},{7,5},{8,10},{10,8},{12,... | collective-permute-start | bytes 200 | tf_op jit(solution)/shard_map/ppermute | solution.py:31
  589.7 2.4 collective-permute-start.43
  592.1 2.0 collective-permute-done.43
  595.7 2.0 collective-permute-done.44
  598.4 4.3 shard_map.47
  602.8 4.0 collective-permute-start.45
  607.4 12.6 %shard_map.48 = (f32[128,2048]{1,0:T(8,128)}, f32[128,2048]{1,0:T(8,128)}, f32[128,2048]{1,0:T(8,128)}) custom-call(s32[3]{0:T(128)} %pad_add_fusion.1.places, f32[4]{0:T(128)} %select_reduce_fusion.factor, f32[4,128,2048]{2,1,0:T(8,128)} %collective-permute-done.7.refs_0_, f32[4,128,2048]{2,1,0:T(8,128)} %collective-permute-done.6.refs_1_, ...), custom_call_target="tpu_custom_call" | custom-call | flops 18874368 | bytes 18874368 | tf_op jit(solution)/shard_map/pallas_call | solution.py:66
  619.9 2.3 collective-permute-start.49
  622.2 8.3 %collective-permute-done.45 = f32[128,2048]{1,0:T(8,128)S(1)} collective-permute-done((f32[128,2048]{1,0:T(8,128)}, f32[128,2048]{1,0:T(8,128)S(1)}, u32[]{:S(2)}, u32[]{:S(2)}) %collective-permute-start.45) | collective-permute-done | bytes 1048608 | tf_op jit(solution)/shard_map/ppermute | solution.py:37
  632.4 6.5 collective-permute-start.48
  638.9 14.1 %collective-permute-done.49 = f32[128,2048]{1,0:T(8,128)} collective-permute-done((f32[128,2048]{1,0:T(8,128)}, f32[128,2048]{1,0:T(8,128)}, u32[]{:S(2)}, u32[]{:S(2)}) %collective-permute-start.49) | collective-permute-done | bytes 1048608 | tf_op jit(solution)/shard_map/ppermute | solution.py:37
  653.0 1.7 add.209
  655.4 1.9 fusion.7
  658.6 6.4 multiply_reduce_fusion
  666.5 3.6 collective-permute-done.48
  670.1 6.2 collective-permute-done.47
  (147 shorter events, 61.4 us)
Async XLA Ops:
  11.5 373.8 %all-to-all-start = ((f32[16,96,2048]{2,1,0:T(8,128)}), f32[16,96,2048]{2,1,0:T(8,128)}, u32[]{:S(2)}, u32[]{:S(2)}) async-start(f32[16,96,2048]{2,1,0:T(8,128)} %slice.28), calls=%async_computation | async-start | bytes 25165824 | tf_op jit(solution)/shard_map/all_to_all | solution.py:263
  19.1 225.8 %collective-permute-start = (f32[128,2048]{1,0:T(8,128)S(1)}, f32[128,2048]{1,0:T(8,128)}, u32[]{:S(2)}, u32[]{:S(2)}) collective-permute-start(f32[128,2048]{1,0:T(8,128)S(1)} %slice.24), channel_id=1, source_target_pairs={{0,2},{2,0},{4,6},{6,4},{1,3},{3,1},{5,7},{7,5},{8,10},{10,8},{12,... | collective-permute-start | bytes 3145736 | tf_op jit(solution)/shard_map/ppermute | solution.py:37
  35.2 335.7 %collective-permute-start.5 = (f32[4,128,2048]{2,1,0:T(8,128)}, f32[4,128,2048]{2,1,0:T(8,128)}, u32[]{:S(2)}, u32[]{:S(2)}) collective-permute-start(f32[4,128,2048]{2,1,0:T(8,128)} %constant_dynamic-slice_fusion.1), channel_id=1, source_target_pairs={{0,8},{8,0},{16,24},{24,16},{1,9},{9,1},{17,25},{25,17},{2,10},{10... | collective-permute-start | bytes 12582920 | tf_op jit(solution)/shard_map/ppermute | solution.py:37
  35.2 341.0 %collective-permute-start.6 = (f32[4,128,2048]{2,1,0:T(8,128)}, f32[4,128,2048]{2,1,0:T(8,128)}, u32[]{:S(2)}, u32[]{:S(2)}) collective-permute-start(f32[4,128,2048]{2,1,0:T(8,128)} %constant_dynamic-slice_fusion.2), channel_id=1, source_target_pairs={{0,24},{8,16},{16,8},{24,0},{1,25},{9,17},{17,9},{25,1},{2,26},{10... | collective-permute-start | bytes 12582920 | tf_op jit(solution)/shard_map/ppermute | solution.py:37
  36.8 211.5 %collective-permute-start.3 = (f32[128,2048]{1,0:T(8,128)S(1)}, f32[128,2048]{1,0:T(8,128)}, u32[]{:S(2)}, u32[]{:S(2)}) collective-permute-start(f32[128,2048]{1,0:T(8,128)S(1)} %slice.24), channel_id=1, source_target_pairs={{2,4},{4,2},{3,5},{5,3},{10,12},{12,10},{11,13},{13,11},{18,20},{2... | collective-permute-start | bytes 3145736 | tf_op jit(solution)/shard_map/ppermute | solution.py:37
  245.0 4.6 collective-permute-start.1
  246.6 134.1 %collective-permute-start.7 = (f32[4,128,2048]{2,1,0:T(8,128)}, f32[4,128,2048]{2,1,0:T(8,128)}, u32[]{:S(2)}, u32[]{:S(2)}) collective-permute-start(f32[4,128,2048]{2,1,0:T(8,128)} %constant_dynamic-slice_fusion.3), channel_id=1, source_target_pairs={{0,16},{8,24},{16,0},{24,8},{1,17},{9,25},{17,1},{25,9},{2,18},{10... | collective-permute-start | bytes 12582920 | tf_op jit(solution)/shard_map/ppermute | solution.py:37
  248.3 92.0 %collective-permute-start.4 = (f32[128,2048]{1,0:T(8,128)}, f32[128,2048]{1,0:T(8,128)}, u32[]{:S(2)}, u32[]{:S(2)}) collective-permute-start(f32[128,2048]{1,0:T(8,128)} %collective-permute-done.3), channel_id=1, source_target_pairs={{2,0},{4,6},{3,1},{5,7},{10,8},{12,14},{11,9},{13,15},{18,16},{20,... | collective-permute-start | bytes 3145736 | tf_op jit(solution)/shard_map/ppermute | solution.py:37
  249.6 113.2 %collective-permute-start.2 = (f32[128,2048]{1,0:T(8,128)}, f32[128,2048]{1,0:T(8,128)}, u32[]{:S(2)}, u32[]{:S(2)}) collective-permute-start(f32[128,2048]{1,0:T(8,128)} %collective-permute-done.1), channel_id=1, source_target_pairs={{2,0},{4,6},{3,1},{5,7},{10,8},{12,14},{11,9},{13,15},{18,16},{20,... | collective-permute-start | bytes 3145736 | tf_op jit(solution)/shard_map/ppermute | solution.py:37
  370.2 10.6 %copy-start = (f32[4,128,2048]{2,1,0:T(8,128)}, f32[4,128,2048]{2,1,0:T(8,128)S(1)}, u32[]{:S(2)}) copy-start(f32[4,128,2048]{2,1,0:T(8,128)S(1)} %get-tuple-element.51) | copy-start | bytes 12582916
  385.3 22.8 %copy-start.1 = (f32[4,128,2048]{2,1,0:T(8,128)S(1)}, f32[4,128,2048]{2,1,0:T(8,128)}, u32[]{:S(2)}) copy-start(f32[4,128,2048]{2,1,0:T(8,128)} %copy-done) | copy-start | bytes 12582916
  385.3 22.7 %copy-start.2 = (f32[4,128,2048]{2,1,0:T(8,128)S(1)}, f32[4,128,2048]{2,1,0:T(8,128)}, u32[]{:S(2)}) copy-start(f32[4,128,2048]{2,1,0:T(8,128)} %get-tuple-element.88.refs_3_) | copy-start | bytes 12582916
  391.5 1.2 collective-permute-start.8
  392.7 3.6 collective-permute-start.9
  396.2 3.6 collective-permute-start.10
  399.8 4.5 collective-permute-start.11
  404.3 3.6 collective-permute-start.12
  411.9 14.2 %collective-permute-start.22 = (f32[64,2048]{1,0:T(8,128)S(1)}, f32[64,2048]{1,0:T(8,128)S(1)}, u32[]{:S(2)}, u32[]{:S(2)}) collective-permute-start(f32[64,2048]{1,0:T(8,128)S(1)} %shard_map.39), channel_id=1, source_target_pairs={{0,2},{6,4},{1,3},{7,5},{8,10},{14,12},{9,11},{15,13},{16,18},{22,... | collective-permute-start | bytes 1572872 | tf_op jit(solution)/shard_map/ppermute | solution.py:37
  413.8 19.7 %collective-permute-start.17 = (f32[32,2048]{1,0:T(8,128)S(1)}, f32[32,2048]{1,0:T(8,128)S(1)}, u32[]{:S(2)}, u32[]{:S(2)}) collective-permute-start(f32[32,2048]{1,0:T(8,128)S(1)} %shard_map.38), channel_id=1, source_target_pairs={{0,2},{6,4},{1,3},{7,5},{8,10},{14,12},{9,11},{15,13},{16,18},{22,... | collective-permute-start | bytes 786440 | tf_op jit(solution)/shard_map/ppermute | solution.py:37
  419.9 23.0 %collective-permute-start.16 = (f32[64,2048]{1,0:T(8,128)S(1)}, f32[64,2048]{1,0:T(8,128)S(1)}, u32[]{:S(2)}, u32[]{:S(2)}) collective-permute-start(f32[64,2048]{1,0:T(8,128)S(1)} %get-tuple-element.56), channel_id=1, source_target_pairs={{0,2},{6,4},{1,3},{7,5},{8,10},{14,12},{9,11},{15,13},{16,18},{22,... | collective-permute-start | bytes 1572872 | tf_op jit(solution)/shard_map/ppermute | solution.py:37
  426.2 35.2 %collective-permute-start.23 = (f32[64,2048]{1,0:T(8,128)S(1)}, f32[64,2048]{1,0:T(8,128)S(1)}, u32[]{:S(2)}, u32[]{:S(2)}) collective-permute-start(f32[64,2048]{1,0:T(8,128)S(1)} %add.187), channel_id=1, source_target_pairs={{2,4},{4,2},{3,5},{5,3},{10,12},{12,10},{11,13},{13,11},{18,20},{2... | collective-permute-start | bytes 1572872 | tf_op jit(solution)/shard_map/ppermute | solution.py:37
  426.9 34.6 %collective-permute-start.24 = (f32[64,2048]{1,0:T(8,128)S(1)}, f32[64,2048]{1,0:T(8,128)S(1)}, u32[]{:S(2)}, u32[]{:S(2)}) collective-permute-start(f32[64,2048]{1,0:T(8,128)S(1)} %get-tuple-element.65), channel_id=1, source_target_pairs={{0,2},{6,4},{1,3},{7,5},{8,10},{14,12},{9,11},{15,13},{16,18},{22,... | collective-permute-start | bytes 1572872 | tf_op jit(solution)/shard_map/ppermute | solution.py:37
  433.5 0.7 collective-permute-start.18
  434.3 51.1 %copy-start.10 = (f32[32,2048]{1,0:T(8,128)}, f32[32,2048]{1,0:T(8,128)S(1)}, u32[]{:S(2)}) copy-start(f32[32,2048]{1,0:T(8,128)S(1)} %add.180.refs_4_) | copy-start | bytes 786436
  443.0 31.2 %collective-permute-start.19 = (f32[64,2048]{1,0:T(8,128)S(1)}, f32[64,2048]{1,0:T(8,128)S(1)}, u32[]{:S(2)}, u32[]{:S(2)}) collective-permute-start(f32[64,2048]{1,0:T(8,128)S(1)} %add.181), channel_id=1, source_target_pairs={{2,4},{4,2},{3,5},{5,3},{10,12},{12,10},{11,13},{13,11},{18,20},{2... | collective-permute-start | bytes 1572872 | tf_op jit(solution)/shard_map/ppermute | solution.py:37
  454.6 21.1 %collective-permute-start.15 = (f32[64,2048]{1,0:T(8,128)S(1)}, f32[64,2048]{1,0:T(8,128)S(1)}, u32[]{:S(2)}, u32[]{:S(2)}) collective-permute-start(f32[64,2048]{1,0:T(8,128)S(1)} %get-tuple-element.60), channel_id=1, source_target_pairs={{0,2},{6,4},{1,3},{7,5},{8,10},{14,12},{9,11},{15,13},{16,18},{22,... | collective-permute-start | bytes 1572872 | tf_op jit(solution)/shard_map/ppermute | solution.py:37
  461.4 28.7 %copy-start.5 = (f32[64,2048]{1,0:T(8,128)}, f32[64,2048]{1,0:T(8,128)S(1)}, u32[]{:S(2)}) copy-start(f32[64,2048]{1,0:T(8,128)S(1)} %add.188.refs_5_) | copy-start | bytes 1572868
  461.5 15.0 %collective-permute-start.25 = (f32[64,2048]{1,0:T(8,128)S(1)}, f32[64,2048]{1,0:T(8,128)S(1)}, u32[]{:S(2)}, u32[]{:S(2)}) collective-permute-start(f32[64,2048]{1,0:T(8,128)S(1)} %add.189), channel_id=1, source_target_pairs={{2,4},{4,2},{3,5},{5,3},{10,12},{12,10},{11,13},{13,11},{18,20},{2... | collective-permute-start | bytes 1572872 | tf_op jit(solution)/shard_map/ppermute | solution.py:37
  462.2 22.3 %collective-permute-start.33 = (f32[64,2048]{1,0:T(8,128)S(1)}, f32[64,2048]{1,0:T(8,128)S(1)}, u32[]{:S(2)}, u32[]{:S(2)}) collective-permute-start(f32[64,2048]{1,0:T(8,128)S(1)} %get-tuple-element.71), channel_id=1, source_target_pairs={{0,2},{6,4},{1,3},{7,5},{8,10},{14,12},{9,11},{15,13},{16,18},{22,... | collective-permute-start | bytes 1572872 | tf_op jit(solution)/shard_map/ppermute | solution.py:37
  465.8 24.4 %collective-permute-start.14 = (f32[64,2048]{1,0:T(8,128)S(1)}, f32[64,2048]{1,0:T(8,128)S(1)}, u32[]{:S(2)}, u32[]{:S(2)}) collective-permute-start(f32[64,2048]{1,0:T(8,128)S(1)} %get-tuple-element.59), channel_id=1, source_target_pairs={{0,2},{6,4},{1,3},{7,5},{8,10},{14,12},{9,11},{15,13},{16,18},{22,... | collective-permute-start | bytes 1572872 | tf_op jit(solution)/shard_map/ppermute | solution.py:37
  474.3 21.5 %collective-permute-start.32 = (f32[64,2048]{1,0:T(8,128)S(1)}, f32[64,2048]{1,0:T(8,128)S(1)}, u32[]{:S(2)}, u32[]{:S(2)}) collective-permute-start(f32[64,2048]{1,0:T(8,128)S(1)} %get-tuple-element.70), channel_id=1, source_target_pairs={{0,2},{6,4},{1,3},{7,5},{8,10},{14,12},{9,11},{15,13},{16,18},{22,... | collective-permute-start | bytes 1572872 | tf_op jit(solution)/shard_map/ppermute | solution.py:37
  475.7 26.0 %copy-start.6 = (f32[64,2048]{1,0:T(8,128)}, f32[64,2048]{1,0:T(8,128)S(1)}, u32[]{:S(2)}) copy-start(f32[64,2048]{1,0:T(8,128)S(1)} %add.182.refs_6_) | copy-start | bytes 1572868
  475.8 21.3 %collective-permute-start.20 = (f32[64,2048]{1,0:T(8,128)S(1)}, f32[64,2048]{1,0:T(8,128)S(1)}, u32[]{:S(2)}, u32[]{:S(2)}) collective-permute-start(f32[64,2048]{1,0:T(8,128)S(1)} %add.183), channel_id=1, source_target_pairs={{2,4},{4,2},{3,5},{5,3},{10,12},{12,10},{11,13},{13,11},{18,20},{2... | collective-permute-start | bytes 1572872 | tf_op jit(solution)/shard_map/ppermute | solution.py:37
  476.6 57.1 %copy-start.7 = (f32[64,2048]{1,0:T(8,128)}, f32[64,2048]{1,0:T(8,128)S(1)}, u32[]{:S(2)}) copy-start(f32[64,2048]{1,0:T(8,128)S(1)} %add.190.refs_7_) | copy-start | bytes 1572868
  484.6 14.7 %collective-permute-start.34 = (f32[64,2048]{1,0:T(8,128)S(1)}, f32[64,2048]{1,0:T(8,128)S(1)}, u32[]{:S(2)}, u32[]{:S(2)}) collective-permute-start(f32[64,2048]{1,0:T(8,128)S(1)} %add.193), channel_id=1, source_target_pairs={{2,4},{4,2},{3,5},{5,3},{10,12},{12,10},{11,13},{13,11},{18,20},{2... | collective-permute-start | bytes 1572872 | tf_op jit(solution)/shard_map/ppermute | solution.py:37
  485.3 17.2 %collective-permute-start.26 = (f32[32,2048]{1,0:T(8,128)S(1)}, f32[32,2048]{1,0:T(8,128)S(1)}, u32[]{:S(2)}, u32[]{:S(2)}) collective-permute-start(f32[32,2048]{1,0:T(8,128)S(1)} %add.180.refs_4_), channel_id=1, source_target_pairs={{2,0},{4,6},{3,1},{5,7},{10,8},{12,14},{11,9},{13,15},{18,16},{20,... | collective-permute-start | bytes 786440 | tf_op jit(solution)/shard_map/ppermute | solution.py:37
  490.2 19.6 %collective-permute-start.27 = (f32[64,2048]{1,0:T(8,128)S(1)}, f32[64,2048]{1,0:T(8,128)S(1)}, u32[]{:S(2)}, u32[]{:S(2)}) collective-permute-start(f32[64,2048]{1,0:T(8,128)S(1)} %add.188.refs_5_), channel_id=1, source_target_pairs={{2,0},{4,6},{3,1},{5,7},{10,8},{12,14},{11,9},{13,15},{18,16},{20,... | collective-permute-start | bytes 1572872 | tf_op jit(solution)/shard_map/ppermute | solution.py:37
  495.8 25.3 %collective-permute-start.28 = (f32[64,2048]{1,0:T(8,128)S(1)}, f32[64,2048]{1,0:T(8,128)}, u32[]{:S(2)}, u32[]{:S(2)}) collective-permute-start(f32[64,2048]{1,0:T(8,128)S(1)} %add.182.refs_6_), channel_id=1, source_target_pairs={{2,0},{4,6},{3,1},{5,7},{10,8},{12,14},{11,9},{13,15},{18,16},{20,... | collective-permute-start | bytes 1572872 | tf_op jit(solution)/shard_map/ppermute | solution.py:37
  497.1 35.3 %collective-permute-start.29 = (f32[64,2048]{1,0:T(8,128)S(1)}, f32[64,2048]{1,0:T(8,128)}, u32[]{:S(2)}, u32[]{:S(2)}) collective-permute-start(f32[64,2048]{1,0:T(8,128)S(1)} %add.190.refs_7_), channel_id=1, source_target_pairs={{2,0},{4,6},{3,1},{5,7},{10,8},{12,14},{11,9},{13,15},{18,16},{20,... | collective-permute-start | bytes 1572872 | tf_op jit(solution)/shard_map/ppermute | solution.py:37
  499.3 45.2 %collective-permute-start.21 = (f32[64,2048]{1,0:T(8,128)S(1)}, f32[64,2048]{1,0:T(8,128)}, u32[]{:S(2)}, u32[]{:S(2)}) collective-permute-start(f32[64,2048]{1,0:T(8,128)S(1)} %add.185), channel_id=1, source_target_pairs={{2,4},{4,2},{3,5},{5,3},{10,12},{12,10},{11,13},{13,11},{18,20},{2... | collective-permute-start | bytes 1572872 | tf_op jit(solution)/shard_map/ppermute | solution.py:37
  502.5 31.1 %copy-start.15 = (f32[32,2048]{1,0:T(8,128)}, f32[32,2048]{1,0:T(8,128)S(1)}, u32[]{:S(2)}) copy-start(f32[32,2048]{1,0:T(8,128)S(1)} %collective-permute-done.26.refs_8_) | copy-start | bytes 786436
  502.6 44.4 %collective-permute-start.35 = (f32[64,2048]{1,0:T(8,128)}, f32[64,2048]{1,0:T(8,128)}, u32[]{:S(2)}, u32[]{:S(2)}) collective-permute-start(f32[64,2048]{1,0:T(8,128)} %add.195), channel_id=1, source_target_pairs={{2,4},{4,2},{3,5},{5,3},{10,12},{12,10},{11,13},{13,11},{18,20},{2... | collective-permute-start | bytes 1572872 | tf_op jit(solution)/shard_map/ppermute | solution.py:37
  510.6 38.9 %collective-permute-start.13 = (f32[32,2048]{1,0:T(8,128)S(1)}, f32[32,2048]{1,0:T(8,128)}, u32[]{:S(2)}, u32[]{:S(2)}) collective-permute-start(f32[32,2048]{1,0:T(8,128)S(1)} %get-tuple-element.58), channel_id=1, source_target_pairs={{0,2},{6,4},{1,3},{7,5},{8,10},{14,12},{9,11},{15,13},{16,18},{22,... | collective-permute-start | bytes 786440 | tf_op jit(solution)/shard_map/ppermute | solution.py:37
  521.1 31.6 %collective-permute-start.38 = (f32[64,2048]{1,0:T(8,128)}, f32[64,2048]{1,0:T(8,128)}, u32[]{:S(2)}, u32[]{:S(2)}) collective-permute-start(f32[64,2048]{1,0:T(8,128)} %add.184.refs_4_), channel_id=1, source_target_pairs={{2,0},{4,6},{3,1},{5,7},{10,8},{12,14},{11,9},{13,15},{18,16},{20,... | collective-permute-start | bytes 1572872 | tf_op jit(solution)/shard_map/ppermute | solution.py:37
  532.3 22.5 %collective-permute-start.39 = (f32[64,2048]{1,0:T(8,128)}, f32[64,2048]{1,0:T(8,128)}, u32[]{:S(2)}, u32[]{:S(2)}) collective-permute-start(f32[64,2048]{1,0:T(8,128)} %add.194.refs_5_), channel_id=1, source_target_pairs={{2,0},{4,6},{3,1},{5,7},{10,8},{12,14},{11,9},{13,15},{18,16},{20,... | collective-permute-start | bytes 1572872 | tf_op jit(solution)/shard_map/ppermute | solution.py:37
  545.6 15.6 %copy-start.9 = (f32[64,2048]{1,0:T(8,128)}, f32[64,2048]{1,0:T(8,128)S(1)}, u32[]{:S(2)}) copy-start(f32[64,2048]{1,0:T(8,128)S(1)} %add.186.refs_4_) | copy-start | bytes 1572868
  545.6 16.5 %collective-permute-start.37 = (f32[64,2048]{1,0:T(8,128)S(1)}, f32[64,2048]{1,0:T(8,128)S(1)}, u32[]{:S(2)}, u32[]{:S(2)}) collective-permute-start(f32[64,2048]{1,0:T(8,128)S(1)} %add.186.refs_4_), channel_id=1, source_target_pairs={{2,0},{4,6},{3,1},{5,7},{10,8},{12,14},{11,9},{13,15},{18,16},{20,... | collective-permute-start | bytes 1572872 | tf_op jit(solution)/shard_map/ppermute | solution.py:37
  548.2 13.1 %copy-start.8 = (f32[64,2048]{1,0:T(8,128)}, f32[64,2048]{1,0:T(8,128)S(1)}, u32[]{:S(2)}) copy-start(f32[64,2048]{1,0:T(8,128)S(1)} %add.196.refs_4_) | copy-start | bytes 1572868
  548.2 19.6 %collective-permute-start.36 = (f32[64,2048]{1,0:T(8,128)S(1)}, f32[64,2048]{1,0:T(8,128)S(1)}, u32[]{:S(2)}, u32[]{:S(2)}) collective-permute-start(f32[64,2048]{1,0:T(8,128)S(1)} %add.196.refs_4_), channel_id=1, source_target_pairs={{2,0},{4,6},{3,1},{5,7},{10,8},{12,14},{11,9},{13,15},{18,16},{20,... | collective-permute-start | bytes 1572872 | tf_op jit(solution)/shard_map/ppermute | solution.py:37
  550.5 0.7 collective-permute-start.30
  551.2 10.0 %copy-start.11 = (f32[32,2048]{1,0:T(8,128)}, f32[32,2048]{1,0:T(8,128)S(1)}, u32[]{:S(2)}) copy-start(f32[32,2048]{1,0:T(8,128)S(1)} %add.192.refs_4_) | copy-start | bytes 786436
  551.2 21.1 %collective-permute-start.31 = (f32[32,2048]{1,0:T(8,128)S(1)}, f32[32,2048]{1,0:T(8,128)S(1)}, u32[]{:S(2)}, u32[]{:S(2)}) collective-permute-start(f32[32,2048]{1,0:T(8,128)S(1)} %add.192.refs_4_), channel_id=1, source_target_pairs={{2,0},{4,6},{3,1},{5,7},{10,8},{12,14},{11,9},{13,15},{18,16},{20,... | collective-permute-start | bytes 786440 | tf_op jit(solution)/shard_map/ppermute | solution.py:37
  576.2 1.2 collective-permute-start.40
  577.4 3.6 collective-permute-start.41
  581.0 8.7 %collective-permute-start.42 = (f32[16]{0:T(128)S(1)}, f32[16]{0:T(128)S(1)}, u32[]{:S(2)}, u32[]{:S(2)}) collective-permute-start(f32[16]{0:T(128)S(1)} %add.199), channel_id=1, source_target_pairs={{0,2},{2,0},{4,6},{6,4},{1,3},{3,1},{5,7},{7,5},{8,10},{10,8},{12,... | collective-permute-start | bytes 200 | tf_op jit(solution)/shard_map/ppermute | solution.py:31
  589.7 4.5 collective-permute-start.43
  594.1 3.6 collective-permute-start.44
  602.8 27.8 %collective-permute-start.45 = (f32[128,2048]{1,0:T(8,128)}, f32[128,2048]{1,0:T(8,128)S(1)}, u32[]{:S(2)}, u32[]{:S(2)}) collective-permute-start(f32[128,2048]{1,0:T(8,128)} %shard_map.47), channel_id=1, source_target_pairs={{0,2},{6,4},{1,3},{7,5},{8,10},{14,12},{9,11},{15,13},{16,18},{22,... | collective-permute-start | bytes 3145736 | tf_op jit(solution)/shard_map/ppermute | solution.py:37
  607.4 23.2 %copy-start.4 = (f32[128,2048]{1,0:T(8,128)S(1)}, f32[128,2048]{1,0:T(8,128)}, u32[]{:S(2)}) copy-start(f32[128,2048]{1,0:T(8,128)} %shard_map.47) | copy-start | bytes 3145732
  619.9 33.1 %collective-permute-start.49 = (f32[128,2048]{1,0:T(8,128)}, f32[128,2048]{1,0:T(8,128)}, u32[]{:S(2)}, u32[]{:S(2)}) collective-permute-start(f32[128,2048]{1,0:T(8,128)} %get-tuple-element.86), channel_id=1, source_target_pairs={{0,2},{6,4},{1,3},{7,5},{8,10},{14,12},{9,11},{15,13},{16,18},{22,... | collective-permute-start | bytes 3145736 | tf_op jit(solution)/shard_map/ppermute | solution.py:37
  631.6 23.8 %collective-permute-start.46 = (f32[128,2048]{1,0:T(8,128)}, f32[128,2048]{1,0:T(8,128)S(1)}, u32[]{:S(2)}, u32[]{:S(2)}) collective-permute-start(f32[128,2048]{1,0:T(8,128)} %add.207), channel_id=1, source_target_pairs={{2,4},{4,2},{3,5},{5,3},{10,12},{12,10},{11,13},{13,11},{18,20},{2... | collective-permute-start | bytes 3145736 | tf_op jit(solution)/shard_map/ppermute | solution.py:37
  632.4 37.7 %collective-permute-start.48 = (f32[128,2048]{1,0:T(8,128)}, f32[128,2048]{1,0:T(8,128)S(1)}, u32[]{:S(2)}, u32[]{:S(2)}) collective-permute-start(f32[128,2048]{1,0:T(8,128)} %get-tuple-element.85), channel_id=1, source_target_pairs={{0,2},{6,4},{1,3},{7,5},{8,10},{14,12},{9,11},{15,13},{16,18},{22,... | collective-permute-start | bytes 3145736 | tf_op jit(solution)/shard_map/ppermute | solution.py:37
  654.7 15.4 %collective-permute-start.50 = (f32[128,2048]{1,0:T(8,128)S(1)}, f32[128,2048]{1,0:T(8,128)S(1)}, u32[]{:S(2)}, u32[]{:S(2)}) collective-permute-start(f32[128,2048]{1,0:T(8,128)S(1)} %add.209), channel_id=1, source_target_pairs={{2,4},{4,2},{3,5},{5,3},{10,12},{12,10},{11,13},{13,11},{18,20},{2... | collective-permute-start | bytes 3145736 | tf_op jit(solution)/shard_map/ppermute | solution.py:37
  657.3 19.0 %collective-permute-start.47 = (f32[128,2048]{1,0:T(8,128)S(1)}, f32[128,2048]{1,0:T(8,128)S(1)}, u32[]{:S(2)}, u32[]{:S(2)}) collective-permute-start(f32[128,2048]{1,0:T(8,128)S(1)} %get-tuple-element.96), channel_id=1, source_target_pairs={{2,0},{4,6},{3,1},{5,7},{10,8},{12,14},{11,9},{13,15},{18,16},{20,... | collective-permute-start | bytes 3145736 | tf_op jit(solution)/shard_map/ppermute | solution.py:37
  (5 other events, 10.7 us)

commit v13 on v12

--- a/solution.py
+++ b/solution.py
@@ -52,8 +52,8 @@
     units = rest * outers // UNIT
     if outers != LINE or rest % TILE or units < 22 or not cut:
         return None
-    body = units - 4
-    sizes = [2] + [4] * (body // 4) + [body % 4] * (body % 4 > 0) + [2]
+    body = units - 12
+    sizes = [2, 4] + [5] * (body // 5) + [body % 5] * (body % 5 > 0) + [4, 2]
     return cut, sizes
 
 
@@ -285,7 +285,7 @@
         return factor, jnp.sum(jnp.where(hit, factor[None], 0.0), axis=1)
 
     line_sq, v = jnp.zeros((worker_count,), jnp.float32), line_v
-    for place in reversed(range(workers)):
+    for place in [workers - 1, *range(workers // 2, workers - 1), *range(workers // 2)]:
         square = jnp.sum(jnp.square(held[place] - v))
         line_sq = lax.optimization_barrier(line_sq + jnp.where(hit[place], square, 0.0))
         v = tie(v, line_sq)
@@ -296,7 +296,7 @@
     flat_v = line_v.reshape(outers * rest, columns)
     end_flag = is_end.astype(jnp.int32).reshape(1)
     next_spread_v, spread_sq = move_spread(share, factor, spread, spread_v)
-    early = {2: next_spread_v}
+    early = {3: next_spread_v}
     count, places = len(sizes), begins(sizes)
     own = step_chunks(line_factor, flat, flat_v, 0, sizes[:1])
     own += step_chunks(line_factor, flat, tie(flat_v, own[0]), places[1], sizes[1:2])

time: 680 us -> 679 us (level)
  starting transfers between devices: 97.8 us -> 84.5 us
  waiting for transfers between devices: 427 us -> 440 us
    ppermute x41 -> x38, waiting for transfers between devices: 406 us -> 415 us  [send(): return lax.ppermute(value, axis, pairs)]
    ppermute x10, starting transfers between devices: 16.2 us -> 7.11 us  [sum_over_devices(): lax.ppermute(value, axis, [(i, i ^ step) for i in range(size)])]
    ppermute x41 -> x38, starting transfers between devices: 74 us -> 69.9 us  [send(): return lax.ppermute(value, axis, pairs)]
  transfers between devices with their start and end apart: 52 -> 49, of which waited for: 28 -> 23; matrix products, arithmetic and copies ran while one was open for 8% -> 8% of each run, Pallas kernels for 9% -> 9%
where the time goes in v13:
time: 679 us; the launch traced here: 676 us
  waiting for transfers between devices  440 us (65%)
  starting transfers between devices  84.5 us (12%)
  Pallas kernels  70.2 us (10%)
  other arithmetic  50.8 us (7%)
  local copies, waits for them, and re-layouts  28.6 us (4%)
    ppermute x38, waiting for transfers between devices, send(): return lax.ppermute(value, axis, pairs)  415 us
    pallas_call x12, Pallas kernels, run(): pl.pallas_call(kernel, grid_spec=pltpu.PrefetchScalarGridSpec(num_scalar_...  70.2 us
    ppermute x38, starting transfers between devices, send(): return lax.ppermute(value, axis, pairs)  69.9 us
    ppermute x10, waiting for transfers between devices, sum_over_devices(): lax.ppermute(value, axis, [(i, i ^ step) for i in range(size)])  24.9 us
    reduce_sum x4, other arithmetic, on_device(): square = jnp.sum(jnp.square(held[place] - v))  17.3 us
    dynamic_slice x3, local copies, waits for them, and re-layouts, line_rows(): lax.dynamic_slice(source, (worker * outers, cut, 0), (outers, rest, colum...  14.1 us
  transfers between devices with their start and end apart: 49, of which 23 were waited for; matrix products, arithmetic and copies ran while one was open for 8% of the time, Pallas kernels for 9%

profile of v13, /device:TPU:0, one launch (start us, length us, event | category | flops | bytes accessed | tf_op | source)
XLA Modules:
  0.0 676.0 jit_solution(18415703057177478798)
XLA Ops:
  0.0 11.5 %slice.28 = f32[16,96,2048]{2,1,0:T(8,128)} slice(f32[16,224,2048]{2,1,0:T(8,128)} %bitcast.62), slice={[0:16], [0:96], [0:2048]} | slice | bytes 25165824 | tf_op jit(solution)/shard_map/slice | solution.py:264
  11.5 7.6 %all-to-all-start = ((f32[16,96,2048]{2,1,0:T(8,128)}), f32[16,96,2048]{2,1,0:T(8,128)}, u32[]{:S(2)}, u32[]{:S(2)}) async-start(f32[16,96,2048]{2,1,0:T(8,128)} %slice.28), calls=%async_computation | async-start | bytes 25165824 | tf_op jit(solution)/shard_map/all_to_all | solution.py:263
  19.1 1.9 collective-permute-start
  21.1 4.7 constant_dynamic-slice_fusion.3
  25.8 4.7 constant_dynamic-slice_fusion.2
  30.5 4.7 constant_dynamic-slice_fusion.1
  35.2 1.5 collective-permute-start.6
  36.7 1.6 collective-permute-start.3
  38.3 206.7 %collective-permute-done = f32[128,2048]{1,0:T(8,128)} collective-permute-done((f32[128,2048]{1,0:T(8,128)S(1)}, f32[128,2048]{1,0:T(8,128)}, u32[]{:S(2)}, u32[]{:S(2)}) %collective-permute-start) | collective-permute-done | bytes 1048608 | tf_op jit(solution)/shard_map/ppermute | solution.py:37
  245.0 1.6 collective-permute-start.1
  250.3 90.0 %collective-permute-done.4 = f32[128,2048]{1,0:T(8,128)} collective-permute-done((f32[128,2048]{1,0:T(8,128)}, f32[128,2048]{1,0:T(8,128)}, u32[]{:S(2)}, u32[]{:S(2)}) %collective-permute-start.4) | collective-permute-done | bytes 1048608 | tf_op jit(solution)/shard_map/ppermute | solution.py:37
  340.3 22.5 %collective-permute-done.2 = f32[128,2048]{1,0:T(8,128)} collective-permute-done((f32[128,2048]{1,0:T(8,128)}, f32[128,2048]{1,0:T(8,128)}, u32[]{:S(2)}, u32[]{:S(2)}) %collective-permute-start.2) | collective-permute-done | bytes 1048608 | tf_op jit(solution)/shard_map/ppermute | solution.py:37
  362.8 2.5 select_bitcast_fusion.3
  365.3 4.9 multiply_reduce_fusion.5
  370.9 4.7 multiply_reduce_fusion.4
  376.2 3.9 multiply_reduce_fusion.3
  380.8 3.9 multiply_reduce_fusion.2
  385.3 6.2 multiply_reduce_fusion.1
  392.7 1.5 collective-permute-start.9
  394.1 2.1 collective-permute-done.9
  396.2 3.6 collective-permute-done.10
  400.9 3.4 collective-permute-done.11
  404.3 1.5 collective-permute-start.12
  405.8 2.0 collective-permute-done.12
  409.4 2.5 shard_map.39
  411.9 1.9 collective-permute-start.16
  413.8 5.9 shard_map.40
  423.8 20.8 %collective-permute-done.20 = f32[32,2048]{1,0:T(8,128)S(1)} collective-permute-done((f32[32,2048]{1,0:T(8,128)S(1)}, f32[32,2048]{1,0:T(8,128)S(1)}, u32[]{:S(2)}, u32[]{:S(2)}) %collective-permute-start.20) | collective-permute-done | bytes 262176 | tf_op jit(solution)/shard_map/ppermute | solution.py:37
  446.1 9.6 %shard_map.41 = (f32[80,2048]{1,0:T(8,128)S(1)}, f32[80,2048]{1,0:T(8,128)S(1)}, f32[64,2048]{1,0:T(8,128)S(1)}, f32[32,2048]{1,0:T(8,128)S(1)}) custom-call(f32[4]{0:T(128)S(1)} %select_reduce_fusion.2.factor, f32[512,2048]{1,0:T(8,128)} %bitcast.16.refs_0_, f32[512,2048]{1,0:T(8,128)} %bitcast.17.refs_1_, f32[512,2048]{1,0:T(8,128)} %bitcast.18.refs_2_, ...), custom_call_target="tpu_custom_call" | custom-call | flops 12582912 | bytes 12582912 | tf_op jit(solution)/shard_map/pallas_call | solution.py:66
  456.5 11.3 %collective-permute-start.30 = (f32[80,2048]{1,0:T(8,128)S(1)}, f32[80,2048]{1,0:T(8,128)S(1)}, u32[]{:S(2)}, u32[]{:S(2)}) collective-permute-start(f32[80,2048]{1,0:T(8,128)S(1)} %get-tuple-element.67), channel_id=1, source_target_pairs={{0,2},{6,4},{1,3},{7,5},{8,10},{14,12},{9,11},{15,13},{16,18},{22,... | collective-permute-start | bytes 1966088 | tf_op jit(solution)/shard_map/ppermute | solution.py:37
  469.5 3.6 collective-permute-start.14
  473.1 9.5 %collective-permute-done.30 = f32[80,2048]{1,0:T(8,128)S(1)} collective-permute-done((f32[80,2048]{1,0:T(8,128)S(1)}, f32[80,2048]{1,0:T(8,128)S(1)}, u32[]{:S(2)}, u32[]{:S(2)}) %collective-permute-start.30) | collective-permute-done | bytes 655392 | tf_op jit(solution)/shard_map/ppermute | solution.py:37
  483.5 6.7 collective-permute-start.29
  491.5 7.1 %shard_map.37 = (f32[96,2048]{1,0:T(8,128)S(1)}, f32[16,8,128]{2,1,0:T(8,128)S(1)}) custom-call(f32[16]{0:T(128)S(1)} %multiply_minimum_fusion.1.factor, f32[96,2048]{1,0:T(8,128)S(1)} %slice.22.v, f32[16,96,2048]{2,1,0:T(8,128)} %all-to-all-done.values), custom_call_target="tpu_custom_call" | custom-call | flops 14155776 | bytes 14155776 | tf_op jit(solution)/shard_map/pallas_call | solution.py:66
  499.7 1.5 collective-permute-start.19
  503.5 1.5 collective-permute-start.32
  506.3 16.4 %collective-permute-done.24.refs_7_ = f32[32,2048]{1,0:T(8,128)S(1)} collective-permute-done((f32[32,2048]{1,0:T(8,128)S(1)}, f32[32,2048]{1,0:T(8,128)S(1)}, u32[]{:S(2)}, u32[]{:S(2)}) %collective-permute-start.24) | collective-permute-done | bytes 262176 | tf_op jit(solution)/shard_map/ppermute | solution.py:37
  523.4 1.5 collective-permute-start.13
  527.5 8.7 %shard_map.42 = (f32[512,2048]{1,0:T(8,128)}, f32[4,8,128]{2,1,0:T(8,128)}) custom-call(s32[1]{0:T(128)} %bitcast.14.is_end, f32[512,2048]{1,0:T(8,128)} %bitcast.41, f32[512,2048]{1,0:T(8,128)} %bitcast.16.refs_0_, f32[512,2048]{1,0:T(8,128)} %bitcast.17.refs_1_, f32[512,2048]{1,0:T(8,128)} %bitcast.18.refs_2_, f32[512,2048]{1,0:T(8,128)} %bitcast.50, ...), custom_call_target="tpu_custom_call" | custom-call | flops 11534336 | bytes 11534336 | tf_op jit(solution)/shard_map/pallas_call | solution.py:66
  538.9 2.1 add.188.refs_4_
  544.6 14.0 %collective-permute-done.36.refs_7_ = f32[80,2048]{1,0:T(8,128)} collective-permute-done((f32[80,2048]{1,0:T(8,128)S(1)}, f32[80,2048]{1,0:T(8,128)}, u32[]{:S(2)}, u32[]{:S(2)}) %collective-permute-start.36) | collective-permute-done | bytes 655392 | tf_op jit(solution)/shard_map/ppermute | solution.py:37
  558.5 7.7 %shard_map.43 = (f32[512,2048]{1,0:T(8,128)}, f32[4,8,128]{2,1,0:T(8,128)}) custom-call(s32[1]{0:T(128)} %bitcast.14.is_end, f32[512,2048]{1,0:T(8,128)} %bitcast.42, f32[512,2048]{1,0:T(8,128)} %bitcast.16.refs_0_, f32[512,2048]{1,0:T(8,128)} %bitcast.17.refs_1_, f32[512,2048]{1,0:T(8,128)} %bitcast.18.refs_2_, ...), custom_call_target="tpu_custom_call", output_to_operand_aliasing={{0}: (10, {}), {1}: (11, {})} | custom-call | flops 10485760 | bytes 10485760 | tf_op jit(solution)/shard_map/pallas_call | solution.py:66
  566.3 1.9 collective-permute-done.34.refs_5_
  568.2 4.5 shard_map.44
  573.8 3.8 shard_map.45
  578.4 2.2 shard_map.46
  582.7 1.6 collective-permute-start.38
  584.4 1.9 collective-permute-done.38
  586.3 3.6 collective-permute-done.39
  590.4 4.0 collective-permute-done.40
  594.3 1.5 collective-permute-start.41
  595.9 2.0 collective-permute-done.41
  598.7 4.3 shard_map.47
  603.0 2.0 collective-permute-start.42
  605.6 12.5 %shard_map.48 = (f32[128,2048]{1,0:T(8,128)}, f32[128,2048]{1,0:T(8,128)}, f32[128,2048]{1,0:T(8,128)}) custom-call(s32[3]{0:T(128)} %pad_add_fusion.1.places, f32[4]{0:T(128)} %select_reduce_fusion.factor, f32[4,128,2048]{2,1,0:T(8,128)} %collective-permute-done.6.refs_0_, f32[4,128,2048]{2,1,0:T(8,128)} %collective-permute-done.7.refs_1_, ...), custom_call_target="tpu_custom_call" | custom-call | flops 18874368 | bytes 18874368 | tf_op jit(solution)/shard_map/pallas_call | solution.py:66
  618.1 2.3 collective-permute-start.46
  620.4 8.4 %collective-permute-done.42 = f32[128,2048]{1,0:T(8,128)S(1)} collective-permute-done((f32[128,2048]{1,0:T(8,128)}, f32[128,2048]{1,0:T(8,128)S(1)}, u32[]{:S(2)}, u32[]{:S(2)}) %collective-permute-start.42) | collective-permute-done | bytes 1048608 | tf_op jit(solution)/shard_map/ppermute | solution.py:37
  630.6 6.6 collective-permute-start.45
  637.2 14.1 %collective-permute-done.46 = f32[128,2048]{1,0:T(8,128)} collective-permute-done((f32[128,2048]{1,0:T(8,128)}, f32[128,2048]{1,0:T(8,128)}, u32[]{:S(2)}, u32[]{:S(2)}) %collective-permute-start.46) | collective-permute-done | bytes 1048608 | tf_op jit(solution)/shard_map/ppermute | solution.py:37
  651.2 1.7 add.201
  653.7 1.9 fusion.7
  656.8 6.4 multiply_reduce_fusion
  664.8 3.8 collective-permute-done.45
  668.6 6.1 collective-permute-done.44
  (131 shorter events, 46.1 us)
Async XLA Ops:
  11.5 7.6 %copy-start.3 = (f32[224,2048]{1,0:T(8,128)S(1)}, f32[224,2048]{1,0:T(8,128)}, u32[]{:S(2)}) copy-start(f32[224,2048]{1,0:T(8,128)} %param.4) | copy-start | bytes 5505028
  11.5 373.8 %all-to-all-start = ((f32[16,96,2048]{2,1,0:T(8,128)}), f32[16,96,2048]{2,1,0:T(8,128)}, u32[]{:S(2)}, u32[]{:S(2)}) async-start(f32[16,96,2048]{2,1,0:T(8,128)} %slice.28), calls=%async_computation | async-start | bytes 25165824 | tf_op jit(solution)/shard_map/all_to_all | solution.py:263
  19.1 225.8 %collective-permute-start = (f32[128,2048]{1,0:T(8,128)S(1)}, f32[128,2048]{1,0:T(8,128)}, u32[]{:S(2)}, u32[]{:S(2)}) collective-permute-start(f32[128,2048]{1,0:T(8,128)S(1)} %slice.24), channel_id=1, source_target_pairs={{0,2},{2,0},{4,6},{6,4},{1,3},{3,1},{5,7},{7,5},{8,10},{10,8},{12,... | collective-permute-start | bytes 3145736 | tf_op jit(solution)/shard_map/ppermute | solution.py:37
  35.2 335.7 %collective-permute-start.5 = (f32[4,128,2048]{2,1,0:T(8,128)}, f32[4,128,2048]{2,1,0:T(8,128)}, u32[]{:S(2)}, u32[]{:S(2)}) collective-permute-start(f32[4,128,2048]{2,1,0:T(8,128)} %constant_dynamic-slice_fusion.1), channel_id=1, source_target_pairs={{0,8},{8,0},{16,24},{24,16},{1,9},{9,1},{17,25},{25,17},{2,10},{10... | collective-permute-start | bytes 12582920 | tf_op jit(solution)/shard_map/ppermute | solution.py:37
  35.2 341.0 %collective-permute-start.6 = (f32[4,128,2048]{2,1,0:T(8,128)}, f32[4,128,2048]{2,1,0:T(8,128)}, u32[]{:S(2)}, u32[]{:S(2)}) collective-permute-start(f32[4,128,2048]{2,1,0:T(8,128)} %constant_dynamic-slice_fusion.3), channel_id=1, source_target_pairs={{0,16},{8,24},{16,0},{24,8},{1,17},{9,25},{17,1},{25,9},{2,18},{10... | collective-permute-start | bytes 12582920 | tf_op jit(solution)/shard_map/ppermute | solution.py:37
  36.7 210.7 %collective-permute-start.3 = (f32[128,2048]{1,0:T(8,128)S(1)}, f32[128,2048]{1,0:T(8,128)}, u32[]{:S(2)}, u32[]{:S(2)}) collective-permute-start(f32[128,2048]{1,0:T(8,128)S(1)} %slice.24), channel_id=1, source_target_pairs={{2,4},{4,2},{3,5},{5,3},{10,12},{12,10},{11,13},{13,11},{18,20},{2... | collective-permute-start | bytes 3145736 | tf_op jit(solution)/shard_map/ppermute | solution.py:37
  245.0 3.7 collective-permute-start.1
  246.6 134.1 %collective-permute-start.7 = (f32[4,128,2048]{2,1,0:T(8,128)}, f32[4,128,2048]{2,1,0:T(8,128)}, u32[]{:S(2)}, u32[]{:S(2)}) collective-permute-start(f32[4,128,2048]{2,1,0:T(8,128)} %constant_dynamic-slice_fusion.2), channel_id=1, source_target_pairs={{0,24},{8,16},{16,8},{24,0},{1,25},{9,17},{17,9},{25,1},{2,26},{10... | collective-permute-start | bytes 12582920 | tf_op jit(solution)/shard_map/ppermute | solution.py:37
  247.4 92.9 %collective-permute-start.4 = (f32[128,2048]{1,0:T(8,128)}, f32[128,2048]{1,0:T(8,128)}, u32[]{:S(2)}, u32[]{:S(2)}) collective-permute-start(f32[128,2048]{1,0:T(8,128)} %collective-permute-done.3), channel_id=1, source_target_pairs={{2,0},{4,6},{3,1},{5,7},{10,8},{12,14},{11,9},{13,15},{18,16},{20,... | collective-permute-start | bytes 3145736 | tf_op jit(solution)/shard_map/ppermute | solution.py:37
  248.7 114.1 %collective-permute-start.2 = (f32[128,2048]{1,0:T(8,128)}, f32[128,2048]{1,0:T(8,128)}, u32[]{:S(2)}, u32[]{:S(2)}) collective-permute-start(f32[128,2048]{1,0:T(8,128)} %collective-permute-done.1), channel_id=1, source_target_pairs={{2,0},{4,6},{3,1},{5,7},{10,8},{12,14},{11,9},{13,15},{18,16},{20,... | collective-permute-start | bytes 3145736 | tf_op jit(solution)/shard_map/ppermute | solution.py:37
  370.2 10.6 %copy-start = (f32[4,128,2048]{2,1,0:T(8,128)}, f32[4,128,2048]{2,1,0:T(8,128)S(1)}, u32[]{:S(2)}) copy-start(f32[4,128,2048]{2,1,0:T(8,128)S(1)} %get-tuple-element.49) | copy-start | bytes 12582916
  385.3 22.8 %copy-start.1 = (f32[4,128,2048]{2,1,0:T(8,128)S(1)}, f32[4,128,2048]{2,1,0:T(8,128)}, u32[]{:S(2)}) copy-start(f32[4,128,2048]{2,1,0:T(8,128)} %copy-done) | copy-start | bytes 12582916
  385.3 22.7 %copy-start.2 = (f32[4,128,2048]{2,1,0:T(8,128)S(1)}, f32[4,128,2048]{2,1,0:T(8,128)}, u32[]{:S(2)}) copy-start(f32[4,128,2048]{2,1,0:T(8,128)} %get-tuple-element.84.refs_3_) | copy-start | bytes 12582916
  391.5 1.2 collective-permute-start.8
  392.7 3.6 collective-permute-start.9
  396.2 3.6 collective-permute-start.10
  399.8 4.5 collective-permute-start.11
  404.3 3.6 collective-permute-start.12
  411.9 33.4 %collective-permute-start.16 = (f32[64,2048]{1,0:T(8,128)S(1)}, f32[64,2048]{1,0:T(8,128)S(1)}, u32[]{:S(2)}, u32[]{:S(2)}) collective-permute-start(f32[64,2048]{1,0:T(8,128)S(1)} %shard_map.39), channel_id=1, source_target_pairs={{0,2},{6,4},{1,3},{7,5},{8,10},{14,12},{9,11},{15,13},{16,18},{22,... | collective-permute-start | bytes 1572872 | tf_op jit(solution)/shard_map/ppermute | solution.py:37
  419.8 36.0 %collective-permute-start.22 = (f32[80,2048]{1,0:T(8,128)S(1)}, f32[80,2048]{1,0:T(8,128)S(1)}, u32[]{:S(2)}, u32[]{:S(2)}) collective-permute-start(f32[80,2048]{1,0:T(8,128)S(1)} %get-tuple-element.54), channel_id=1, source_target_pairs={{0,2},{6,4},{1,3},{7,5},{8,10},{14,12},{9,11},{15,13},{16,18},{22,... | collective-permute-start | bytes 1966088 | tf_op jit(solution)/shard_map/ppermute | solution.py:37
  421.1 23.5 %collective-permute-start.20 = (f32[32,2048]{1,0:T(8,128)S(1)}, f32[32,2048]{1,0:T(8,128)S(1)}, u32[]{:S(2)}, u32[]{:S(2)}) collective-permute-start(f32[32,2048]{1,0:T(8,128)S(1)} %shard_map.38), channel_id=1, source_target_pairs={{0,2},{6,4},{1,3},{7,5},{8,10},{14,12},{9,11},{15,13},{16,18},{22,... | collective-permute-start | bytes 786440 | tf_op jit(solution)/shard_map/ppermute | solution.py:37
  422.4 46.3 %collective-permute-start.15 = (f32[80,2048]{1,0:T(8,128)S(1)}, f32[80,2048]{1,0:T(8,128)S(1)}, u32[]{:S(2)}, u32[]{:S(2)}) collective-permute-start(f32[80,2048]{1,0:T(8,128)S(1)} %get-tuple-element.58), channel_id=1, source_target_pairs={{0,2},{6,4},{1,3},{7,5},{8,10},{14,12},{9,11},{15,13},{16,18},{22,... | collective-permute-start | bytes 1966088 | tf_op jit(solution)/shard_map/ppermute | solution.py:37
  444.6 11.0 %collective-permute-start.21 = (f32[32,2048]{1,0:T(8,128)S(1)}, f32[32,2048]{1,0:T(8,128)S(1)}, u32[]{:S(2)}, u32[]{:S(2)}) collective-permute-start(f32[32,2048]{1,0:T(8,128)S(1)} %add.179), channel_id=1, source_target_pairs={{2,4},{4,2},{3,5},{5,3},{10,12},{12,10},{11,13},{13,11},{18,20},{2... | collective-permute-start | bytes 786440 | tf_op jit(solution)/shard_map/ppermute | solution.py:37
  445.4 22.4 %collective-permute-start.17 = (f32[64,2048]{1,0:T(8,128)S(1)}, f32[64,2048]{1,0:T(8,128)S(1)}, u32[]{:S(2)}, u32[]{:S(2)}) collective-permute-start(f32[64,2048]{1,0:T(8,128)S(1)} %add.173), channel_id=1, source_target_pairs={{2,4},{4,2},{3,5},{5,3},{10,12},{12,10},{11,13},{13,11},{18,20},{2... | collective-permute-start | bytes 1572872 | tf_op jit(solution)/shard_map/ppermute | solution.py:37
  455.7 49.3 %copy-start.9 = (f32[32,2048]{1,0:T(8,128)}, f32[32,2048]{1,0:T(8,128)S(1)}, u32[]{:S(2)}) copy-start(f32[32,2048]{1,0:T(8,128)S(1)} %add.180.refs_4_) | copy-start | bytes 786436
  455.8 17.2 %collective-permute-start.23 = (f32[80,2048]{1,0:T(8,128)S(1)}, f32[80,2048]{1,0:T(8,128)S(1)}, u32[]{:S(2)}, u32[]{:S(2)}) collective-permute-start(f32[80,2048]{1,0:T(8,128)S(1)} %add.181), channel_id=1, source_target_pairs={{2,4},{4,2},{3,5},{5,3},{10,12},{12,10},{11,13},{13,11},{18,20},{2... | collective-permute-start | bytes 1966088 | tf_op jit(solution)/shard_map/ppermute | solution.py:37
  456.5 26.1 %collective-permute-start.30 = (f32[80,2048]{1,0:T(8,128)S(1)}, f32[80,2048]{1,0:T(8,128)S(1)}, u32[]{:S(2)}, u32[]{:S(2)}) collective-permute-start(f32[80,2048]{1,0:T(8,128)S(1)} %get-tuple-element.67), channel_id=1, source_target_pairs={{0,2},{6,4},{1,3},{7,5},{8,10},{14,12},{9,11},{15,13},{16,18},{22,... | collective-permute-start | bytes 1966088 | tf_op jit(solution)/shard_map/ppermute | solution.py:37
  468.8 29.8 %collective-permute-start.18 = (f32[80,2048]{1,0:T(8,128)S(1)}, f32[80,2048]{1,0:T(8,128)S(1)}, u32[]{:S(2)}, u32[]{:S(2)}) collective-permute-start(f32[80,2048]{1,0:T(8,128)S(1)} %add.175), channel_id=1, source_target_pairs={{2,4},{4,2},{3,5},{5,3},{10,12},{12,10},{11,13},{13,11},{18,20},{2... | collective-permute-start | bytes 1966088 | tf_op jit(solution)/shard_map/ppermute | solution.py:37
  469.5 29.2 %collective-permute-start.14 = (f32[80,2048]{1,0:T(8,128)S(1)}, f32[80,2048]{1,0:T(8,128)S(1)}, u32[]{:S(2)}, u32[]{:S(2)}) collective-permute-start(f32[80,2048]{1,0:T(8,128)S(1)} %get-tuple-element.57), channel_id=1, source_target_pairs={{0,2},{6,4},{1,3},{7,5},{8,10},{14,12},{9,11},{15,13},{16,18},{22,... | collective-permute-start | bytes 1966088 | tf_op jit(solution)/shard_map/ppermute | solution.py:37
  473.1 25.4 %copy-start.7 = (f32[80,2048]{1,0:T(8,128)}, f32[80,2048]{1,0:T(8,128)S(1)}, u32[]{:S(2)}) copy-start(f32[80,2048]{1,0:T(8,128)S(1)} %add.182.refs_6_) | copy-start | bytes 1966084
  482.8 19.7 %collective-permute-start.31 = (f32[80,2048]{1,0:T(8,128)S(1)}, f32[80,2048]{1,0:T(8,128)S(1)}, u32[]{:S(2)}, u32[]{:S(2)}) collective-permute-start(f32[80,2048]{1,0:T(8,128)S(1)} %add.185), channel_id=1, source_target_pairs={{2,4},{4,2},{3,5},{5,3},{10,12},{12,10},{11,13},{13,11},{18,20},{2... | collective-permute-start | bytes 1966088 | tf_op jit(solution)/shard_map/ppermute | solution.py:37
  483.5 19.1 %collective-permute-start.29 = (f32[64,2048]{1,0:T(8,128)S(1)}, f32[64,2048]{1,0:T(8,128)S(1)}, u32[]{:S(2)}, u32[]{:S(2)}) collective-permute-start(f32[64,2048]{1,0:T(8,128)S(1)} %get-tuple-element.66), channel_id=1, source_target_pairs={{0,2},{6,4},{1,3},{7,5},{8,10},{14,12},{9,11},{15,13},{16,18},{22,... | collective-permute-start | bytes 1572872 | tf_op jit(solution)/shard_map/ppermute | solution.py:37
  490.2 36.0 %collective-permute-start.26 = (f32[80,2048]{1,0:T(8,128)S(1)}, f32[80,2048]{1,0:T(8,128)}, u32[]{:S(2)}, u32[]{:S(2)}) collective-permute-start(f32[80,2048]{1,0:T(8,128)S(1)} %add.182.refs_6_), channel_id=1, source_target_pairs={{2,0},{4,6},{3,1},{5,7},{10,8},{12,14},{11,9},{13,15},{18,16},{20,... | collective-permute-start | bytes 1966088 | tf_op jit(solution)/shard_map/ppermute | solution.py:37
  498.7 37.5 %copy-start.5 = (f32[80,2048]{1,0:T(8,128)}, f32[80,2048]{1,0:T(8,128)S(1)}, u32[]{:S(2)}) copy-start(f32[80,2048]{1,0:T(8,128)S(1)} %add.176.refs_4_) | copy-start | bytes 1966084
  499.7 36.5 %collective-permute-start.19 = (f32[80,2048]{1,0:T(8,128)}, f32[80,2048]{1,0:T(8,128)}, u32[]{:S(2)}, u32[]{:S(2)}) collective-permute-start(f32[80,2048]{1,0:T(8,128)} %add.177), channel_id=1, source_target_pairs={{2,4},{4,2},{3,5},{5,3},{10,12},{12,10},{11,13},{13,11},{18,20},{2... | collective-permute-start | bytes 1966088 | tf_op jit(solution)/shard_map/ppermute | solution.py:37
  501.2 23.7 %collective-permute-start.25 = (f32[64,2048]{1,0:T(8,128)}, f32[64,2048]{1,0:T(8,128)}, u32[]{:S(2)}, u32[]{:S(2)}) collective-permute-start(f32[64,2048]{1,0:T(8,128)} %add.174.refs_5_), channel_id=1, source_target_pairs={{2,0},{4,6},{3,1},{5,7},{10,8},{12,14},{11,9},{13,15},{18,16},{20,... | collective-permute-start | bytes 1572872 | tf_op jit(solution)/shard_map/ppermute | solution.py:37
  502.6 33.6 %copy-start.6 = (f32[80,2048]{1,0:T(8,128)}, f32[80,2048]{1,0:T(8,128)S(1)}, u32[]{:S(2)}) copy-start(f32[80,2048]{1,0:T(8,128)S(1)} %add.186.refs_5_) | copy-start | bytes 1966084
  503.5 35.4 %collective-permute-start.32 = (f32[64,2048]{1,0:T(8,128)}, f32[64,2048]{1,0:T(8,128)}, u32[]{:S(2)}, u32[]{:S(2)}) collective-permute-start(f32[64,2048]{1,0:T(8,128)} %add.187), channel_id=1, source_target_pairs={{2,4},{4,2},{3,5},{5,3},{10,12},{12,10},{11,13},{13,11},{18,20},{2... | collective-permute-start | bytes 1572872 | tf_op jit(solution)/shard_map/ppermute | solution.py:37
  505.0 17.7 %collective-permute-start.24 = (f32[32,2048]{1,0:T(8,128)S(1)}, f32[32,2048]{1,0:T(8,128)S(1)}, u32[]{:S(2)}, u32[]{:S(2)}) collective-permute-start(f32[32,2048]{1,0:T(8,128)S(1)} %add.180.refs_4_), channel_id=1, source_target_pairs={{2,0},{4,6},{3,1},{5,7},{10,8},{12,14},{11,9},{13,15},{18,16},{20,... | collective-permute-start | bytes 786440 | tf_op jit(solution)/shard_map/ppermute | solution.py:37
  522.7 0.7 copy-start.12
  523.4 18.9 %collective-permute-start.13 = (f32[32,2048]{1,0:T(8,128)S(1)}, f32[32,2048]{1,0:T(8,128)S(1)}, u32[]{:S(2)}, u32[]{:S(2)}) collective-permute-start(f32[32,2048]{1,0:T(8,128)S(1)} %get-tuple-element.56), channel_id=1, source_target_pairs={{0,2},{6,4},{1,3},{7,5},{8,10},{14,12},{9,11},{15,13},{16,18},{22,... | collective-permute-start | bytes 786440 | tf_op jit(solution)/shard_map/ppermute | solution.py:37
  524.9 19.7 %collective-permute-start.35 = (f32[80,2048]{1,0:T(8,128)S(1)}, f32[80,2048]{1,0:T(8,128)}, u32[]{:S(2)}, u32[]{:S(2)}) collective-permute-start(f32[80,2048]{1,0:T(8,128)S(1)} %add.176.refs_4_), channel_id=1, source_target_pairs={{2,0},{4,6},{3,1},{5,7},{10,8},{12,14},{11,9},{13,15},{18,16},{20,... | collective-permute-start | bytes 1966088 | tf_op jit(solution)/shard_map/ppermute | solution.py:37
  526.2 32.3 %collective-permute-start.36 = (f32[80,2048]{1,0:T(8,128)S(1)}, f32[80,2048]{1,0:T(8,128)}, u32[]{:S(2)}, u32[]{:S(2)}) collective-permute-start(f32[80,2048]{1,0:T(8,128)S(1)} %add.186.refs_5_), channel_id=1, source_target_pairs={{2,0},{4,6},{3,1},{5,7},{10,8},{12,14},{11,9},{13,15},{18,16},{20,... | collective-permute-start | bytes 1966088 | tf_op jit(solution)/shard_map/ppermute | solution.py:37
  537.6 28.6 %copy-start.8 = (f32[80,2048]{1,0:T(8,128)}, f32[80,2048]{1,0:T(8,128)S(1)}, u32[]{:S(2)}) copy-start(f32[80,2048]{1,0:T(8,128)S(1)} %add.178.refs_4_) | copy-start | bytes 1966084
  537.6 30.6 %collective-permute-start.34 = (f32[80,2048]{1,0:T(8,128)S(1)}, f32[80,2048]{1,0:T(8,128)}, u32[]{:S(2)}, u32[]{:S(2)}) collective-permute-start(f32[80,2048]{1,0:T(8,128)S(1)} %add.178.refs_4_), channel_id=1, source_target_pairs={{2,0},{4,6},{3,1},{5,7},{10,8},{12,14},{11,9},{13,15},{18,16},{20,... | collective-permute-start | bytes 1966088 | tf_op jit(solution)/shard_map/ppermute | solution.py:37
  541.0 32.8 %collective-permute-start.33 = (f32[64,2048]{1,0:T(8,128)}, f32[64,2048]{1,0:T(8,128)}, u32[]{:S(2)}, u32[]{:S(2)}) collective-permute-start(f32[64,2048]{1,0:T(8,128)} %add.188.refs_4_), channel_id=1, source_target_pairs={{2,0},{4,6},{3,1},{5,7},{10,8},{12,14},{11,9},{13,15},{18,16},{20,... | collective-permute-start | bytes 1572872 | tf_op jit(solution)/shard_map/ppermute | solution.py:37
  542.3 0.7 collective-permute-start.27
  543.1 23.2 %copy-start.10 = (f32[32,2048]{1,0:T(8,128)}, f32[32,2048]{1,0:T(8,128)S(1)}, u32[]{:S(2)}) copy-start(f32[32,2048]{1,0:T(8,128)S(1)} %add.184.refs_4_) | copy-start | bytes 786436
  543.1 34.6 %collective-permute-start.28 = (f32[32,2048]{1,0:T(8,128)S(1)}, f32[32,2048]{1,0:T(8,128)S(1)}, u32[]{:S(2)}, u32[]{:S(2)}) collective-permute-start(f32[32,2048]{1,0:T(8,128)S(1)} %add.184.refs_4_), channel_id=1, source_target_pairs={{2,0},{4,6},{3,1},{5,7},{10,8},{12,14},{11,9},{13,15},{18,16},{20,... | collective-permute-start | bytes 786440 | tf_op jit(solution)/shard_map/ppermute | solution.py:37
  577.7 0.7 copy-start.11
  581.5 1.2 collective-permute-start.37
  582.7 3.6 collective-permute-start.38
  586.3 3.6 collective-permute-start.39
  589.9 4.5 collective-permute-start.40
  594.3 3.6 collective-permute-start.41
  603.0 25.8 %collective-permute-start.42 = (f32[128,2048]{1,0:T(8,128)}, f32[128,2048]{1,0:T(8,128)S(1)}, u32[]{:S(2)}, u32[]{:S(2)}) collective-permute-start(f32[128,2048]{1,0:T(8,128)} %shard_map.47), channel_id=1, source_target_pairs={{0,2},{6,4},{1,3},{7,5},{8,10},{14,12},{9,11},{15,13},{16,18},{22,... | collective-permute-start | bytes 3145736 | tf_op jit(solution)/shard_map/ppermute | solution.py:37
  605.6 23.2 %copy-start.4 = (f32[128,2048]{1,0:T(8,128)S(1)}, f32[128,2048]{1,0:T(8,128)}, u32[]{:S(2)}) copy-start(f32[128,2048]{1,0:T(8,128)} %shard_map.47) | copy-start | bytes 3145732
  618.1 33.1 %collective-permute-start.46 = (f32[128,2048]{1,0:T(8,128)}, f32[128,2048]{1,0:T(8,128)}, u32[]{:S(2)}, u32[]{:S(2)}) collective-permute-start(f32[128,2048]{1,0:T(8,128)} %get-tuple-element.82), channel_id=1, source_target_pairs={{0,2},{6,4},{1,3},{7,5},{8,10},{14,12},{9,11},{15,13},{16,18},{22,... | collective-permute-start | bytes 3145736 | tf_op jit(solution)/shard_map/ppermute | solution.py:37
  629.9 23.8 %collective-permute-start.43 = (f32[128,2048]{1,0:T(8,128)}, f32[128,2048]{1,0:T(8,128)S(1)}, u32[]{:S(2)}, u32[]{:S(2)}) collective-permute-start(f32[128,2048]{1,0:T(8,128)} %add.199), channel_id=1, source_target_pairs={{2,4},{4,2},{3,5},{5,3},{10,12},{12,10},{11,13},{13,11},{18,20},{2... | collective-permute-start | bytes 3145736 | tf_op jit(solution)/shard_map/ppermute | solution.py:37
  630.6 38.0 %collective-permute-start.45 = (f32[128,2048]{1,0:T(8,128)}, f32[128,2048]{1,0:T(8,128)S(1)}, u32[]{:S(2)}, u32[]{:S(2)}) collective-permute-start(f32[128,2048]{1,0:T(8,128)} %get-tuple-element.81), channel_id=1, source_target_pairs={{0,2},{6,4},{1,3},{7,5},{8,10},{14,12},{9,11},{15,13},{16,18},{22,... | collective-permute-start | bytes 3145736 | tf_op jit(solution)/shard_map/ppermute | solution.py:37
  652.9 15.7 %collective-permute-start.47 = (f32[128,2048]{1,0:T(8,128)S(1)}, f32[128,2048]{1,0:T(8,128)S(1)}, u32[]{:S(2)}, u32[]{:S(2)}) collective-permute-start(f32[128,2048]{1,0:T(8,128)S(1)} %add.201), channel_id=1, source_target_pairs={{2,4},{4,2},{3,5},{5,3},{10,12},{12,10},{11,13},{13,11},{18,20},{2... | collective-permute-start | bytes 3145736 | tf_op jit(solution)/shard_map/ppermute | solution.py:37
  655.5 19.2 %collective-permute-start.44 = (f32[128,2048]{1,0:T(8,128)S(1)}, f32[128,2048]{1,0:T(8,128)S(1)}, u32[]{:S(2)}, u32[]{:S(2)}) collective-permute-start(f32[128,2048]{1,0:T(8,128)S(1)} %get-tuple-element.92), channel_id=1, source_target_pairs={{2,0},{4,6},{3,1},{5,7},{10,8},{12,14},{11,9},{13,15},{18,16},{20,... | collective-permute-start | bytes 3145736 | tf_op jit(solution)/shard_map/ppermute | solution.py:37
